TPU v7x, 32 devices: a whole 2x2x4 slice. The times are simulated.
32 devices in a mesh: dp: 4 (over z), row: 2 (over core), col: 4 (over y, x).
Axes of the slice: x: 2, y: 2, z: 4, core: 2. Of those that a mesh axis runs over, the one named last changes fastest.
Arguments:
- block_input: bfloat16 [2048, 1024], P('dp', 'col'), may hold values from -6 to 6
- segments: int32 [2048], P('dp'), may hold values from 0 to 3, as said below
- positions: int32 [2048], P('dp'), may hold values from 0 to 1023, as said below
- attention_gain: float32 [1024], P('col'), may hold values from 0.25 to 1.75
- query_weight: bfloat16 [1024, 1024], P('col', 'row'), may hold values from -0.1875 to 0.1875
- key_weight: bfloat16 [1024, 512], P('col', 'row'), may hold values from -0.1875 to 0.1875
- value_weight: bfloat16 [1024, 512], P('col', 'row'), may hold values from -0.1875 to 0.1875
- query_gain: float32 [64], replicated, may hold values from 0.6 to 1.6
- key_gain: float32 [64], replicated, may hold values from 0.6 to 1.6
- output_weight: bfloat16 [1024, 1024], P('row', 'col'), may hold values from -0.75 to 0.75
- feedforward_gain: float32 [1024], P('col'), may hold values from 0.25 to 1.75
- gate_weight: bfloat16 [1024, 4608], P('col', 'row'), may hold values from -0.1875 to 0.1875
- up_weight: bfloat16 [1024, 4608], P('col', 'row'), may hold values from -0.1875 to 0.1875
- down_weight: bfloat16 [4608, 1024], P('row', 'col'), may hold values from -0.1875 to 0.1875
- cotangent: bfloat16 [2048, 1024], P('dp', 'col'), may hold values from -6 to 6
Outputs:
- block_output: bfloat16 [2048, 1024], P('dp', 'col')
- input_grad: float32 [2048, 1024], P('dp', 'col')
- attention_gain_grad: float32 [1024], P(('col', 'dp'))
- query_weight_grad: float32 [1024, 1024], P(('col', 'dp'), 'row')
- key_weight_grad: float32 [1024, 512], P(('col', 'dp'), 'row')
- value_weight_grad: float32 [1024, 512], P(('col', 'dp'), 'row')
- query_gain_grad: float32 [64], replicated
- key_gain_grad: float32 [64], replicated
- output_weight_grad: float32 [1024, 1024], P('row', ('col', 'dp'))
- feedforward_gain_grad: float32 [1024], P(('col', 'dp'))
- gate_weight_grad: float32 [1024, 4608], P(('col', 'dp'), 'row')
- up_weight_grad: float32 [1024, 4608], P(('col', 'dp'), 'row')
- down_weight_grad: float32 [4608, 1024], P('row', ('col', 'dp'))
Inputs may be any that keep to these rules, and one draw needn't show every extreme that they name: `segments`: a document is a run of consecutive tokens that may run across sequences; whole documents have max(2, 200) to min(2000, 1024) tokens; the first document is cut at its start and may be shorter, the second has the most, the last may be cut, and a fourth document always begins; documents are numbered 0, 1, 2, 3, 0, 1, ... in order, so tokens of one sequence share a number exactly when they belong to one document. `positions`: the number of earlier tokens of the same document, counted across sequences and including tokens of a cut first document that lie before the first token.
All inputs are finite; a program needn't handle non-finite values.
Results may differ from a plain program's by a relative error of at most 0.017.
Values may be sent and summed in bfloat16 or wider, within the bound.
No kernel may reach another device: no remote copies, remote signals or barrier semaphores. Data moves between devices by JAX's collectives and lax.ppermute only.
A program may use at most 128 MiB of HBM per device.

v0:
```python
import jax
import jax.numpy as jnp
from jax import lax
from jax.experimental import pallas as pl
from jax.experimental.pallas import tpu as pltpu
from jax.sharding import PartitionSpec as P


EPSILON = 1e-05
THETA = 1000000.0
NEGATIVE = -1e30


F32 = jnp.float32
BF16 = jnp.bfloat16


def matmul(left, right):
    return jnp.dot(left, right, preferred_element_type=F32)


def matmul_nt(left, right):
    return lax.dot_general(left, right, (((1,), (1,)), ((), ())), preferred_element_type=F32)


def matmul_tn(left, right):
    return lax.dot_general(left, right, (((0,), (0,)), ((), ())), preferred_element_type=F32)


def flip(values, axis, distance):
    size = lax.axis_size(axis)
    return lax.ppermute(values, axis, [(i, i ^ distance) for i in range(size)])


def spread(values):
    return [values] + [flip(values, "col", k) for k in range(1, lax.axis_size("col"))]


def exchange(pieces):
    return [pieces[0]] + [flip(pieces[k], "col", k) for k in range(1, len(pieces))]


def total(parts):
    result = parts[0].astype(F32)
    for part in parts[1:]:
        result = result + part.astype(F32)
    return result


def kernel_call(kernel, outs, *args, scalars=None, scratch=()):
    specs = [pl.BlockSpec(memory_space=pltpu.VMEM)] * len(args)
    if scalars is not None:
        args = (scalars,) + args
        specs = [pl.BlockSpec(memory_space=pltpu.SMEM)] + specs
    return pl.pallas_call(
        kernel,
        out_shape=[jax.ShapeDtypeStruct(shape, dtype) for shape, dtype in outs],
        in_specs=specs,
        out_specs=[pl.BlockSpec(memory_space=pltpu.VMEM)] * len(outs),
        scratch_shapes=[pltpu.VMEM(shape, dtype) for shape, dtype in scratch],
        compiler_params=pltpu.CompilerParams(vmem_limit_bytes=48 * 1024 * 1024),
    )(*args)


def pack_one_kernel(where, x, gains, query, key, value, *outs):
    row, col = where[0], where[1]
    half = x.shape[0] // 2
    cols = len(outs)
    q_size, kv_size = query.shape[1] // cols, key.shape[1] // cols
    line = lax.broadcasted_iota(jnp.int32, (16, x.shape[1]), 0)
    rows = jnp.zeros((16, x.shape[1]), F32)
    for g in range(2):
        rest = gains[g : g + 1, :]
        for p in range(3):
            part = rest.astype(BF16).astype(F32)
            rows = jnp.where(line == 3 * g + p, part, rows)
            rest = rest - part
    mine = x[pl.ds(pl.multiple_of(row * half, half), half), :]
    for k, out in enumerate(outs):
        block = col ^ k
        out[:half, :] = mine
        out[half : half + 16, :] = rows.astype(BF16)
        out[half + 16 :, :q_size] = query[:, pl.ds(pl.multiple_of(block * q_size, q_size), q_size)]
        pair = pl.multiple_of((block >> 1) * (2 * kv_size), 2 * kv_size)
        odd = (block & 1) == 1
        both = []
        for weight in (key, value):
            two = weight[:, pl.ds(pair, 2 * kv_size)]
            both.append(jnp.where(odd, two[:, kv_size:], two[:, :kv_size]))
        out[half + 16 :, q_size:] = jnp.concatenate(both, axis=1)


def pack_two_kernel(where, weight, cot, *outs):
    row, col = where[0], where[1]
    half = cot.shape[0] // 2
    cols = len(outs)
    size = weight.shape[0] // cols
    for k, out in enumerate(outs):
        for j in range(cols):
            source = pl.multiple_of((col ^ (k ^ j)) * size, size)
            out[j * size : (j + 1) * size, :] = weight[pl.ds(source, size), :]
        out[cols * size :, :] = cot[pl.ds(pl.multiple_of(row * half, half), half), :]


def pack_gate_kernel(where, gate, up, *outs):
    col, odd_plane = where[1], (where[2] & 1) == 1
    cols = len(outs) - 1
    size = gate.shape[1] // cols

    def piece(weight, block):
        two = weight[:, pl.ds(pl.multiple_of((block >> 1) * (2 * size), 2 * size), 2 * size)]
        return jnp.where((block & 1) == 1, two[:, size:], two[:, :size])

    @pl.when(jnp.logical_not(odd_plane))
    def _():
        for k in range(cols):
            outs[k][...] = piece(gate, col ^ k)
        outs[cols][...] = piece(up, col)

    @pl.when(odd_plane)
    def _():
        for k in range(cols):
            outs[k][...] = piece(up, col ^ k)
        outs[cols][...] = piece(gate, col)


def join_kernel(first0, first1, first2, first3, ready, out):
    part = first0.shape[1]
    for k, piece in enumerate((first0, first1, first2, first3)):
        out[:, k * part : (k + 1) * part] = piece[...]


def forward_kernel(
    where, mine, other, context_near, context_far, joined, joined_far,
    near0, near1, near2, near3, far0, far1, far2, far3, first0, first1, first2, first3,
    normed_out, gate_out, up_out, hidden_out, own_out, share_out, sum_scratch,
):
    buffers = (first0, first1, first2, first3)
    half, part = mine.shape[0], near0.shape[0]
    size = context_near.shape[1]
    share = share_out.shape[0]
    top = mine[...].astype(F32) + matmul(context_near[:half, :], joined[:size, :])
    top = top + matmul(context_far[half:, :], joined_far[:size, :])
    low = other[...].astype(F32) + matmul(context_near[half:, :], joined[:size, :])
    low = low + matmul(context_far[:half, :], joined_far[:size, :])
    sum_scratch[...] = top
    own_out[...] = top[:, :part]
    share_out[...] = sum_scratch[pl.ds(pl.multiple_of(where[1] * share, share), share), :]
    gain = jnp.concatenate([gain_row(buffers, half + 3, k) for k in range(len(buffers))], axis=1)
    first_pre = second_pre = None
    for i, rows in enumerate((top, low)):
        root = lax.rsqrt(jnp.mean(rows * rows, axis=1, keepdims=True) + EPSILON)
        normed_out[i * half : (i + 1) * half, :] = (rows * root * gain).astype(BF16)
    for k, (near, far) in enumerate(
        ((near0, far0), (near1, far1), (near2, far2), (near3, far3))
    ):
        block = normed_out[:, k * part : (k + 1) * part]
        one, two = matmul(block, near[...]), matmul(block, far[...])
        first_pre = one if k == 0 else first_pre + one
        second_pre = two if k == 0 else second_pre + two
    even = (where[2] & 1) == 0
    gate_pre = jnp.where(even, first_pre, second_pre)
    up_pre = jnp.where(even, second_pre, first_pre)
    gate_out[...] = gate_pre
    up_out[...] = up_pre
    hidden_out[...] = (gate_pre * (1.0 / (1.0 + jnp.exp(-gate_pre))) * up_pre).astype(BF16)


def backward_kernel(
    where, joined, joined_far, gate_in, up_in, down0, down1, down2, down3,
    near0, near1, near2, near3, far0, far1, far2, far3,
    gate_grad_out, up_grad_out, mine_out, other_out,
):
    half, part = mine_out.shape[0], near0.shape[0]
    start = joined.shape[0] - half
    parts = []
    for rows in (joined, joined_far):
        grad = None
        for k, down in enumerate((down0, down1, down2, down3)):
            term = matmul_nt(rows[start:, k * part : (k + 1) * part], down[...])
            grad = term if k == 0 else grad + term
        parts.append(grad)
    hidden_grad = jnp.concatenate(parts, axis=0)
    gate_pre, up_pre = gate_in[...], up_in[...]
    sigmoid_gate = 1.0 / (1.0 + jnp.exp(-gate_pre))
    gate_grad = (
        hidden_grad * up_pre * sigmoid_gate * (1.0 + gate_pre * (1.0 - sigmoid_gate))
    ).astype(BF16)
    up_grad = (hidden_grad * (gate_pre * sigmoid_gate)).astype(BF16)
    gate_grad_out[...] = gate_grad
    up_grad_out[...] = up_grad
    even = (where[2] & 1) == 0
    near_grad = jnp.where(even, gate_grad, up_grad)
    far_grad = jnp.where(even, up_grad, gate_grad)
    for k, (near, far) in enumerate(
        ((near0, far0), (near1, far1), (near2, far2), (near3, far3))
    ):
        block = matmul_nt(near_grad, near[...]) + matmul_nt(far_grad, far[...])
        mine_out[:, k * part : (k + 1) * part] = block[:half].astype(BF16)
        other_out[:, k * part : (k + 1) * part] = block[half:].astype(BF16)


def result_kernel(hidden, down0, down1, down2, down3, mine_out, other_out):
    half, part = mine_out.shape[0], down0.shape[1]
    for k, down in enumerate((down0, down1, down2, down3)):
        block = matmul(hidden[...], down[...])
        mine_out[:, k * part : (k + 1) * part] = block[:half].astype(BF16)
        other_out[:, k * part : (k + 1) * part] = block[half:].astype(BF16)


def deal(where, scratch, k, send, keep, rows):
    for j in range(2):
        for out, m in ((send, 1 + 2 * j), (keep, 2 * j)):
            start = pl.multiple_of((where[2] ^ m) * rows, rows)
            out[j, k, :rows, :] = scratch[pl.ds(start, rows), :]


def weight_grad_kernel(
    where, joined, joined_far, hidden, normed, gate_grad, up_grad,
    down_send, gate_send, up_send, down_keep, gate_keep, up_keep, scratch,
):
    half = hidden.shape[0] // 2
    start = joined.shape[0] - half
    cols = down_send.shape[1]
    part = joined.shape[1] // cols
    rows = down_send.shape[2]
    for k in range(cols):
        span = slice(k * part, (k + 1) * part)
        grad = matmul_tn(joined[start:, span], hidden[:half, :])
        grad = grad + matmul_tn(joined_far[start:, span], hidden[half:, :])
        scratch[...] = grad.astype(BF16)
        deal(where, scratch, k, down_send, down_keep, rows)
    for upstream, send, keep in ((gate_grad, gate_send, gate_keep), (up_grad, up_send, up_keep)):
        for k in range(cols):
            span = slice(k * part, (k + 1) * part)
            scratch[...] = matmul_tn(normed[:, span], upstream[...]).astype(BF16)
            deal(where, scratch, k, send, keep, rows)


def pack_tokens_kernel(where, ours, came, out0, out1, out2, out3, scratch):
    outs = (out0, out1, out2, out3)
    share, part = out0.shape[0], out0.shape[1] // len(outs)
    scratch[...] = (ours[...].astype(F32) + came[...].astype(F32)).astype(BF16)
    for k, out in enumerate(outs):
        rows = pl.ds(pl.multiple_of((where[1] ^ k) * share, share), share)
        for j in range(len(outs)):
            source = k ^ j
            out[:, j * part : (j + 1) * part] = scratch[rows, source * part : (source + 1) * part]


def second_norm_kernel(
    where, came0, came1, came2, came3, sums, joined, first0, first1, first2, first3,
    out0, out1, out2, out3, gain_out,
):
    buffers = (first0, first1, first2, first3)
    outs = (out0, out1, out2, out3)
    share, part = out0.shape[0], out0.shape[1] // len(outs)
    half = share * len(outs)
    grad = came0[...].astype(F32) + came1[...].astype(F32)
    grad = grad + came2[...].astype(F32) + came3[...].astype(F32)
    gain = jnp.concatenate([gain_row(buffers, half + 3, k) for k in range(len(buffers))], axis=1)
    rows = sums[...]
    root = lax.rsqrt(jnp.mean(rows * rows, axis=1, keepdims=True) + EPSILON)
    normal = rows * root
    weighted = grad * gain
    gain_out[...] = jnp.sum(grad * normal, axis=0, keepdims=True)
    inner = jnp.mean(weighted * normal, axis=1, keepdims=True)
    start = pl.multiple_of(joined.shape[0] - half + where[1] * share, share)
    cot = joined[pl.ds(start, share), :].astype(F32)
    first = (cot + root * (weighted - normal * inner)).astype(BF16)
    for k, out in enumerate(outs):
        for j in range(len(outs)):
            source = k ^ j
            out[:, j * part : (j + 1) * part] = first[:, source * part : (source + 1) * part]


def join_tokens_kernel(where, came0, came1, came2, came3, out):
    share = came0.shape[0]
    for k, came in enumerate((came0, came1, came2, came3)):
        out[pl.ds(pl.multiple_of((where[1] ^ k) * share, share), share), :] = came[...]


def pack_features_kernel(ours, came, out0, out1, out2, out3):
    part = out0.shape[1]
    for k, out in enumerate((out0, out1, out2, out3)):
        span = slice(k * part, (k + 1) * part)
        out[...] = (ours[:, span].astype(F32) + came[:, span].astype(F32)).astype(BF16)


def pack_last_kernel(ours, came, inner, inner_came, out0, out1, out2, out3):
    half, part = ours.shape[0], out0.shape[1]
    line = lax.broadcasted_iota(jnp.int32, (16, part), 0)
    rows = jnp.zeros((16, part), F32)
    rest = inner[0:1, :half] + inner_came[0:1, :]
    for p in range(3):
        piece = rest.astype(BF16).astype(F32)
        rows = jnp.where(line == p, piece, rows)
        rest = rest - piece
    for k, out in enumerate((out0, out1, out2, out3)):
        span = slice(k * part, (k + 1) * part)
        out[:half, :] = (ours[:, span].astype(F32) + came[:, span].astype(F32)).astype(BF16)
        out[half:, :] = rows.astype(BF16)


def lane_is_first(size):
    return lax.broadcasted_iota(jnp.int32, (1, 2 * size), 1) < size


def head_scale(values, first):
    size = values.shape[1] // 2
    squares = values * values
    left = jnp.sum(jnp.where(first, squares, 0.0), axis=1, keepdims=True)
    right = jnp.sum(jnp.where(first, 0.0, squares), axis=1, keepdims=True)
    return lax.rsqrt(jnp.where(first, left, right) / size + EPSILON)


def turn(values, cosine, sine):
    width = values.shape[1]
    quarter = width // 4
    lane = lax.broadcasted_iota(jnp.int32, (1, width), 1)
    low = (lane & quarter) == 0
    other = jnp.where(
        low, pltpu.roll(values, width - quarter, 1), pltpu.roll(values, quarter, 1)
    )
    return values * cosine + other * sine


def root_and_input(mine, other):
    rows = jnp.concatenate([mine[...], other[...]], axis=0).astype(F32)
    mean = jnp.mean(rows * rows, axis=1, keepdims=True)
    return rows, lax.rsqrt(mean + EPSILON)


def gain_row(buffers, start, k):
    rows = buffers[k][start : start + 16, :].astype(F32)
    return rows[0:1] + rows[1:2] + rows[2:3]


def allowed_of(down, across):
    return (across[0:1, :] <= down[:, 0:1]) & (across[1:2, :] == down[:, 1:2])


def attend_kernel(
    mine, other, first0, first1, first2, first3, cosine, sine, gains, down, across,
    qkv_out, turned_out, context_out, log_out,
):
    buffers = (first0, first1, first2, first3)
    half, part = mine.shape[0], first0.shape[1]
    rows, root = root_and_input(mine, other)
    start = half + 16
    qkv = None
    for k, buffer in enumerate(buffers):
        block = rows[:, k * part : (k + 1) * part] * root * gain_row(buffers, half, k)
        term = matmul(block.astype(BF16), buffer[start:, :])
        qkv = term if qkv is None else qkv + term
    qkv_out[...] = qkv
    two = qkv.shape[1] // 2
    size = two // 2
    first = lane_is_first(size)
    query, pair = qkv[:, :two], qkv[:, two:]
    query_turned = turn(
        query * head_scale(query, first) * gains[0:1, :], cosine[...], sine[...]
    ).astype(BF16)
    key_turned = turn(pair * head_scale(pair, first) * gains[1:2, :], cosine[...], sine[...])
    pair_rounded = jnp.where(first, key_turned, pair).astype(BF16)
    turned_out[:, :two] = query_turned
    turned_out[:, two:] = pair_rounded
    key, value = pair_rounded[:, :size], pair_rounded[:, size:]
    allowed = allowed_of(down, across)
    contexts, logs = [], []
    for h in range(2):
        raw = matmul_nt(query_turned[:, h * size : (h + 1) * size], key)
        scores = jnp.where(allowed, raw * size ** (-0.5), NEGATIVE)
        top = jnp.max(scores, axis=1, keepdims=True)
        powers = jnp.exp(scores - top)
        sums = jnp.sum(powers, axis=1, keepdims=True)
        prob = (powers * (1.0 / sums)).astype(BF16)
        contexts.append(matmul(prob, value))
        logs.append(top + jnp.log(sums))
    context_out[...] = jnp.concatenate(contexts, axis=1).astype(BF16)
    log_out[...] = jnp.where(first, logs[0], logs[1])


def attend_back_kernel(
    where, mine, other, first0, first1, first2, first3, cosine, sine, gains, down, across,
    qkv_in, turned, context_in, logs, grad_mine, grad_other, out_weight,
    gain_in, one_mine, one_other, inner_out, mixed_send, mixed_keep, mixed,
):
    buffers = (first0, first1, first2, first3)
    half, part = mine.shape[0], first0.shape[1]
    two = context_in.shape[1]
    size = two // 2
    first = lane_is_first(size)
    upstream = jnp.concatenate([grad_mine[...], grad_other[...]], axis=0)
    context = context_in[...]
    context_grad = matmul_nt(upstream, out_weight[:two, :]).astype(BF16)
    key, value = turned[:, two : two + size], turned[:, two + size :]
    allowed = allowed_of(down, across)
    products = context_grad.astype(F32) * context.astype(F32)
    query_grads = []
    key_grad = value_grad = None
    for h in range(2):
        query = turned[:, h * size : (h + 1) * size]
        grad = context_grad[:, h * size : (h + 1) * size]
        raw = matmul_nt(query, key)
        scores = jnp.where(allowed, raw * size ** (-0.5), NEGATIVE)
        prob = jnp.exp(scores - logs[:, h * size : h * size + 1])
        delta = jnp.sum(
            jnp.where(first if h == 0 else jnp.logical_not(first), products, 0.0),
            axis=1,
            keepdims=True,
        )
        value_term = matmul_tn(prob.astype(BF16), grad)
        score_grad = (prob * (matmul_nt(grad, value) - delta) * size ** (-0.5)).astype(BF16)
        query_grads.append(matmul(score_grad, key))
        key_term = matmul_tn(score_grad, query)
        key_grad = key_term if h == 0 else key_grad + key_term
        value_grad = value_term if h == 0 else value_grad + value_term
    pieces, head_parts = [], []
    for i, grad in enumerate(
        (jnp.concatenate(query_grads, axis=1), jnp.concatenate([key_grad, value_grad], axis=1))
    ):
        normed = turn(grad, cosine[...], -sine[...])
        proj = qkv_in[:, i * two : (i + 1) * two]
        scale = head_scale(proj, first)
        hat = proj * scale
        weighted = normed * gains[i : i + 1, :]
        product = weighted * hat
        left = jnp.sum(jnp.where(first, product, 0.0), axis=1, keepdims=True)
        right = jnp.sum(jnp.where(first, 0.0, product), axis=1, keepdims=True)
        inner = jnp.where(first, left, right) / size
        result = scale * (weighted - hat * inner)
        pieces.append(result if i == 0 else jnp.where(first, result, grad))
        head_parts.append(jnp.sum(normed * hat, axis=0, keepdims=True))
    head_line = head_parts[0] + pltpu.roll(head_parts[0], size, 1)
    head_line = jnp.where(first, head_line, pltpu.roll(head_parts[1], size, 1))
    rows_here = mixed_send.shape[2] - 16
    line = lax.broadcasted_iota(jnp.int32, (16, part), 0)
    qkv_grad = jnp.concatenate(pieces, axis=1).astype(BF16)
    rows, root = root_and_input(mine, other)
    inner_sum = jnp.zeros((2 * half, 1), F32)
    for k, buffer in enumerate(buffers):
        span = slice(k * part, (k + 1) * part)
        gain = gain_row(buffers, half, k)
        hat = rows[:, span] * root
        grad = matmul_nt(qkv_grad, buffer[half + 16 :, :])
        product = grad * hat
        lines = jnp.where(line == 0, jnp.sum(product, axis=0, keepdims=True), 0.0)
        lines = jnp.where(line == 1, gain_in[:, span], lines).astype(BF16)
        inner_sum = inner_sum + jnp.sum(product * gain, axis=1, keepdims=True)
        one_mine[:, span] = grad[:half].astype(BF16)
        one_other[:, span] = grad[half:].astype(BF16)
        mixed[:, : 2 * two] = matmul_tn((hat * gain).astype(BF16), qkv_grad).astype(BF16)
        mixed[:, 2 * two :] = matmul_tn(upstream[:, span], context).astype(BF16)
        heads = jnp.broadcast_to(head_line, (16, two)).astype(BF16)
        if mixed_send.shape[0] == 2:
            deal(where, mixed, k, mixed_send, mixed_keep, rows_here)
            for out in (mixed_send, mixed_keep):
                for j in range(2):
                    out[j, k, rows_here:, : 2 * two] = lines
                    out[j, k, rows_here:, 2 * two :] = heads
        else:
            mixed_send[k, ...] = mixed[...]
            mixed_keep[k, :, : 2 * two] = lines
            mixed_keep[k, :, 2 * two :] = heads
    wide = jnp.broadcast_to(inner_sum / (part * len(buffers)), (2 * half, 128))
    inner_out[...] = jnp.transpose(wide)[:8, :]


def rope_tables(places, head_size):
    half_size = head_size // 2
    frequency = THETA ** (-(jnp.arange(half_size).astype(F32) * 2.0 / head_size))
    angles = places.astype(F32)[:, None] * frequency[None, :]
    return (jnp.cos(angles), jnp.sin(angles))


def body(
    block_input,
    segments,
    positions,
    attention_gain,
    query_weight,
    key_weight,
    value_weight,
    query_gain,
    key_gain,
    output_weight,
    feedforward_gain,
    gate_weight,
    up_weight,
    down_weight,
    cotangent,
):
    tokens = block_input.shape[0]
    part = block_input.shape[1]
    head = query_gain.shape[0]
    cols = lax.axis_size("col")
    planes = lax.axis_size("dp")
    width = part * cols
    half = tokens // 2
    row = lax.axis_index("row")
    col = lax.axis_index("col")
    plane = lax.axis_index("dp")
    kin = [col ^ k for k in range(cols)]

    def mine_first(values):
        return jnp.where(row == 0, values, jnp.roll(values, half, axis=0))

    def natural(values):
        return jnp.where(row == 0, values, jnp.roll(values, half, axis=0))

    def both_rows(values):
        return jnp.concatenate([values, flip(values, "row", 1)], axis=0)

    def chosen(blocks):
        stacked = jnp.stack(blocks)
        return [lax.dynamic_index_in_dim(stacked, kin[k], 0, keepdims=False) for k in range(cols)]

    def row_blocks(weight):
        size = weight.shape[0] // cols
        return [lax.dynamic_slice_in_dim(weight, kin[k] * size, size, 0) for k in range(cols)]

    q_size = query_weight.shape[1] // cols
    units = gate_weight.shape[1] // cols
    where = jnp.stack([row, col, plane]).astype(jnp.int32)
    shapes = [((half + 16 + part, part), BF16)] * cols
    first_in = exchange(
        kernel_call(
            pack_one_kernel,
            shapes,
            block_input,
            jnp.stack([attention_gain, feedforward_gain]),
            query_weight,
            key_weight,
            value_weight,
            scalars=where,
        ),
    )
    input_mine = jnp.concatenate([v[:half] for v in first_in], axis=1)
    gain_parts = jnp.concatenate([v[half : half + 16] for v in first_in], axis=1).astype(F32)
    gain_one = gain_parts[0] + gain_parts[1] + gain_parts[2]
    input_other = flip(input_mine, "row", 1)
    gate_in = kernel_call(
        pack_gate_kernel,
        [((part, units), BF16)] * (cols + 1),
        gate_weight,
        up_weight,
        scalars=where,
    )
    near_parts = exchange(gate_in[:cols])
    far_parts = [gate_in[cols]] + [flip(v, "dp", 1) for v in near_parts[1:]]
    second_parts = exchange(
        kernel_call(
            pack_two_kernel,
            [((output_weight.shape[0] + half, part), BF16)] * cols,
            output_weight,
            cotangent,
            scalars=where,
        ),
    )
    down_parts = exchange(row_blocks(down_weight))

    segment_ids = mine_first(segments)
    places = mine_first(positions)
    index = mine_first(jnp.arange(tokens))

    cosine, sine_part = rope_tables(places, head)
    group = q_size // head
    cos_lanes = jnp.concatenate([cosine] * (2 * group), axis=1)
    sin_lanes = jnp.concatenate([-sine_part, sine_part] * group, axis=1)
    head_gains = jnp.stack([jnp.tile(query_gain, group), jnp.tile(key_gain, group)])
    down = jnp.stack([index, segment_ids], axis=1)
    across = jnp.stack([index, segment_ids])
    common = (
        input_mine,
        input_other,
        *first_in,
        cos_lanes,
        sin_lanes,
        head_gains,
        down,
        across,
    )
    qkv, turned, context, logs = kernel_call(
        attend_kernel,
        [
            ((tokens, 2 * q_size), F32),
            ((tokens, 2 * q_size), BF16),
            ((tokens, q_size), BF16),
            ((tokens, q_size), F32),
        ],
        *common,
    )

    context_parts = spread(context)
    (second_in,) = kernel_call(
        join_kernel,
        [((output_weight.shape[0] + half, width), BF16)],
        *second_parts,
        context,
    )
    (context_near,) = kernel_call(
        join_kernel, [((tokens, output_weight.shape[0]), BF16)], *context_parts, context
    )
    second_far = flip(second_in, "row", 1)
    context_far = flip(context_near, "row", 1)

    share = half // cols
    normed_two, gate_pre, up_pre, hidden, first_block, first_share = kernel_call(
        forward_kernel,
        [
            ((tokens, width), BF16),
            ((tokens, units), F32),
            ((tokens, units), F32),
            ((tokens, units), BF16),
            ((half, part), F32),
            ((share, width), F32),
        ],
        input_mine,
        input_other,
        context_near,
        context_far,
        second_in,
        second_far,
        *near_parts,
        *far_parts,
        *first_in,
        scalars=where,
        scratch=[((half, width), F32)],
    )
    gate_grad, up_grad, two_mine, two_other = kernel_call(
        backward_kernel,
        [((tokens, units), BF16)] * 2 + [((half, width), BF16)] * 2,
        second_in,
        second_far,
        gate_pre,
        up_pre,
        *down_parts,
        *near_parts,
        *far_parts,
        scalars=where,
    )

    two_came = flip(two_other, "row", 1)
    two_pieces = kernel_call(
        pack_tokens_kernel,
        [((share, width), BF16)] * cols,
        two_mine,
        two_came,
        scalars=where,
        scratch=[((half, width), BF16)],
    )
    two_in = exchange(two_pieces)
    *first_pieces, feedforward_part = kernel_call(
        second_norm_kernel,
        [((share, width), BF16)] * cols + [((1, width), F32)],
        *two_in,
        first_share,
        second_in,
        *first_in,
        scalars=where,
    )
    (first_half,) = kernel_call(
        join_tokens_kernel,
        [((half, width), BF16)],
        *exchange(first_pieces),
        scalars=where,
    )
    first_other = flip(first_half, "row", 1)

    def summed(send, keep):
        came = flip(send, "dp", 1)
        rest = (keep[1].astype(F32) + came[1].astype(F32)).astype(BF16)
        far = flip(rest, "dp", 2)
        return total([keep[0], came[0], far]).astype(BF16)

    def scattered(split):
        return lax.psum_scatter(split, "dp", scatter_dimension=0, tiled=True)[0]

    def arranged(pieces):
        return [v.astype(F32) for v in chosen(exchange(pieces))]

    rows = part // planes
    if planes == 4:
        dealt = kernel_call(
            weight_grad_kernel,
            [((2, cols, rows, units), BF16)] * 6,
            second_in,
            second_far,
            hidden,
            normed_two,
            gate_grad,
            up_grad,
            scalars=where,
            scratch=[((part, units), BF16)],
        )
        sums = [summed(dealt[i], dealt[i + 3]) for i in range(3)]
    else:
        cot_all = jnp.concatenate([second_in[-half:], second_far[-half:]], axis=0)
        sums = [
            scattered(
                jnp.moveaxis(grad.astype(BF16).reshape(cols, planes, rows, units), 1, 0)
            )
            for grad in (
                matmul_tn(cot_all, hidden),
                matmul_tn(normed_two, gate_grad),
                matmul_tn(normed_two, up_grad),
            )
        ]
    shares = arranged([jnp.concatenate([v[k] for v in sums], axis=0) for k in range(cols)])
    down_share, gate_share, up_share = [
        jnp.concatenate([v[i * rows : (i + 1) * rows] for v in shares], axis=1) for i in range(3)
    ]

    result_mine, result_other = kernel_call(
        result_kernel, [((half, width), BF16)] * 2, hidden, *down_parts
    )
    result_came = flip(result_other, "row", 1)
    result_pieces = kernel_call(
        pack_features_kernel, [((half, part), BF16)] * cols, result_mine, result_came
    )
    result_in = exchange(result_pieces)
    result_mine = (first_block + total(result_in)).astype(BF16)
    block_output = natural(both_rows(result_mine))

    mixed_size = 3 * q_size
    if planes == 4:
        mixed_outs = [((2, cols, rows + 16, mixed_size), BF16)] * 2
    else:
        mixed_outs = [((cols, part, mixed_size), BF16), ((cols, 16, mixed_size), BF16)]
    one_mine, one_other, inner_part, mixed_first, mixed_second = kernel_call(
        attend_back_kernel,
        [((half, width), BF16), ((half, width), BF16), ((8, tokens), F32)] + mixed_outs,
        *common,
        qkv,
        turned,
        context,
        logs,
        first_half,
        first_other,
        second_in,
        feedforward_part,
        scalars=where,
        scratch=[((part, mixed_size), BF16)],
    )
    one_came = flip(one_other, "row", 1)
    inner_came = flip(inner_part[:, half:], "row", 1)
    one_pieces = kernel_call(
        pack_last_kernel,
        [((half + 16, part), BF16)] * cols,
        one_mine,
        one_came,
        inner_part,
        inner_came,
    )
    one_in = exchange(one_pieces)
    one_grad = total([v[:half] for v in one_in])
    inner_one = jnp.sum(total([v[half:] for v in one_in])[:3], axis=0)[:, None]
    weighted_one = one_grad * gain_one[:part]
    own_input = input_mine.astype(F32)
    root_one = lax.rsqrt(jnp.mean(own_input * own_input, axis=1, keepdims=True) + EPSILON)
    normal_one = own_input[:, :part] * root_one
    input_mine_grad = first_half[:, :part].astype(F32) + root_one * (
        weighted_one - normal_one * inner_one
    )
    input_grad = natural(both_rows(input_mine_grad))

    if planes == 4:
        mixed_sum = summed(mixed_first, mixed_second)
    else:
        lines = jnp.broadcast_to(mixed_second[:, None], (cols, planes, 16, mixed_size))
        blocks = mixed_first.reshape(cols, planes, rows, mixed_size)
        mixed_sum = scattered(jnp.moveaxis(jnp.concatenate([blocks, lines], axis=2), 1, 0))
    mixed_share = arranged([mixed_sum[k] for k in range(cols)])
    kv_start = q_size + head
    query_share = jnp.concatenate([v[:rows, :q_size] for v in mixed_share], axis=1)
    key_share = jnp.concatenate([v[:rows, q_size:kv_start] for v in mixed_share], axis=1)
    value_share = jnp.concatenate(
        [v[:rows, kv_start : kv_start + head] for v in mixed_share], axis=1
    )
    output_share = jnp.concatenate([v[:rows, kv_start + head :] for v in mixed_share], axis=1)
    gain_sums = total([v[rows : rows + 8] for v in mixed_share])
    gain_sums = gain_sums + flip(gain_sums, "row", 1)
    attention_share = lax.dynamic_slice_in_dim(gain_sums[0], plane * rows, rows, 0)
    feedforward_share = lax.dynamic_slice_in_dim(gain_sums[1], plane * rows, rows, 0)
    query_gain_grad = gain_sums[0, 2 * q_size : 2 * q_size + head]
    key_gain_grad = gain_sums[0, 2 * q_size + head :]
    return (
        block_output,
        input_grad,
        attention_share,
        query_share,
        key_share,
        value_share,
        query_gain_grad,
        key_gain_grad,
        output_share.T,
        feedforward_share,
        gate_share,
        up_share,
        down_share.T,
    )


def solution(mesh):
    placed = (
        P("dp", "col"),
        P("dp"),
        P("dp"),
        P("col"),
        P("col", "row"),
        P("col", "row"),
        P("col", "row"),
        P(),
        P(),
        P("row", "col"),
        P("col"),
        P("col", "row"),
        P("col", "row"),
        P("row", "col"),
        P("dp", "col"),
    )

    return jax.shard_map(
        body,
        mesh=mesh,
        in_specs=placed,
        out_specs=(
            P("dp", "col"),
            P("dp", "col"),
            P(("col", "dp")),
            P(("col", "dp"), "row"),
            P(("col", "dp"), "row"),
            P(("col", "dp"), "row"),
            P(),
            P(),
            P("row", ("col", "dp")),
            P(("col", "dp")),
            P(("col", "dp"), "row"),
            P(("col", "dp"), "row"),
            P("row", ("col", "dp")),
        ),
        check_vma=False,
    )
```

profile of v0, /device:TPU:0, one launch (start us, length us, event | category | flops | bytes accessed | tf_op | source)
XLA Modules:
  0.0 262.3 jit_solution(554119285600915128)
XLA Ops:
  6.2 3.0 %collective-permute-start = (bf16[528,256]{1,0:T(8,128)(2,1)S(1)}, bf16[528,256]{1,0:T(8,128)(2,1)S(1)}, u32[]{:S(2)}, u32[]{:S(2)}) collective-permute-start(bf16[528,256]{1,0:T(8,128)(2,1)S(1)} %get-tuple-element.71), channel_id=1, source_target_pairs={{0,1},{1,0},{2,3},{3,2},{4,5},{5,4},{6,7},{7,6},{8,9},{9,8},{10,11... | collective-permute-start | bytes 811016 | tf_op jit(solution)/shard_map/ppermute | solution.py:32
  15.1 2.9 %collective-permute-start.10 = (bf16[768,256]{1,0:T(8,128)(2,1)}, bf16[768,256]{1,0:T(8,128)(2,1)S(1)}, u32[]{:S(2)}, u32[]{:S(2)}) collective-permute-start(bf16[768,256]{1,0:T(8,128)(2,1)} %get-tuple-element.78), channel_id=1, source_target_pairs={{0,3},{1,2},{2,1},{3,0},{4,7},{5,6},{6,5},{7,4},{8,11},{9,10},{10,... | collective-permute-start | bytes 1179656 | tf_op jit(solution)/shard_map/ppermute | solution.py:32
  20.7 11.1 %collective-permute-done.1.first2 = bf16[528,256]{1,0:T(8,128)(2,1)S(1)} collective-permute-done((bf16[528,256]{1,0:T(8,128)(2,1)S(1)}, bf16[528,256]{1,0:T(8,128)(2,1)S(1)}, u32[]{:S(2)}, u32[]{:S(2)}) %collective-permute-start.1) | collective-permute-done | bytes 270368 | tf_op jit(solution)/shard_map/ppermute | solution.py:32
  34.3 4.4 %shard_map.247 = (f32[512,256]{1,0:T(8,128)S(1)}, bf16[512,256]{1,0:T(8,128)(2,1)S(1)}, bf16[512,128]{1,0:T(8,128)(2,1)S(1)}, f32[512,128]{1,0:T(8,128)S(1)}) custom-call(bf16[256,1024]{1,0:T(8,128)(2,1)S(1)} %get-tuple-element.128.mine, bf16[256,1024]{1,0:T(8,128)(2,1)S(1)} %collective-permute-done.3.other, bf16[528,256]{1,0:T(8,128)(2,1)S(1)} %get-tuple-element.70.first0, ...), custom_call_target="tpu_custom_call" | custom-call | tf_op jit(solution)/shard_map/pallas_call | solution.py:55
  47.5 2.5 collective-permute-start.13
  52.0 6.2 %collective-permute-done.12.near1 = bf16[256,576]{1,0:T(8,128)(2,1)} collective-permute-done((bf16[256,576]{1,0:T(8,128)(2,1)S(1)}, bf16[256,576]{1,0:T(8,128)(2,1)}, u32[]{:S(2)}, u32[]{:S(2)}) %collective-permute-start.12) | collective-permute-done | bytes 294944 | tf_op jit(solution)/shard_map/ppermute | solution.py:32
  58.2 2.5 collective-permute-start.5
  60.7 4.5 %collective-permute-done.13.near2 = bf16[256,576]{1,0:T(8,128)(2,1)} collective-permute-done((bf16[256,576]{1,0:T(8,128)(2,1)S(1)}, bf16[256,576]{1,0:T(8,128)(2,1)}, u32[]{:S(2)}, u32[]{:S(2)}) %collective-permute-start.13) | collective-permute-done | bytes 294944 | tf_op jit(solution)/shard_map/ppermute | solution.py:32
  65.2 4.0 %collective-permute-start.6 = (bf16[512,128]{1,0:T(8,128)(2,1)S(1)}, bf16[512,128]{1,0:T(8,128)(2,1)S(1)}, u32[]{:S(2)}, u32[]{:S(2)}) collective-permute-start(bf16[512,128]{1,0:T(8,128)(2,1)S(1)} %get-tuple-element.74.first0.ready.context_in), channel_id=1, source_target_pairs={{0,3},{1,2},{2,1},{3,0},{4,7},{5,6},{6,5},{7,4},{8,11},{9,10},{10,... | collective-permute-start | bytes 393224 | tf_op jit(solution)/shard_map/ppermute | solution.py:32
  75.0 5.1 %collective-permute-done.15.far1 = bf16[256,576]{1,0:T(8,128)(2,1)} collective-permute-done((bf16[256,576]{1,0:T(8,128)(2,1)}, bf16[256,576]{1,0:T(8,128)(2,1)}, u32[]{:S(2)}, u32[]{:S(2)}) %collective-permute-start.15) | collective-permute-done | bytes 294944 | tf_op jit(solution)/shard_map/ppermute | solution.py:32
  80.1 6.9 %collective-permute-done.16.far2 = bf16[256,576]{1,0:T(8,128)(2,1)} collective-permute-done((bf16[256,576]{1,0:T(8,128)(2,1)}, bf16[256,576]{1,0:T(8,128)(2,1)}, u32[]{:S(2)}, u32[]{:S(2)}) %collective-permute-start.16) | collective-permute-done | bytes 294944 | tf_op jit(solution)/shard_map/ppermute | solution.py:32
  87.1 4.0 %collective-permute-done.17.far3 = bf16[256,576]{1,0:T(8,128)(2,1)} collective-permute-done((bf16[256,576]{1,0:T(8,128)(2,1)}, bf16[256,576]{1,0:T(8,128)(2,1)}, u32[]{:S(2)}, u32[]{:S(2)}) %collective-permute-start.17) | collective-permute-done | bytes 294944 | tf_op jit(solution)/shard_map/ppermute | solution.py:32
  91.4 7.7 %shard_map.252 = (bf16[512,1024]{1,0:T(8,128)(2,1)}, f32[512,576]{1,0:T(8,128)}, f32[512,576]{1,0:T(8,128)}, bf16[512,576]{1,0:T(8,128)(2,1)}, f32[256,256]{1,0:T(8,128)S(1)}, /*index=5*/f32[64,1024]{1,0:T(8,128)S(1)}) custom-call(s32[3]{0:T(128)S(1)} %pad_add_fusion.2.where, bf16[256,1024]{1,0:T(8,128)(2,1)S(1)} %get-tuple-element.128.mine, ...), custom_call_target="tpu_custom_call" | custom-call | tf_op jit(solution)/shard_map/pallas_call | solution.py:55
  100.1 7.2 %shard_map.255 = (bf16[512,576]{1,0:T(8,128)(2,1)S(1)}, bf16[512,576]{1,0:T(8,128)(2,1)S(1)}, bf16[256,1024]{1,0:T(8,128)(2,1)S(1)}, bf16[256,1024]{1,0:T(8,128)(2,1)}) custom-call(s32[3]{0:T(128)S(1)} %pad_add_fusion.2.where, bf16[768,1024]{1,0:T(8,128)(2,1)} %copy-done, bf16[768,1024]{1,0:T(8,128)(2,1)} %collective-permute-done.11.joined_far, ...), custom_call_target="tpu_custom_call" | custom-call | tf_op jit(solution)/shard_map/pallas_call | solution.py:55
  108.2 5.9 %shard_map.261 = (bf16[2,4,64,576]{3,2,1,0:T(8,128)(2,1)}, bf16[2,4,64,576]{3,2,1,0:T(8,128)(2,1)}, bf16[2,4,64,576]{3,2,1,0:T(8,128)(2,1)S(1)}, bf16[2,4,64,576...) custom-call(s32[3]{0:T(128)S(1)} %pad_add_fusion.2.where, ...), custom_call_target="tpu_custom_call" | custom-call | tf_op jit(solution)/shard_map/pallas_call | solution.py:55
  123.6 2.6 collective-permute-start.28
  127.3 5.4 %collective-permute-done.46 = bf16[2,4,64,576]{3,2,1,0:T(8,128)(2,1)} collective-permute-done((bf16[2,4,64,576]{3,2,1,0:T(8,128)(2,1)}, bf16[2,4,64,576]{3,2,1,0:T(8,128)(2,1)}, u32[]{:S(2)}, u32[]{:S(2)}) %collective-permute-start.46) | collective-permute-done | bytes 589856 | tf_op jit(solution)/shard_map/ppermute | solution.py:32
  132.8 2.3 collective-permute-start.29
  136.3 10.5 %collective-permute-done.48 = bf16[2,4,64,576]{3,2,1,0:T(8,128)(2,1)} collective-permute-done((bf16[2,4,64,576]{3,2,1,0:T(8,128)(2,1)}, bf16[2,4,64,576]{3,2,1,0:T(8,128)(2,1)}, u32[]{:S(2)}, u32[]{:S(2)}) %collective-permute-start.48) | collective-permute-done | bytes 589856 | tf_op jit(solution)/shard_map/ppermute | solution.py:32
  148.2 8.3 %collective-permute-done.50 = bf16[2,4,64,576]{3,2,1,0:T(8,128)(2,1)S(1)} collective-permute-done((bf16[2,4,64,576]{3,2,1,0:T(8,128)(2,1)S(1)}, bf16[2,4,64,576]{3,2,1,0:T(8,128)(2,1)S(1)}, u32[]{:S(2)}, u32[]{:S(2)}) %collective-permute-start.50) | collective-permute-done | bytes 589856 | tf_op jit(solution)/shard_map/ppermute | solution.py:32
  158.9 2.3 collective-permute-start.47
  168.0 2.3 collective-permute-start.51
  172.2 14.8 %collective-permute-done.47 = bf16[4,64,576]{2,1,0:T(8,128)(2,1)S(1)} collective-permute-done((bf16[4,64,576]{2,1,0:T(8,128)(2,1)S(1)}, bf16[4,64,576]{2,1,0:T(8,128)(2,1)S(1)}, u32[]{:S(2)}, u32[]{:S(2)}) %collective-permute-start.47) | collective-permute-done | bytes 294944 | tf_op jit(solution)/shard_map/ppermute | solution.py:32
  188.1 5.9 %collective-permute-done.49 = bf16[4,64,576]{2,1,0:T(8,128)(2,1)S(1)} collective-permute-done((bf16[4,64,576]{2,1,0:T(8,128)(2,1)S(1)}, bf16[4,64,576]{2,1,0:T(8,128)(2,1)S(1)}, u32[]{:S(2)}, u32[]{:S(2)}) %collective-permute-start.49) | collective-permute-done | bytes 294944 | tf_op jit(solution)/shard_map/ppermute | solution.py:32
  195.2 5.0 %collective-permute-done.51 = bf16[4,64,576]{2,1,0:T(8,128)(2,1)S(1)} collective-permute-done((bf16[4,64,576]{2,1,0:T(8,128)(2,1)S(1)}, bf16[4,64,576]{2,1,0:T(8,128)(2,1)S(1)}, u32[]{:S(2)}, u32[]{:S(2)}) %collective-permute-start.51) | collective-permute-done | bytes 294944 | tf_op jit(solution)/shard_map/ppermute | solution.py:32
  205.0 4.3 %collective-permute-done.52 = bf16[192,576]{1,0:T(8,128)(2,1)S(1)} collective-permute-done((bf16[192,576]{1,0:T(8,128)(2,1)S(1)}, bf16[192,576]{1,0:T(8,128)(2,1)S(1)}, u32[]{:S(2)}, u32[]{:S(2)}) %collective-permute-start.52) | collective-permute-done | bytes 221216 | tf_op jit(solution)/shard_map/ppermute | solution.py:32
  209.3 3.5 %collective-permute-done.53 = bf16[192,576]{1,0:T(8,128)(2,1)S(1)} collective-permute-done((bf16[192,576]{1,0:T(8,128)(2,1)S(1)}, bf16[192,576]{1,0:T(8,128)(2,1)S(1)}, u32[]{:S(2)}, u32[]{:S(2)}) %collective-permute-start.53) | collective-permute-done | bytes 221216 | tf_op jit(solution)/shard_map/ppermute | solution.py:32
  215.9 7.0 %shard_map.259 = (bf16[256,1024]{1,0:T(8,128)(2,1)S(1)}, bf16[256,1024]{1,0:T(8,128)(2,1)S(1)}, f32[8,512]{1,0:T(8,128)S(1)}, bf16[2,4,80,384]{3,2,1,0:T(8,128)(2,1)S(1)}, bf16[2,4,80,384]{3,2,1,0:T(8,128)(2,1)S(1)}) custom-call(s32[3]{0:T(128)S(1)} %pad_add_fusion.2.where, bf16[256,1024]{1,0:T(8,128)(2,1)S(1)} %get-tuple-element.128.mine, ...), custom_call_target="tpu_custom_call" | custom-call | tf_op jit(solution)/shard_map/pallas_call | solution.py:55
  224.9 9.8 %collective-permute-done.40 = bf16[2,4,80,384]{3,2,1,0:T(8,128)(2,1)S(1)} collective-permute-done((bf16[2,4,80,384]{3,2,1,0:T(8,128)(2,1)S(1)}, bf16[2,4,80,384]{3,2,1,0:T(8,128)(2,1)S(1)}, u32[]{:S(2)}, u32[]{:S(2)}) %collective-permute-start.40) | collective-permute-done | bytes 491552 | tf_op jit(solution)/shard_map/ppermute | solution.py:32
  235.6 3.4 %collective-permute-start.41 = (bf16[4,80,384]{2,1,0:T(8,128)(2,1)}, bf16[4,80,384]{2,1,0:T(8,128)(2,1)}, u32[]{:S(2)}, u32[]{:S(2)}) collective-permute-start(bf16[4,80,384]{2,1,0:T(8,128)(2,1)} %fusion.11), channel_id=1, source_target_pairs={{0,16},{8,24},{16,0},{24,8},{1,17},{9,25},{17,1},{25,9},{2,18},{10... | collective-permute-start | bytes 737288 | tf_op jit(solution)/shard_map/ppermute | solution.py:32
  240.3 2.3 collective-permute-start.38
  251.2 2.7 %collective-permute-start.44 = (bf16[80,384]{1,0:T(8,128)(2,1)S(1)}, bf16[80,384]{1,0:T(8,128)(2,1)S(1)}, u32[]{:S(2)}, u32[]{:S(2)}) collective-permute-start(bf16[80,384]{1,0:T(8,128)(2,1)S(1)} %get-tuple-element.170), channel_id=1, source_target_pairs={{0,3},{1,2},{2,1},{3,0},{4,7},{5,6},{6,5},{7,4},{8,11},{9,10},{10,... | collective-permute-start | bytes 184328 | tf_op jit(solution)/shard_map/ppermute | solution.py:32
  (293 shorter events, 90.3 us)
Async XLA Ops:
  6.2 14.4 %collective-permute-start = (bf16[528,256]{1,0:T(8,128)(2,1)S(1)}, bf16[528,256]{1,0:T(8,128)(2,1)S(1)}, u32[]{:S(2)}, u32[]{:S(2)}) collective-permute-start(bf16[528,256]{1,0:T(8,128)(2,1)S(1)} %get-tuple-element.71), channel_id=1, source_target_pairs={{0,1},{1,0},{2,3},{3,2},{4,5},{5,4},{6,7},{7,6},{8,9},{9,8},{10,11... | collective-permute-start | bytes 811016 | tf_op jit(solution)/shard_map/ppermute | solution.py:32
  9.3 22.6 %collective-permute-start.1 = (bf16[528,256]{1,0:T(8,128)(2,1)S(1)}, bf16[528,256]{1,0:T(8,128)(2,1)S(1)}, u32[]{:S(2)}, u32[]{:S(2)}) collective-permute-start(bf16[528,256]{1,0:T(8,128)(2,1)S(1)} %get-tuple-element.72), channel_id=1, source_target_pairs={{0,2},{1,3},{2,0},{3,1},{4,6},{5,7},{6,4},{7,5},{8,10},{9,11},{10,... | collective-permute-start | bytes 811016 | tf_op jit(solution)/shard_map/ppermute | solution.py:32
  10.8 21.1 %collective-permute-start.2 = (bf16[528,256]{1,0:T(8,128)(2,1)S(1)}, bf16[528,256]{1,0:T(8,128)(2,1)S(1)}, u32[]{:S(2)}, u32[]{:S(2)}) collective-permute-start(bf16[528,256]{1,0:T(8,128)(2,1)S(1)} %get-tuple-element.73), channel_id=1, source_target_pairs={{0,3},{1,2},{2,1},{3,0},{4,7},{5,6},{6,5},{7,4},{8,11},{9,10},{10,... | collective-permute-start | bytes 811016 | tf_op jit(solution)/shard_map/ppermute | solution.py:32
  15.1 25.0 %collective-permute-start.10 = (bf16[768,256]{1,0:T(8,128)(2,1)}, bf16[768,256]{1,0:T(8,128)(2,1)S(1)}, u32[]{:S(2)}, u32[]{:S(2)}) collective-permute-start(bf16[768,256]{1,0:T(8,128)(2,1)} %get-tuple-element.78), channel_id=1, source_target_pairs={{0,3},{1,2},{2,1},{3,0},{4,7},{5,6},{6,5},{7,4},{8,11},{9,10},{10,... | collective-permute-start | bytes 1179656 | tf_op jit(solution)/shard_map/ppermute | solution.py:32
  18.0 22.9 %collective-permute-start.8 = (bf16[768,256]{1,0:T(8,128)(2,1)}, bf16[768,256]{1,0:T(8,128)(2,1)S(1)}, u32[]{:S(2)}, u32[]{:S(2)}) collective-permute-start(bf16[768,256]{1,0:T(8,128)(2,1)} %get-tuple-element.76), channel_id=1, source_target_pairs={{0,1},{1,0},{2,3},{3,2},{4,5},{5,4},{6,7},{7,6},{8,9},{9,8},{10,11... | collective-permute-start | bytes 1179656 | tf_op jit(solution)/shard_map/ppermute | solution.py:32
  20.7 21.0 %collective-permute-start.9 = (bf16[768,256]{1,0:T(8,128)(2,1)}, bf16[768,256]{1,0:T(8,128)(2,1)}, u32[]{:S(2)}, u32[]{:S(2)}) collective-permute-start(bf16[768,256]{1,0:T(8,128)(2,1)} %get-tuple-element.77), channel_id=1, source_target_pairs={{0,2},{1,3},{2,0},{3,1},{4,6},{5,7},{6,4},{7,5},{8,10},{9,11},{10,... | collective-permute-start | bytes 1179656 | tf_op jit(solution)/shard_map/ppermute | solution.py:32
  45.0 46.3 %collective-permute-start.11 = (bf16[768,1024]{1,0:T(8,128)(2,1)S(1)}, bf16[768,1024]{1,0:T(8,128)(2,1)}, u32[]{:S(2)}, u32[]{:S(2)}) collective-permute-start(bf16[768,1024]{1,0:T(8,128)(2,1)S(1)} %shard_map.250.joined.out_weight), channel_id=1, source_target_pairs={{0,4},{4,0},{1,5},{5,1},{2,6},{6,2},{3,7},{7,3},{8,12},{12,8},{9,1... | collective-permute-start | bytes 4718600 | tf_op jit(solution)/shard_map/ppermute | solution.py:32
  47.5 17.7 %collective-permute-start.13 = (bf16[256,576]{1,0:T(8,128)(2,1)S(1)}, bf16[256,576]{1,0:T(8,128)(2,1)}, u32[]{:S(2)}, u32[]{:S(2)}) collective-permute-start(bf16[256,576]{1,0:T(8,128)(2,1)S(1)} %get-tuple-element.81), channel_id=1, source_target_pairs={{0,2},{1,3},{2,0},{3,1},{4,6},{5,7},{6,4},{7,5},{8,10},{9,11},{10,... | collective-permute-start | bytes 884744 | tf_op jit(solution)/shard_map/ppermute | solution.py:32
  50.1 19.1 %collective-permute-start.14 = (bf16[256,576]{1,0:T(8,128)(2,1)S(1)}, bf16[256,576]{1,0:T(8,128)(2,1)}, u32[]{:S(2)}, u32[]{:S(2)}) collective-permute-start(bf16[256,576]{1,0:T(8,128)(2,1)S(1)} %get-tuple-element.82), channel_id=1, source_target_pairs={{0,3},{1,2},{2,1},{3,0},{4,7},{5,6},{6,5},{7,4},{8,11},{9,10},{10,... | collective-permute-start | bytes 884744 | tf_op jit(solution)/shard_map/ppermute | solution.py:32
  51.5 19.0 %collective-permute-start.4 = (bf16[512,128]{1,0:T(8,128)(2,1)S(1)}, bf16[512,128]{1,0:T(8,128)(2,1)S(1)}, u32[]{:S(2)}, u32[]{:S(2)}) collective-permute-start(bf16[512,128]{1,0:T(8,128)(2,1)S(1)} %get-tuple-element.74.first0.ready.context_in), channel_id=1, source_target_pairs={{0,1},{1,0},{2,3},{3,2},{4,5},{5,4},{6,7},{7,6},{8,9},{9,8},{10,11... | collective-permute-start | bytes 393224 | tf_op jit(solution)/shard_map/ppermute | solution.py:32
  58.2 13.0 %collective-permute-start.5 = (bf16[512,128]{1,0:T(8,128)(2,1)S(1)}, bf16[512,128]{1,0:T(8,128)(2,1)S(1)}, u32[]{:S(2)}, u32[]{:S(2)}) collective-permute-start(bf16[512,128]{1,0:T(8,128)(2,1)S(1)} %get-tuple-element.74.first0.ready.context_in), channel_id=1, source_target_pairs={{0,2},{1,3},{2,0},{3,1},{4,6},{5,7},{6,4},{7,5},{8,10},{9,11},{10,... | collective-permute-start | bytes 393224 | tf_op jit(solution)/shard_map/ppermute | solution.py:32
  70.5 16.6 %collective-permute-start.16 = (bf16[256,576]{1,0:T(8,128)(2,1)}, bf16[256,576]{1,0:T(8,128)(2,1)}, u32[]{:S(2)}, u32[]{:S(2)}) collective-permute-start(bf16[256,576]{1,0:T(8,128)(2,1)} %collective-permute-done.13.near2), channel_id=1, source_target_pairs={{0,8},{8,0},{16,24},{24,16},{1,9},{9,1},{17,25},{25,17},{2,10},{10... | collective-permute-start | bytes 884744 | tf_op jit(solution)/shard_map/ppermute | solution.py:32
  71.2 19.9 %collective-permute-start.17 = (bf16[256,576]{1,0:T(8,128)(2,1)}, bf16[256,576]{1,0:T(8,128)(2,1)}, u32[]{:S(2)}, u32[]{:S(2)}) collective-permute-start(bf16[256,576]{1,0:T(8,128)(2,1)} %collective-permute-done.14.near3), channel_id=1, source_target_pairs={{0,8},{8,0},{16,24},{24,16},{1,9},{9,1},{17,25},{25,17},{2,10},{10... | collective-permute-start | bytes 884744 | tf_op jit(solution)/shard_map/ppermute | solution.py:32
  73.4 17.9 %collective-permute-start.7 = (bf16[512,512]{1,0:T(8,128)(2,1)}, bf16[512,512]{1,0:T(8,128)(2,1)}, u32[]{:S(2)}, u32[]{:S(2)}) collective-permute-start(bf16[512,512]{1,0:T(8,128)(2,1)} %shard_map.248.context_near), channel_id=1, source_target_pairs={{0,4},{4,0},{1,5},{5,1},{2,6},{6,2},{3,7},{7,3},{8,12},{12,8},{9,1... | collective-permute-start | bytes 1572872 | tf_op jit(solution)/shard_map/ppermute | solution.py:32
  80.1 19.7 %collective-permute-start.18 = (bf16[576,256]{1,0:T(8,128)(2,1)S(1)}, bf16[576,256]{1,0:T(8,128)(2,1)S(1)}, u32[]{:S(2)}, u32[]{:S(2)}) collective-permute-start(bf16[576,256]{1,0:T(8,128)(2,1)S(1)} %get-tuple-element.130), channel_id=1, source_target_pairs={{0,1},{1,0},{2,3},{3,2},{4,5},{5,4},{6,7},{7,6},{8,9},{9,8},{10,11... | collective-permute-start | bytes 884744 | tf_op jit(solution)/shard_map/ppermute | solution.py:32
  87.1 13.0 %collective-permute-start.19 = (bf16[576,256]{1,0:T(8,128)(2,1)S(1)}, bf16[576,256]{1,0:T(8,128)(2,1)S(1)}, u32[]{:S(2)}, u32[]{:S(2)}) collective-permute-start(bf16[576,256]{1,0:T(8,128)(2,1)S(1)} %get-tuple-element.132), channel_id=1, source_target_pairs={{0,2},{1,3},{2,0},{3,1},{4,6},{5,7},{6,4},{7,5},{8,10},{9,11},{10,... | collective-permute-start | bytes 884744 | tf_op jit(solution)/shard_map/ppermute | solution.py:32
  114.9 17.9 %collective-permute-start.46 = (bf16[2,4,64,576]{3,2,1,0:T(8,128)(2,1)}, bf16[2,4,64,576]{3,2,1,0:T(8,128)(2,1)}, u32[]{:S(2)}, u32[]{:S(2)}) collective-permute-start(bf16[2,4,64,576]{3,2,1,0:T(8,128)(2,1)} %get-tuple-element.122), channel_id=1, source_target_pairs={{0,8},{8,0},{16,24},{24,16},{1,9},{9,1},{17,25},{25,17},{2,10},{10... | collective-permute-start | bytes 1769480 | tf_op jit(solution)/shard_map/ppermute | solution.py:32
  118.5 28.3 %collective-permute-start.48 = (bf16[2,4,64,576]{3,2,1,0:T(8,128)(2,1)}, bf16[2,4,64,576]{3,2,1,0:T(8,128)(2,1)}, u32[]{:S(2)}, u32[]{:S(2)}) collective-permute-start(bf16[2,4,64,576]{3,2,1,0:T(8,128)(2,1)} %get-tuple-element.124), channel_id=1, source_target_pairs={{0,8},{8,0},{16,24},{24,16},{1,9},{9,1},{17,25},{25,17},{2,10},{10... | collective-permute-start | bytes 1769480 | tf_op jit(solution)/shard_map/ppermute | solution.py:32
  120.4 36.1 %collective-permute-start.50 = (bf16[2,4,64,576]{3,2,1,0:T(8,128)(2,1)S(1)}, bf16[2,4,64,576]{3,2,1,0:T(8,128)(2,1)S(1)}, u32[]{:S(2)}, u32[]{:S(2)}) collective-permute-start(bf16[2,4,64,576]{3,2,1,0:T(8,128)(2,1)S(1)} %copy-done.46), channel_id=1, source_target_pairs={{0,8},{8,0},{16,24},{24,16},{1,9},{9,1},{17,25},{25,17},{2,10},{10... | collective-permute-start | bytes 1769480 | tf_op jit(solution)/shard_map/ppermute | solution.py:32
  123.2 34.8 %collective-permute-start.27 = (bf16[64,1024]{1,0:T(8,128)(2,1)S(1)}, bf16[64,1024]{1,0:T(8,128)(2,1)S(1)}, u32[]{:S(2)}, u32[]{:S(2)}) collective-permute-start(bf16[64,1024]{1,0:T(8,128)(2,1)S(1)} %get-tuple-element.97), channel_id=1, source_target_pairs={{0,1},{1,0},{2,3},{3,2},{4,5},{5,4},{6,7},{7,6},{8,9},{9,8},{10,11... | collective-permute-start | bytes 393224 | tf_op jit(solution)/shard_map/ppermute | solution.py:32
  123.6 35.3 %collective-permute-start.28 = (bf16[64,1024]{1,0:T(8,128)(2,1)S(1)}, bf16[64,1024]{1,0:T(8,128)(2,1)S(1)}, u32[]{:S(2)}, u32[]{:S(2)}) collective-permute-start(bf16[64,1024]{1,0:T(8,128)(2,1)S(1)} %get-tuple-element.98), channel_id=1, source_target_pairs={{0,2},{1,3},{2,0},{3,1},{4,6},{5,7},{6,4},{7,5},{8,10},{9,11},{10,... | collective-permute-start | bytes 393224 | tf_op jit(solution)/shard_map/ppermute | solution.py:32
  132.8 28.6 %collective-permute-start.29 = (bf16[64,1024]{1,0:T(8,128)(2,1)S(1)}, bf16[64,1024]{1,0:T(8,128)(2,1)S(1)}, u32[]{:S(2)}, u32[]{:S(2)}) collective-permute-start(bf16[64,1024]{1,0:T(8,128)(2,1)S(1)} %get-tuple-element.99), channel_id=1, source_target_pairs={{0,3},{1,2},{2,1},{3,0},{4,7},{5,6},{6,5},{7,4},{8,11},{9,10},{10,... | collective-permute-start | bytes 393224 | tf_op jit(solution)/shard_map/ppermute | solution.py:32
  146.8 16.2 %collective-permute-start.22 = (bf16[256,256]{1,0:T(8,128)(2,1)S(1)}, bf16[256,256]{1,0:T(8,128)(2,1)S(1)}, u32[]{:S(2)}, u32[]{:S(2)}) collective-permute-start(bf16[256,256]{1,0:T(8,128)(2,1)S(1)} %get-tuple-element.89), channel_id=1, source_target_pairs={{0,1},{1,0},{2,3},{3,2},{4,5},{5,4},{6,7},{7,6},{8,9},{9,8},{10,11... | collective-permute-start | bytes 393224 | tf_op jit(solution)/shard_map/ppermute | solution.py:32
  158.9 28.1 %collective-permute-start.47 = (bf16[4,64,576]{2,1,0:T(8,128)(2,1)S(1)}, bf16[4,64,576]{2,1,0:T(8,128)(2,1)S(1)}, u32[]{:S(2)}, u32[]{:S(2)}) collective-permute-start(bf16[4,64,576]{2,1,0:T(8,128)(2,1)S(1)} %fusion.4), channel_id=1, source_target_pairs={{0,16},{8,24},{16,0},{24,8},{1,17},{9,25},{17,1},{25,9},{2,18},{10... | collective-permute-start | bytes 884744 | tf_op jit(solution)/shard_map/ppermute | solution.py:32
  161.3 32.7 %collective-permute-start.49 = (bf16[4,64,576]{2,1,0:T(8,128)(2,1)S(1)}, bf16[4,64,576]{2,1,0:T(8,128)(2,1)S(1)}, u32[]{:S(2)}, u32[]{:S(2)}) collective-permute-start(bf16[4,64,576]{2,1,0:T(8,128)(2,1)S(1)} %fusion.5), channel_id=1, source_target_pairs={{0,16},{8,24},{16,0},{24,8},{1,17},{9,25},{17,1},{25,9},{2,18},{10... | collective-permute-start | bytes 884744 | tf_op jit(solution)/shard_map/ppermute | solution.py:32
  168.0 32.1 %collective-permute-start.51 = (bf16[4,64,576]{2,1,0:T(8,128)(2,1)S(1)}, bf16[4,64,576]{2,1,0:T(8,128)(2,1)S(1)}, u32[]{:S(2)}, u32[]{:S(2)}) collective-permute-start(bf16[4,64,576]{2,1,0:T(8,128)(2,1)S(1)} %fusion.6), channel_id=1, source_target_pairs={{0,16},{8,24},{16,0},{24,8},{1,17},{9,25},{17,1},{25,9},{2,18},{10... | collective-permute-start | bytes 884744 | tf_op jit(solution)/shard_map/ppermute | solution.py:32
  170.4 33.7 %collective-permute-start.25 = (bf16[256,256]{1,0:T(8,128)(2,1)S(1)}, bf16[256,256]{1,0:T(8,128)(2,1)S(1)}, u32[]{:S(2)}, u32[]{:S(2)}) collective-permute-start(bf16[256,256]{1,0:T(8,128)(2,1)S(1)} %add_convert_fusion.4), channel_id=1, source_target_pairs={{0,4},{4,0},{1,5},{5,1},{2,6},{6,2},{3,7},{7,3},{8,12},{12,8},{9,1... | collective-permute-start | bytes 393224 | tf_op jit(solution)/shard_map/ppermute | solution.py:32
  172.2 42.3 %collective-permute-start.33 = (bf16[256,1024]{1,0:T(8,128)(2,1)S(1)}, bf16[256,1024]{1,0:T(8,128)(2,1)S(1)}, u32[]{:S(2)}, u32[]{:S(2)}) collective-permute-start(bf16[256,1024]{1,0:T(8,128)(2,1)S(1)} %shard_map.258.grad_mine), channel_id=1, source_target_pairs={{0,4},{4,0},{1,5},{5,1},{2,6},{6,2},{3,7},{7,3},{8,12},{12,8},{9,1... | collective-permute-start | bytes 1572872 | tf_op jit(solution)/shard_map/ppermute | solution.py:32
  222.9 11.8 %collective-permute-start.40 = (bf16[2,4,80,384]{3,2,1,0:T(8,128)(2,1)S(1)}, bf16[2,4,80,384]{3,2,1,0:T(8,128)(2,1)S(1)}, u32[]{:S(2)}, u32[]{:S(2)}) collective-permute-start(bf16[2,4,80,384]{3,2,1,0:T(8,128)(2,1)S(1)} %get-tuple-element.117), channel_id=1, source_target_pairs={{0,8},{8,0},{16,24},{24,16},{1,9},{9,1},{17,25},{25,17},{2,10},{10... | collective-permute-start | bytes 1474568 | tf_op jit(solution)/shard_map/ppermute | solution.py:32
  224.2 14.7 %collective-permute-start.34 = (bf16[256,1024]{1,0:T(8,128)(2,1)S(1)}, bf16[256,1024]{1,0:T(8,128)(2,1)S(1)}, u32[]{:S(2)}, u32[]{:S(2)}) collective-permute-start(bf16[256,1024]{1,0:T(8,128)(2,1)S(1)} %get-tuple-element.110), channel_id=1, source_target_pairs={{0,4},{4,0},{1,5},{5,1},{2,6},{6,2},{3,7},{7,3},{8,12},{12,8},{9,1... | collective-permute-start | bytes 1572872 | tf_op jit(solution)/shard_map/ppermute | solution.py:32
  224.4 14.6 %collective-permute-start.35 = (f32[8,256]{1,0:T(8,128)S(1)}, f32[8,256]{1,0:T(8,128)S(1)}, u32[]{:S(2)}, u32[]{:S(2)}) collective-permute-start(f32[8,256]{1,0:T(8,128)S(1)} %slice.362), channel_id=1, source_target_pairs={{0,4},{4,0},{1,5},{5,1},{2,6},{6,2},{3,7},{7,3},{8,12},{12,8},{9,1... | collective-permute-start | bytes 24584 | tf_op jit(solution)/shard_map/ppermute | solution.py:32
  235.6 13.7 %collective-permute-start.41 = (bf16[4,80,384]{2,1,0:T(8,128)(2,1)}, bf16[4,80,384]{2,1,0:T(8,128)(2,1)}, u32[]{:S(2)}, u32[]{:S(2)}) collective-permute-start(bf16[4,80,384]{2,1,0:T(8,128)(2,1)} %fusion.11), channel_id=1, source_target_pairs={{0,16},{8,24},{16,0},{24,8},{1,17},{9,25},{17,1},{25,9},{2,18},{10... | collective-permute-start | bytes 737288 | tf_op jit(solution)/shard_map/ppermute | solution.py:32
  (77 other events, 602.5 us)
where the time goes:
time: 263 us; the launch traced here: 262 us
  waiting for transfers between devices  112 us (43%)
  starting transfers between devices  60.9 us (23%)
  Pallas kernels  44.9 us (17%)
  local copies, waits for them, and re-layouts  24.5 us (9%)
  other arithmetic  18.8 us (7%)
    ppermute x55, waiting for transfers between devices, flip(): return lax.ppermute(values, axis, [(i, i ^ distance) for i in range(size)])  112 us
    ppermute x55, starting transfers between devices, flip(): return lax.ppermute(values, axis, [(i, i ^ distance) for i in range(size)])  60.9 us
    pallas_call x16, Pallas kernels, kernel_call(): pl.pallas_call(kernel, out_shape=[jax.ShapeDtypeStruct(shape, dtype) for...  44.9 us
    unnamed x108, local copies, waits for them, and re-layouts  15.4 us
  transfers between devices with their start and end apart: 55, of which 23 were waited for; matrix products, arithmetic and copies ran while one was open for 10% of the time, Pallas kernels for 9%

commit v1 on v0

--- a/solution.py
+++ b/solution.py
@@ -47,8 +47,13 @@
     return result
 
 
-def kernel_call(kernel, outs, *args, scalars=None, scratch=()):
-    specs = [pl.BlockSpec(memory_space=pltpu.VMEM)] * len(args)
+def kernel_call(kernel, outs, *args, scalars=None, scratch=(), fetch=0):
+    specs = [pl.BlockSpec(memory_space=pl.ANY)] * fetch
+    specs = specs + [pl.BlockSpec(memory_space=pltpu.VMEM)] * (len(args) - fetch)
+    scratch_shapes = [pltpu.VMEM(shape, dtype) for shape, dtype in scratch]
+    if fetch:
+        scratch_shapes = [pltpu.VMEM(v.shape, v.dtype) for v in args[:fetch]] + scratch_shapes
+        scratch_shapes.append(pltpu.SemaphoreType.DMA((fetch,)))
     if scalars is not None:
         args = (scalars,) + args
         specs = [pl.BlockSpec(memory_space=pltpu.SMEM)] + specs
@@ -57,20 +62,36 @@
         out_shape=[jax.ShapeDtypeStruct(shape, dtype) for shape, dtype in outs],
         in_specs=specs,
         out_specs=[pl.BlockSpec(memory_space=pltpu.VMEM)] * len(outs),
-        scratch_shapes=[pltpu.VMEM(shape, dtype) for shape, dtype in scratch],
+        scratch_shapes=scratch_shapes,
         compiler_params=pltpu.CompilerParams(vmem_limit_bytes=48 * 1024 * 1024),
     )(*args)
 
 
-def pack_one_kernel(where, x, gains, query, key, value, *outs):
+def fetched(sources, targets, semaphores):
+    copies = [
+        pltpu.make_async_copy(source, target, semaphores.at[i])
+        for i, (source, target) in enumerate(zip(sources, targets))
+    ]
+    for copy in copies:
+        copy.start()
+    for copy in copies:
+        copy.wait()
+
+
+def pack_one_kernel(
+    where, x_in, query_in, key_in, value_in, gain_first, gain_second,
+    out0, out1, out2, out3, x, query, key, value, semaphores,
+):
+    fetched((x_in, query_in, key_in, value_in), (x, query, key, value), semaphores)
+    outs = (out0, out1, out2, out3)
     row, col = where[0], where[1]
     half = x.shape[0] // 2
     cols = len(outs)
     q_size, kv_size = query.shape[1] // cols, key.shape[1] // cols
     line = lax.broadcasted_iota(jnp.int32, (16, x.shape[1]), 0)
     rows = jnp.zeros((16, x.shape[1]), F32)
-    for g in range(2):
-        rest = gains[g : g + 1, :]
+    for g, gain in enumerate((gain_first, gain_second)):
+        rest = gain[...]
         for p in range(3):
             part = rest.astype(BF16).astype(F32)
             rows = jnp.where(line == 3 * g + p, part, rows)
@@ -90,19 +111,30 @@
         out[half + 16 :, q_size:] = jnp.concatenate(both, axis=1)
 
 
-def pack_two_kernel(where, weight, cot, *outs):
-    row, col = where[0], where[1]
-    half = cot.shape[0] // 2
-    cols = len(outs)
-    size = weight.shape[0] // cols
+def pack_two_kernel(where, weight_in, out0, out1, out2, out3, weight, semaphores):
+    fetched((weight_in,), (weight,), semaphores)
+    outs = (out0, out1, out2, out3)
+    size = weight.shape[0] // len(outs)
     for k, out in enumerate(outs):
-        for j in range(cols):
-            source = pl.multiple_of((col ^ (k ^ j)) * size, size)
+        for j in range(len(outs)):
+            source = pl.multiple_of((where[1] ^ (k ^ j)) * size, size)
             out[j * size : (j + 1) * size, :] = weight[pl.ds(source, size), :]
-        out[cols * size :, :] = cot[pl.ds(pl.multiple_of(row * half, half), half), :]
-
-
-def pack_gate_kernel(where, gate, up, *outs):
+
+
+def pack_three_kernel(where, down_in, cot_in, out0, out1, out2, out3, down, cot, semaphores):
+    fetched((down_in, cot_in), (down, cot), semaphores)
+    outs = (out0, out1, out2, out3)
+    size, half = down.shape[0] // len(outs), cot.shape[0] // 2
+    for k, out in enumerate(outs):
+        out[:size, :] = down[pl.ds(pl.multiple_of((where[1] ^ k) * size, size), size), :]
+        out[size:, :] = cot[pl.ds(pl.multiple_of(where[0] * half, half), half), :]
+
+
+def pack_gate_kernel(
+    where, gate_in, up_in, out0, out1, out2, out3, out4, gate, up, semaphores
+):
+    fetched((gate_in, up_in), (gate, up), semaphores)
+    outs = (out0, out1, out2, out3, out4)
     col, odd_plane = where[1], (where[2] & 1) == 1
     cols = len(outs) - 1
     size = gate.shape[1] // cols
@@ -124,10 +156,10 @@
         outs[cols][...] = piece(gate, col)
 
 
-def join_kernel(first0, first1, first2, first3, ready, out):
-    part = first0.shape[1]
+def join_kernel(first0, first1, first2, first3, out):
+    part, size = first0.shape[1], out.shape[0]
     for k, piece in enumerate((first0, first1, first2, first3)):
-        out[:, k * part : (k + 1) * part] = piece[...]
+        out[:, k * part : (k + 1) * part] = piece[piece.shape[0] - size :, :]
 
 
 def forward_kernel(
@@ -167,17 +199,17 @@
 
 
 def backward_kernel(
-    where, joined, joined_far, gate_in, up_in, down0, down1, down2, down3,
+    where, cot_mine, cot_other, gate_in, up_in, down0, down1, down2, down3,
     near0, near1, near2, near3, far0, far1, far2, far3,
     gate_grad_out, up_grad_out, mine_out, other_out,
 ):
     half, part = mine_out.shape[0], near0.shape[0]
-    start = joined.shape[0] - half
+    size = gate_in.shape[1]
     parts = []
-    for rows in (joined, joined_far):
+    for rows in (cot_mine, cot_other):
         grad = None
         for k, down in enumerate((down0, down1, down2, down3)):
-            term = matmul_nt(rows[start:, k * part : (k + 1) * part], down[...])
+            term = matmul_nt(rows[:, k * part : (k + 1) * part], down[:size, :])
             grad = term if k == 0 else grad + term
         parts.append(grad)
     hidden_grad = jnp.concatenate(parts, axis=0)
@@ -203,7 +235,7 @@
 def result_kernel(hidden, down0, down1, down2, down3, mine_out, other_out):
     half, part = mine_out.shape[0], down0.shape[1]
     for k, down in enumerate((down0, down1, down2, down3)):
-        block = matmul(hidden[...], down[...])
+        block = matmul(hidden[...], down[: hidden.shape[1], :])
         mine_out[:, k * part : (k + 1) * part] = block[:half].astype(BF16)
         other_out[:, k * part : (k + 1) * part] = block[half:].astype(BF16)
 
@@ -216,18 +248,17 @@
 
 
 def weight_grad_kernel(
-    where, joined, joined_far, hidden, normed, gate_grad, up_grad,
+    where, cot_mine, cot_other, hidden, normed, gate_grad, up_grad,
     down_send, gate_send, up_send, down_keep, gate_keep, up_keep, scratch,
 ):
     half = hidden.shape[0] // 2
-    start = joined.shape[0] - half
     cols = down_send.shape[1]
-    part = joined.shape[1] // cols
+    part = cot_mine.shape[1] // cols
     rows = down_send.shape[2]
     for k in range(cols):
         span = slice(k * part, (k + 1) * part)
-        grad = matmul_tn(joined[start:, span], hidden[:half, :])
-        grad = grad + matmul_tn(joined_far[start:, span], hidden[half:, :])
+        grad = matmul_tn(cot_mine[:, span], hidden[:half, :])
+        grad = grad + matmul_tn(cot_other[:, span], hidden[half:, :])
         scratch[...] = grad.astype(BF16)
         deal(where, scratch, k, down_send, down_keep, rows)
     for upstream, send, keep in ((gate_grad, gate_send, gate_keep), (up_grad, up_send, up_keep)):
@@ -249,7 +280,7 @@
 
 
 def second_norm_kernel(
-    where, came0, came1, came2, came3, sums, joined, first0, first1, first2, first3,
+    where, came0, came1, came2, came3, sums, cot_mine, first0, first1, first2, first3,
     out0, out1, out2, out3, gain_out,
 ):
     buffers = (first0, first1, first2, first3)
@@ -265,8 +296,7 @@
     weighted = grad * gain
     gain_out[...] = jnp.sum(grad * normal, axis=0, keepdims=True)
     inner = jnp.mean(weighted * normal, axis=1, keepdims=True)
-    start = pl.multiple_of(joined.shape[0] - half + where[1] * share, share)
-    cot = joined[pl.ds(start, share), :].astype(F32)
+    cot = cot_mine[pl.ds(pl.multiple_of(where[1] * share, share), share), :].astype(F32)
     first = (cot + root * (weighted - normal * inner)).astype(BF16)
     for k, out in enumerate(outs):
         for j in range(len(outs)):
@@ -434,8 +464,8 @@
         head_parts.append(jnp.sum(normed * hat, axis=0, keepdims=True))
     head_line = head_parts[0] + pltpu.roll(head_parts[0], size, 1)
     head_line = jnp.where(first, head_line, pltpu.roll(head_parts[1], size, 1))
-    rows_here = mixed_send.shape[2] - 16
-    line = lax.broadcasted_iota(jnp.int32, (16, part), 0)
+    rows_here = mixed_send.shape[2] - 8
+    line = lax.broadcasted_iota(jnp.int32, (8, part), 0)
     qkv_grad = jnp.concatenate(pieces, axis=1).astype(BF16)
     rows, root = root_and_input(mine, other)
     inner_sum = jnp.zeros((2 * half, 1), F32)
@@ -452,7 +482,7 @@
         one_other[:, span] = grad[half:].astype(BF16)
         mixed[:, : 2 * two] = matmul_tn((hat * gain).astype(BF16), qkv_grad).astype(BF16)
         mixed[:, 2 * two :] = matmul_tn(upstream[:, span], context).astype(BF16)
-        heads = jnp.broadcast_to(head_line, (16, two)).astype(BF16)
+        heads = jnp.broadcast_to(head_line, (8, two)).astype(BF16)
         if mixed_send.shape[0] == 2:
             deal(where, mixed, k, mixed_send, mixed_keep, rows_here)
             for out in (mixed_send, mixed_keep):
@@ -516,10 +546,6 @@
         stacked = jnp.stack(blocks)
         return [lax.dynamic_index_in_dim(stacked, kin[k], 0, keepdims=False) for k in range(cols)]
 
-    def row_blocks(weight):
-        size = weight.shape[0] // cols
-        return [lax.dynamic_slice_in_dim(weight, kin[k] * size, size, 0) for k in range(cols)]
-
     q_size = query_weight.shape[1] // cols
     units = gate_weight.shape[1] // cols
     where = jnp.stack([row, col, plane]).astype(jnp.int32)
@@ -529,11 +555,13 @@
             pack_one_kernel,
             shapes,
             block_input,
-            jnp.stack([attention_gain, feedforward_gain]),
             query_weight,
             key_weight,
             value_weight,
+            attention_gain.reshape(1, part),
+            feedforward_gain.reshape(1, part),
             scalars=where,
+            fetch=4,
         ),
     )
     input_mine = jnp.concatenate([v[:half] for v in first_in], axis=1)
@@ -546,19 +574,30 @@
         gate_weight,
         up_weight,
         scalars=where,
+        fetch=2,
     )
     near_parts = exchange(gate_in[:cols])
     far_parts = [gate_in[cols]] + [flip(v, "dp", 1) for v in near_parts[1:]]
+    inner_size = output_weight.shape[0]
     second_parts = exchange(
         kernel_call(
             pack_two_kernel,
-            [((output_weight.shape[0] + half, part), BF16)] * cols,
+            [((inner_size, part), BF16)] * cols,
             output_weight,
+            scalars=where,
+            fetch=1,
+        ),
+    )
+    down_parts = exchange(
+        kernel_call(
+            pack_three_kernel,
+            [((units + half, part), BF16)] * cols,
+            down_weight,
             cotangent,
             scalars=where,
+            fetch=2,
         ),
     )
-    down_parts = exchange(row_blocks(down_weight))
 
     segment_ids = mine_first(segments)
     places = mine_first(positions)
@@ -593,17 +632,12 @@
     )
 
     context_parts = spread(context)
-    (second_in,) = kernel_call(
-        join_kernel,
-        [((output_weight.shape[0] + half, width), BF16)],
-        *second_parts,
-        context,
-    )
-    (context_near,) = kernel_call(
-        join_kernel, [((tokens, output_weight.shape[0]), BF16)], *context_parts, context
-    )
+    (context_near,) = kernel_call(join_kernel, [((tokens, inner_size), BF16)], *context_parts)
+    context_far = flip(context_near, "row", 1)
+    (second_in,) = kernel_call(join_kernel, [((inner_size, width), BF16)], *second_parts)
     second_far = flip(second_in, "row", 1)
-    context_far = flip(context_near, "row", 1)
+    (cot_mine,) = kernel_call(join_kernel, [((half, width), BF16)], *down_parts)
+    cot_other = flip(cot_mine, "row", 1)
 
     share = half // cols
     normed_two, gate_pre, up_pre, hidden, first_block, first_share = kernel_call(
@@ -631,8 +665,8 @@
     gate_grad, up_grad, two_mine, two_other = kernel_call(
         backward_kernel,
         [((tokens, units), BF16)] * 2 + [((half, width), BF16)] * 2,
-        second_in,
-        second_far,
+        cot_mine,
+        cot_other,
         gate_pre,
         up_pre,
         *down_parts,
@@ -656,7 +690,7 @@
         [((share, width), BF16)] * cols + [((1, width), F32)],
         *two_in,
         first_share,
-        second_in,
+        cot_mine,
         *first_in,
         scalars=where,
     )
@@ -685,8 +719,8 @@
         dealt = kernel_call(
             weight_grad_kernel,
             [((2, cols, rows, units), BF16)] * 6,
-            second_in,
-            second_far,
+            cot_mine,
+            cot_other,
             hidden,
             normed_two,
             gate_grad,
@@ -696,7 +730,7 @@
         )
         sums = [summed(dealt[i], dealt[i + 3]) for i in range(3)]
     else:
-        cot_all = jnp.concatenate([second_in[-half:], second_far[-half:]], axis=0)
+        cot_all = jnp.concatenate([cot_mine, cot_other], axis=0)
         sums = [
             scattered(
                 jnp.moveaxis(grad.astype(BF16).reshape(cols, planes, rows, units), 1, 0)
@@ -725,9 +759,9 @@
 
     mixed_size = 3 * q_size
     if planes == 4:
-        mixed_outs = [((2, cols, rows + 16, mixed_size), BF16)] * 2
+        mixed_outs = [((2, cols, rows + 8, mixed_size), BF16)] * 2
     else:
-        mixed_outs = [((cols, part, mixed_size), BF16), ((cols, 16, mixed_size), BF16)]
+        mixed_outs = [((cols, part, mixed_size), BF16), ((cols, 8, mixed_size), BF16)]
     one_mine, one_other, inner_part, mixed_first, mixed_second = kernel_call(
         attend_back_kernel,
         [((half, width), BF16), ((half, width), BF16), ((8, tokens), F32)] + mixed_outs,
@@ -768,7 +802,7 @@
     if planes == 4:
         mixed_sum = summed(mixed_first, mixed_second)
     else:
-        lines = jnp.broadcast_to(mixed_second[:, None], (cols, planes, 16, mixed_size))
+        lines = jnp.broadcast_to(mixed_second[:, None], (cols, planes, 8, mixed_size))
         blocks = mixed_first.reshape(cols, planes, rows, mixed_size)
         mixed_sum = scattered(jnp.moveaxis(jnp.concatenate([blocks, lines], axis=2), 1, 0))
     mixed_share = arranged([mixed_sum[k] for k in range(cols)])
@@ -821,6 +855,7 @@
         P("dp", "col"),
     )
 
+
     return jax.shard_map(
         body,
         mesh=mesh,

time: 263 us -> 274 us (1.042)
  local copies, waits for them, and re-layouts: 24.5 us -> 30.9 us
  other arithmetic: 18.8 us -> 15.4 us
  starting transfers between devices: 60.9 us -> 64.1 us
  waiting for transfers between devices: 112 us -> 115 us
    unnamed x108 -> x140, local copies, waits for them, and re-layouts: 15.4 us -> 22.3 us
    ppermute x55 -> x56, waiting for transfers between devices: 112 us -> 115 us  [flip(): return lax.ppermute(values, axis, [(i, i ^ distance) for i in range(size)])]
    ppermute x55 -> x56, starting transfers between devices: 60.9 us -> 64.1 us  [flip(): return lax.ppermute(values, axis, [(i, i ^ distance) for i in range(size)])]
    pallas_call x16 -> x18, Pallas kernels: 44.9 us -> 45.7 us  [kernel_call(): pl.pallas_call(kernel, out_shape=[jax.ShapeDtypeStruct(shape, dtype) for...]
  transfers between devices with their start and end apart: 55 -> 56, of which waited for: 23 -> 19; matrix products, arithmetic and copies ran while one was open for 10% -> 8% of each run, Pallas kernels for 9% -> 9%
where the time goes in v1:
time: 274 us; the launch traced here: 273 us
  waiting for transfers between devices  115 us (42%)
  starting transfers between devices  64.1 us (23%)
  Pallas kernels  45.7 us (17%)
  local copies, waits for them, and re-layouts  30.9 us (11%)
  other arithmetic  15.4 us (6%)
    ppermute x56, waiting for transfers between devices, flip(): return lax.ppermute(values, axis, [(i, i ^ distance) for i in range(size)])  115 us
    ppermute x56, starting transfers between devices, flip(): return lax.ppermute(values, axis, [(i, i ^ distance) for i in range(size)])  64.1 us
    pallas_call x18, Pallas kernels, kernel_call(): pl.pallas_call(kernel, out_shape=[jax.ShapeDtypeStruct(shape, dtype) for...  45.7 us
    unnamed x140, local copies, waits for them, and re-layouts  22.3 us
  transfers between devices with their start and end apart: 56, of which 19 were waited for; matrix products, arithmetic and copies ran while one was open for 8% of the time, Pallas kernels for 9%

profile of v1, /device:TPU:0, one launch (start us, length us, event | category | flops | bytes accessed | tf_op | source)
XLA Modules:
  0.0 273.0 jit_solution(192671355891488829)
XLA Ops:
  8.2 3.0 %collective-permute-start = (bf16[528,256]{1,0:T(8,128)(2,1)}, bf16[528,256]{1,0:T(8,128)(2,1)S(1)}, u32[]{:S(2)}, u32[]{:S(2)}) collective-permute-start(bf16[528,256]{1,0:T(8,128)(2,1)} %get-tuple-element.75), channel_id=1, source_target_pairs={{0,1},{1,0},{2,3},{3,2},{4,5},{5,4},{6,7},{7,6},{8,9},{9,8},{10,11... | collective-permute-start | bytes 811016 | tf_op jit(solution)/shard_map/ppermute | solution.py:32
  15.9 2.9 %collective-permute-start.10 = (bf16[512,256]{1,0:T(8,128)(2,1)}, bf16[512,256]{1,0:T(8,128)(2,1)}, u32[]{:S(2)}, u32[]{:S(2)}) collective-permute-start(bf16[512,256]{1,0:T(8,128)(2,1)} %get-tuple-element.82), channel_id=1, source_target_pairs={{0,3},{1,2},{2,1},{3,0},{4,7},{5,6},{6,5},{7,4},{8,11},{9,10},{10,... | collective-permute-start | bytes 786440 | tf_op jit(solution)/shard_map/ppermute | solution.py:32
  25.7 5.7 %collective-permute-done.1.first2 = bf16[528,256]{1,0:T(8,128)(2,1)S(1)} collective-permute-done((bf16[528,256]{1,0:T(8,128)(2,1)}, bf16[528,256]{1,0:T(8,128)(2,1)S(1)}, u32[]{:S(2)}, u32[]{:S(2)}) %collective-permute-start.1) | collective-permute-done | bytes 270368 | tf_op jit(solution)/shard_map/ppermute | solution.py:32
  45.5 4.4 %shard_map.247 = (f32[512,256]{1,0:T(8,128)S(1)}, bf16[512,256]{1,0:T(8,128)(2,1)S(1)}, bf16[512,128]{1,0:T(8,128)(2,1)S(1)}, f32[512,128]{1,0:T(8,128)S(1)}) custom-call(bf16[256,1024]{1,0:T(8,128)(2,1)S(1)} %get-tuple-element.136.mine, bf16[256,1024]{1,0:T(8,128)(2,1)S(1)} %collective-permute-done.3.other, bf16[528,256]{1,0:T(8,128)(2,1)S(1)} %get-tuple-element.74.first0, ...), custom_call_target="tpu_custom_call" | custom-call | tf_op jit(solution)/shard_map/pallas_call | solution.py:60
  55.5 6.3 %collective-permute-done.19.down2.first2 = bf16[832,256]{1,0:T(8,128)(2,1)S(1)} collective-permute-done((bf16[832,256]{1,0:T(8,128)(2,1)S(1)}, bf16[832,256]{1,0:T(8,128)(2,1)S(1)}, u32[]{:S(2)}, u32[]{:S(2)}) %collective-permute-start.19) | collective-permute-done | bytes 426016 | tf_op jit(solution)/shard_map/ppermute | solution.py:32
  61.8 2.5 collective-permute-start.5
  65.8 8.6 %collective-permute-done.5.first2 = bf16[512,128]{1,0:T(8,128)(2,1)S(1)} collective-permute-done((bf16[512,128]{1,0:T(8,128)(2,1)S(1)}, bf16[512,128]{1,0:T(8,128)(2,1)S(1)}, u32[]{:S(2)}, u32[]{:S(2)}) %collective-permute-start.5) | collective-permute-done | bytes 131104 | tf_op jit(solution)/shard_map/ppermute | solution.py:32
  79.2 5.7 %collective-permute-done.14.near3 = bf16[256,576]{1,0:T(8,128)(2,1)S(1)} collective-permute-done((bf16[256,576]{1,0:T(8,128)(2,1)S(1)}, bf16[256,576]{1,0:T(8,128)(2,1)S(1)}, u32[]{:S(2)}, u32[]{:S(2)}) %collective-permute-start.14) | collective-permute-done | bytes 294944 | tf_op jit(solution)/shard_map/ppermute | solution.py:32
  86.9 8.6 %collective-permute-done.16.far2 = bf16[256,576]{1,0:T(8,128)(2,1)S(1)} collective-permute-done((bf16[256,576]{1,0:T(8,128)(2,1)S(1)}, bf16[256,576]{1,0:T(8,128)(2,1)S(1)}, u32[]{:S(2)}, u32[]{:S(2)}) %collective-permute-start.16) | collective-permute-done | bytes 294944 | tf_op jit(solution)/shard_map/ppermute | solution.py:32
  95.4 5.1 %collective-permute-done.17.far3 = bf16[256,576]{1,0:T(8,128)(2,1)S(1)} collective-permute-done((bf16[256,576]{1,0:T(8,128)(2,1)S(1)}, bf16[256,576]{1,0:T(8,128)(2,1)S(1)}, u32[]{:S(2)}, u32[]{:S(2)}) %collective-permute-start.17) | collective-permute-done | bytes 294944 | tf_op jit(solution)/shard_map/ppermute | solution.py:32
  101.7 6.7 %shard_map.252 = (bf16[512,1024]{1,0:T(8,128)(2,1)}, f32[512,576]{1,0:T(8,128)}, f32[512,576]{1,0:T(8,128)}, bf16[512,576]{1,0:T(8,128)(2,1)}, f32[256,256]{1,0:T(8,128)S(1)}, /*index=5*/f32[64,1024]{1,0:T(8,128)S(1)}) custom-call(s32[3]{0:T(128)S(1)} %pad_add_fusion.2.where, bf16[256,1024]{1,0:T(8,128)(2,1)S(1)} %get-tuple-element.136.mine, ...), custom_call_target="tpu_custom_call" | custom-call | tf_op jit(solution)/shard_map/pallas_call | solution.py:60
  110.5 6.3 %shard_map.257 = (bf16[512,576]{1,0:T(8,128)(2,1)}, bf16[512,576]{1,0:T(8,128)(2,1)}, bf16[256,1024]{1,0:T(8,128)(2,1)S(1)}, bf16[256,1024]{1,0:T(8,128)(2,1)}) custom-call(s32[3]{0:T(128)S(1)} %pad_add_fusion.2.where, bf16[256,1024]{1,0:T(8,128)(2,1)S(1)} %shard_map.256.cot_mine, bf16[256,1024]{1,0:T(8,128)(2,1)} %copy-done.12, ...), custom_call_target="tpu_custom_call" | custom-call | tf_op jit(solution)/shard_map/pallas_call | solution.py:60
  118.7 5.0 %shard_map.263 = (bf16[2,4,64,576]{3,2,1,0:T(8,128)(2,1)}, bf16[2,4,64,576]{3,2,1,0:T(8,128)(2,1)}, bf16[2,4,64,576]{3,2,1,0:T(8,128)(2,1)S(1)}, bf16[2,4,64,576...) custom-call(s32[3]{0:T(128)S(1)} %pad_add_fusion.2.where, ...), custom_call_target="tpu_custom_call" | custom-call | tf_op jit(solution)/shard_map/pallas_call | solution.py:60
  126.3 2.8 %shard_map.254 = (bf16[256,1024]{1,0:T(8,128)(2,1)S(1)}, bf16[256,1024]{1,0:T(8,128)(2,1)}) custom-call(bf16[512,576]{1,0:T(8,128)(2,1)S(1)} %copy-done.7, bf16[832,256]{1,0:T(8,128)(2,1)S(1)} %copy-done.5, bf16[832,256]{1,0:T(8,128)(2,1)} %collective-permute-done.18.down1.first1, bf16[832,256]{1,0:T(8,128)(2,1)S(1)} %collective-permute-done.19.down2.first2, ...), custom_call_target="tpu_custom_call" | custom-call | tf_op jit(solution)/shard_map/pallas_call | solution.py:60
  138.3 4.2 %collective-permute-done.47 = bf16[2,4,64,576]{3,2,1,0:T(8,128)(2,1)} collective-permute-done((bf16[2,4,64,576]{3,2,1,0:T(8,128)(2,1)}, bf16[2,4,64,576]{3,2,1,0:T(8,128)(2,1)}, u32[]{:S(2)}, u32[]{:S(2)}) %collective-permute-start.47) | collective-permute-done | bytes 589856 | tf_op jit(solution)/shard_map/ppermute | solution.py:32
  145.0 11.6 %collective-permute-done.49 = bf16[2,4,64,576]{3,2,1,0:T(8,128)(2,1)} collective-permute-done((bf16[2,4,64,576]{3,2,1,0:T(8,128)(2,1)}, bf16[2,4,64,576]{3,2,1,0:T(8,128)(2,1)}, u32[]{:S(2)}, u32[]{:S(2)}) %collective-permute-start.49) | collective-permute-done | bytes 589856 | tf_op jit(solution)/shard_map/ppermute | solution.py:32
  159.0 8.8 %collective-permute-done.51 = bf16[2,4,64,576]{3,2,1,0:T(8,128)(2,1)S(1)} collective-permute-done((bf16[2,4,64,576]{3,2,1,0:T(8,128)(2,1)S(1)}, bf16[2,4,64,576]{3,2,1,0:T(8,128)(2,1)S(1)}, u32[]{:S(2)}, u32[]{:S(2)}) %collective-permute-start.51) | collective-permute-done | bytes 589856 | tf_op jit(solution)/shard_map/ppermute | solution.py:32
  167.9 2.8 %collective-permute-start.24 = (bf16[256,256]{1,0:T(8,128)(2,1)S(1)}, bf16[256,256]{1,0:T(8,128)(2,1)S(1)}, u32[]{:S(2)}, u32[]{:S(2)}) collective-permute-start(bf16[256,256]{1,0:T(8,128)(2,1)S(1)} %get-tuple-element.99), channel_id=1, source_target_pairs={{0,3},{1,2},{2,1},{3,0},{4,7},{5,6},{6,5},{7,4},{8,11},{9,10},{10,... | collective-permute-start | bytes 393224 | tf_op jit(solution)/shard_map/ppermute | solution.py:32
  170.7 2.6 collective-permute-start.48
  175.3 2.8 %collective-permute-start.33 = (bf16[64,1024]{1,0:T(8,128)(2,1)S(1)}, bf16[64,1024]{1,0:T(8,128)(2,1)S(1)}, u32[]{:S(2)}, u32[]{:S(2)}) collective-permute-start(bf16[64,1024]{1,0:T(8,128)(2,1)S(1)} %get-tuple-element.112), channel_id=1, source_target_pairs={{0,3},{1,2},{2,1},{3,0},{4,7},{5,6},{6,5},{7,4},{8,11},{9,10},{10,... | collective-permute-start | bytes 393224 | tf_op jit(solution)/shard_map/ppermute | solution.py:32
  179.6 2.6 collective-permute-start.52
  183.4 16.9 %collective-permute-done.48 = bf16[4,64,576]{2,1,0:T(8,128)(2,1)S(1)} collective-permute-done((bf16[4,64,576]{2,1,0:T(8,128)(2,1)S(1)}, bf16[4,64,576]{2,1,0:T(8,128)(2,1)S(1)}, u32[]{:S(2)}, u32[]{:S(2)}) %collective-permute-start.48) | collective-permute-done | bytes 294944 | tf_op jit(solution)/shard_map/ppermute | solution.py:32
  201.4 5.9 %collective-permute-done.50 = bf16[4,64,576]{2,1,0:T(8,128)(2,1)S(1)} collective-permute-done((bf16[4,64,576]{2,1,0:T(8,128)(2,1)S(1)}, bf16[4,64,576]{2,1,0:T(8,128)(2,1)S(1)}, u32[]{:S(2)}, u32[]{:S(2)}) %collective-permute-start.50) | collective-permute-done | bytes 294944 | tf_op jit(solution)/shard_map/ppermute | solution.py:32
  208.5 4.7 %collective-permute-done.52 = bf16[4,64,576]{2,1,0:T(8,128)(2,1)S(1)} collective-permute-done((bf16[4,64,576]{2,1,0:T(8,128)(2,1)S(1)}, bf16[4,64,576]{2,1,0:T(8,128)(2,1)S(1)}, u32[]{:S(2)}, u32[]{:S(2)}) %collective-permute-start.52) | collective-permute-done | bytes 294944 | tf_op jit(solution)/shard_map/ppermute | solution.py:32
  214.7 2.4 collective-permute-start.55
  218.0 4.3 %collective-permute-done.53 = bf16[192,576]{1,0:T(8,128)(2,1)S(1)} collective-permute-done((bf16[192,576]{1,0:T(8,128)(2,1)S(1)}, bf16[192,576]{1,0:T(8,128)(2,1)S(1)}, u32[]{:S(2)}, u32[]{:S(2)}) %collective-permute-start.53) | collective-permute-done | bytes 221216 | tf_op jit(solution)/shard_map/ppermute | solution.py:32
  222.3 3.9 %collective-permute-done.54 = bf16[192,576]{1,0:T(8,128)(2,1)S(1)} collective-permute-done((bf16[192,576]{1,0:T(8,128)(2,1)S(1)}, bf16[192,576]{1,0:T(8,128)(2,1)S(1)}, u32[]{:S(2)}, u32[]{:S(2)}) %collective-permute-start.54) | collective-permute-done | bytes 221216 | tf_op jit(solution)/shard_map/ppermute | solution.py:32
  228.2 7.4 %shard_map.261 = (bf16[256,1024]{1,0:T(8,128)(2,1)S(1)}, bf16[256,1024]{1,0:T(8,128)(2,1)}, f32[8,512]{1,0:T(8,128)S(1)}, bf16[2,4,72,384]{3,2,1,0:T(8,128)(2,1)S(1)}, bf16[2,4,72,384]{3,2,1,0:T(8,128)(2,1)S(1)}) custom-call(s32[3]{0:T(128)S(1)} %pad_add_fusion.2.where, bf16[256,1024]{1,0:T(8,128)(2,1)S(1)} %get-tuple-element.136.mine, ...), custom_call_target="tpu_custom_call" | custom-call | tf_op jit(solution)/shard_map/pallas_call | solution.py:60
  238.2 8.3 %collective-permute-done.41 = bf16[2,4,72,384]{3,2,1,0:T(8,128)(2,1)S(1)} collective-permute-done((bf16[2,4,72,384]{3,2,1,0:T(8,128)(2,1)S(1)}, bf16[2,4,72,384]{3,2,1,0:T(8,128)(2,1)S(1)}, u32[]{:S(2)}, u32[]{:S(2)}) %collective-permute-start.41) | collective-permute-done | bytes 442400 | tf_op jit(solution)/shard_map/ppermute | solution.py:32
  247.3 3.4 %collective-permute-start.42 = (bf16[4,72,384]{2,1,0:T(8,128)(2,1)}, bf16[4,72,384]{2,1,0:T(8,128)(2,1)S(1)}, u32[]{:S(2)}, u32[]{:S(2)}) collective-permute-start(bf16[4,72,384]{2,1,0:T(8,128)(2,1)} %fusion.11), channel_id=1, source_target_pairs={{0,16},{8,24},{16,0},{24,8},{1,17},{9,25},{17,1},{25,9},{2,18},{10... | collective-permute-start | bytes 663560 | tf_op jit(solution)/shard_map/ppermute | solution.py:32
  259.5 2.5 collective-permute-start.44
  264.2 2.8 %collective-permute-done.45 = bf16[72,384]{1,0:T(8,128)(2,1)S(1)} collective-permute-done((bf16[72,384]{1,0:T(8,128)(2,1)S(1)}, bf16[72,384]{1,0:T(8,128)(2,1)S(1)}, u32[]{:S(2)}, u32[]{:S(2)}) %collective-permute-start.45) | collective-permute-done | bytes 55328 | tf_op jit(solution)/shard_map/ppermute | solution.py:32
  (327 shorter events, 100.0 us)
Async XLA Ops:
  8.2 17.4 %collective-permute-start = (bf16[528,256]{1,0:T(8,128)(2,1)}, bf16[528,256]{1,0:T(8,128)(2,1)S(1)}, u32[]{:S(2)}, u32[]{:S(2)}) collective-permute-start(bf16[528,256]{1,0:T(8,128)(2,1)} %get-tuple-element.75), channel_id=1, source_target_pairs={{0,1},{1,0},{2,3},{3,2},{4,5},{5,4},{6,7},{7,6},{8,9},{9,8},{10,11... | collective-permute-start | bytes 811016 | tf_op jit(solution)/shard_map/ppermute | solution.py:32
  11.2 20.1 %collective-permute-start.1 = (bf16[528,256]{1,0:T(8,128)(2,1)}, bf16[528,256]{1,0:T(8,128)(2,1)S(1)}, u32[]{:S(2)}, u32[]{:S(2)}) collective-permute-start(bf16[528,256]{1,0:T(8,128)(2,1)} %get-tuple-element.76), channel_id=1, source_target_pairs={{0,2},{1,3},{2,0},{3,1},{4,6},{5,7},{6,4},{7,5},{8,10},{9,11},{10,... | collective-permute-start | bytes 811016 | tf_op jit(solution)/shard_map/ppermute | solution.py:32
  12.7 18.6 %collective-permute-start.2 = (bf16[528,256]{1,0:T(8,128)(2,1)}, bf16[528,256]{1,0:T(8,128)(2,1)S(1)}, u32[]{:S(2)}, u32[]{:S(2)}) collective-permute-start(bf16[528,256]{1,0:T(8,128)(2,1)} %get-tuple-element.77), channel_id=1, source_target_pairs={{0,3},{1,2},{2,1},{3,0},{4,7},{5,6},{6,5},{7,4},{8,11},{9,10},{10,... | collective-permute-start | bytes 811016 | tf_op jit(solution)/shard_map/ppermute | solution.py:32
  15.9 22.1 %collective-permute-start.10 = (bf16[512,256]{1,0:T(8,128)(2,1)}, bf16[512,256]{1,0:T(8,128)(2,1)}, u32[]{:S(2)}, u32[]{:S(2)}) collective-permute-start(bf16[512,256]{1,0:T(8,128)(2,1)} %get-tuple-element.82), channel_id=1, source_target_pairs={{0,3},{1,2},{2,1},{3,0},{4,7},{5,6},{6,5},{7,4},{8,11},{9,10},{10,... | collective-permute-start | bytes 786440 | tf_op jit(solution)/shard_map/ppermute | solution.py:32
  18.8 21.3 %collective-permute-start.8 = (bf16[512,256]{1,0:T(8,128)(2,1)}, bf16[512,256]{1,0:T(8,128)(2,1)}, u32[]{:S(2)}, u32[]{:S(2)}) collective-permute-start(bf16[512,256]{1,0:T(8,128)(2,1)} %get-tuple-element.80), channel_id=1, source_target_pairs={{0,1},{1,0},{2,3},{3,2},{4,5},{5,4},{6,7},{7,6},{8,9},{9,8},{10,11... | collective-permute-start | bytes 786440 | tf_op jit(solution)/shard_map/ppermute | solution.py:32
  25.6 16.9 %collective-permute-start.9 = (bf16[512,256]{1,0:T(8,128)(2,1)}, bf16[512,256]{1,0:T(8,128)(2,1)S(1)}, u32[]{:S(2)}, u32[]{:S(2)}) collective-permute-start(bf16[512,256]{1,0:T(8,128)(2,1)} %get-tuple-element.81), channel_id=1, source_target_pairs={{0,2},{1,3},{2,0},{3,1},{4,6},{5,7},{6,4},{7,5},{8,10},{9,11},{10,... | collective-permute-start | bytes 786440 | tf_op jit(solution)/shard_map/ppermute | solution.py:32
  31.3 22.7 %collective-permute-start.18 = (bf16[832,256]{1,0:T(8,128)(2,1)}, bf16[832,256]{1,0:T(8,128)(2,1)}, u32[]{:S(2)}, u32[]{:S(2)}) collective-permute-start(bf16[832,256]{1,0:T(8,128)(2,1)} %get-tuple-element.91), channel_id=1, source_target_pairs={{0,1},{1,0},{2,3},{3,2},{4,5},{5,4},{6,7},{7,6},{8,9},{9,8},{10,11... | collective-permute-start | bytes 1277960 | tf_op jit(solution)/shard_map/ppermute | solution.py:32
  31.6 13.8 %collective-permute-start.3 = (bf16[256,1024]{1,0:T(8,128)(2,1)S(1)}, bf16[256,1024]{1,0:T(8,128)(2,1)S(1)}, u32[]{:S(2)}, u32[]{:S(2)}) collective-permute-start(bf16[256,1024]{1,0:T(8,128)(2,1)S(1)} %get-tuple-element.136.mine), channel_id=1, source_target_pairs={{0,4},{4,0},{1,5},{5,1},{2,6},{6,2},{3,7},{7,3},{8,12},{12,8},{9,1... | collective-permute-start | bytes 1572872 | tf_op jit(solution)/shard_map/ppermute | solution.py:32
  38.0 14.0 %collective-permute-start.12 = (bf16[256,576]{1,0:T(8,128)(2,1)S(1)}, bf16[256,576]{1,0:T(8,128)(2,1)S(1)}, u32[]{:S(2)}, u32[]{:S(2)}) collective-permute-start(bf16[256,576]{1,0:T(8,128)(2,1)S(1)} %get-tuple-element.84), channel_id=1, source_target_pairs={{0,1},{1,0},{2,3},{3,2},{4,5},{5,4},{6,7},{7,6},{8,9},{9,8},{10,11... | collective-permute-start | bytes 884744 | tf_op jit(solution)/shard_map/ppermute | solution.py:32
  40.1 21.7 %collective-permute-start.19 = (bf16[832,256]{1,0:T(8,128)(2,1)S(1)}, bf16[832,256]{1,0:T(8,128)(2,1)S(1)}, u32[]{:S(2)}, u32[]{:S(2)}) collective-permute-start(bf16[832,256]{1,0:T(8,128)(2,1)S(1)} %copy-done.58), channel_id=1, source_target_pairs={{0,2},{1,3},{2,0},{3,1},{4,6},{5,7},{6,4},{7,5},{8,10},{9,11},{10,... | collective-permute-start | bytes 1277960 | tf_op jit(solution)/shard_map/ppermute | solution.py:32
  45.3 55.2 %collective-permute-start.11 = (bf16[512,1024]{1,0:T(8,128)(2,1)S(1)}, bf16[512,1024]{1,0:T(8,128)(2,1)S(1)}, u32[]{:S(2)}, u32[]{:S(2)}) collective-permute-start(bf16[512,1024]{1,0:T(8,128)(2,1)S(1)} %shard_map.250.joined.out_weight), channel_id=1, source_target_pairs={{0,4},{4,0},{1,5},{5,1},{2,6},{6,2},{3,7},{7,3},{8,12},{12,8},{9,1... | collective-permute-start | bytes 3145736 | tf_op jit(solution)/shard_map/ppermute | solution.py:32
  45.4 32.0 %collective-permute-start.20 = (bf16[832,256]{1,0:T(8,128)(2,1)S(1)}, bf16[832,256]{1,0:T(8,128)(2,1)S(1)}, u32[]{:S(2)}, u32[]{:S(2)}) collective-permute-start(bf16[832,256]{1,0:T(8,128)(2,1)S(1)} %copy-done.56), channel_id=1, source_target_pairs={{0,3},{1,2},{2,1},{3,0},{4,7},{5,6},{6,5},{7,4},{8,11},{9,10},{10,... | collective-permute-start | bytes 1277960 | tf_op jit(solution)/shard_map/ppermute | solution.py:32
  52.0 12.3 %collective-permute-start.4 = (bf16[512,128]{1,0:T(8,128)(2,1)S(1)}, bf16[512,128]{1,0:T(8,128)(2,1)S(1)}, u32[]{:S(2)}, u32[]{:S(2)}) collective-permute-start(bf16[512,128]{1,0:T(8,128)(2,1)S(1)} %get-tuple-element.78.first0.context_in), channel_id=1, source_target_pairs={{0,1},{1,0},{2,3},{3,2},{4,5},{5,4},{6,7},{7,6},{8,9},{9,8},{10,11... | collective-permute-start | bytes 393224 | tf_op jit(solution)/shard_map/ppermute | solution.py:32
  54.0 24.6 %collective-permute-start.13 = (bf16[256,576]{1,0:T(8,128)(2,1)S(1)}, bf16[256,576]{1,0:T(8,128)(2,1)S(1)}, u32[]{:S(2)}, u32[]{:S(2)}) collective-permute-start(bf16[256,576]{1,0:T(8,128)(2,1)S(1)} %get-tuple-element.85), channel_id=1, source_target_pairs={{0,2},{1,3},{2,0},{3,1},{4,6},{5,7},{6,4},{7,5},{8,10},{9,11},{10,... | collective-permute-start | bytes 884744 | tf_op jit(solution)/shard_map/ppermute | solution.py:32
  61.8 12.6 %collective-permute-start.5 = (bf16[512,128]{1,0:T(8,128)(2,1)S(1)}, bf16[512,128]{1,0:T(8,128)(2,1)S(1)}, u32[]{:S(2)}, u32[]{:S(2)}) collective-permute-start(bf16[512,128]{1,0:T(8,128)(2,1)S(1)} %get-tuple-element.78.first0.context_in), channel_id=1, source_target_pairs={{0,2},{1,3},{2,0},{3,1},{4,6},{5,7},{6,4},{7,5},{8,10},{9,11},{10,... | collective-permute-start | bytes 393224 | tf_op jit(solution)/shard_map/ppermute | solution.py:32
  77.4 23.1 %collective-permute-start.7 = (bf16[512,512]{1,0:T(8,128)(2,1)S(1)}, bf16[512,512]{1,0:T(8,128)(2,1)S(1)}, u32[]{:S(2)}, u32[]{:S(2)}) collective-permute-start(bf16[512,512]{1,0:T(8,128)(2,1)S(1)} %shard_map.248.context_near), channel_id=1, source_target_pairs={{0,4},{4,0},{1,5},{5,1},{2,6},{6,2},{3,7},{7,3},{8,12},{12,8},{9,1... | collective-permute-start | bytes 1572872 | tf_op jit(solution)/shard_map/ppermute | solution.py:32
  78.7 31.1 %collective-permute-start.26 = (bf16[256,1024]{1,0:T(8,128)(2,1)S(1)}, bf16[256,1024]{1,0:T(8,128)(2,1)S(1)}, u32[]{:S(2)}, u32[]{:S(2)}) collective-permute-start(bf16[256,1024]{1,0:T(8,128)(2,1)S(1)} %shard_map.256.cot_mine), channel_id=1, source_target_pairs={{0,4},{4,0},{1,5},{5,1},{2,6},{6,2},{3,7},{7,3},{8,12},{12,8},{9,1... | collective-permute-start | bytes 1572872 | tf_op jit(solution)/shard_map/ppermute | solution.py:32
  86.4 14.1 %collective-permute-start.17 = (bf16[256,576]{1,0:T(8,128)(2,1)S(1)}, bf16[256,576]{1,0:T(8,128)(2,1)S(1)}, u32[]{:S(2)}, u32[]{:S(2)}) collective-permute-start(bf16[256,576]{1,0:T(8,128)(2,1)S(1)} %collective-permute-done.14.near3), channel_id=1, source_target_pairs={{0,8},{8,0},{16,24},{24,16},{1,9},{9,1},{17,25},{25,17},{2,10},{10... | collective-permute-start | bytes 884744 | tf_op jit(solution)/shard_map/ppermute | solution.py:32
  124.6 17.9 %collective-permute-start.47 = (bf16[2,4,64,576]{3,2,1,0:T(8,128)(2,1)}, bf16[2,4,64,576]{3,2,1,0:T(8,128)(2,1)}, u32[]{:S(2)}, u32[]{:S(2)}) collective-permute-start(bf16[2,4,64,576]{3,2,1,0:T(8,128)(2,1)} %get-tuple-element.130), channel_id=1, source_target_pairs={{0,8},{8,0},{16,24},{24,16},{1,9},{9,1},{17,25},{25,17},{2,10},{10... | collective-permute-start | bytes 1769480 | tf_op jit(solution)/shard_map/ppermute | solution.py:32
  130.4 26.1 %collective-permute-start.49 = (bf16[2,4,64,576]{3,2,1,0:T(8,128)(2,1)}, bf16[2,4,64,576]{3,2,1,0:T(8,128)(2,1)}, u32[]{:S(2)}, u32[]{:S(2)}) collective-permute-start(bf16[2,4,64,576]{3,2,1,0:T(8,128)(2,1)} %get-tuple-element.132), channel_id=1, source_target_pairs={{0,8},{8,0},{16,24},{24,16},{1,9},{9,1},{17,25},{25,17},{2,10},{10... | collective-permute-start | bytes 1769480 | tf_op jit(solution)/shard_map/ppermute | solution.py:32
  132.0 35.9 %collective-permute-start.51 = (bf16[2,4,64,576]{3,2,1,0:T(8,128)(2,1)S(1)}, bf16[2,4,64,576]{3,2,1,0:T(8,128)(2,1)S(1)}, u32[]{:S(2)}, u32[]{:S(2)}) collective-permute-start(bf16[2,4,64,576]{3,2,1,0:T(8,128)(2,1)S(1)} %copy-done.54), channel_id=1, source_target_pairs={{0,8},{8,0},{16,24},{24,16},{1,9},{9,1},{17,25},{25,17},{2,10},{10... | collective-permute-start | bytes 1769480 | tf_op jit(solution)/shard_map/ppermute | solution.py:32
  136.1 31.8 %collective-permute-start.28 = (bf16[64,1024]{1,0:T(8,128)(2,1)S(1)}, bf16[64,1024]{1,0:T(8,128)(2,1)S(1)}, u32[]{:S(2)}, u32[]{:S(2)}) collective-permute-start(bf16[64,1024]{1,0:T(8,128)(2,1)S(1)} %get-tuple-element.105), channel_id=1, source_target_pairs={{0,1},{1,0},{2,3},{3,2},{4,5},{5,4},{6,7},{7,6},{8,9},{9,8},{10,11... | collective-permute-start | bytes 393224 | tf_op jit(solution)/shard_map/ppermute | solution.py:32
  137.4 33.3 %collective-permute-start.29 = (bf16[64,1024]{1,0:T(8,128)(2,1)S(1)}, bf16[64,1024]{1,0:T(8,128)(2,1)S(1)}, u32[]{:S(2)}, u32[]{:S(2)}) collective-permute-start(bf16[64,1024]{1,0:T(8,128)(2,1)S(1)} %get-tuple-element.106), channel_id=1, source_target_pairs={{0,2},{1,3},{2,0},{3,1},{4,6},{5,7},{6,4},{7,5},{8,10},{9,11},{10,... | collective-permute-start | bytes 393224 | tf_op jit(solution)/shard_map/ppermute | solution.py:32
  142.5 30.9 %collective-permute-start.30 = (bf16[64,1024]{1,0:T(8,128)(2,1)S(1)}, bf16[64,1024]{1,0:T(8,128)(2,1)S(1)}, u32[]{:S(2)}, u32[]{:S(2)}) collective-permute-start(bf16[64,1024]{1,0:T(8,128)(2,1)S(1)} %get-tuple-element.107), channel_id=1, source_target_pairs={{0,3},{1,2},{2,1},{3,0},{4,7},{5,6},{6,5},{7,4},{8,11},{9,10},{10,... | collective-permute-start | bytes 393224 | tf_op jit(solution)/shard_map/ppermute | solution.py:32
  156.6 18.0 %collective-permute-start.22 = (bf16[256,256]{1,0:T(8,128)(2,1)S(1)}, bf16[256,256]{1,0:T(8,128)(2,1)S(1)}, u32[]{:S(2)}, u32[]{:S(2)}) collective-permute-start(bf16[256,256]{1,0:T(8,128)(2,1)S(1)} %get-tuple-element.97), channel_id=1, source_target_pairs={{0,1},{1,0},{2,3},{3,2},{4,5},{5,4},{6,7},{7,6},{8,9},{9,8},{10,11... | collective-permute-start | bytes 393224 | tf_op jit(solution)/shard_map/ppermute | solution.py:32
  170.7 29.6 %collective-permute-start.48 = (bf16[4,64,576]{2,1,0:T(8,128)(2,1)S(1)}, bf16[4,64,576]{2,1,0:T(8,128)(2,1)S(1)}, u32[]{:S(2)}, u32[]{:S(2)}) collective-permute-start(bf16[4,64,576]{2,1,0:T(8,128)(2,1)S(1)} %fusion.4), channel_id=1, source_target_pairs={{0,16},{8,24},{16,0},{24,8},{1,17},{9,25},{17,1},{25,9},{2,18},{10... | collective-permute-start | bytes 884744 | tf_op jit(solution)/shard_map/ppermute | solution.py:32
  173.4 33.9 %collective-permute-start.50 = (bf16[4,64,576]{2,1,0:T(8,128)(2,1)S(1)}, bf16[4,64,576]{2,1,0:T(8,128)(2,1)S(1)}, u32[]{:S(2)}, u32[]{:S(2)}) collective-permute-start(bf16[4,64,576]{2,1,0:T(8,128)(2,1)S(1)} %fusion.5), channel_id=1, source_target_pairs={{0,16},{8,24},{16,0},{24,8},{1,17},{9,25},{17,1},{25,9},{2,18},{10... | collective-permute-start | bytes 884744 | tf_op jit(solution)/shard_map/ppermute | solution.py:32
  179.6 33.6 %collective-permute-start.52 = (bf16[4,64,576]{2,1,0:T(8,128)(2,1)S(1)}, bf16[4,64,576]{2,1,0:T(8,128)(2,1)S(1)}, u32[]{:S(2)}, u32[]{:S(2)}) collective-permute-start(bf16[4,64,576]{2,1,0:T(8,128)(2,1)S(1)} %fusion.6), channel_id=1, source_target_pairs={{0,16},{8,24},{16,0},{24,8},{1,17},{9,25},{17,1},{25,9},{2,18},{10... | collective-permute-start | bytes 884744 | tf_op jit(solution)/shard_map/ppermute | solution.py:32
  182.2 34.9 %collective-permute-start.25 = (bf16[256,256]{1,0:T(8,128)(2,1)S(1)}, bf16[256,256]{1,0:T(8,128)(2,1)S(1)}, u32[]{:S(2)}, u32[]{:S(2)}) collective-permute-start(bf16[256,256]{1,0:T(8,128)(2,1)S(1)} %add_convert_fusion.4), channel_id=1, source_target_pairs={{0,4},{4,0},{1,5},{5,1},{2,6},{6,2},{3,7},{7,3},{8,12},{12,8},{9,1... | collective-permute-start | bytes 393224 | tf_op jit(solution)/shard_map/ppermute | solution.py:32
  182.8 44.6 %collective-permute-start.34 = (bf16[256,1024]{1,0:T(8,128)(2,1)S(1)}, bf16[256,1024]{1,0:T(8,128)(2,1)S(1)}, u32[]{:S(2)}, u32[]{:S(2)}) collective-permute-start(bf16[256,1024]{1,0:T(8,128)(2,1)S(1)} %shard_map.260.grad_mine), channel_id=1, source_target_pairs={{0,4},{4,0},{1,5},{5,1},{2,6},{6,2},{3,7},{7,3},{8,12},{12,8},{9,1... | collective-permute-start | bytes 1572872 | tf_op jit(solution)/shard_map/ppermute | solution.py:32
  237.5 16.1 %collective-permute-start.35 = (bf16[256,1024]{1,0:T(8,128)(2,1)}, bf16[256,1024]{1,0:T(8,128)(2,1)S(1)}, u32[]{:S(2)}, u32[]{:S(2)}) collective-permute-start(bf16[256,1024]{1,0:T(8,128)(2,1)} %get-tuple-element.118), channel_id=1, source_target_pairs={{0,4},{4,0},{1,5},{5,1},{2,6},{6,2},{3,7},{7,3},{8,12},{12,8},{9,1... | collective-permute-start | bytes 1572872 | tf_op jit(solution)/shard_map/ppermute | solution.py:32
  237.6 16.0 %collective-permute-start.36 = (f32[8,256]{1,0:T(8,128)S(1)}, f32[8,256]{1,0:T(8,128)S(1)}, u32[]{:S(2)}, u32[]{:S(2)}) collective-permute-start(f32[8,256]{1,0:T(8,128)S(1)} %slice.362), channel_id=1, source_target_pairs={{0,4},{4,0},{1,5},{5,1},{2,6},{6,2},{3,7},{7,3},{8,12},{12,8},{9,1... | collective-permute-start | bytes 24584 | tf_op jit(solution)/shard_map/ppermute | solution.py:32
  (94 other events, 652.0 us)

commit v2 on v1

--- a/solution.py
+++ b/solution.py
@@ -48,7 +48,7 @@
 
 
 def kernel_call(kernel, outs, *args, scalars=None, scratch=(), fetch=0):
-    specs = [pl.BlockSpec(memory_space=pl.ANY)] * fetch
+    specs = [pl.BlockSpec(memory_space=pltpu.HBM)] * fetch
     specs = specs + [pl.BlockSpec(memory_space=pltpu.VMEM)] * (len(args) - fetch)
     scratch_shapes = [pltpu.VMEM(shape, dtype) for shape, dtype in scratch]
     if fetch:
@@ -111,23 +111,25 @@
         out[half + 16 :, q_size:] = jnp.concatenate(both, axis=1)
 
 
-def pack_two_kernel(where, weight_in, out0, out1, out2, out3, weight, semaphores):
-    fetched((weight_in,), (weight,), semaphores)
+def pack_two_kernel(
+    where, weight_in, cot_in, out0, out1, out2, out3, weight, cot, semaphores
+):
+    fetched((weight_in, cot_in), (weight, cot), semaphores)
     outs = (out0, out1, out2, out3)
-    size = weight.shape[0] // len(outs)
+    size, half = weight.shape[0] // len(outs), cot.shape[0] // 2
     for k, out in enumerate(outs):
+        out[:half, :] = cot[pl.ds(pl.multiple_of(where[0] * half, half), half), :]
         for j in range(len(outs)):
             source = pl.multiple_of((where[1] ^ (k ^ j)) * size, size)
-            out[j * size : (j + 1) * size, :] = weight[pl.ds(source, size), :]
-
-
-def pack_three_kernel(where, down_in, cot_in, out0, out1, out2, out3, down, cot, semaphores):
-    fetched((down_in, cot_in), (down, cot), semaphores)
+            out[half + j * size : half + (j + 1) * size, :] = weight[pl.ds(source, size), :]
+
+
+def pack_three_kernel(where, down_in, out0, out1, out2, out3, down, semaphores):
+    fetched((down_in,), (down,), semaphores)
     outs = (out0, out1, out2, out3)
-    size, half = down.shape[0] // len(outs), cot.shape[0] // 2
+    size = down.shape[0] // len(outs)
     for k, out in enumerate(outs):
-        out[:size, :] = down[pl.ds(pl.multiple_of((where[1] ^ k) * size, size), size), :]
-        out[size:, :] = cot[pl.ds(pl.multiple_of(where[0] * half, half), half), :]
+        out[...] = down[pl.ds(pl.multiple_of((where[1] ^ k) * size, size), size), :]
 
 
 def pack_gate_kernel(
@@ -162,31 +164,36 @@
         out[:, k * part : (k + 1) * part] = piece[piece.shape[0] - size :, :]
 
 
-def forward_kernel(
+def project_kernel(
     where, mine, other, context_near, context_far, joined, joined_far,
-    near0, near1, near2, near3, far0, far1, far2, far3, first0, first1, first2, first3,
-    normed_out, gate_out, up_out, hidden_out, own_out, share_out, sum_scratch,
+    first0, first1, first2, first3, normed_out, own_out, share_out, sum_scratch,
 ):
     buffers = (first0, first1, first2, first3)
-    half, part = mine.shape[0], near0.shape[0]
-    size = context_near.shape[1]
+    half, part = mine.shape[0], first0.shape[1]
     share = share_out.shape[0]
-    top = mine[...].astype(F32) + matmul(context_near[:half, :], joined[:size, :])
-    top = top + matmul(context_far[half:, :], joined_far[:size, :])
-    low = other[...].astype(F32) + matmul(context_near[half:, :], joined[:size, :])
-    low = low + matmul(context_far[:half, :], joined_far[:size, :])
+    top = mine[...].astype(F32) + matmul(context_near[:half, :], joined[...])
+    top = top + matmul(context_far[half:, :], joined_far[...])
+    low = other[...].astype(F32) + matmul(context_near[half:, :], joined[...])
+    low = low + matmul(context_far[:half, :], joined_far[...])
     sum_scratch[...] = top
     own_out[...] = top[:, :part]
     share_out[...] = sum_scratch[pl.ds(pl.multiple_of(where[1] * share, share), share), :]
     gain = jnp.concatenate([gain_row(buffers, half + 3, k) for k in range(len(buffers))], axis=1)
-    first_pre = second_pre = None
     for i, rows in enumerate((top, low)):
         root = lax.rsqrt(jnp.mean(rows * rows, axis=1, keepdims=True) + EPSILON)
         normed_out[i * half : (i + 1) * half, :] = (rows * root * gain).astype(BF16)
+
+
+def hidden_kernel(
+    where, normed, near0, near1, near2, near3, far0, far1, far2, far3,
+    gate_out, up_out, hidden_out,
+):
+    part = near0.shape[0]
+    first_pre = second_pre = None
     for k, (near, far) in enumerate(
         ((near0, far0), (near1, far1), (near2, far2), (near3, far3))
     ):
-        block = normed_out[:, k * part : (k + 1) * part]
+        block = normed[:, k * part : (k + 1) * part]
         one, two = matmul(block, near[...]), matmul(block, far[...])
         first_pre = one if k == 0 else first_pre + one
         second_pre = two if k == 0 else second_pre + two
@@ -247,20 +254,23 @@
             out[j, k, :rows, :] = scratch[pl.ds(start, rows), :]
 
 
-def weight_grad_kernel(
-    where, cot_mine, cot_other, hidden, normed, gate_grad, up_grad,
-    down_send, gate_send, up_send, down_keep, gate_keep, up_keep, scratch,
-):
+def down_grad_kernel(where, cot_mine, cot_other, hidden, send, keep, scratch):
     half = hidden.shape[0] // 2
-    cols = down_send.shape[1]
+    cols, rows = send.shape[1], send.shape[2]
     part = cot_mine.shape[1] // cols
-    rows = down_send.shape[2]
     for k in range(cols):
         span = slice(k * part, (k + 1) * part)
         grad = matmul_tn(cot_mine[:, span], hidden[:half, :])
         grad = grad + matmul_tn(cot_other[:, span], hidden[half:, :])
         scratch[...] = grad.astype(BF16)
-        deal(where, scratch, k, down_send, down_keep, rows)
+        deal(where, scratch, k, send, keep, rows)
+
+
+def weight_grad_kernel(
+    where, normed, gate_grad, up_grad, gate_send, gate_keep, up_send, up_keep, scratch
+):
+    cols, rows = gate_send.shape[1], gate_send.shape[2]
+    part = normed.shape[1] // cols
     for upstream, send, keep in ((gate_grad, gate_send, gate_keep), (up_grad, up_send, up_keep)):
         for k in range(cols):
             span = slice(k * part, (k + 1) * part)
@@ -330,6 +340,46 @@
         span = slice(k * part, (k + 1) * part)
         out[:half, :] = (ours[:, span].astype(F32) + came[:, span].astype(F32)).astype(BF16)
         out[half:, :] = rows.astype(BF16)
+
+
+def join_first_kernel(first0, first1, first2, first3, out):
+    part, size = first0.shape[1], out.shape[0]
+    for k, piece in enumerate((first0, first1, first2, first3)):
+        out[:, k * part : (k + 1) * part] = piece[:size, :]
+
+
+def in_chip_order(where, pieces):
+    odd, high = (where[1] & 1) == 1, (where[1] & 2) == 2
+    ordered = []
+    for s in range(4):
+        low_pair = jnp.where(odd, pieces[s ^ 1], pieces[s])
+        high_pair = jnp.where(odd, pieces[s ^ 3], pieces[s ^ 2])
+        ordered.append(jnp.where(high, high_pair, low_pair))
+    return ordered
+
+
+def unpack_feed_kernel(where, came0, came1, came2, came3, down_out, gate_out, up_out):
+    rows = gate_out.shape[0]
+    pieces = in_chip_order(where, [v[...] for v in (came0, came1, came2, came3)])
+    for i, out in enumerate((down_out, gate_out, up_out)):
+        span = slice(i * rows, (i + 1) * rows)
+        out[...] = jnp.concatenate([v[span].astype(F32) for v in pieces], axis=1)
+
+
+def unpack_mixed_kernel(
+    where, came0, came1, came2, came3, query_out, key_out, value_out, output_out, gain_out
+):
+    rows = query_out.shape[0]
+    pieces = in_chip_order(where, [v[...] for v in (came0, came1, came2, came3)])
+    two = query_out.shape[1] // len(pieces)
+    size = two // 2
+    pieces = [v.astype(F32) for v in pieces]
+    for out, start, wide in (
+        (query_out, 0, two), (key_out, two, size), (value_out, two + size, size),
+        (output_out, 2 * two, two),
+    ):
+        out[...] = jnp.concatenate([v[:rows, start : start + wide] for v in pieces], axis=1)
+    gain_out[...] = pieces[0][rows:] + pieces[1][rows:] + pieces[2][rows:] + pieces[3][rows:]
 
 
 def lane_is_first(size):
@@ -531,7 +581,6 @@
     row = lax.axis_index("row")
     col = lax.axis_index("col")
     plane = lax.axis_index("dp")
-    kin = [col ^ k for k in range(cols)]
 
     def mine_first(values):
         return jnp.where(row == 0, values, jnp.roll(values, half, axis=0))
@@ -541,10 +590,6 @@
 
     def both_rows(values):
         return jnp.concatenate([values, flip(values, "row", 1)], axis=0)
-
-    def chosen(blocks):
-        stacked = jnp.stack(blocks)
-        return [lax.dynamic_index_in_dim(stacked, kin[k], 0, keepdims=False) for k in range(cols)]
 
     q_size = query_weight.shape[1] // cols
     units = gate_weight.shape[1] // cols
@@ -564,7 +609,7 @@
             fetch=4,
         ),
     )
-    input_mine = jnp.concatenate([v[:half] for v in first_in], axis=1)
+    (input_mine,) = kernel_call(join_first_kernel, [((half, width), BF16)], *first_in)
     gain_parts = jnp.concatenate([v[half : half + 16] for v in first_in], axis=1).astype(F32)
     gain_one = gain_parts[0] + gain_parts[1] + gain_parts[2]
     input_other = flip(input_mine, "row", 1)
@@ -579,32 +624,30 @@
     near_parts = exchange(gate_in[:cols])
     far_parts = [gate_in[cols]] + [flip(v, "dp", 1) for v in near_parts[1:]]
     inner_size = output_weight.shape[0]
-    second_parts = exchange(
-        kernel_call(
-            pack_two_kernel,
-            [((inner_size, part), BF16)] * cols,
-            output_weight,
-            scalars=where,
-            fetch=1,
-        ),
-    )
-    down_parts = exchange(
-        kernel_call(
-            pack_three_kernel,
-            [((units + half, part), BF16)] * cols,
-            down_weight,
-            cotangent,
-            scalars=where,
-            fetch=2,
-        ),
-    )
-
+    two_out = kernel_call(
+        pack_two_kernel,
+        [((half + inner_size, part), BF16)] * cols,
+        output_weight,
+        cotangent,
+        scalars=where,
+        fetch=2,
+    )
+    second_parts = exchange(two_out)
+    three_out = kernel_call(
+        pack_three_kernel,
+        [((units, part), BF16)] * cols,
+        down_weight,
+        scalars=where,
+        fetch=1,
+    )
+    down_parts = exchange(three_out)
+
+    group = q_size // head
     segment_ids = mine_first(segments)
     places = mine_first(positions)
     index = mine_first(jnp.arange(tokens))
 
     cosine, sine_part = rope_tables(places, head)
-    group = q_size // head
     cos_lanes = jnp.concatenate([cosine] * (2 * group), axis=1)
     sin_lanes = jnp.concatenate([-sine_part, sine_part] * group, axis=1)
     head_gains = jnp.stack([jnp.tile(query_gain, group), jnp.tile(key_gain, group)])
@@ -636,32 +679,42 @@
     context_far = flip(context_near, "row", 1)
     (second_in,) = kernel_call(join_kernel, [((inner_size, width), BF16)], *second_parts)
     second_far = flip(second_in, "row", 1)
-    (cot_mine,) = kernel_call(join_kernel, [((half, width), BF16)], *down_parts)
+    (cot_mine,) = kernel_call(join_first_kernel, [((half, width), BF16)], *second_parts)
     cot_other = flip(cot_mine, "row", 1)
 
     share = half // cols
-    normed_two, gate_pre, up_pre, hidden, first_block, first_share = kernel_call(
-        forward_kernel,
-        [
-            ((tokens, width), BF16),
-            ((tokens, units), F32),
-            ((tokens, units), F32),
-            ((tokens, units), BF16),
-            ((half, part), F32),
-            ((share, width), F32),
-        ],
+    normed_two, first_block, first_share = kernel_call(
+        project_kernel,
+        [((tokens, width), BF16), ((half, part), F32), ((share, width), F32)],
         input_mine,
         input_other,
         context_near,
         context_far,
         second_in,
         second_far,
-        *near_parts,
-        *far_parts,
         *first_in,
         scalars=where,
         scratch=[((half, width), F32)],
     )
+    gate_pre, up_pre, hidden = kernel_call(
+        hidden_kernel,
+        [((tokens, units), F32), ((tokens, units), F32), ((tokens, units), BF16)],
+        normed_two,
+        *near_parts,
+        *far_parts,
+        scalars=where,
+    )
+    rows = part // planes
+    if planes == 4:
+        down_dealt = kernel_call(
+            down_grad_kernel,
+            [((2, cols, rows, units), BF16)] * 2,
+            cot_mine,
+            cot_other,
+            hidden,
+            scalars=where,
+            scratch=[((part, units), BF16)],
+        )
     gate_grad, up_grad, two_mine, two_other = kernel_call(
         backward_kernel,
         [((tokens, units), BF16)] * 2 + [((half, width), BF16)] * 2,
@@ -694,11 +747,9 @@
         *first_in,
         scalars=where,
     )
+    first_back = exchange(first_pieces)
     (first_half,) = kernel_call(
-        join_tokens_kernel,
-        [((half, width), BF16)],
-        *exchange(first_pieces),
-        scalars=where,
+        join_tokens_kernel, [((half, width), BF16)], *first_back, scalars=where
     )
     first_other = flip(first_half, "row", 1)
 
@@ -711,24 +762,18 @@
     def scattered(split):
         return lax.psum_scatter(split, "dp", scatter_dimension=0, tiled=True)[0]
 
-    def arranged(pieces):
-        return [v.astype(F32) for v in chosen(exchange(pieces))]
-
-    rows = part // planes
     if planes == 4:
         dealt = kernel_call(
             weight_grad_kernel,
-            [((2, cols, rows, units), BF16)] * 6,
-            cot_mine,
-            cot_other,
-            hidden,
+            [((2, cols, rows, units), BF16)] * 4,
             normed_two,
             gate_grad,
             up_grad,
             scalars=where,
             scratch=[((part, units), BF16)],
         )
-        sums = [summed(dealt[i], dealt[i + 3]) for i in range(3)]
+        dealt = list(down_dealt) + list(dealt)
+        sums = [summed(dealt[2 * i], dealt[2 * i + 1]) for i in range(3)]
     else:
         cot_all = jnp.concatenate([cot_mine, cot_other], axis=0)
         sums = [
@@ -741,10 +786,10 @@
                 matmul_tn(normed_two, up_grad),
             )
         ]
-    shares = arranged([jnp.concatenate([v[k] for v in sums], axis=0) for k in range(cols)])
-    down_share, gate_share, up_share = [
-        jnp.concatenate([v[i * rows : (i + 1) * rows] for v in shares], axis=1) for i in range(3)
-    ]
+    feed_in = exchange([jnp.concatenate([v[k] for v in sums], axis=0) for k in range(cols)])
+    down_share, gate_share, up_share = kernel_call(
+        unpack_feed_kernel, [((rows, cols * units), F32)] * 3, *feed_in, scalars=where
+    )
 
     result_mine, result_other = kernel_call(
         result_kernel, [((half, width), BF16)] * 2, hidden, *down_parts
@@ -805,15 +850,19 @@
         lines = jnp.broadcast_to(mixed_second[:, None], (cols, planes, 8, mixed_size))
         blocks = mixed_first.reshape(cols, planes, rows, mixed_size)
         mixed_sum = scattered(jnp.moveaxis(jnp.concatenate([blocks, lines], axis=2), 1, 0))
-    mixed_share = arranged([mixed_sum[k] for k in range(cols)])
-    kv_start = q_size + head
-    query_share = jnp.concatenate([v[:rows, :q_size] for v in mixed_share], axis=1)
-    key_share = jnp.concatenate([v[:rows, q_size:kv_start] for v in mixed_share], axis=1)
-    value_share = jnp.concatenate(
-        [v[:rows, kv_start : kv_start + head] for v in mixed_share], axis=1
-    )
-    output_share = jnp.concatenate([v[:rows, kv_start + head :] for v in mixed_share], axis=1)
-    gain_sums = total([v[rows : rows + 8] for v in mixed_share])
+    mixed_in = exchange([mixed_sum[k] for k in range(cols)])
+    query_share, key_share, value_share, output_share, gain_sums = kernel_call(
+        unpack_mixed_kernel,
+        [
+            ((rows, cols * q_size), F32),
+            ((rows, cols * head), F32),
+            ((rows, cols * head), F32),
+            ((rows, cols * q_size), F32),
+            ((8, mixed_size), F32),
+        ],
+        *mixed_in,
+        scalars=where,
+    )
     gain_sums = gain_sums + flip(gain_sums, "row", 1)
     attention_share = lax.dynamic_slice_in_dim(gain_sums[0], plane * rows, rows, 0)
     feedforward_share = lax.dynamic_slice_in_dim(gain_sums[1], plane * rows, rows, 0)

time: 274 us -> 239 us (0.87)
  waiting for transfers between devices: 115 us -> 104 us
  local copies, waits for them, and re-layouts: 30.9 us -> 20.7 us
  other arithmetic: 15.4 us -> 7.82 us
  starting transfers between devices: 64.1 us -> 58.8 us
    ppermute x56, waiting for transfers between devices: 115 us -> 104 us  [flip(): return lax.ppermute(values, axis, [(i, i ^ distance) for i in range(size)])]
    ppermute x56, starting transfers between devices: 64.1 us -> 58.8 us  [flip(): return lax.ppermute(values, axis, [(i, i ^ distance) for i in range(size)])]
    unnamed x140 -> x112, local copies, waits for them, and re-layouts: 22.3 us -> 18.5 us
    concatenate x3 -> x0, local copies, waits for them, and re-layouts: 2.92 us -> none  [body(): jnp.concatenate([v[i * rows:(i + 1) * rows] for v in shares], axis=1)]
    pallas_call x18 -> x23, Pallas kernels: 45.7 us -> 44.8 us  [kernel_call(): pl.pallas_call(kernel, out_shape=[jax.ShapeDtypeStruct(shape, dtype) for...]
  transfers between devices with their start and end apart: 56 -> 56, of which waited for: 19 -> 22; matrix products, arithmetic and copies ran while one was open for 8% -> 4% of each run, Pallas kernels for 9% -> 17%
where the time goes in v2:
time: 239 us; the launch traced here: 238 us
  waiting for transfers between devices  104 us (44%)
  starting transfers between devices  58.8 us (25%)
  Pallas kernels  44.8 us (19%)
  local copies, waits for them, and re-layouts  20.7 us (9%)
  other arithmetic  7.82 us (3%)
    ppermute x56, waiting for transfers between devices, flip(): return lax.ppermute(values, axis, [(i, i ^ distance) for i in range(size)])  104 us
    ppermute x56, starting transfers between devices, flip(): return lax.ppermute(values, axis, [(i, i ^ distance) for i in range(size)])  58.8 us
    pallas_call x23, Pallas kernels, kernel_call(): pl.pallas_call(kernel, out_shape=[jax.ShapeDtypeStruct(shape, dtype) for...  44.8 us
    unnamed x112, local copies, waits for them, and re-layouts  18.5 us
  transfers between devices with their start and end apart: 56, of which 22 were waited for; matrix products, arithmetic and copies ran while one was open for 4% of the time, Pallas kernels for 17%

profile of v2, /device:TPU:0, one launch (start us, length us, event | category | flops | bytes accessed | tf_op | source)
XLA Modules:
  0.0 237.9 jit_solution(4697728573498300968)
XLA Ops:
  5.8 2.2 shard_map.246
  8.1 3.0 %collective-permute-start = (bf16[528,256]{1,0:T(8,128)(2,1)}, bf16[528,256]{1,0:T(8,128)(2,1)S(1)}, u32[]{:S(2)}, u32[]{:S(2)}) collective-permute-start(bf16[528,256]{1,0:T(8,128)(2,1)} %get-tuple-element.83), channel_id=1, source_target_pairs={{0,1},{1,0},{2,3},{3,2},{4,5},{5,4},{6,7},{7,6},{8,9},{9,8},{10,11... | collective-permute-start | bytes 811016 | tf_op jit(solution)/shard_map/ppermute | solution.py:32
  17.0 2.9 %collective-permute-start.10 = (bf16[768,256]{1,0:T(8,128)(2,1)}, bf16[768,256]{1,0:T(8,128)(2,1)S(1)}, u32[]{:S(2)}, u32[]{:S(2)}) collective-permute-start(bf16[768,256]{1,0:T(8,128)(2,1)} %get-tuple-element.90), channel_id=1, source_target_pairs={{0,3},{1,2},{2,1},{3,0},{4,7},{5,6},{6,5},{7,4},{8,11},{9,10},{10,... | collective-permute-start | bytes 1179656 | tf_op jit(solution)/shard_map/ppermute | solution.py:32
  21.9 12.1 %collective-permute-done.1.first2 = bf16[528,256]{1,0:T(8,128)(2,1)S(1)} collective-permute-done((bf16[528,256]{1,0:T(8,128)(2,1)}, bf16[528,256]{1,0:T(8,128)(2,1)S(1)}, u32[]{:S(2)}, u32[]{:S(2)}) %collective-permute-start.1) | collective-permute-done | bytes 270368 | tf_op jit(solution)/shard_map/ppermute | solution.py:32
  35.1 5.3 %collective-permute-done.8.first1 = bf16[768,256]{1,0:T(8,128)(2,1)S(1)} collective-permute-done((bf16[768,256]{1,0:T(8,128)(2,1)}, bf16[768,256]{1,0:T(8,128)(2,1)S(1)}, u32[]{:S(2)}, u32[]{:S(2)}) %collective-permute-start.8) | collective-permute-done | bytes 393248 | tf_op jit(solution)/shard_map/ppermute | solution.py:32
  44.7 4.4 %shard_map.248 = (f32[512,256]{1,0:T(8,128)S(1)}, bf16[512,256]{1,0:T(8,128)(2,1)S(1)}, bf16[512,128]{1,0:T(8,128)(2,1)S(1)}, f32[512,128]{1,0:T(8,128)S(1)}) custom-call(bf16[256,1024]{1,0:T(8,128)(2,1)S(1)} %shard_map.247.mine, bf16[256,1024]{1,0:T(8,128)(2,1)S(1)} %collective-permute-done.3.other, bf16[528,256]{1,0:T(8,128)(2,1)S(1)} %get-tuple-element.82.first0, ...), custom_call_target="tpu_custom_call" | custom-call | tf_op jit(solution)/shard_map/pallas_call | solution.py:60
  54.2 2.1 shard_map.253
  59.8 2.7 %collective-permute-start.14 = (bf16[256,576]{1,0:T(8,128)(2,1)S(1)}, bf16[256,576]{1,0:T(8,128)(2,1)S(1)}, u32[]{:S(2)}, u32[]{:S(2)}) collective-permute-start(bf16[256,576]{1,0:T(8,128)(2,1)S(1)} %get-tuple-element.96), channel_id=1, source_target_pairs={{0,3},{1,2},{2,1},{3,0},{4,7},{5,6},{6,5},{7,4},{8,11},{9,10},{10,... | collective-permute-start | bytes 884744 | tf_op jit(solution)/shard_map/ppermute | solution.py:32
  62.7 4.3 %collective-permute-done.12.near1 = bf16[256,576]{1,0:T(8,128)(2,1)S(1)} collective-permute-done((bf16[256,576]{1,0:T(8,128)(2,1)S(1)}, bf16[256,576]{1,0:T(8,128)(2,1)S(1)}, u32[]{:S(2)}, u32[]{:S(2)}) %collective-permute-start.12) | collective-permute-done | bytes 294944 | tf_op jit(solution)/shard_map/ppermute | solution.py:32
  68.6 4.7 %collective-permute-done.13.near2 = bf16[256,576]{1,0:T(8,128)(2,1)S(1)} collective-permute-done((bf16[256,576]{1,0:T(8,128)(2,1)S(1)}, bf16[256,576]{1,0:T(8,128)(2,1)S(1)}, u32[]{:S(2)}, u32[]{:S(2)}) %collective-permute-start.13) | collective-permute-done | bytes 294944 | tf_op jit(solution)/shard_map/ppermute | solution.py:32
  75.1 2.6 %collective-permute-done.15.far1 = bf16[256,576]{1,0:T(8,128)(2,1)S(1)} collective-permute-done((bf16[256,576]{1,0:T(8,128)(2,1)S(1)}, bf16[256,576]{1,0:T(8,128)(2,1)S(1)}, u32[]{:S(2)}, u32[]{:S(2)}) %collective-permute-start.15) | collective-permute-done | bytes 294944 | tf_op jit(solution)/shard_map/ppermute | solution.py:32
  80.3 4.4 %collective-permute-done.16.far2 = bf16[256,576]{1,0:T(8,128)(2,1)S(1)} collective-permute-done((bf16[256,576]{1,0:T(8,128)(2,1)S(1)}, bf16[256,576]{1,0:T(8,128)(2,1)S(1)}, u32[]{:S(2)}, u32[]{:S(2)}) %collective-permute-start.16) | collective-permute-done | bytes 294944 | tf_op jit(solution)/shard_map/ppermute | solution.py:32
  88.1 2.7 %shard_map.252 = (bf16[512,1024]{1,0:T(8,128)(2,1)S(1)}, f32[256,256]{1,0:T(8,128)S(1)}, f32[64,1024]{1,0:T(8,128)S(1)}) custom-call(s32[3]{0:T(128)S(1)} %pad_add_fusion.2.where, bf16[256,1024]{1,0:T(8,128)(2,1)S(1)} %shard_map.247.mine, bf16[256,1024]{1,0:T(8,128)(2,1)S(1)} %collective-permute-done.3.other, bf16[512,512]{1,0:T(8,128)(2,1)S(1)} %shard_map.249.context_near, ...), custom_call_target="tpu_custom_call" | custom-call | tf_op jit(solution)/shard_map/pallas_call | solution.py:60
  90.9 3.6 %shard_map.254 = (f32[512,576]{1,0:T(8,128)S(1)}, f32[512,576]{1,0:T(8,128)}, bf16[512,576]{1,0:T(8,128)(2,1)S(1)}) custom-call(s32[3]{0:T(128)S(1)} %pad_add_fusion.2.where, bf16[512,1024]{1,0:T(8,128)(2,1)S(1)} %get-tuple-element.92.normed, bf16[256,576]{1,0:T(8,128)(2,1)S(1)} %get-tuple-element.93.near0, ...), custom_call_target="tpu_custom_call" | custom-call | tf_op jit(solution)/shard_map/pallas_call | solution.py:60
  95.6 2.5 %shard_map.266 = (bf16[2,4,64,576]{3,2,1,0:T(8,128)(2,1)}, bf16[2,4,64,576]{3,2,1,0:T(8,128)(2,1)S(1)}) custom-call(s32[3]{0:T(128)S(1)} %pad_add_fusion.2.where, bf16[256,1024]{1,0:T(8,128)(2,1)S(1)} %shard_map.258.cot_mine, bf16[256,1024]{1,0:T(8,128)(2,1)S(1)} %collective-permute-done.26.cot_other, bf16[512,576]{1,0:T(8,128)(2,1)S(1)} %get-tuple-element.98.hidden), custom_call_target="tpu_custom_call" | custom-call | tf_op jit(solution)/shard_map/pallas_call | solution.py:60
  99.6 5.9 %shard_map.259 = (bf16[512,576]{1,0:T(8,128)(2,1)}, bf16[512,576]{1,0:T(8,128)(2,1)}, bf16[256,1024]{1,0:T(8,128)(2,1)S(1)}, bf16[256,1024]{1,0:T(8,128)(2,1)}) custom-call(s32[3]{0:T(128)S(1)} %pad_add_fusion.2.where, bf16[256,1024]{1,0:T(8,128)(2,1)S(1)} %shard_map.258.cot_mine, bf16[256,1024]{1,0:T(8,128)(2,1)S(1)} %collective-permute-done.26.cot_other, ...), custom_call_target="tpu_custom_call" | custom-call | tf_op jit(solution)/shard_map/pallas_call | solution.py:60
  106.4 1.8 shard_map.256
  111.7 2.5 %shard_map.267 = (bf16[2,4,64,576]{3,2,1,0:T(8,128)(2,1)S(1)}, bf16[2,4,64,576]{3,2,1,0:T(8,128)(2,1)S(1)}, bf16[2,4,64,576]{3,2,1,0:T(8,128)(2,1)S(1)}, bf16[2,4,64,576]{3,2,1,0:T(8,128)(2,1)S(1)}) custom-call(s32[3]{0:T(128)S(1)} %pad_add_fusion.2.where, bf16[512,1024]{1,0:T(8,128)(2,1)S(1)} %copy-done.4, bf16[512,576]{1,0:T(8,128)(2,1)S(1)} %copy-done.22, ...), custom_call_target="tpu_custom_call" | custom-call | tf_op jit(solution)/shard_map/pallas_call | solution.py:60
  123.9 7.9 %collective-permute-done.49 = bf16[2,4,64,576]{3,2,1,0:T(8,128)(2,1)S(1)} collective-permute-done((bf16[2,4,64,576]{3,2,1,0:T(8,128)(2,1)S(1)}, bf16[2,4,64,576]{3,2,1,0:T(8,128)(2,1)S(1)}, u32[]{:S(2)}, u32[]{:S(2)}) %collective-permute-start.49) | collective-permute-done | bytes 589856 | tf_op jit(solution)/shard_map/ppermute | solution.py:32
  133.1 11.8 %collective-permute-done.51 = bf16[2,4,64,576]{3,2,1,0:T(8,128)(2,1)S(1)} collective-permute-done((bf16[2,4,64,576]{3,2,1,0:T(8,128)(2,1)S(1)}, bf16[2,4,64,576]{3,2,1,0:T(8,128)(2,1)S(1)}, u32[]{:S(2)}, u32[]{:S(2)}) %collective-permute-start.51) | collective-permute-done | bytes 589856 | tf_op jit(solution)/shard_map/ppermute | solution.py:32
  144.9 1.7 collective-permute-start.23
  147.6 2.6 %collective-permute-start.48 = (bf16[4,64,576]{2,1,0:T(8,128)(2,1)S(1)}, bf16[4,64,576]{2,1,0:T(8,128)(2,1)S(1)}, u32[]{:S(2)}, u32[]{:S(2)}) collective-permute-start(bf16[4,64,576]{2,1,0:T(8,128)(2,1)S(1)} %fusion.4), channel_id=1, source_target_pairs={{0,16},{8,24},{16,0},{24,8},{1,17},{9,25},{17,1},{25,9},{2,18},{10... | collective-permute-start | bytes 884744 | tf_op jit(solution)/shard_map/ppermute | solution.py:32
  155.5 2.4 %collective-permute-done.31.came1 = bf16[64,1024]{1,0:T(8,128)(2,1)S(1)} collective-permute-done((bf16[64,1024]{1,0:T(8,128)(2,1)S(1)}, bf16[64,1024]{1,0:T(8,128)(2,1)S(1)}, u32[]{:S(2)}, u32[]{:S(2)}) %collective-permute-start.31) | collective-permute-done | bytes 131104 | tf_op jit(solution)/shard_map/ppermute | solution.py:32
  157.9 2.6 %collective-permute-start.52 = (bf16[4,64,576]{2,1,0:T(8,128)(2,1)S(1)}, bf16[4,64,576]{2,1,0:T(8,128)(2,1)S(1)}, u32[]{:S(2)}, u32[]{:S(2)}) collective-permute-start(bf16[4,64,576]{2,1,0:T(8,128)(2,1)S(1)} %fusion.6), channel_id=1, source_target_pairs={{0,16},{8,24},{16,0},{24,8},{1,17},{9,25},{17,1},{25,9},{2,18},{10... | collective-permute-start | bytes 884744 | tf_op jit(solution)/shard_map/ppermute | solution.py:32
  161.7 16.1 %collective-permute-done.48 = bf16[4,64,576]{2,1,0:T(8,128)(2,1)S(1)} collective-permute-done((bf16[4,64,576]{2,1,0:T(8,128)(2,1)S(1)}, bf16[4,64,576]{2,1,0:T(8,128)(2,1)S(1)}, u32[]{:S(2)}, u32[]{:S(2)}) %collective-permute-start.48) | collective-permute-done | bytes 294944 | tf_op jit(solution)/shard_map/ppermute | solution.py:32
  178.9 5.9 %collective-permute-done.50 = bf16[4,64,576]{2,1,0:T(8,128)(2,1)S(1)} collective-permute-done((bf16[4,64,576]{2,1,0:T(8,128)(2,1)S(1)}, bf16[4,64,576]{2,1,0:T(8,128)(2,1)S(1)}, u32[]{:S(2)}, u32[]{:S(2)}) %collective-permute-start.50) | collective-permute-done | bytes 294944 | tf_op jit(solution)/shard_map/ppermute | solution.py:32
  185.3 6.4 %collective-permute-done.52 = bf16[4,64,576]{2,1,0:T(8,128)(2,1)S(1)} collective-permute-done((bf16[4,64,576]{2,1,0:T(8,128)(2,1)S(1)}, bf16[4,64,576]{2,1,0:T(8,128)(2,1)S(1)}, u32[]{:S(2)}, u32[]{:S(2)}) %collective-permute-start.52) | collective-permute-done | bytes 294944 | tf_op jit(solution)/shard_map/ppermute | solution.py:32
  192.7 6.7 %shard_map.263 = (bf16[256,1024]{1,0:T(8,128)(2,1)S(1)}, bf16[256,1024]{1,0:T(8,128)(2,1)S(1)}, f32[8,512]{1,0:T(8,128)S(1)}, bf16[2,4,72,384]{3,2,1,0:T(8,128)(2,1)S(1)}, bf16[2,4,72,384]{3,2,1,0:T(8,128)(2,1)S(1)}) custom-call(s32[3]{0:T(128)S(1)} %pad_add_fusion.2.where, bf16[256,1024]{1,0:T(8,128)(2,1)S(1)} %shard_map.247.mine, ...), custom_call_target="tpu_custom_call" | custom-call | tf_op jit(solution)/shard_map/pallas_call | solution.py:60
  199.6 2.0 collective-permute-start.55
  202.0 9.6 %collective-permute-done.41 = bf16[2,4,72,384]{3,2,1,0:T(8,128)(2,1)S(1)} collective-permute-done((bf16[2,4,72,384]{3,2,1,0:T(8,128)(2,1)S(1)}, bf16[2,4,72,384]{3,2,1,0:T(8,128)(2,1)S(1)}, u32[]{:S(2)}, u32[]{:S(2)}) %collective-permute-start.41) | collective-permute-done | bytes 442400 | tf_op jit(solution)/shard_map/ppermute | solution.py:32
  213.8 4.8 %collective-permute-done.53.came1 = bf16[192,576]{1,0:T(8,128)(2,1)S(1)} collective-permute-done((bf16[192,576]{1,0:T(8,128)(2,1)S(1)}, bf16[192,576]{1,0:T(8,128)(2,1)S(1)}, u32[]{:S(2)}, u32[]{:S(2)}) %collective-permute-start.53) | collective-permute-done | bytes 221216 | tf_op jit(solution)/shard_map/ppermute | solution.py:32
  218.6 1.9 shard_map.268
  (276 shorter events, 84.1 us)
Async XLA Ops:
  8.1 12.8 %collective-permute-start = (bf16[528,256]{1,0:T(8,128)(2,1)}, bf16[528,256]{1,0:T(8,128)(2,1)S(1)}, u32[]{:S(2)}, u32[]{:S(2)}) collective-permute-start(bf16[528,256]{1,0:T(8,128)(2,1)} %get-tuple-element.83), channel_id=1, source_target_pairs={{0,1},{1,0},{2,3},{3,2},{4,5},{5,4},{6,7},{7,6},{8,9},{9,8},{10,11... | collective-permute-start | bytes 811016 | tf_op jit(solution)/shard_map/ppermute | solution.py:32
  11.1 22.9 %collective-permute-start.1 = (bf16[528,256]{1,0:T(8,128)(2,1)}, bf16[528,256]{1,0:T(8,128)(2,1)S(1)}, u32[]{:S(2)}, u32[]{:S(2)}) collective-permute-start(bf16[528,256]{1,0:T(8,128)(2,1)} %get-tuple-element.84), channel_id=1, source_target_pairs={{0,2},{1,3},{2,0},{3,1},{4,6},{5,7},{6,4},{7,5},{8,10},{9,11},{10,... | collective-permute-start | bytes 811016 | tf_op jit(solution)/shard_map/ppermute | solution.py:32
  12.6 21.4 %collective-permute-start.2 = (bf16[528,256]{1,0:T(8,128)(2,1)S(1)}, bf16[528,256]{1,0:T(8,128)(2,1)S(1)}, u32[]{:S(2)}, u32[]{:S(2)}) collective-permute-start(bf16[528,256]{1,0:T(8,128)(2,1)S(1)} %get-tuple-element.85), channel_id=1, source_target_pairs={{0,3},{1,2},{2,1},{3,0},{4,7},{5,6},{6,5},{7,4},{8,11},{9,10},{10,... | collective-permute-start | bytes 811016 | tf_op jit(solution)/shard_map/ppermute | solution.py:32
  17.0 17.4 %collective-permute-start.10 = (bf16[768,256]{1,0:T(8,128)(2,1)}, bf16[768,256]{1,0:T(8,128)(2,1)S(1)}, u32[]{:S(2)}, u32[]{:S(2)}) collective-permute-start(bf16[768,256]{1,0:T(8,128)(2,1)} %get-tuple-element.90), channel_id=1, source_target_pairs={{0,3},{1,2},{2,1},{3,0},{4,7},{5,6},{6,5},{7,4},{8,11},{9,10},{10,... | collective-permute-start | bytes 1179656 | tf_op jit(solution)/shard_map/ppermute | solution.py:32
  19.9 20.6 %collective-permute-start.8 = (bf16[768,256]{1,0:T(8,128)(2,1)}, bf16[768,256]{1,0:T(8,128)(2,1)S(1)}, u32[]{:S(2)}, u32[]{:S(2)}) collective-permute-start(bf16[768,256]{1,0:T(8,128)(2,1)} %get-tuple-element.88), channel_id=1, source_target_pairs={{0,1},{1,0},{2,3},{3,2},{4,5},{5,4},{6,7},{7,6},{8,9},{9,8},{10,11... | collective-permute-start | bytes 1179656 | tf_op jit(solution)/shard_map/ppermute | solution.py:32
  20.9 21.0 %collective-permute-start.9 = (bf16[768,256]{1,0:T(8,128)(2,1)}, bf16[768,256]{1,0:T(8,128)(2,1)S(1)}, u32[]{:S(2)}, u32[]{:S(2)}) collective-permute-start(bf16[768,256]{1,0:T(8,128)(2,1)} %get-tuple-element.89), channel_id=1, source_target_pairs={{0,2},{1,3},{2,0},{3,1},{4,6},{5,7},{6,4},{7,5},{8,10},{9,11},{10,... | collective-permute-start | bytes 1179656 | tf_op jit(solution)/shard_map/ppermute | solution.py:32
  44.0 41.8 %collective-permute-start.11 = (bf16[512,1024]{1,0:T(8,128)(2,1)S(1)}, bf16[512,1024]{1,0:T(8,128)(2,1)S(1)}, u32[]{:S(2)}, u32[]{:S(2)}) collective-permute-start(bf16[512,1024]{1,0:T(8,128)(2,1)S(1)} %shard_map.251.joined.out_weight), channel_id=1, source_target_pairs={{0,4},{4,0},{1,5},{5,1},{2,6},{6,2},{3,7},{7,3},{8,12},{12,8},{9,1... | collective-permute-start | bytes 3145736 | tf_op jit(solution)/shard_map/ppermute | solution.py:32
  57.7 15.6 %collective-permute-start.13 = (bf16[256,576]{1,0:T(8,128)(2,1)S(1)}, bf16[256,576]{1,0:T(8,128)(2,1)S(1)}, u32[]{:S(2)}, u32[]{:S(2)}) collective-permute-start(bf16[256,576]{1,0:T(8,128)(2,1)S(1)} %get-tuple-element.95), channel_id=1, source_target_pairs={{0,2},{1,3},{2,0},{3,1},{4,6},{5,7},{6,4},{7,5},{8,10},{9,11},{10,... | collective-permute-start | bytes 884744 | tf_op jit(solution)/shard_map/ppermute | solution.py:32
  59.8 15.2 %collective-permute-start.14 = (bf16[256,576]{1,0:T(8,128)(2,1)S(1)}, bf16[256,576]{1,0:T(8,128)(2,1)S(1)}, u32[]{:S(2)}, u32[]{:S(2)}) collective-permute-start(bf16[256,576]{1,0:T(8,128)(2,1)S(1)} %get-tuple-element.96), channel_id=1, source_target_pairs={{0,3},{1,2},{2,1},{3,0},{4,7},{5,6},{6,5},{7,4},{8,11},{9,10},{10,... | collective-permute-start | bytes 884744 | tf_op jit(solution)/shard_map/ppermute | solution.py:32
  62.7 24.7 %collective-permute-start.7 = (bf16[512,512]{1,0:T(8,128)(2,1)S(1)}, bf16[512,512]{1,0:T(8,128)(2,1)S(1)}, u32[]{:S(2)}, u32[]{:S(2)}) collective-permute-start(bf16[512,512]{1,0:T(8,128)(2,1)S(1)} %shard_map.249.context_near), channel_id=1, source_target_pairs={{0,4},{4,0},{1,5},{5,1},{2,6},{6,2},{3,7},{7,3},{8,12},{12,8},{9,1... | collective-permute-start | bytes 1572872 | tf_op jit(solution)/shard_map/ppermute | solution.py:32
  75.0 20.6 %collective-permute-start.26 = (bf16[256,1024]{1,0:T(8,128)(2,1)S(1)}, bf16[256,1024]{1,0:T(8,128)(2,1)S(1)}, u32[]{:S(2)}, u32[]{:S(2)}) collective-permute-start(bf16[256,1024]{1,0:T(8,128)(2,1)S(1)} %shard_map.258.cot_mine), channel_id=1, source_target_pairs={{0,4},{4,0},{1,5},{5,1},{2,6},{6,2},{3,7},{7,3},{8,12},{12,8},{9,1... | collective-permute-start | bytes 1572872 | tf_op jit(solution)/shard_map/ppermute | solution.py:32
  77.6 13.3 %collective-permute-start.17 = (bf16[256,576]{1,0:T(8,128)(2,1)S(1)}, bf16[256,576]{1,0:T(8,128)(2,1)S(1)}, u32[]{:S(2)}, u32[]{:S(2)}) collective-permute-start(bf16[256,576]{1,0:T(8,128)(2,1)S(1)} %collective-permute-done.14.near3), channel_id=1, source_target_pairs={{0,8},{8,0},{16,24},{24,16},{1,9},{9,1},{17,25},{25,17},{2,10},{10... | collective-permute-start | bytes 884744 | tf_op jit(solution)/shard_map/ppermute | solution.py:32
  84.6 15.0 %collective-permute-start.18 = (bf16[576,256]{1,0:T(8,128)(2,1)S(1)}, bf16[576,256]{1,0:T(8,128)(2,1)S(1)}, u32[]{:S(2)}, u32[]{:S(2)}) collective-permute-start(bf16[576,256]{1,0:T(8,128)(2,1)S(1)} %get-tuple-element.100), channel_id=1, source_target_pairs={{0,1},{1,0},{2,3},{3,2},{4,5},{5,4},{6,7},{7,6},{8,9},{9,8},{10,11... | collective-permute-start | bytes 884744 | tf_op jit(solution)/shard_map/ppermute | solution.py:32
  85.9 13.8 %collective-permute-start.19 = (bf16[576,256]{1,0:T(8,128)(2,1)S(1)}, bf16[576,256]{1,0:T(8,128)(2,1)S(1)}, u32[]{:S(2)}, u32[]{:S(2)}) collective-permute-start(bf16[576,256]{1,0:T(8,128)(2,1)S(1)} %get-tuple-element.101), channel_id=1, source_target_pairs={{0,2},{1,3},{2,0},{3,1},{4,6},{5,7},{6,4},{7,5},{8,10},{9,11},{10,... | collective-permute-start | bytes 884744 | tf_op jit(solution)/shard_map/ppermute | solution.py:32
  87.4 12.3 %collective-permute-start.20 = (bf16[576,256]{1,0:T(8,128)(2,1)S(1)}, bf16[576,256]{1,0:T(8,128)(2,1)S(1)}, u32[]{:S(2)}, u32[]{:S(2)}) collective-permute-start(bf16[576,256]{1,0:T(8,128)(2,1)S(1)} %get-tuple-element.102), channel_id=1, source_target_pairs={{0,3},{1,2},{2,1},{3,0},{4,7},{5,6},{6,5},{7,4},{8,11},{9,10},{10,... | collective-permute-start | bytes 884744 | tf_op jit(solution)/shard_map/ppermute | solution.py:32
  98.0 23.9 %collective-permute-start.47 = (bf16[2,4,64,576]{3,2,1,0:T(8,128)(2,1)}, bf16[2,4,64,576]{3,2,1,0:T(8,128)(2,1)}, u32[]{:S(2)}, u32[]{:S(2)}) collective-permute-start(bf16[2,4,64,576]{3,2,1,0:T(8,128)(2,1)} %get-tuple-element.141), channel_id=1, source_target_pairs={{0,8},{8,0},{16,24},{24,16},{1,9},{9,1},{17,25},{25,17},{2,10},{10... | collective-permute-start | bytes 1769480 | tf_op jit(solution)/shard_map/ppermute | solution.py:32
  114.2 17.7 %collective-permute-start.49 = (bf16[2,4,64,576]{3,2,1,0:T(8,128)(2,1)S(1)}, bf16[2,4,64,576]{3,2,1,0:T(8,128)(2,1)S(1)}, u32[]{:S(2)}, u32[]{:S(2)}) collective-permute-start(bf16[2,4,64,576]{3,2,1,0:T(8,128)(2,1)S(1)} %get-tuple-element.145), channel_id=1, source_target_pairs={{0,8},{8,0},{16,24},{24,16},{1,9},{9,1},{17,25},{25,17},{2,10},{10... | collective-permute-start | bytes 1769480 | tf_op jit(solution)/shard_map/ppermute | solution.py:32
  115.0 29.9 %collective-permute-start.51 = (bf16[2,4,64,576]{3,2,1,0:T(8,128)(2,1)S(1)}, bf16[2,4,64,576]{3,2,1,0:T(8,128)(2,1)S(1)}, u32[]{:S(2)}, u32[]{:S(2)}) collective-permute-start(bf16[2,4,64,576]{3,2,1,0:T(8,128)(2,1)S(1)} %get-tuple-element.147), channel_id=1, source_target_pairs={{0,8},{8,0},{16,24},{24,16},{1,9},{9,1},{17,25},{25,17},{2,10},{10... | collective-permute-start | bytes 1769480 | tf_op jit(solution)/shard_map/ppermute | solution.py:32
  118.0 28.6 %collective-permute-start.28 = (bf16[64,1024]{1,0:T(8,128)(2,1)S(1)}, bf16[64,1024]{1,0:T(8,128)(2,1)S(1)}, u32[]{:S(2)}, u32[]{:S(2)}) collective-permute-start(bf16[64,1024]{1,0:T(8,128)(2,1)S(1)} %get-tuple-element.114), channel_id=1, source_target_pairs={{0,1},{1,0},{2,3},{3,2},{4,5},{5,4},{6,7},{7,6},{8,9},{9,8},{10,11... | collective-permute-start | bytes 393224 | tf_op jit(solution)/shard_map/ppermute | solution.py:32
  119.3 28.3 %collective-permute-start.29 = (bf16[64,1024]{1,0:T(8,128)(2,1)S(1)}, bf16[64,1024]{1,0:T(8,128)(2,1)S(1)}, u32[]{:S(2)}, u32[]{:S(2)}) collective-permute-start(bf16[64,1024]{1,0:T(8,128)(2,1)S(1)} %get-tuple-element.115), channel_id=1, source_target_pairs={{0,2},{1,3},{2,0},{3,1},{4,6},{5,7},{6,4},{7,5},{8,10},{9,11},{10,... | collective-permute-start | bytes 393224 | tf_op jit(solution)/shard_map/ppermute | solution.py:32
  122.0 28.3 %collective-permute-start.30 = (bf16[64,1024]{1,0:T(8,128)(2,1)S(1)}, bf16[64,1024]{1,0:T(8,128)(2,1)S(1)}, u32[]{:S(2)}, u32[]{:S(2)}) collective-permute-start(bf16[64,1024]{1,0:T(8,128)(2,1)S(1)} %get-tuple-element.116), channel_id=1, source_target_pairs={{0,3},{1,2},{2,1},{3,0},{4,7},{5,6},{6,5},{7,4},{8,11},{9,10},{10,... | collective-permute-start | bytes 393224 | tf_op jit(solution)/shard_map/ppermute | solution.py:32
  131.8 19.7 %collective-permute-start.22 = (bf16[256,256]{1,0:T(8,128)(2,1)S(1)}, bf16[256,256]{1,0:T(8,128)(2,1)S(1)}, u32[]{:S(2)}, u32[]{:S(2)}) collective-permute-start(bf16[256,256]{1,0:T(8,128)(2,1)S(1)} %get-tuple-element.106), channel_id=1, source_target_pairs={{0,1},{1,0},{2,3},{3,2},{4,5},{5,4},{6,7},{7,6},{8,9},{9,8},{10,11... | collective-permute-start | bytes 393224 | tf_op jit(solution)/shard_map/ppermute | solution.py:32
  147.6 30.1 %collective-permute-start.48 = (bf16[4,64,576]{2,1,0:T(8,128)(2,1)S(1)}, bf16[4,64,576]{2,1,0:T(8,128)(2,1)S(1)}, u32[]{:S(2)}, u32[]{:S(2)}) collective-permute-start(bf16[4,64,576]{2,1,0:T(8,128)(2,1)S(1)} %fusion.4), channel_id=1, source_target_pairs={{0,16},{8,24},{16,0},{24,8},{1,17},{9,25},{17,1},{25,9},{2,18},{10... | collective-permute-start | bytes 884744 | tf_op jit(solution)/shard_map/ppermute | solution.py:32
  150.3 34.5 %collective-permute-start.50 = (bf16[4,64,576]{2,1,0:T(8,128)(2,1)S(1)}, bf16[4,64,576]{2,1,0:T(8,128)(2,1)S(1)}, u32[]{:S(2)}, u32[]{:S(2)}) collective-permute-start(bf16[4,64,576]{2,1,0:T(8,128)(2,1)S(1)} %fusion.5), channel_id=1, source_target_pairs={{0,16},{8,24},{16,0},{24,8},{1,17},{9,25},{17,1},{25,9},{2,18},{10... | collective-permute-start | bytes 884744 | tf_op jit(solution)/shard_map/ppermute | solution.py:32
  157.9 33.8 %collective-permute-start.52 = (bf16[4,64,576]{2,1,0:T(8,128)(2,1)S(1)}, bf16[4,64,576]{2,1,0:T(8,128)(2,1)S(1)}, u32[]{:S(2)}, u32[]{:S(2)}) collective-permute-start(bf16[4,64,576]{2,1,0:T(8,128)(2,1)S(1)} %fusion.6), channel_id=1, source_target_pairs={{0,16},{8,24},{16,0},{24,8},{1,17},{9,25},{17,1},{25,9},{2,18},{10... | collective-permute-start | bytes 884744 | tf_op jit(solution)/shard_map/ppermute | solution.py:32
  160.5 51.9 %collective-permute-start.25 = (bf16[256,256]{1,0:T(8,128)(2,1)S(1)}, bf16[256,256]{1,0:T(8,128)(2,1)S(1)}, u32[]{:S(2)}, u32[]{:S(2)}) collective-permute-start(bf16[256,256]{1,0:T(8,128)(2,1)S(1)} %add_convert_fusion.4), channel_id=1, source_target_pairs={{0,4},{4,0},{1,5},{5,1},{2,6},{6,2},{3,7},{7,3},{8,12},{12,8},{9,1... | collective-permute-start | bytes 393224 | tf_op jit(solution)/shard_map/ppermute | solution.py:32
  161.1 30.7 %collective-permute-start.34 = (bf16[256,1024]{1,0:T(8,128)(2,1)S(1)}, bf16[256,1024]{1,0:T(8,128)(2,1)S(1)}, u32[]{:S(2)}, u32[]{:S(2)}) collective-permute-start(bf16[256,1024]{1,0:T(8,128)(2,1)S(1)} %shard_map.262.grad_mine), channel_id=1, source_target_pairs={{0,4},{4,0},{1,5},{5,1},{2,6},{6,2},{3,7},{7,3},{8,12},{12,8},{9,1... | collective-permute-start | bytes 1572872 | tf_op jit(solution)/shard_map/ppermute | solution.py:32
  199.4 12.1 %collective-permute-start.41 = (bf16[2,4,72,384]{3,2,1,0:T(8,128)(2,1)S(1)}, bf16[2,4,72,384]{3,2,1,0:T(8,128)(2,1)S(1)}, u32[]{:S(2)}, u32[]{:S(2)}) collective-permute-start(bf16[2,4,72,384]{3,2,1,0:T(8,128)(2,1)S(1)} %get-tuple-element.134), channel_id=1, source_target_pairs={{0,8},{8,0},{16,24},{24,16},{1,9},{9,1},{17,25},{25,17},{2,10},{10... | collective-permute-start | bytes 1327112 | tf_op jit(solution)/shard_map/ppermute | solution.py:32
  199.6 14.2 %collective-permute-start.55 = (bf16[192,576]{1,0:T(8,128)(2,1)S(1)}, bf16[192,576]{1,0:T(8,128)(2,1)S(1)}, u32[]{:S(2)}, u32[]{:S(2)}) collective-permute-start(bf16[192,576]{1,0:T(8,128)(2,1)S(1)} %pad_maximum_fusion.5), channel_id=1, source_target_pairs={{0,3},{1,2},{2,1},{3,0},{4,7},{5,6},{6,5},{7,4},{8,11},{9,10},{10,... | collective-permute-start | bytes 663560 | tf_op jit(solution)/shard_map/ppermute | solution.py:32
  201.6 12.1 %collective-permute-start.54 = (bf16[192,576]{1,0:T(8,128)(2,1)S(1)}, bf16[192,576]{1,0:T(8,128)(2,1)S(1)}, u32[]{:S(2)}, u32[]{:S(2)}) collective-permute-start(bf16[192,576]{1,0:T(8,128)(2,1)S(1)} %pad_maximum_fusion.4), channel_id=1, source_target_pairs={{0,2},{1,3},{2,0},{3,1},{4,6},{5,7},{6,4},{7,5},{8,10},{9,11},{10,... | collective-permute-start | bytes 663560 | tf_op jit(solution)/shard_map/ppermute | solution.py:32
  202.0 18.6 %collective-permute-start.35 = (bf16[256,1024]{1,0:T(8,128)(2,1)S(1)}, bf16[256,1024]{1,0:T(8,128)(2,1)S(1)}, u32[]{:S(2)}, u32[]{:S(2)}) collective-permute-start(bf16[256,1024]{1,0:T(8,128)(2,1)S(1)} %get-tuple-element.127), channel_id=1, source_target_pairs={{0,4},{4,0},{1,5},{5,1},{2,6},{6,2},{3,7},{7,3},{8,12},{12,8},{9,1... | collective-permute-start | bytes 1572872 | tf_op jit(solution)/shard_map/ppermute | solution.py:32
  212.4 11.9 %collective-permute-start.42 = (bf16[4,72,384]{2,1,0:T(8,128)(2,1)S(1)}, bf16[4,72,384]{2,1,0:T(8,128)(2,1)S(1)}, u32[]{:S(2)}, u32[]{:S(2)}) collective-permute-start(bf16[4,72,384]{2,1,0:T(8,128)(2,1)S(1)} %fusion.11), channel_id=1, source_target_pairs={{0,16},{8,24},{16,0},{24,8},{1,17},{9,25},{17,1},{25,9},{2,18},{10... | collective-permute-start | bytes 663560 | tf_op jit(solution)/shard_map/ppermute | solution.py:32
  (80 other events, 662.0 us)

commit v3 on v2

--- a/solution.py
+++ b/solution.py
@@ -47,7 +47,7 @@
     return result
 
 
-def kernel_call(kernel, outs, *args, scalars=None, scratch=(), fetch=0):
+def kernel_call(kernel, outs, *args, scalars=None, scratch=(), fetch=0, room=8):
     specs = [pl.BlockSpec(memory_space=pltpu.HBM)] * fetch
     specs = specs + [pl.BlockSpec(memory_space=pltpu.VMEM)] * (len(args) - fetch)
     scratch_shapes = [pltpu.VMEM(shape, dtype) for shape, dtype in scratch]
@@ -63,7 +63,7 @@
         in_specs=specs,
         out_specs=[pl.BlockSpec(memory_space=pltpu.VMEM)] * len(outs),
         scratch_shapes=scratch_shapes,
-        compiler_params=pltpu.CompilerParams(vmem_limit_bytes=48 * 1024 * 1024),
+        compiler_params=pltpu.CompilerParams(vmem_limit_bytes=room * 1024 * 1024),
     )(*args)
 
 
@@ -606,10 +606,9 @@
             attention_gain.reshape(1, part),
             feedforward_gain.reshape(1, part),
             scalars=where,
-            fetch=4,
-        ),
-    )
-    (input_mine,) = kernel_call(join_first_kernel, [((half, width), BF16)], *first_in)
+            fetch=4, room=60),
+    )
+    (input_mine,) = kernel_call(join_first_kernel, [((half, width), BF16)], *first_in, room=10)
     gain_parts = jnp.concatenate([v[half : half + 16] for v in first_in], axis=1).astype(F32)
     gain_one = gain_parts[0] + gain_parts[1] + gain_parts[2]
     input_other = flip(input_mine, "row", 1)
@@ -619,8 +618,7 @@
         gate_weight,
         up_weight,
         scalars=where,
-        fetch=2,
-    )
+        fetch=2, room=12)
     near_parts = exchange(gate_in[:cols])
     far_parts = [gate_in[cols]] + [flip(v, "dp", 1) for v in near_parts[1:]]
     inner_size = output_weight.shape[0]
@@ -671,15 +669,14 @@
             ((tokens, q_size), BF16),
             ((tokens, q_size), F32),
         ],
-        *common,
-    )
+        *common, room=26)
 
     context_parts = spread(context)
-    (context_near,) = kernel_call(join_kernel, [((tokens, inner_size), BF16)], *context_parts)
+    (context_near,) = kernel_call(join_kernel, [((tokens, inner_size), BF16)], *context_parts, room=10)
     context_far = flip(context_near, "row", 1)
-    (second_in,) = kernel_call(join_kernel, [((inner_size, width), BF16)], *second_parts)
+    (second_in,) = kernel_call(join_kernel, [((inner_size, width), BF16)], *second_parts, room=10)
     second_far = flip(second_in, "row", 1)
-    (cot_mine,) = kernel_call(join_first_kernel, [((half, width), BF16)], *second_parts)
+    (cot_mine,) = kernel_call(join_first_kernel, [((half, width), BF16)], *second_parts, room=10)
     cot_other = flip(cot_mine, "row", 1)
 
     share = half // cols
@@ -694,16 +691,14 @@
         second_far,
         *first_in,
         scalars=where,
-        scratch=[((half, width), F32)],
-    )
+        scratch=[((half, width), F32)], room=24)
     gate_pre, up_pre, hidden = kernel_call(
         hidden_kernel,
         [((tokens, units), F32), ((tokens, units), F32), ((tokens, units), BF16)],
         normed_two,
         *near_parts,
         *far_parts,
-        scalars=where,
-    )
+        scalars=where, room=24)
     rows = part // planes
     if planes == 4:
         down_dealt = kernel_call(
@@ -713,8 +708,7 @@
             cot_other,
             hidden,
             scalars=where,
-            scratch=[((part, units), BF16)],
-        )
+            scratch=[((part, units), BF16)], room=14)
     gate_grad, up_grad, two_mine, two_other = kernel_call(
         backward_kernel,
         [((tokens, units), BF16)] * 2 + [((half, width), BF16)] * 2,
@@ -725,8 +719,7 @@
         *down_parts,
         *near_parts,
         *far_parts,
-        scalars=where,
-    )
+        scalars=where, room=30)
 
     two_came = flip(two_other, "row", 1)
     two_pieces = kernel_call(
@@ -770,8 +763,7 @@
             gate_grad,
             up_grad,
             scalars=where,
-            scratch=[((part, units), BF16)],
-        )
+            scratch=[((part, units), BF16)], room=20)
         dealt = list(down_dealt) + list(dealt)
         sums = [summed(dealt[2 * i], dealt[2 * i + 1]) for i in range(3)]
     else:
@@ -788,12 +780,10 @@
         ]
     feed_in = exchange([jnp.concatenate([v[k] for v in sums], axis=0) for k in range(cols)])
     down_share, gate_share, up_share = kernel_call(
-        unpack_feed_kernel, [((rows, cols * units), F32)] * 3, *feed_in, scalars=where
-    )
+        unpack_feed_kernel, [((rows, cols * units), F32)] * 3, *feed_in, scalars=where, room=12)
 
     result_mine, result_other = kernel_call(
-        result_kernel, [((half, width), BF16)] * 2, hidden, *down_parts
-    )
+        result_kernel, [((half, width), BF16)] * 2, hidden, *down_parts, room=12)
     result_came = flip(result_other, "row", 1)
     result_pieces = kernel_call(
         pack_features_kernel, [((half, part), BF16)] * cols, result_mine, result_came
@@ -820,8 +810,7 @@
         second_in,
         feedforward_part,
         scalars=where,
-        scratch=[((part, mixed_size), BF16)],
-    )
+        scratch=[((part, mixed_size), BF16)], room=34)
     one_came = flip(one_other, "row", 1)
     inner_came = flip(inner_part[:, half:], "row", 1)
     one_pieces = kernel_call(
@@ -830,8 +819,7 @@
         one_mine,
         one_came,
         inner_part,
-        inner_came,
-    )
+        inner_came, room=10)
     one_in = exchange(one_pieces)
     one_grad = total([v[:half] for v in one_in])
     inner_one = jnp.sum(total([v[half:] for v in one_in])[:3], axis=0)[:, None]

time: 239 us -> 228 us (0.954)
  local copies, waits for them, and re-layouts: 20.7 us -> 14.2 us
  Pallas kernels: 44.8 us -> 41.7 us
    unnamed x112 -> x100, local copies, waits for them, and re-layouts: 18.5 us -> 12 us
    pallas_call x23, Pallas kernels: 44.8 us -> 41.7 us  [kernel_call(): pl.pallas_call(kernel, out_shape=[jax.ShapeDtypeStruct(shape, dtype) for...]
  transfers between devices with their start and end apart: 56 -> 56, of which waited for: 22 -> 22; matrix products, arithmetic and copies ran while one was open for 4% -> 4% of each run, Pallas kernels for 17% -> 16%
where the time goes in v3:
time: 228 us
  waiting for transfers between devices  103 us (45%)
  starting transfers between devices  60 us (26%)
  Pallas kernels  41.7 us (18%)
  local copies, waits for them, and re-layouts  14.2 us (6%)
  other arithmetic  7.46 us (3%)
    ppermute x56, waiting for transfers between devices, flip(): return lax.ppermute(values, axis, [(i, i ^ distance) for i in range(size)])  103 us
    ppermute x56, starting transfers between devices, flip(): return lax.ppermute(values, axis, [(i, i ^ distance) for i in range(size)])  60 us
    pallas_call x23, Pallas kernels, kernel_call(): pl.pallas_call(kernel, out_shape=[jax.ShapeDtypeStruct(shape, dtype) for...  41.7 us
    unnamed x100, local copies, waits for them, and re-layouts  12 us
  transfers between devices with their start and end apart: 56, of which 22 were waited for; matrix products, arithmetic and copies ran while one was open for 4% of the time, Pallas kernels for 16%

profile of v3, /device:TPU:0, one launch (start us, length us, event | category | flops | bytes accessed | tf_op | source)
XLA Modules:
  0.0 227.9 jit_solution(1283865118525386896)
XLA Ops:
  1.3 3.3 %shard_map.246 = (bf16[528,256]{1,0:T(8,128)(2,1)}, bf16[528,256]{1,0:T(8,128)(2,1)}, bf16[528,256]{1,0:T(8,128)(2,1)}, bf16[528,256]{1,0:T(8,128)(2,1)}) custom-call(s32[3]{0:T(128)} %pad_add_fusion.2.where, bf16[512,256]{1,0:T(8,128)(2,1)} %x_in.1, bf16[256,512]{1,0:T(8,128)(2,1)} %query_in.1, bf16[256,256]{1,0:T(8,128)(2,1)} %key_in.1, ...), custom_call_target="tpu_custom_call" | custom-call | tf_op jit(solution)/shard_map/pallas_call | solution.py:60
  4.6 3.0 %collective-permute-start = (bf16[528,256]{1,0:T(8,128)(2,1)}, bf16[528,256]{1,0:T(8,128)(2,1)S(1)}, u32[]{:S(2)}, u32[]{:S(2)}) collective-permute-start(bf16[528,256]{1,0:T(8,128)(2,1)} %get-tuple-element.83), channel_id=1, source_target_pairs={{0,1},{1,0},{2,3},{3,2},{4,5},{5,4},{6,7},{7,6},{8,9},{9,8},{10,11... | collective-permute-start | bytes 811016 | tf_op jit(solution)/shard_map/ppermute | solution.py:32
  14.2 2.9 %collective-permute-start.10 = (bf16[768,256]{1,0:T(8,128)(2,1)}, bf16[768,256]{1,0:T(8,128)(2,1)S(1)}, u32[]{:S(2)}, u32[]{:S(2)}) collective-permute-start(bf16[768,256]{1,0:T(8,128)(2,1)} %get-tuple-element.90), channel_id=1, source_target_pairs={{0,3},{1,2},{2,1},{3,0},{4,7},{5,6},{6,5},{7,4},{8,11},{9,10},{10,... | collective-permute-start | bytes 1179656 | tf_op jit(solution)/shard_map/ppermute | solution.py:32
  19.1 11.4 %collective-permute-done.1.first2 = bf16[528,256]{1,0:T(8,128)(2,1)S(1)} collective-permute-done((bf16[528,256]{1,0:T(8,128)(2,1)}, bf16[528,256]{1,0:T(8,128)(2,1)S(1)}, u32[]{:S(2)}, u32[]{:S(2)}) %collective-permute-start.1) | collective-permute-done | bytes 270368 | tf_op jit(solution)/shard_map/ppermute | solution.py:32
  31.7 5.3 %collective-permute-done.8.first1 = bf16[768,256]{1,0:T(8,128)(2,1)S(1)} collective-permute-done((bf16[768,256]{1,0:T(8,128)(2,1)}, bf16[768,256]{1,0:T(8,128)(2,1)S(1)}, u32[]{:S(2)}, u32[]{:S(2)}) %collective-permute-start.8) | collective-permute-done | bytes 393248 | tf_op jit(solution)/shard_map/ppermute | solution.py:32
  41.3 4.4 %shard_map.248 = (f32[512,256]{1,0:T(8,128)S(1)}, bf16[512,256]{1,0:T(8,128)(2,1)S(1)}, bf16[512,128]{1,0:T(8,128)(2,1)S(1)}, f32[512,128]{1,0:T(8,128)S(1)}) custom-call(bf16[256,1024]{1,0:T(8,128)(2,1)S(1)} %shard_map.247.mine, bf16[256,1024]{1,0:T(8,128)(2,1)S(1)} %collective-permute-done.3.other, bf16[528,256]{1,0:T(8,128)(2,1)S(1)} %copy-done, ...), custom_call_target="tpu_custom_call" | custom-call | tf_op jit(solution)/shard_map/pallas_call | solution.py:60
  49.3 2.1 shard_map.253
  54.9 2.7 %collective-permute-start.14 = (bf16[256,576]{1,0:T(8,128)(2,1)S(1)}, bf16[256,576]{1,0:T(8,128)(2,1)S(1)}, u32[]{:S(2)}, u32[]{:S(2)}) collective-permute-start(bf16[256,576]{1,0:T(8,128)(2,1)S(1)} %get-tuple-element.96), channel_id=1, source_target_pairs={{0,3},{1,2},{2,1},{3,0},{4,7},{5,6},{6,5},{7,4},{8,11},{9,10},{10,... | collective-permute-start | bytes 884744 | tf_op jit(solution)/shard_map/ppermute | solution.py:32
  57.8 4.3 %collective-permute-done.12.near1 = bf16[256,576]{1,0:T(8,128)(2,1)S(1)} collective-permute-done((bf16[256,576]{1,0:T(8,128)(2,1)S(1)}, bf16[256,576]{1,0:T(8,128)(2,1)S(1)}, u32[]{:S(2)}, u32[]{:S(2)}) %collective-permute-start.12) | collective-permute-done | bytes 294944 | tf_op jit(solution)/shard_map/ppermute | solution.py:32
  63.7 4.7 %collective-permute-done.13.near2 = bf16[256,576]{1,0:T(8,128)(2,1)S(1)} collective-permute-done((bf16[256,576]{1,0:T(8,128)(2,1)S(1)}, bf16[256,576]{1,0:T(8,128)(2,1)S(1)}, u32[]{:S(2)}, u32[]{:S(2)}) %collective-permute-start.13) | collective-permute-done | bytes 294944 | tf_op jit(solution)/shard_map/ppermute | solution.py:32
  70.1 2.6 %collective-permute-done.15.far1 = bf16[256,576]{1,0:T(8,128)(2,1)S(1)} collective-permute-done((bf16[256,576]{1,0:T(8,128)(2,1)S(1)}, bf16[256,576]{1,0:T(8,128)(2,1)S(1)}, u32[]{:S(2)}, u32[]{:S(2)}) %collective-permute-start.15) | collective-permute-done | bytes 294944 | tf_op jit(solution)/shard_map/ppermute | solution.py:32
  75.4 4.4 %collective-permute-done.16.far2 = bf16[256,576]{1,0:T(8,128)(2,1)S(1)} collective-permute-done((bf16[256,576]{1,0:T(8,128)(2,1)S(1)}, bf16[256,576]{1,0:T(8,128)(2,1)S(1)}, u32[]{:S(2)}, u32[]{:S(2)}) %collective-permute-start.16) | collective-permute-done | bytes 294944 | tf_op jit(solution)/shard_map/ppermute | solution.py:32
  83.2 2.0 shard_map.252
  85.3 2.6 %shard_map.254 = (f32[512,576]{1,0:T(8,128)S(1)}, f32[512,576]{1,0:T(8,128)S(1)}, bf16[512,576]{1,0:T(8,128)(2,1)S(1)}) custom-call(s32[3]{0:T(128)S(1)} %copy-done.45, bf16[512,1024]{1,0:T(8,128)(2,1)S(1)} %get-tuple-element.92.normed, bf16[256,576]{1,0:T(8,128)(2,1)S(1)} %get-tuple-element.93.near0, bf16[256,576]{1,0:T(8,128)(2,1)S(1)} %collective-permute-done.12.near1, ...), custom_call_target="tpu_custom_call" | custom-call | tf_op jit(solution)/shard_map/pallas_call | solution.py:60
  87.9 2.5 %shard_map.266 = (bf16[2,4,64,576]{3,2,1,0:T(8,128)(2,1)}, bf16[2,4,64,576]{3,2,1,0:T(8,128)(2,1)S(1)}) custom-call(s32[3]{0:T(128)S(1)} %copy-done.45, bf16[256,1024]{1,0:T(8,128)(2,1)S(1)} %shard_map.258.cot_mine, bf16[256,1024]{1,0:T(8,128)(2,1)S(1)} %collective-permute-done.26.cot_other, bf16[512,576]{1,0:T(8,128)(2,1)S(1)} %get-tuple-element.98.hidden), custom_call_target="tpu_custom_call" | custom-call | tf_op jit(solution)/shard_map/pallas_call | solution.py:60
  92.8 4.6 %shard_map.259 = (bf16[512,576]{1,0:T(8,128)(2,1)S(1)}, bf16[512,576]{1,0:T(8,128)(2,1)S(1)}, bf16[256,1024]{1,0:T(8,128)(2,1)S(1)}, bf16[256,1024]{1,0:T(8,128)(2,1)}) custom-call(s32[3]{0:T(128)S(1)} %copy-done.45, bf16[256,1024]{1,0:T(8,128)(2,1)S(1)} %shard_map.258.cot_mine, bf16[256,1024]{1,0:T(8,128)(2,1)S(1)} %collective-permute-done.26.cot_other, ...), custom_call_target="tpu_custom_call" | custom-call | tf_op jit(solution)/shard_map/pallas_call | solution.py:60
  103.9 2.4 %shard_map.267 = (bf16[2,4,64,576]{3,2,1,0:T(8,128)(2,1)S(1)}, bf16[2,4,64,576]{3,2,1,0:T(8,128)(2,1)S(1)}, bf16[2,4,64,576]{3,2,1,0:T(8,128)(2,1)S(1)}, bf16[2,4,64,576]{3,2,1,0:T(8,128)(2,1)S(1)}) custom-call(s32[3]{0:T(128)S(1)} %copy-done.45, bf16[512,1024]{1,0:T(8,128)(2,1)S(1)} %copy-done.4, bf16[512,576]{1,0:T(8,128)(2,1)S(1)} %copy-done.21, ...), custom_call_target="tpu_custom_call" | custom-call | tf_op jit(solution)/shard_map/pallas_call | solution.py:60
  116.1 7.9 %collective-permute-done.49 = bf16[2,4,64,576]{3,2,1,0:T(8,128)(2,1)S(1)} collective-permute-done((bf16[2,4,64,576]{3,2,1,0:T(8,128)(2,1)S(1)}, bf16[2,4,64,576]{3,2,1,0:T(8,128)(2,1)S(1)}, u32[]{:S(2)}, u32[]{:S(2)}) %collective-permute-start.49) | collective-permute-done | bytes 589856 | tf_op jit(solution)/shard_map/ppermute | solution.py:32
  125.3 11.8 %collective-permute-done.51 = bf16[2,4,64,576]{3,2,1,0:T(8,128)(2,1)S(1)} collective-permute-done((bf16[2,4,64,576]{3,2,1,0:T(8,128)(2,1)S(1)}, bf16[2,4,64,576]{3,2,1,0:T(8,128)(2,1)S(1)}, u32[]{:S(2)}, u32[]{:S(2)}) %collective-permute-start.51) | collective-permute-done | bytes 589856 | tf_op jit(solution)/shard_map/ppermute | solution.py:32
  139.8 2.6 %collective-permute-start.48 = (bf16[4,64,576]{2,1,0:T(8,128)(2,1)S(1)}, bf16[4,64,576]{2,1,0:T(8,128)(2,1)S(1)}, u32[]{:S(2)}, u32[]{:S(2)}) collective-permute-start(bf16[4,64,576]{2,1,0:T(8,128)(2,1)S(1)} %fusion.4), channel_id=1, source_target_pairs={{0,16},{8,24},{16,0},{24,8},{1,17},{9,25},{17,1},{25,9},{2,18},{10... | collective-permute-start | bytes 884744 | tf_op jit(solution)/shard_map/ppermute | solution.py:32
  147.7 2.4 %collective-permute-done.31.came1 = bf16[64,1024]{1,0:T(8,128)(2,1)S(1)} collective-permute-done((bf16[64,1024]{1,0:T(8,128)(2,1)S(1)}, bf16[64,1024]{1,0:T(8,128)(2,1)S(1)}, u32[]{:S(2)}, u32[]{:S(2)}) %collective-permute-start.31) | collective-permute-done | bytes 131104 | tf_op jit(solution)/shard_map/ppermute | solution.py:32
  150.1 2.6 %collective-permute-start.52 = (bf16[4,64,576]{2,1,0:T(8,128)(2,1)S(1)}, bf16[4,64,576]{2,1,0:T(8,128)(2,1)S(1)}, u32[]{:S(2)}, u32[]{:S(2)}) collective-permute-start(bf16[4,64,576]{2,1,0:T(8,128)(2,1)S(1)} %fusion.6), channel_id=1, source_target_pairs={{0,16},{8,24},{16,0},{24,8},{1,17},{9,25},{17,1},{25,9},{2,18},{10... | collective-permute-start | bytes 884744 | tf_op jit(solution)/shard_map/ppermute | solution.py:32
  153.9 16.1 %collective-permute-done.48 = bf16[4,64,576]{2,1,0:T(8,128)(2,1)S(1)} collective-permute-done((bf16[4,64,576]{2,1,0:T(8,128)(2,1)S(1)}, bf16[4,64,576]{2,1,0:T(8,128)(2,1)S(1)}, u32[]{:S(2)}, u32[]{:S(2)}) %collective-permute-start.48) | collective-permute-done | bytes 294944 | tf_op jit(solution)/shard_map/ppermute | solution.py:32
  171.1 5.9 %collective-permute-done.50 = bf16[4,64,576]{2,1,0:T(8,128)(2,1)S(1)} collective-permute-done((bf16[4,64,576]{2,1,0:T(8,128)(2,1)S(1)}, bf16[4,64,576]{2,1,0:T(8,128)(2,1)S(1)}, u32[]{:S(2)}, u32[]{:S(2)}) %collective-permute-start.50) | collective-permute-done | bytes 294944 | tf_op jit(solution)/shard_map/ppermute | solution.py:32
  177.6 6.4 %collective-permute-done.52 = bf16[4,64,576]{2,1,0:T(8,128)(2,1)S(1)} collective-permute-done((bf16[4,64,576]{2,1,0:T(8,128)(2,1)S(1)}, bf16[4,64,576]{2,1,0:T(8,128)(2,1)S(1)}, u32[]{:S(2)}, u32[]{:S(2)}) %collective-permute-start.52) | collective-permute-done | bytes 294944 | tf_op jit(solution)/shard_map/ppermute | solution.py:32
  184.2 5.7 %shard_map.263 = (bf16[256,1024]{1,0:T(8,128)(2,1)S(1)}, bf16[256,1024]{1,0:T(8,128)(2,1)S(1)}, f32[8,512]{1,0:T(8,128)S(1)}, bf16[2,4,72,384]{3,2,1,0:T(8,128)(2,1)S(1)}, bf16[2,4,72,384]{3,2,1,0:T(8,128)(2,1)S(1)}) custom-call(s32[3]{0:T(128)S(1)} %copy-done.45, bf16[256,1024]{1,0:T(8,128)(2,1)S(1)} %shard_map.247.mine, bf16[256,1024]{1,0:T(8,128)(2,1)S(1)} %copy-done.2, ...), custom_call_target="tpu_custom_call" | custom-call | tf_op jit(solution)/shard_map/pallas_call | solution.py:60
  190.0 2.0 collective-permute-start.55
  192.7 9.4 %collective-permute-done.41 = bf16[2,4,72,384]{3,2,1,0:T(8,128)(2,1)S(1)} collective-permute-done((bf16[2,4,72,384]{3,2,1,0:T(8,128)(2,1)S(1)}, bf16[2,4,72,384]{3,2,1,0:T(8,128)(2,1)S(1)}, u32[]{:S(2)}, u32[]{:S(2)}) %collective-permute-start.41) | collective-permute-done | bytes 442400 | tf_op jit(solution)/shard_map/ppermute | solution.py:32
  205.1 3.9 %collective-permute-done.53.came1 = bf16[192,576]{1,0:T(8,128)(2,1)S(1)} collective-permute-done((bf16[192,576]{1,0:T(8,128)(2,1)S(1)}, bf16[192,576]{1,0:T(8,128)(2,1)S(1)}, u32[]{:S(2)}, u32[]{:S(2)}) %collective-permute-start.53) | collective-permute-done | bytes 221216 | tf_op jit(solution)/shard_map/ppermute | solution.py:32
  209.1 1.9 shard_map.268
  211.5 2.2 collective-permute-start.38
  220.9 1.8 collective-permute-done.45.came3
  (264 shorter events, 78.3 us)
Async XLA Ops:
  4.6 13.5 %collective-permute-start = (bf16[528,256]{1,0:T(8,128)(2,1)}, bf16[528,256]{1,0:T(8,128)(2,1)S(1)}, u32[]{:S(2)}, u32[]{:S(2)}) collective-permute-start(bf16[528,256]{1,0:T(8,128)(2,1)} %get-tuple-element.83), channel_id=1, source_target_pairs={{0,1},{1,0},{2,3},{3,2},{4,5},{5,4},{6,7},{7,6},{8,9},{9,8},{10,11... | collective-permute-start | bytes 811016 | tf_op jit(solution)/shard_map/ppermute | solution.py:32
  7.6 22.9 %collective-permute-start.1 = (bf16[528,256]{1,0:T(8,128)(2,1)}, bf16[528,256]{1,0:T(8,128)(2,1)S(1)}, u32[]{:S(2)}, u32[]{:S(2)}) collective-permute-start(bf16[528,256]{1,0:T(8,128)(2,1)} %get-tuple-element.84), channel_id=1, source_target_pairs={{0,2},{1,3},{2,0},{3,1},{4,6},{5,7},{6,4},{7,5},{8,10},{9,11},{10,... | collective-permute-start | bytes 811016 | tf_op jit(solution)/shard_map/ppermute | solution.py:32
  9.1 21.4 %collective-permute-start.2 = (bf16[528,256]{1,0:T(8,128)(2,1)}, bf16[528,256]{1,0:T(8,128)(2,1)S(1)}, u32[]{:S(2)}, u32[]{:S(2)}) collective-permute-start(bf16[528,256]{1,0:T(8,128)(2,1)} %get-tuple-element.85), channel_id=1, source_target_pairs={{0,3},{1,2},{2,1},{3,0},{4,7},{5,6},{6,5},{7,4},{8,11},{9,10},{10,... | collective-permute-start | bytes 811016 | tf_op jit(solution)/shard_map/ppermute | solution.py:32
  14.2 16.8 %collective-permute-start.10 = (bf16[768,256]{1,0:T(8,128)(2,1)}, bf16[768,256]{1,0:T(8,128)(2,1)S(1)}, u32[]{:S(2)}, u32[]{:S(2)}) collective-permute-start(bf16[768,256]{1,0:T(8,128)(2,1)} %get-tuple-element.90), channel_id=1, source_target_pairs={{0,3},{1,2},{2,1},{3,0},{4,7},{5,6},{6,5},{7,4},{8,11},{9,10},{10,... | collective-permute-start | bytes 1179656 | tf_op jit(solution)/shard_map/ppermute | solution.py:32
  17.1 19.9 %collective-permute-start.8 = (bf16[768,256]{1,0:T(8,128)(2,1)}, bf16[768,256]{1,0:T(8,128)(2,1)S(1)}, u32[]{:S(2)}, u32[]{:S(2)}) collective-permute-start(bf16[768,256]{1,0:T(8,128)(2,1)} %get-tuple-element.88), channel_id=1, source_target_pairs={{0,1},{1,0},{2,3},{3,2},{4,5},{5,4},{6,7},{7,6},{8,9},{9,8},{10,11... | collective-permute-start | bytes 1179656 | tf_op jit(solution)/shard_map/ppermute | solution.py:32
  18.1 20.3 %collective-permute-start.9 = (bf16[768,256]{1,0:T(8,128)(2,1)}, bf16[768,256]{1,0:T(8,128)(2,1)S(1)}, u32[]{:S(2)}, u32[]{:S(2)}) collective-permute-start(bf16[768,256]{1,0:T(8,128)(2,1)} %get-tuple-element.89), channel_id=1, source_target_pairs={{0,2},{1,3},{2,0},{3,1},{4,6},{5,7},{6,4},{7,5},{8,10},{9,11},{10,... | collective-permute-start | bytes 1179656 | tf_op jit(solution)/shard_map/ppermute | solution.py:32
  40.6 40.4 %collective-permute-start.11 = (bf16[512,1024]{1,0:T(8,128)(2,1)S(1)}, bf16[512,1024]{1,0:T(8,128)(2,1)S(1)}, u32[]{:S(2)}, u32[]{:S(2)}) collective-permute-start(bf16[512,1024]{1,0:T(8,128)(2,1)S(1)} %shard_map.251.joined.out_weight), channel_id=1, source_target_pairs={{0,4},{4,0},{1,5},{5,1},{2,6},{6,2},{3,7},{7,3},{8,12},{12,8},{9,1... | collective-permute-start | bytes 3145736 | tf_op jit(solution)/shard_map/ppermute | solution.py:32
  52.8 15.6 %collective-permute-start.13 = (bf16[256,576]{1,0:T(8,128)(2,1)S(1)}, bf16[256,576]{1,0:T(8,128)(2,1)S(1)}, u32[]{:S(2)}, u32[]{:S(2)}) collective-permute-start(bf16[256,576]{1,0:T(8,128)(2,1)S(1)} %get-tuple-element.95), channel_id=1, source_target_pairs={{0,2},{1,3},{2,0},{3,1},{4,6},{5,7},{6,4},{7,5},{8,10},{9,11},{10,... | collective-permute-start | bytes 884744 | tf_op jit(solution)/shard_map/ppermute | solution.py:32
  54.9 15.2 %collective-permute-start.14 = (bf16[256,576]{1,0:T(8,128)(2,1)S(1)}, bf16[256,576]{1,0:T(8,128)(2,1)S(1)}, u32[]{:S(2)}, u32[]{:S(2)}) collective-permute-start(bf16[256,576]{1,0:T(8,128)(2,1)S(1)} %get-tuple-element.96), channel_id=1, source_target_pairs={{0,3},{1,2},{2,1},{3,0},{4,7},{5,6},{6,5},{7,4},{8,11},{9,10},{10,... | collective-permute-start | bytes 884744 | tf_op jit(solution)/shard_map/ppermute | solution.py:32
  57.7 24.7 %collective-permute-start.7 = (bf16[512,512]{1,0:T(8,128)(2,1)S(1)}, bf16[512,512]{1,0:T(8,128)(2,1)S(1)}, u32[]{:S(2)}, u32[]{:S(2)}) collective-permute-start(bf16[512,512]{1,0:T(8,128)(2,1)S(1)} %shard_map.249.context_near), channel_id=1, source_target_pairs={{0,4},{4,0},{1,5},{5,1},{2,6},{6,2},{3,7},{7,3},{8,12},{12,8},{9,1... | collective-permute-start | bytes 1572872 | tf_op jit(solution)/shard_map/ppermute | solution.py:32
  70.1 17.8 %collective-permute-start.26 = (bf16[256,1024]{1,0:T(8,128)(2,1)S(1)}, bf16[256,1024]{1,0:T(8,128)(2,1)S(1)}, u32[]{:S(2)}, u32[]{:S(2)}) collective-permute-start(bf16[256,1024]{1,0:T(8,128)(2,1)S(1)} %shard_map.258.cot_mine), channel_id=1, source_target_pairs={{0,4},{4,0},{1,5},{5,1},{2,6},{6,2},{3,7},{7,3},{8,12},{12,8},{9,1... | collective-permute-start | bytes 1572872 | tf_op jit(solution)/shard_map/ppermute | solution.py:32
  72.7 12.5 %collective-permute-start.17 = (bf16[256,576]{1,0:T(8,128)(2,1)S(1)}, bf16[256,576]{1,0:T(8,128)(2,1)S(1)}, u32[]{:S(2)}, u32[]{:S(2)}) collective-permute-start(bf16[256,576]{1,0:T(8,128)(2,1)S(1)} %collective-permute-done.14.near3), channel_id=1, source_target_pairs={{0,8},{8,0},{16,24},{24,16},{1,9},{9,1},{17,25},{25,17},{2,10},{10... | collective-permute-start | bytes 884744 | tf_op jit(solution)/shard_map/ppermute | solution.py:32
  79.7 13.0 %collective-permute-start.18 = (bf16[576,256]{1,0:T(8,128)(2,1)S(1)}, bf16[576,256]{1,0:T(8,128)(2,1)S(1)}, u32[]{:S(2)}, u32[]{:S(2)}) collective-permute-start(bf16[576,256]{1,0:T(8,128)(2,1)S(1)} %get-tuple-element.100), channel_id=1, source_target_pairs={{0,1},{1,0},{2,3},{3,2},{4,5},{5,4},{6,7},{7,6},{8,9},{9,8},{10,11... | collective-permute-start | bytes 884744 | tf_op jit(solution)/shard_map/ppermute | solution.py:32
  81.0 11.8 %collective-permute-start.19 = (bf16[576,256]{1,0:T(8,128)(2,1)S(1)}, bf16[576,256]{1,0:T(8,128)(2,1)S(1)}, u32[]{:S(2)}, u32[]{:S(2)}) collective-permute-start(bf16[576,256]{1,0:T(8,128)(2,1)S(1)} %get-tuple-element.101), channel_id=1, source_target_pairs={{0,2},{1,3},{2,0},{3,1},{4,6},{5,7},{6,4},{7,5},{8,10},{9,11},{10,... | collective-permute-start | bytes 884744 | tf_op jit(solution)/shard_map/ppermute | solution.py:32
  91.2 23.0 %collective-permute-start.47 = (bf16[2,4,64,576]{3,2,1,0:T(8,128)(2,1)}, bf16[2,4,64,576]{3,2,1,0:T(8,128)(2,1)}, u32[]{:S(2)}, u32[]{:S(2)}) collective-permute-start(bf16[2,4,64,576]{3,2,1,0:T(8,128)(2,1)} %get-tuple-element.141), channel_id=1, source_target_pairs={{0,8},{8,0},{16,24},{24,16},{1,9},{9,1},{17,25},{25,17},{2,10},{10... | collective-permute-start | bytes 1769480 | tf_op jit(solution)/shard_map/ppermute | solution.py:32
  100.0 11.6 %collective-permute-start.21 = (bf16[256,1024]{1,0:T(8,128)(2,1)}, bf16[256,1024]{1,0:T(8,128)(2,1)}, u32[]{:S(2)}, u32[]{:S(2)}) collective-permute-start(bf16[256,1024]{1,0:T(8,128)(2,1)} %get-tuple-element.104), channel_id=1, source_target_pairs={{0,4},{4,0},{1,5},{5,1},{2,6},{6,2},{3,7},{7,3},{8,12},{12,8},{9,1... | collective-permute-start | bytes 1572872 | tf_op jit(solution)/shard_map/ppermute | solution.py:32
  106.3 17.7 %collective-permute-start.49 = (bf16[2,4,64,576]{3,2,1,0:T(8,128)(2,1)S(1)}, bf16[2,4,64,576]{3,2,1,0:T(8,128)(2,1)S(1)}, u32[]{:S(2)}, u32[]{:S(2)}) collective-permute-start(bf16[2,4,64,576]{3,2,1,0:T(8,128)(2,1)S(1)} %get-tuple-element.145), channel_id=1, source_target_pairs={{0,8},{8,0},{16,24},{24,16},{1,9},{9,1},{17,25},{25,17},{2,10},{10... | collective-permute-start | bytes 1769480 | tf_op jit(solution)/shard_map/ppermute | solution.py:32
  107.7 29.4 %collective-permute-start.51 = (bf16[2,4,64,576]{3,2,1,0:T(8,128)(2,1)S(1)}, bf16[2,4,64,576]{3,2,1,0:T(8,128)(2,1)S(1)}, u32[]{:S(2)}, u32[]{:S(2)}) collective-permute-start(bf16[2,4,64,576]{3,2,1,0:T(8,128)(2,1)S(1)} %get-tuple-element.147), channel_id=1, source_target_pairs={{0,8},{8,0},{16,24},{24,16},{1,9},{9,1},{17,25},{25,17},{2,10},{10... | collective-permute-start | bytes 1769480 | tf_op jit(solution)/shard_map/ppermute | solution.py:32
  110.2 28.6 %collective-permute-start.28 = (bf16[64,1024]{1,0:T(8,128)(2,1)S(1)}, bf16[64,1024]{1,0:T(8,128)(2,1)S(1)}, u32[]{:S(2)}, u32[]{:S(2)}) collective-permute-start(bf16[64,1024]{1,0:T(8,128)(2,1)S(1)} %get-tuple-element.114), channel_id=1, source_target_pairs={{0,1},{1,0},{2,3},{3,2},{4,5},{5,4},{6,7},{7,6},{8,9},{9,8},{10,11... | collective-permute-start | bytes 393224 | tf_op jit(solution)/shard_map/ppermute | solution.py:32
  111.5 28.3 %collective-permute-start.29 = (bf16[64,1024]{1,0:T(8,128)(2,1)S(1)}, bf16[64,1024]{1,0:T(8,128)(2,1)S(1)}, u32[]{:S(2)}, u32[]{:S(2)}) collective-permute-start(bf16[64,1024]{1,0:T(8,128)(2,1)S(1)} %get-tuple-element.115), channel_id=1, source_target_pairs={{0,2},{1,3},{2,0},{3,1},{4,6},{5,7},{6,4},{7,5},{8,10},{9,11},{10,... | collective-permute-start | bytes 393224 | tf_op jit(solution)/shard_map/ppermute | solution.py:32
  114.2 28.4 %collective-permute-start.30 = (bf16[64,1024]{1,0:T(8,128)(2,1)S(1)}, bf16[64,1024]{1,0:T(8,128)(2,1)S(1)}, u32[]{:S(2)}, u32[]{:S(2)}) collective-permute-start(bf16[64,1024]{1,0:T(8,128)(2,1)S(1)} %get-tuple-element.116), channel_id=1, source_target_pairs={{0,3},{1,2},{2,1},{3,0},{4,7},{5,6},{6,5},{7,4},{8,11},{9,10},{10,... | collective-permute-start | bytes 393224 | tf_op jit(solution)/shard_map/ppermute | solution.py:32
  124.0 19.7 %collective-permute-start.22 = (bf16[256,256]{1,0:T(8,128)(2,1)S(1)}, bf16[256,256]{1,0:T(8,128)(2,1)S(1)}, u32[]{:S(2)}, u32[]{:S(2)}) collective-permute-start(bf16[256,256]{1,0:T(8,128)(2,1)S(1)} %get-tuple-element.106), channel_id=1, source_target_pairs={{0,1},{1,0},{2,3},{3,2},{4,5},{5,4},{6,7},{7,6},{8,9},{9,8},{10,11... | collective-permute-start | bytes 393224 | tf_op jit(solution)/shard_map/ppermute | solution.py:32
  139.8 30.2 %collective-permute-start.48 = (bf16[4,64,576]{2,1,0:T(8,128)(2,1)S(1)}, bf16[4,64,576]{2,1,0:T(8,128)(2,1)S(1)}, u32[]{:S(2)}, u32[]{:S(2)}) collective-permute-start(bf16[4,64,576]{2,1,0:T(8,128)(2,1)S(1)} %fusion.4), channel_id=1, source_target_pairs={{0,16},{8,24},{16,0},{24,8},{1,17},{9,25},{17,1},{25,9},{2,18},{10... | collective-permute-start | bytes 884744 | tf_op jit(solution)/shard_map/ppermute | solution.py:32
  142.5 34.5 %collective-permute-start.50 = (bf16[4,64,576]{2,1,0:T(8,128)(2,1)S(1)}, bf16[4,64,576]{2,1,0:T(8,128)(2,1)S(1)}, u32[]{:S(2)}, u32[]{:S(2)}) collective-permute-start(bf16[4,64,576]{2,1,0:T(8,128)(2,1)S(1)} %fusion.5), channel_id=1, source_target_pairs={{0,16},{8,24},{16,0},{24,8},{1,17},{9,25},{17,1},{25,9},{2,18},{10... | collective-permute-start | bytes 884744 | tf_op jit(solution)/shard_map/ppermute | solution.py:32
  150.1 33.9 %collective-permute-start.52 = (bf16[4,64,576]{2,1,0:T(8,128)(2,1)S(1)}, bf16[4,64,576]{2,1,0:T(8,128)(2,1)S(1)}, u32[]{:S(2)}, u32[]{:S(2)}) collective-permute-start(bf16[4,64,576]{2,1,0:T(8,128)(2,1)S(1)} %fusion.6), channel_id=1, source_target_pairs={{0,16},{8,24},{16,0},{24,8},{1,17},{9,25},{17,1},{25,9},{2,18},{10... | collective-permute-start | bytes 884744 | tf_op jit(solution)/shard_map/ppermute | solution.py:32
  152.7 49.8 %collective-permute-start.25 = (bf16[256,256]{1,0:T(8,128)(2,1)S(1)}, bf16[256,256]{1,0:T(8,128)(2,1)S(1)}, u32[]{:S(2)}, u32[]{:S(2)}) collective-permute-start(bf16[256,256]{1,0:T(8,128)(2,1)S(1)} %add_convert_fusion.4), channel_id=1, source_target_pairs={{0,4},{4,0},{1,5},{5,1},{2,6},{6,2},{3,7},{7,3},{8,12},{12,8},{9,1... | collective-permute-start | bytes 393224 | tf_op jit(solution)/shard_map/ppermute | solution.py:32
  153.3 30.8 %collective-permute-start.34 = (bf16[256,1024]{1,0:T(8,128)(2,1)S(1)}, bf16[256,1024]{1,0:T(8,128)(2,1)S(1)}, u32[]{:S(2)}, u32[]{:S(2)}) collective-permute-start(bf16[256,1024]{1,0:T(8,128)(2,1)S(1)} %shard_map.262.grad_mine), channel_id=1, source_target_pairs={{0,4},{4,0},{1,5},{5,1},{2,6},{6,2},{3,7},{7,3},{8,12},{12,8},{9,1... | collective-permute-start | bytes 1572872 | tf_op jit(solution)/shard_map/ppermute | solution.py:32
  189.9 12.1 %collective-permute-start.41 = (bf16[2,4,72,384]{3,2,1,0:T(8,128)(2,1)S(1)}, bf16[2,4,72,384]{3,2,1,0:T(8,128)(2,1)S(1)}, u32[]{:S(2)}, u32[]{:S(2)}) collective-permute-start(bf16[2,4,72,384]{3,2,1,0:T(8,128)(2,1)S(1)} %get-tuple-element.134), channel_id=1, source_target_pairs={{0,8},{8,0},{16,24},{24,16},{1,9},{9,1},{17,25},{25,17},{2,10},{10... | collective-permute-start | bytes 1327112 | tf_op jit(solution)/shard_map/ppermute | solution.py:32
  190.0 15.1 %collective-permute-start.55 = (bf16[192,576]{1,0:T(8,128)(2,1)S(1)}, bf16[192,576]{1,0:T(8,128)(2,1)S(1)}, u32[]{:S(2)}, u32[]{:S(2)}) collective-permute-start(bf16[192,576]{1,0:T(8,128)(2,1)S(1)} %pad_maximum_fusion.5), channel_id=1, source_target_pairs={{0,3},{1,2},{2,1},{3,0},{4,7},{5,6},{6,5},{7,4},{8,11},{9,10},{10,... | collective-permute-start | bytes 663560 | tf_op jit(solution)/shard_map/ppermute | solution.py:32
  192.0 13.1 %collective-permute-start.54 = (bf16[192,576]{1,0:T(8,128)(2,1)S(1)}, bf16[192,576]{1,0:T(8,128)(2,1)S(1)}, u32[]{:S(2)}, u32[]{:S(2)}) collective-permute-start(bf16[192,576]{1,0:T(8,128)(2,1)S(1)} %pad_maximum_fusion.4), channel_id=1, source_target_pairs={{0,2},{1,3},{2,0},{3,1},{4,6},{5,7},{6,4},{7,5},{8,10},{9,11},{10,... | collective-permute-start | bytes 663560 | tf_op jit(solution)/shard_map/ppermute | solution.py:32
  192.6 18.4 %collective-permute-start.35 = (bf16[256,1024]{1,0:T(8,128)(2,1)S(1)}, bf16[256,1024]{1,0:T(8,128)(2,1)S(1)}, u32[]{:S(2)}, u32[]{:S(2)}) collective-permute-start(bf16[256,1024]{1,0:T(8,128)(2,1)S(1)} %get-tuple-element.127), channel_id=1, source_target_pairs={{0,4},{4,0},{1,5},{5,1},{2,6},{6,2},{3,7},{7,3},{8,12},{12,8},{9,1... | collective-permute-start | bytes 1572872 | tf_op jit(solution)/shard_map/ppermute | solution.py:32
  202.6 12.1 %collective-permute-start.42 = (bf16[4,72,384]{2,1,0:T(8,128)(2,1)S(1)}, bf16[4,72,384]{2,1,0:T(8,128)(2,1)S(1)}, u32[]{:S(2)}, u32[]{:S(2)}) collective-permute-start(bf16[4,72,384]{2,1,0:T(8,128)(2,1)S(1)} %fusion.11), channel_id=1, source_target_pairs={{0,16},{8,24},{16,0},{24,8},{1,17},{9,25},{17,1},{25,9},{2,18},{10... | collective-permute-start | bytes 663560 | tf_op jit(solution)/shard_map/ppermute | solution.py:32
  (74 other events, 602.0 us)

commit v4 on v3

--- a/solution.py
+++ b/solution.py
@@ -358,28 +358,56 @@
     return ordered
 
 
-def unpack_feed_kernel(where, came0, came1, came2, came3, down_out, gate_out, up_out):
+def plane_sum(keep, came, far, k):
+    return keep[0, k].astype(F32) + came[0, k].astype(F32) + far[k].astype(F32)
+
+
+def sum_feed_kernel(
+    keep0, came0, far0, keep1, came1, far1, out0, out1, out2, out3
+):
+    rows = keep0.shape[2]
+    for k, out in enumerate((out0, out1, out2, out3)):
+        out[:rows, :] = plane_sum(keep0, came0, far0, k).astype(BF16)
+        out[rows:, :] = plane_sum(keep1, came1, far1, k).astype(BF16)
+
+
+def sum_last_kernel(
+    keep0, came0, far0, keep1, came1, far1, out0, out1, out2, out3
+):
+    rows, size = keep0.shape[2], keep1.shape[3]
+    for k, out in enumerate((out0, out1, out2, out3)):
+        out[:rows, :] = plane_sum(keep0, came0, far0, k).astype(BF16)
+        out[rows:, :size] = plane_sum(keep1, came1, far1, k).astype(BF16)
+        rest = out.shape[1] - size
+        out[rows:, size:] = jnp.zeros((out.shape[0] - rows, rest), BF16)
+
+
+def unpack_feed_kernel(where, came0, came1, came2, came3, down_out, gate_out):
     rows = gate_out.shape[0]
     pieces = in_chip_order(where, [v[...] for v in (came0, came1, came2, came3)])
-    for i, out in enumerate((down_out, gate_out, up_out)):
+    for i, out in enumerate((down_out, gate_out)):
         span = slice(i * rows, (i + 1) * rows)
         out[...] = jnp.concatenate([v[span].astype(F32) for v in pieces], axis=1)
 
 
-def unpack_mixed_kernel(
-    where, came0, came1, came2, came3, query_out, key_out, value_out, output_out, gain_out
+def unpack_last_kernel(
+    where, came0, came1, came2, came3,
+    up_out, query_out, key_out, value_out, output_out, gain_out,
 ):
     rows = query_out.shape[0]
     pieces = in_chip_order(where, [v[...] for v in (came0, came1, came2, came3)])
     two = query_out.shape[1] // len(pieces)
     size = two // 2
     pieces = [v.astype(F32) for v in pieces]
+    up_out[...] = jnp.concatenate([v[:rows] for v in pieces], axis=1)
     for out, start, wide in (
         (query_out, 0, two), (key_out, two, size), (value_out, two + size, size),
         (output_out, 2 * two, two),
     ):
-        out[...] = jnp.concatenate([v[:rows, start : start + wide] for v in pieces], axis=1)
-    gain_out[...] = pieces[0][rows:] + pieces[1][rows:] + pieces[2][rows:] + pieces[3][rows:]
+        blocks = [v[rows : 2 * rows, start : start + wide] for v in pieces]
+        out[...] = jnp.concatenate(blocks, axis=1)
+    gains = [v[2 * rows :, : 3 * two] for v in pieces]
+    gain_out[...] = gains[0] + gains[1] + gains[2] + gains[3]
 
 
 def lane_is_first(size):
@@ -746,11 +774,10 @@
     )
     first_other = flip(first_half, "row", 1)
 
-    def summed(send, keep):
+    def shifted(send, keep):
         came = flip(send, "dp", 1)
         rest = (keep[1].astype(F32) + came[1].astype(F32)).astype(BF16)
-        far = flip(rest, "dp", 2)
-        return total([keep[0], came[0], far]).astype(BF16)
+        return keep, came, flip(rest, "dp", 2)
 
     def scattered(split):
         return lax.psum_scatter(split, "dp", scatter_dimension=0, tiled=True)[0]
@@ -765,7 +792,17 @@
             scalars=where,
             scratch=[((part, units), BF16)], room=20)
         dealt = list(down_dealt) + list(dealt)
-        sums = [summed(dealt[2 * i], dealt[2 * i + 1]) for i in range(3)]
+        down_terms, gate_terms, up_terms = [
+            shifted(dealt[2 * i], dealt[2 * i + 1])
+            for i in range(3)
+        ]
+        feed_out = kernel_call(
+            sum_feed_kernel,
+            [((2 * rows, units), BF16)] * cols,
+            *down_terms,
+            *gate_terms,
+            room=16,
+        )
     else:
         cot_all = jnp.concatenate([cot_mine, cot_other], axis=0)
         sums = [
@@ -778,9 +815,15 @@
                 matmul_tn(normed_two, up_grad),
             )
         ]
-    feed_in = exchange([jnp.concatenate([v[k] for v in sums], axis=0) for k in range(cols)])
-    down_share, gate_share, up_share = kernel_call(
-        unpack_feed_kernel, [((rows, cols * units), F32)] * 3, *feed_in, scalars=where, room=12)
+        feed_out = [jnp.concatenate([v[k] for v in sums[:2]], axis=0) for k in range(cols)]
+    feed_in = exchange(feed_out)
+    down_share, gate_share = kernel_call(
+        unpack_feed_kernel,
+        [((rows, cols * units), F32)] * 2,
+        *feed_in,
+        scalars=where,
+        room=12,
+    )
 
     result_mine, result_other = kernel_call(
         result_kernel, [((half, width), BF16)] * 2, hidden, *down_parts, room=12)
@@ -833,23 +876,34 @@
     input_grad = natural(both_rows(input_mine_grad))
 
     if planes == 4:
-        mixed_sum = summed(mixed_first, mixed_second)
+        mixed_terms = shifted(mixed_first, mixed_second)
+        last_out = kernel_call(
+            sum_last_kernel,
+            [((2 * rows + 8, units), BF16)] * cols,
+            *up_terms,
+            *mixed_terms,
+            room=16,
+        )
     else:
         lines = jnp.broadcast_to(mixed_second[:, None], (cols, planes, 8, mixed_size))
         blocks = mixed_first.reshape(cols, planes, rows, mixed_size)
         mixed_sum = scattered(jnp.moveaxis(jnp.concatenate([blocks, lines], axis=2), 1, 0))
-    mixed_in = exchange([mixed_sum[k] for k in range(cols)])
-    query_share, key_share, value_share, output_share, gain_sums = kernel_call(
-        unpack_mixed_kernel,
+        mixed_sum = jnp.pad(mixed_sum, ((0, 0), (0, 0), (0, units - mixed_size)))
+        last_out = [jnp.concatenate([sums[2][k], mixed_sum[k]], axis=0) for k in range(cols)]
+    last_in = exchange(last_out)
+    up_share, query_share, key_share, value_share, output_share, gain_sums = kernel_call(
+        unpack_last_kernel,
         [
+            ((rows, cols * units), F32),
             ((rows, cols * q_size), F32),
             ((rows, cols * head), F32),
             ((rows, cols * head), F32),
             ((rows, cols * q_size), F32),
             ((8, mixed_size), F32),
         ],
-        *mixed_in,
+        *last_in,
         scalars=where,
+        room=12,
     )
     gain_sums = gain_sums + flip(gain_sums, "row", 1)
     attention_share = lax.dynamic_slice_in_dim(gain_sums[0], plane * rows, rows, 0)

time: 228 us -> 213 us (0.934)
  waiting for transfers between devices: 103 us -> 88.5 us
  Pallas kernels: 41.7 us -> 44.1 us
  starting transfers between devices: 60 us -> 57.6 us
    ppermute x56, waiting for transfers between devices: 103 us -> 88.5 us  [flip(): return lax.ppermute(values, axis, [(i, i ^ distance) for i in range(size)])]
    pallas_call x23 -> x25, Pallas kernels: 41.7 us -> 44.1 us  [kernel_call(): pl.pallas_call(kernel, out_shape=[jax.ShapeDtypeStruct(shape, dtype) for...]
    ppermute x56, starting transfers between devices: 60 us -> 57.6 us  [flip(): return lax.ppermute(values, axis, [(i, i ^ distance) for i in range(size)])]
    unnamed x100 -> x94, local copies, waits for them, and re-layouts: 12 us -> 11.2 us
  transfers between devices with their start and end apart: 56 -> 56, of which waited for: 22 -> 26; matrix products, arithmetic and copies ran while one was open for 4% -> 4% of each run, Pallas kernels for 16% -> 17%
where the time goes in v4:
time: 213 us; the launch traced here: 212 us
  waiting for transfers between devices  88.5 us (42%)
  starting transfers between devices  57.6 us (27%)
  Pallas kernels  44.1 us (21%)
  local copies, waits for them, and re-layouts  14 us (7%)
  other arithmetic  6.66 us (3%)
    ppermute x56, waiting for transfers between devices, flip(): return lax.ppermute(values, axis, [(i, i ^ distance) for i in range(size)])  88.5 us
    ppermute x56, starting transfers between devices, flip(): return lax.ppermute(values, axis, [(i, i ^ distance) for i in range(size)])  57.6 us
    pallas_call x25, Pallas kernels, kernel_call(): pl.pallas_call(kernel, out_shape=[jax.ShapeDtypeStruct(shape, dtype) for...  44.1 us
    unnamed x94, local copies, waits for them, and re-layouts  11.2 us
  transfers between devices with their start and end apart: 56, of which 26 were waited for; matrix products, arithmetic and copies ran while one was open for 4% of the time, Pallas kernels for 17%

profile of v4, /device:TPU:0, one launch (start us, length us, event | category | flops | bytes accessed | tf_op | source)
XLA Modules:
  0.0 212.3 jit_solution(7319830034860309567)
XLA Ops:
  1.3 3.3 %shard_map.246 = (bf16[528,256]{1,0:T(8,128)(2,1)}, bf16[528,256]{1,0:T(8,128)(2,1)}, bf16[528,256]{1,0:T(8,128)(2,1)}, bf16[528,256]{1,0:T(8,128)(2,1)}) custom-call(s32[3]{0:T(128)} %pad_add_fusion.2.where, bf16[512,256]{1,0:T(8,128)(2,1)} %x_in.1, bf16[256,512]{1,0:T(8,128)(2,1)} %query_in.1, bf16[256,256]{1,0:T(8,128)(2,1)} %key_in.1, ...), custom_call_target="tpu_custom_call" | custom-call | tf_op jit(solution)/shard_map/pallas_call | solution.py:60
  4.6 3.0 %collective-permute-start = (bf16[528,256]{1,0:T(8,128)(2,1)}, bf16[528,256]{1,0:T(8,128)(2,1)S(1)}, u32[]{:S(2)}, u32[]{:S(2)}) collective-permute-start(bf16[528,256]{1,0:T(8,128)(2,1)} %get-tuple-element.91), channel_id=1, source_target_pairs={{0,1},{1,0},{2,3},{3,2},{4,5},{5,4},{6,7},{7,6},{8,9},{9,8},{10,11... | collective-permute-start | bytes 811016 | tf_op jit(solution)/shard_map/ppermute | solution.py:32
  14.0 2.9 %collective-permute-start.10 = (bf16[768,256]{1,0:T(8,128)(2,1)}, bf16[768,256]{1,0:T(8,128)(2,1)S(1)}, u32[]{:S(2)}, u32[]{:S(2)}) collective-permute-start(bf16[768,256]{1,0:T(8,128)(2,1)} %get-tuple-element.98), channel_id=1, source_target_pairs={{0,3},{1,2},{2,1},{3,0},{4,7},{5,6},{6,5},{7,4},{8,11},{9,10},{10,... | collective-permute-start | bytes 1179656 | tf_op jit(solution)/shard_map/ppermute | solution.py:32
  19.7 10.8 %collective-permute-done.1.first2 = bf16[528,256]{1,0:T(8,128)(2,1)S(1)} collective-permute-done((bf16[528,256]{1,0:T(8,128)(2,1)}, bf16[528,256]{1,0:T(8,128)(2,1)S(1)}, u32[]{:S(2)}, u32[]{:S(2)}) %collective-permute-start.1) | collective-permute-done | bytes 270368 | tf_op jit(solution)/shard_map/ppermute | solution.py:32
  31.6 5.3 %collective-permute-done.8.first1 = bf16[768,256]{1,0:T(8,128)(2,1)S(1)} collective-permute-done((bf16[768,256]{1,0:T(8,128)(2,1)}, bf16[768,256]{1,0:T(8,128)(2,1)S(1)}, u32[]{:S(2)}, u32[]{:S(2)}) %collective-permute-start.8) | collective-permute-done | bytes 393248 | tf_op jit(solution)/shard_map/ppermute | solution.py:32
  41.5 4.4 %shard_map.248 = (f32[512,256]{1,0:T(8,128)S(1)}, bf16[512,256]{1,0:T(8,128)(2,1)S(1)}, bf16[512,128]{1,0:T(8,128)(2,1)S(1)}, f32[512,128]{1,0:T(8,128)S(1)}) custom-call(bf16[256,1024]{1,0:T(8,128)(2,1)S(1)} %shard_map.247.mine, bf16[256,1024]{1,0:T(8,128)(2,1)S(1)} %collective-permute-done.3.other, bf16[528,256]{1,0:T(8,128)(2,1)S(1)} %copy-done, ...), custom_call_target="tpu_custom_call" | custom-call | tf_op jit(solution)/shard_map/pallas_call | solution.py:60
  49.5 2.1 %shard_map.253 = (bf16[256,576]{1,0:T(8,128)(2,1)S(1)}, bf16[256,576]{1,0:T(8,128)(2,1)S(1)}, bf16[256,576]{1,0:T(8,128)(2,1)S(1)}, bf16[256,576]{1,0:T(8,128)(2,1)S(1)}, bf16[256,576]{1,0:T(8,128)(2,1)S(1)}) custom-call(s32[3]{0:T(128)S(1)} %copy-done.41, bf16[256,2304]{1,0:T(8,128)(2,1)S(1)} %copy-done.19, bf16[256,2304]{1,0:T(8,128)(2,1)S(1)} %copy-done.20), custom_call_target="tpu_custom_call" | custom-call | tf_op jit(solution)/shard_map/pallas_call | solution.py:60
  57.7 4.6 %collective-permute-done.12.near1 = bf16[256,576]{1,0:T(8,128)(2,1)S(1)} collective-permute-done((bf16[256,576]{1,0:T(8,128)(2,1)S(1)}, bf16[256,576]{1,0:T(8,128)(2,1)S(1)}, u32[]{:S(2)}, u32[]{:S(2)}) %collective-permute-start.12) | collective-permute-done | bytes 294944 | tf_op jit(solution)/shard_map/ppermute | solution.py:32
  63.9 4.4 %collective-permute-done.13.near2 = bf16[256,576]{1,0:T(8,128)(2,1)S(1)} collective-permute-done((bf16[256,576]{1,0:T(8,128)(2,1)S(1)}, bf16[256,576]{1,0:T(8,128)(2,1)S(1)}, u32[]{:S(2)}, u32[]{:S(2)}) %collective-permute-start.13) | collective-permute-done | bytes 294944 | tf_op jit(solution)/shard_map/ppermute | solution.py:32
  71.2 1.7 collective-permute-done.15.far1
  74.5 5.4 %collective-permute-done.16.far2 = bf16[256,576]{1,0:T(8,128)(2,1)S(1)} collective-permute-done((bf16[256,576]{1,0:T(8,128)(2,1)S(1)}, bf16[256,576]{1,0:T(8,128)(2,1)S(1)}, u32[]{:S(2)}, u32[]{:S(2)}) %collective-permute-start.16) | collective-permute-done | bytes 294944 | tf_op jit(solution)/shard_map/ppermute | solution.py:32
  83.4 2.0 shard_map.252
  85.4 2.6 %shard_map.254 = (f32[512,576]{1,0:T(8,128)S(1)}, f32[512,576]{1,0:T(8,128)S(1)}, bf16[512,576]{1,0:T(8,128)(2,1)S(1)}) custom-call(s32[3]{0:T(128)S(1)} %copy-done.41, bf16[512,1024]{1,0:T(8,128)(2,1)S(1)} %get-tuple-element.100.normed, bf16[256,576]{1,0:T(8,128)(2,1)S(1)} %get-tuple-element.101.near0, bf16[256,576]{1,0:T(8,128)(2,1)S(1)} %collective-permute-done.12.near1, ...), custom_call_target="tpu_custom_call" | custom-call | tf_op jit(solution)/shard_map/pallas_call | solution.py:60
  88.0 3.6 %collective-permute-done.19.down2 = bf16[576,256]{1,0:T(8,128)(2,1)S(1)} collective-permute-done((bf16[576,256]{1,0:T(8,128)(2,1)S(1)}, bf16[576,256]{1,0:T(8,128)(2,1)S(1)}, u32[]{:S(2)}, u32[]{:S(2)}) %collective-permute-start.19) | collective-permute-done | bytes 294944 | tf_op jit(solution)/shard_map/ppermute | solution.py:32
  91.6 3.8 %shard_map.259 = (bf16[512,576]{1,0:T(8,128)(2,1)S(1)}, bf16[512,576]{1,0:T(8,128)(2,1)S(1)}, bf16[256,1024]{1,0:T(8,128)(2,1)S(1)}, bf16[256,1024]{1,0:T(8,128)(2,1)S(1)}) custom-call(s32[3]{0:T(128)S(1)} %copy-done.41, bf16[256,1024]{1,0:T(8,128)(2,1)S(1)} %shard_map.258.cot_mine, bf16[256,1024]{1,0:T(8,128)(2,1)S(1)} %collective-permute-done.26.cot_other, ...), custom_call_target="tpu_custom_call" | custom-call | tf_op jit(solution)/shard_map/pallas_call | solution.py:60
  95.5 3.0 %shard_map.265 = (bf16[2,4,64,576]{3,2,1,0:T(8,128)(2,1)}, bf16[2,4,64,576]{3,2,1,0:T(8,128)(2,1)S(1)}, bf16[2,4,64,576]{3,2,1,0:T(8,128)(2,1)S(1)}, bf16[2,4,64,576]{3,2,1,0:T(8,128)(2,1)S(1)}) custom-call(s32[3]{0:T(128)S(1)} %copy-done.41, bf16[512,1024]{1,0:T(8,128)(2,1)S(1)} %get-tuple-element.100.normed, ...), custom_call_target="tpu_custom_call" | custom-call | tf_op jit(solution)/shard_map/pallas_call | solution.py:60
  104.3 1.8 shard_map.256
  113.1 2.5 %shard_map.268 = (bf16[2,4,64,576]{3,2,1,0:T(8,128)(2,1)}, bf16[2,4,64,576]{3,2,1,0:T(8,128)(2,1)S(1)}) custom-call(s32[3]{0:T(128)S(1)} %copy-done.41, bf16[256,1024]{1,0:T(8,128)(2,1)S(1)} %shard_map.258.cot_mine, bf16[256,1024]{1,0:T(8,128)(2,1)S(1)} %collective-permute-done.26.cot_other, bf16[512,576]{1,0:T(8,128)(2,1)S(1)} %get-tuple-element.106.hidden), custom_call_target="tpu_custom_call" | custom-call | tf_op jit(solution)/shard_map/pallas_call | solution.py:60
  120.0 3.5 %collective-permute-done.32.came2 = bf16[64,1024]{1,0:T(8,128)(2,1)} collective-permute-done((bf16[64,1024]{1,0:T(8,128)(2,1)}, bf16[64,1024]{1,0:T(8,128)(2,1)}, u32[]{:S(2)}, u32[]{:S(2)}) %collective-permute-start.32) | collective-permute-done | bytes 131104 | tf_op jit(solution)/shard_map/ppermute | solution.py:32
  123.5 1.7 collective-permute-start.41
  130.7 2.4 %collective-permute-start.23 = (bf16[256,256]{1,0:T(8,128)(2,1)S(1)}, bf16[256,256]{1,0:T(8,128)(2,1)S(1)}, u32[]{:S(2)}, u32[]{:S(2)}) collective-permute-start(bf16[256,256]{1,0:T(8,128)(2,1)S(1)} %get-tuple-element.115), channel_id=1, source_target_pairs={{0,2},{1,3},{2,0},{3,1},{4,6},{5,7},{6,4},{7,5},{8,10},{9,11},{10,... | collective-permute-start | bytes 393224 | tf_op jit(solution)/shard_map/ppermute | solution.py:32
  134.4 1.6 collective-permute-start.24
  137.1 2.7 %collective-permute-start.52 = (bf16[4,64,576]{2,1,0:T(8,128)(2,1)S(1)}, bf16[4,64,576]{2,1,0:T(8,128)(2,1)S(1)}, u32[]{:S(2)}, u32[]{:S(2)}) collective-permute-start(bf16[4,64,576]{2,1,0:T(8,128)(2,1)S(1)} %fusion.2), channel_id=1, source_target_pairs={{0,16},{8,24},{16,0},{24,8},{1,17},{9,25},{17,1},{25,9},{2,18},{10... | collective-permute-start | bytes 884744 | tf_op jit(solution)/shard_map/ppermute | solution.py:32
  139.8 6.0 %shard_map.263 = (bf16[256,1024]{1,0:T(8,128)(2,1)S(1)}, bf16[256,1024]{1,0:T(8,128)(2,1)S(1)}, f32[8,512]{1,0:T(8,128)S(1)}, bf16[2,4,72,384]{3,2,1,0:T(8,128)(2,1)S(1)}, bf16[2,4,72,384]{3,2,1,0:T(8,128)(2,1)S(1)}) custom-call(s32[3]{0:T(128)S(1)} %copy-done.41, bf16[256,1024]{1,0:T(8,128)(2,1)S(1)} %shard_map.247.mine, ...), custom_call_target="tpu_custom_call" | custom-call | tf_op jit(solution)/shard_map/pallas_call | solution.py:60
  145.8 7.6 %collective-permute-done.41.came0 = bf16[2,4,64,576]{3,2,1,0:T(8,128)(2,1)S(1)} collective-permute-done((bf16[2,4,64,576]{3,2,1,0:T(8,128)(2,1)}, bf16[2,4,64,576]{3,2,1,0:T(8,128)(2,1)S(1)}, u32[]{:S(2)}, u32[]{:S(2)}) %collective-permute-start.41) | collective-permute-done | bytes 589856 | tf_op jit(solution)/shard_map/ppermute | solution.py:32
  153.6 2.4 %collective-permute-start.43 = (bf16[2,4,72,384]{3,2,1,0:T(8,128)(2,1)S(1)}, bf16[2,4,72,384]{3,2,1,0:T(8,128)(2,1)S(1)}, u32[]{:S(2)}, u32[]{:S(2)}) collective-permute-start(bf16[2,4,72,384]{3,2,1,0:T(8,128)(2,1)S(1)} %get-tuple-element.146), channel_id=1, source_target_pairs={{0,8},{8,0},{16,24},{24,16},{1,9},{9,1},{17,25},{25,17},{2,10},{10... | collective-permute-start | bytes 1327112 | tf_op jit(solution)/shard_map/ppermute | solution.py:32
  156.9 12.7 %collective-permute-done.50.far0 = bf16[4,64,576]{2,1,0:T(8,128)(2,1)S(1)} collective-permute-done((bf16[4,64,576]{2,1,0:T(8,128)(2,1)S(1)}, bf16[4,64,576]{2,1,0:T(8,128)(2,1)S(1)}, u32[]{:S(2)}, u32[]{:S(2)}) %collective-permute-start.50) | collective-permute-done | bytes 294944 | tf_op jit(solution)/shard_map/ppermute | solution.py:32
  177.8 10.6 %collective-permute-done.42.far0 = bf16[4,64,576]{2,1,0:T(8,128)(2,1)S(1)} collective-permute-done((bf16[4,64,576]{2,1,0:T(8,128)(2,1)S(1)}, bf16[4,64,576]{2,1,0:T(8,128)(2,1)S(1)}, u32[]{:S(2)}, u32[]{:S(2)}) %collective-permute-start.42) | collective-permute-done | bytes 294944 | tf_op jit(solution)/shard_map/ppermute | solution.py:32
  190.3 2.7 %collective-permute-done.44.far1 = bf16[4,72,384]{2,1,0:T(8,128)(2,1)S(1)} collective-permute-done((bf16[4,72,384]{2,1,0:T(8,128)(2,1)S(1)}, bf16[4,72,384]{2,1,0:T(8,128)(2,1)S(1)}, u32[]{:S(2)}, u32[]{:S(2)}) %collective-permute-start.44) | collective-permute-done | bytes 221216 | tf_op jit(solution)/shard_map/ppermute | solution.py:32
  199.0 1.7 shard_map.270
  200.8 2.7 %collective-permute-done.45.came1 = bf16[136,576]{1,0:T(8,128)(2,1)S(1)} collective-permute-done((bf16[136,576]{1,0:T(8,128)(2,1)S(1)}, bf16[136,576]{1,0:T(8,128)(2,1)S(1)}, u32[]{:S(2)}, u32[]{:S(2)}) %collective-permute-start.45) | collective-permute-done | bytes 156704 | tf_op jit(solution)/shard_map/ppermute | solution.py:32
  204.2 2.8 %collective-permute-done.47.came3 = bf16[136,576]{1,0:T(8,128)(2,1)S(1)} collective-permute-done((bf16[136,576]{1,0:T(8,128)(2,1)S(1)}, bf16[136,576]{1,0:T(8,128)(2,1)S(1)}, u32[]{:S(2)}, u32[]{:S(2)}) %collective-permute-start.47) | collective-permute-done | bytes 156704 | tf_op jit(solution)/shard_map/ppermute | solution.py:32
  (248 shorter events, 82.6 us)
Async XLA Ops:
  4.6 14.1 %collective-permute-start = (bf16[528,256]{1,0:T(8,128)(2,1)}, bf16[528,256]{1,0:T(8,128)(2,1)S(1)}, u32[]{:S(2)}, u32[]{:S(2)}) collective-permute-start(bf16[528,256]{1,0:T(8,128)(2,1)} %get-tuple-element.91), channel_id=1, source_target_pairs={{0,1},{1,0},{2,3},{3,2},{4,5},{5,4},{6,7},{7,6},{8,9},{9,8},{10,11... | collective-permute-start | bytes 811016 | tf_op jit(solution)/shard_map/ppermute | solution.py:32
  7.6 22.9 %collective-permute-start.1 = (bf16[528,256]{1,0:T(8,128)(2,1)}, bf16[528,256]{1,0:T(8,128)(2,1)S(1)}, u32[]{:S(2)}, u32[]{:S(2)}) collective-permute-start(bf16[528,256]{1,0:T(8,128)(2,1)} %get-tuple-element.92), channel_id=1, source_target_pairs={{0,2},{1,3},{2,0},{3,1},{4,6},{5,7},{6,4},{7,5},{8,10},{9,11},{10,... | collective-permute-start | bytes 811016 | tf_op jit(solution)/shard_map/ppermute | solution.py:32
  9.1 21.4 %collective-permute-start.2 = (bf16[528,256]{1,0:T(8,128)(2,1)}, bf16[528,256]{1,0:T(8,128)(2,1)S(1)}, u32[]{:S(2)}, u32[]{:S(2)}) collective-permute-start(bf16[528,256]{1,0:T(8,128)(2,1)} %get-tuple-element.93), channel_id=1, source_target_pairs={{0,3},{1,2},{2,1},{3,0},{4,7},{5,6},{6,5},{7,4},{8,11},{9,10},{10,... | collective-permute-start | bytes 811016 | tf_op jit(solution)/shard_map/ppermute | solution.py:32
  14.0 16.9 %collective-permute-start.10 = (bf16[768,256]{1,0:T(8,128)(2,1)}, bf16[768,256]{1,0:T(8,128)(2,1)S(1)}, u32[]{:S(2)}, u32[]{:S(2)}) collective-permute-start(bf16[768,256]{1,0:T(8,128)(2,1)} %get-tuple-element.98), channel_id=1, source_target_pairs={{0,3},{1,2},{2,1},{3,0},{4,7},{5,6},{6,5},{7,4},{8,11},{9,10},{10,... | collective-permute-start | bytes 1179656 | tf_op jit(solution)/shard_map/ppermute | solution.py:32
  16.9 20.0 %collective-permute-start.8 = (bf16[768,256]{1,0:T(8,128)(2,1)}, bf16[768,256]{1,0:T(8,128)(2,1)S(1)}, u32[]{:S(2)}, u32[]{:S(2)}) collective-permute-start(bf16[768,256]{1,0:T(8,128)(2,1)} %get-tuple-element.96), channel_id=1, source_target_pairs={{0,1},{1,0},{2,3},{3,2},{4,5},{5,4},{6,7},{7,6},{8,9},{9,8},{10,11... | collective-permute-start | bytes 1179656 | tf_op jit(solution)/shard_map/ppermute | solution.py:32
  18.6 19.8 %collective-permute-start.9 = (bf16[768,256]{1,0:T(8,128)(2,1)S(1)}, bf16[768,256]{1,0:T(8,128)(2,1)S(1)}, u32[]{:S(2)}, u32[]{:S(2)}) collective-permute-start(bf16[768,256]{1,0:T(8,128)(2,1)S(1)} %get-tuple-element.97), channel_id=1, source_target_pairs={{0,2},{1,3},{2,0},{3,1},{4,6},{5,7},{6,4},{7,5},{8,10},{9,11},{10,... | collective-permute-start | bytes 1179656 | tf_op jit(solution)/shard_map/ppermute | solution.py:32
  40.5 40.7 %collective-permute-start.11 = (bf16[512,1024]{1,0:T(8,128)(2,1)S(1)}, bf16[512,1024]{1,0:T(8,128)(2,1)S(1)}, u32[]{:S(2)}, u32[]{:S(2)}) collective-permute-start(bf16[512,1024]{1,0:T(8,128)(2,1)S(1)} %shard_map.251.joined.out_weight), channel_id=1, source_target_pairs={{0,4},{4,0},{1,5},{5,1},{2,6},{6,2},{3,7},{7,3},{8,12},{12,8},{9,1... | collective-permute-start | bytes 3145736 | tf_op jit(solution)/shard_map/ppermute | solution.py:32
  51.7 10.6 %collective-permute-start.12 = (bf16[256,576]{1,0:T(8,128)(2,1)S(1)}, bf16[256,576]{1,0:T(8,128)(2,1)S(1)}, u32[]{:S(2)}, u32[]{:S(2)}) collective-permute-start(bf16[256,576]{1,0:T(8,128)(2,1)S(1)} %get-tuple-element.102), channel_id=1, source_target_pairs={{0,1},{1,0},{2,3},{3,2},{4,5},{5,4},{6,7},{7,6},{8,9},{9,8},{10,11... | collective-permute-start | bytes 884744 | tf_op jit(solution)/shard_map/ppermute | solution.py:32
  53.0 15.4 %collective-permute-start.13 = (bf16[256,576]{1,0:T(8,128)(2,1)S(1)}, bf16[256,576]{1,0:T(8,128)(2,1)S(1)}, u32[]{:S(2)}, u32[]{:S(2)}) collective-permute-start(bf16[256,576]{1,0:T(8,128)(2,1)S(1)} %get-tuple-element.103), channel_id=1, source_target_pairs={{0,2},{1,3},{2,0},{3,1},{4,6},{5,7},{6,4},{7,5},{8,10},{9,11},{10,... | collective-permute-start | bytes 884744 | tf_op jit(solution)/shard_map/ppermute | solution.py:32
  56.3 26.0 %collective-permute-start.7 = (bf16[512,512]{1,0:T(8,128)(2,1)S(1)}, bf16[512,512]{1,0:T(8,128)(2,1)S(1)}, u32[]{:S(2)}, u32[]{:S(2)}) collective-permute-start(bf16[512,512]{1,0:T(8,128)(2,1)S(1)} %shard_map.249.context_near), channel_id=1, source_target_pairs={{0,4},{4,0},{1,5},{5,1},{2,6},{6,2},{3,7},{7,3},{8,12},{12,8},{9,1... | collective-permute-start | bytes 1572872 | tf_op jit(solution)/shard_map/ppermute | solution.py:32
  56.3 13.7 %collective-permute-start.14 = (bf16[256,576]{1,0:T(8,128)(2,1)S(1)}, bf16[256,576]{1,0:T(8,128)(2,1)S(1)}, u32[]{:S(2)}, u32[]{:S(2)}) collective-permute-start(bf16[256,576]{1,0:T(8,128)(2,1)S(1)} %get-tuple-element.104), channel_id=1, source_target_pairs={{0,3},{1,2},{2,1},{3,0},{4,7},{5,6},{6,5},{7,4},{8,11},{9,10},{10,... | collective-permute-start | bytes 884744 | tf_op jit(solution)/shard_map/ppermute | solution.py:32
  68.4 11.6 %collective-permute-start.16 = (bf16[256,576]{1,0:T(8,128)(2,1)S(1)}, bf16[256,576]{1,0:T(8,128)(2,1)S(1)}, u32[]{:S(2)}, u32[]{:S(2)}) collective-permute-start(bf16[256,576]{1,0:T(8,128)(2,1)S(1)} %collective-permute-done.13.near2), channel_id=1, source_target_pairs={{0,8},{8,0},{16,24},{24,16},{1,9},{9,1},{17,25},{25,17},{2,10},{10... | collective-permute-start | bytes 884744 | tf_op jit(solution)/shard_map/ppermute | solution.py:32
  70.0 21.6 %collective-permute-start.26 = (bf16[256,1024]{1,0:T(8,128)(2,1)S(1)}, bf16[256,1024]{1,0:T(8,128)(2,1)S(1)}, u32[]{:S(2)}, u32[]{:S(2)}) collective-permute-start(bf16[256,1024]{1,0:T(8,128)(2,1)S(1)} %shard_map.258.cot_mine), channel_id=1, source_target_pairs={{0,4},{4,0},{1,5},{5,1},{2,6},{6,2},{3,7},{7,3},{8,12},{12,8},{9,1... | collective-permute-start | bytes 1572872 | tf_op jit(solution)/shard_map/ppermute | solution.py:32
  72.9 12.5 %collective-permute-start.17 = (bf16[256,576]{1,0:T(8,128)(2,1)S(1)}, bf16[256,576]{1,0:T(8,128)(2,1)S(1)}, u32[]{:S(2)}, u32[]{:S(2)}) collective-permute-start(bf16[256,576]{1,0:T(8,128)(2,1)S(1)} %collective-permute-done.14.near3), channel_id=1, source_target_pairs={{0,8},{8,0},{16,24},{24,16},{1,9},{9,1},{17,25},{25,17},{2,10},{10... | collective-permute-start | bytes 884744 | tf_op jit(solution)/shard_map/ppermute | solution.py:32
  98.5 32.2 %collective-permute-start.51 = (bf16[2,4,64,576]{3,2,1,0:T(8,128)(2,1)}, bf16[2,4,64,576]{3,2,1,0:T(8,128)(2,1)}, u32[]{:S(2)}, u32[]{:S(2)}) collective-permute-start(bf16[2,4,64,576]{3,2,1,0:T(8,128)(2,1)} %get-tuple-element.159), channel_id=1, source_target_pairs={{0,8},{8,0},{16,24},{24,16},{1,9},{9,1},{17,25},{25,17},{2,10},{10... | collective-permute-start | bytes 1769480 | tf_op jit(solution)/shard_map/ppermute | solution.py:32
  106.1 22.3 %collective-permute-start.21 = (bf16[256,1024]{1,0:T(8,128)(2,1)}, bf16[256,1024]{1,0:T(8,128)(2,1)}, u32[]{:S(2)}, u32[]{:S(2)}) collective-permute-start(bf16[256,1024]{1,0:T(8,128)(2,1)} %get-tuple-element.112), channel_id=1, source_target_pairs={{0,4},{4,0},{1,5},{5,1},{2,6},{6,2},{3,7},{7,3},{8,12},{12,8},{9,1... | collective-permute-start | bytes 1572872 | tf_op jit(solution)/shard_map/ppermute | solution.py:32
  116.5 17.9 %collective-permute-start.49 = (bf16[2,4,64,576]{3,2,1,0:T(8,128)(2,1)}, bf16[2,4,64,576]{3,2,1,0:T(8,128)(2,1)}, u32[]{:S(2)}, u32[]{:S(2)}) collective-permute-start(bf16[2,4,64,576]{3,2,1,0:T(8,128)(2,1)} %get-tuple-element.157), channel_id=1, source_target_pairs={{0,8},{8,0},{16,24},{24,16},{1,9},{9,1},{17,25},{25,17},{2,10},{10... | collective-permute-start | bytes 1769480 | tf_op jit(solution)/shard_map/ppermute | solution.py:32
  123.5 29.9 %collective-permute-start.41 = (bf16[2,4,64,576]{3,2,1,0:T(8,128)(2,1)}, bf16[2,4,64,576]{3,2,1,0:T(8,128)(2,1)S(1)}, u32[]{:S(2)}, u32[]{:S(2)}) collective-permute-start(bf16[2,4,64,576]{3,2,1,0:T(8,128)(2,1)} %copy-done.42), channel_id=1, source_target_pairs={{0,8},{8,0},{16,24},{24,16},{1,9},{9,1},{17,25},{25,17},{2,10},{10... | collective-permute-start | bytes 1769480 | tf_op jit(solution)/shard_map/ppermute | solution.py:32
  129.7 23.9 %collective-permute-start.22 = (bf16[256,256]{1,0:T(8,128)(2,1)S(1)}, bf16[256,256]{1,0:T(8,128)(2,1)S(1)}, u32[]{:S(2)}, u32[]{:S(2)}) collective-permute-start(bf16[256,256]{1,0:T(8,128)(2,1)S(1)} %get-tuple-element.114), channel_id=1, source_target_pairs={{0,1},{1,0},{2,3},{3,2},{4,5},{5,4},{6,7},{7,6},{8,9},{9,8},{10,11... | collective-permute-start | bytes 393224 | tf_op jit(solution)/shard_map/ppermute | solution.py:32
  130.7 25.3 %collective-permute-start.23 = (bf16[256,256]{1,0:T(8,128)(2,1)S(1)}, bf16[256,256]{1,0:T(8,128)(2,1)S(1)}, u32[]{:S(2)}, u32[]{:S(2)}) collective-permute-start(bf16[256,256]{1,0:T(8,128)(2,1)S(1)} %get-tuple-element.115), channel_id=1, source_target_pairs={{0,2},{1,3},{2,0},{3,1},{4,6},{5,7},{6,4},{7,5},{8,10},{9,11},{10,... | collective-permute-start | bytes 393224 | tf_op jit(solution)/shard_map/ppermute | solution.py:32
  134.4 21.7 %collective-permute-start.24 = (bf16[256,256]{1,0:T(8,128)(2,1)S(1)}, bf16[256,256]{1,0:T(8,128)(2,1)S(1)}, u32[]{:S(2)}, u32[]{:S(2)}) collective-permute-start(bf16[256,256]{1,0:T(8,128)(2,1)S(1)} %get-tuple-element.116), channel_id=1, source_target_pairs={{0,3},{1,2},{2,1},{3,0},{4,7},{5,6},{6,5},{7,4},{8,11},{9,10},{10,... | collective-permute-start | bytes 393224 | tf_op jit(solution)/shard_map/ppermute | solution.py:32
  137.1 19.6 %collective-permute-start.52 = (bf16[4,64,576]{2,1,0:T(8,128)(2,1)S(1)}, bf16[4,64,576]{2,1,0:T(8,128)(2,1)S(1)}, u32[]{:S(2)}, u32[]{:S(2)}) collective-permute-start(bf16[4,64,576]{2,1,0:T(8,128)(2,1)S(1)} %fusion.2), channel_id=1, source_target_pairs={{0,16},{8,24},{16,0},{24,8},{1,17},{9,25},{17,1},{25,9},{2,18},{10... | collective-permute-start | bytes 884744 | tf_op jit(solution)/shard_map/ppermute | solution.py:32
  153.4 16.3 %collective-permute-start.50 = (bf16[4,64,576]{2,1,0:T(8,128)(2,1)S(1)}, bf16[4,64,576]{2,1,0:T(8,128)(2,1)S(1)}, u32[]{:S(2)}, u32[]{:S(2)}) collective-permute-start(bf16[4,64,576]{2,1,0:T(8,128)(2,1)S(1)} %fusion.1), channel_id=1, source_target_pairs={{0,16},{8,24},{16,0},{24,8},{1,17},{9,25},{17,1},{25,9},{2,18},{10... | collective-permute-start | bytes 884744 | tf_op jit(solution)/shard_map/ppermute | solution.py:32
  153.6 19.8 %collective-permute-start.43 = (bf16[2,4,72,384]{3,2,1,0:T(8,128)(2,1)S(1)}, bf16[2,4,72,384]{3,2,1,0:T(8,128)(2,1)S(1)}, u32[]{:S(2)}, u32[]{:S(2)}) collective-permute-start(bf16[2,4,72,384]{3,2,1,0:T(8,128)(2,1)S(1)} %get-tuple-element.146), channel_id=1, source_target_pairs={{0,8},{8,0},{16,24},{24,16},{1,9},{9,1},{17,25},{25,17},{2,10},{10... | collective-permute-start | bytes 1327112 | tf_op jit(solution)/shard_map/ppermute | solution.py:32
  156.0 19.2 %collective-permute-start.35 = (bf16[256,1024]{1,0:T(8,128)(2,1)S(1)}, bf16[256,1024]{1,0:T(8,128)(2,1)S(1)}, u32[]{:S(2)}, u32[]{:S(2)}) collective-permute-start(bf16[256,1024]{1,0:T(8,128)(2,1)S(1)} %get-tuple-element.135), channel_id=1, source_target_pairs={{0,4},{4,0},{1,5},{5,1},{2,6},{6,2},{3,7},{7,3},{8,12},{12,8},{9,1... | collective-permute-start | bytes 1572872 | tf_op jit(solution)/shard_map/ppermute | solution.py:32
  156.1 32.3 %collective-permute-start.42 = (bf16[4,64,576]{2,1,0:T(8,128)(2,1)S(1)}, bf16[4,64,576]{2,1,0:T(8,128)(2,1)S(1)}, u32[]{:S(2)}, u32[]{:S(2)}) collective-permute-start(bf16[4,64,576]{2,1,0:T(8,128)(2,1)S(1)} %fusion), channel_id=1, source_target_pairs={{0,16},{8,24},{16,0},{24,8},{1,17},{9,25},{17,1},{25,9},{2,18},{10... | collective-permute-start | bytes 884744 | tf_op jit(solution)/shard_map/ppermute | solution.py:32
  156.7 20.2 %collective-permute-start.25 = (bf16[256,256]{1,0:T(8,128)(2,1)S(1)}, bf16[256,256]{1,0:T(8,128)(2,1)S(1)}, u32[]{:S(2)}, u32[]{:S(2)}) collective-permute-start(bf16[256,256]{1,0:T(8,128)(2,1)S(1)} %add_convert_fusion.4), channel_id=1, source_target_pairs={{0,4},{4,0},{1,5},{5,1},{2,6},{6,2},{3,7},{7,3},{8,12},{12,8},{9,1... | collective-permute-start | bytes 393224 | tf_op jit(solution)/shard_map/ppermute | solution.py:32
  171.2 18.1 %collective-permute-start.53 = (bf16[128,576]{1,0:T(8,128)(2,1)S(1)}, bf16[128,576]{1,0:T(8,128)(2,1)S(1)}, u32[]{:S(2)}, u32[]{:S(2)}) collective-permute-start(bf16[128,576]{1,0:T(8,128)(2,1)S(1)} %get-tuple-element.161), channel_id=1, source_target_pairs={{0,1},{1,0},{2,3},{3,2},{4,5},{5,4},{6,7},{7,6},{8,9},{9,8},{10,11... | collective-permute-start | bytes 442376 | tf_op jit(solution)/shard_map/ppermute | solution.py:32
  174.5 20.1 %collective-permute-start.54 = (bf16[128,576]{1,0:T(8,128)(2,1)S(1)}, bf16[128,576]{1,0:T(8,128)(2,1)S(1)}, u32[]{:S(2)}, u32[]{:S(2)}) collective-permute-start(bf16[128,576]{1,0:T(8,128)(2,1)S(1)} %get-tuple-element.162), channel_id=1, source_target_pairs={{0,2},{1,3},{2,0},{3,1},{4,6},{5,7},{6,4},{7,5},{8,10},{9,11},{10,... | collective-permute-start | bytes 442376 | tf_op jit(solution)/shard_map/ppermute | solution.py:32
  175.2 20.4 %collective-permute-start.55 = (bf16[128,576]{1,0:T(8,128)(2,1)S(1)}, bf16[128,576]{1,0:T(8,128)(2,1)S(1)}, u32[]{:S(2)}, u32[]{:S(2)}) collective-permute-start(bf16[128,576]{1,0:T(8,128)(2,1)S(1)} %get-tuple-element.163), channel_id=1, source_target_pairs={{0,3},{1,2},{2,1},{3,0},{4,7},{5,6},{6,5},{7,4},{8,11},{9,10},{10,... | collective-permute-start | bytes 442376 | tf_op jit(solution)/shard_map/ppermute | solution.py:32
  176.8 16.2 %collective-permute-start.44 = (bf16[4,72,384]{2,1,0:T(8,128)(2,1)S(1)}, bf16[4,72,384]{2,1,0:T(8,128)(2,1)S(1)}, u32[]{:S(2)}, u32[]{:S(2)}) collective-permute-start(bf16[4,72,384]{2,1,0:T(8,128)(2,1)S(1)} %fusion.7), channel_id=1, source_target_pairs={{0,16},{8,24},{16,0},{24,8},{1,17},{9,25},{17,1},{25,9},{2,18},{10... | collective-permute-start | bytes 663560 | tf_op jit(solution)/shard_map/ppermute | solution.py:32
  189.3 11.4 %collective-permute-start.38 = (bf16[272,256]{1,0:T(8,128)(2,1)S(1)}, bf16[272,256]{1,0:T(8,128)(2,1)S(1)}, u32[]{:S(2)}, u32[]{:S(2)}) collective-permute-start(bf16[272,256]{1,0:T(8,128)(2,1)S(1)} %get-tuple-element.139), channel_id=1, source_target_pairs={{0,2},{1,3},{2,0},{3,1},{4,6},{5,7},{6,4},{7,5},{8,10},{9,11},{10,... | collective-permute-start | bytes 417800 | tf_op jit(solution)/shard_map/ppermute | solution.py:32
  (71 other events, 565.3 us)

commit v5 on v4

--- a/solution.py
+++ b/solution.py
@@ -408,6 +408,18 @@
         out[...] = jnp.concatenate(blocks, axis=1)
     gains = [v[2 * rows :, : 3 * two] for v in pieces]
     gain_out[...] = gains[0] + gains[1] + gains[2] + gains[3]
+
+
+def gain_kernel(where, ours, came, attention_out, feed_out, query_out, key_out):
+    lines = ours[...] + came[...]
+    rows, head = attention_out.shape[1], query_out.shape[1]
+    odd, high = (where[2] & 1) == 1, (where[2] & 2) == 2
+    for out, i in ((attention_out, 0), (feed_out, 1)):
+        parts = [lines[i : i + 1, p * rows : (p + 1) * rows] for p in range(4)]
+        low = jnp.where(odd, parts[1], parts[0])
+        out[...] = jnp.where(high, jnp.where(odd, parts[3], parts[2]), low)
+    query_out[...] = lines[0:1, 4 * rows : 4 * rows + head]
+    key_out[...] = lines[0:1, 4 * rows + head :]
 
 
 def lane_is_first(size):
@@ -616,9 +628,6 @@
     def natural(values):
         return jnp.where(row == 0, values, jnp.roll(values, half, axis=0))
 
-    def both_rows(values):
-        return jnp.concatenate([values, flip(values, "row", 1)], axis=0)
-
     q_size = query_weight.shape[1] // cols
     units = gate_weight.shape[1] // cols
     where = jnp.stack([row, col, plane]).astype(jnp.int32)
@@ -833,7 +842,8 @@
     )
     result_in = exchange(result_pieces)
     result_mine = (first_block + total(result_in)).astype(BF16)
-    block_output = natural(both_rows(result_mine))
+    result_far = flip(result_mine, "row", 1)
+    block_output = natural(jnp.concatenate([result_mine, result_far], axis=0))
 
     mixed_size = 3 * q_size
     if planes == 4:
@@ -873,7 +883,8 @@
     input_mine_grad = first_half[:, :part].astype(F32) + root_one * (
         weighted_one - normal_one * inner_one
     )
-    input_grad = natural(both_rows(input_mine_grad))
+    input_far_grad = flip(input_mine_grad, "row", 1)
+    input_grad = natural(jnp.concatenate([input_mine_grad, input_far_grad], axis=0))
 
     if planes == 4:
         mixed_terms = shifted(mixed_first, mixed_second)
@@ -905,11 +916,24 @@
         scalars=where,
         room=12,
     )
-    gain_sums = gain_sums + flip(gain_sums, "row", 1)
-    attention_share = lax.dynamic_slice_in_dim(gain_sums[0], plane * rows, rows, 0)
-    feedforward_share = lax.dynamic_slice_in_dim(gain_sums[1], plane * rows, rows, 0)
-    query_gain_grad = gain_sums[0, 2 * q_size : 2 * q_size + head]
-    key_gain_grad = gain_sums[0, 2 * q_size + head :]
+    gain_came = flip(gain_sums, "row", 1)
+    if planes == 4:
+        attention_share, feedforward_share, query_gain_grad, key_gain_grad = [
+            v.reshape(-1)
+            for v in kernel_call(
+                gain_kernel,
+                [((1, rows), F32), ((1, rows), F32), ((1, head), F32), ((1, head), F32)],
+                gain_sums,
+                gain_came,
+                scalars=where,
+            )
+        ]
+    else:
+        gain_sums = gain_sums + gain_came
+        attention_share = lax.dynamic_slice_in_dim(gain_sums[0], plane * rows, rows, 0)
+        feedforward_share = lax.dynamic_slice_in_dim(gain_sums[1], plane * rows, rows, 0)
+        query_gain_grad = gain_sums[0, 2 * q_size : 2 * q_size + head]
+        key_gain_grad = gain_sums[0, 2 * q_size + head :]
     return (
         block_output,
         input_grad,

time: 213 us -> 227 us (1.066)
  waiting for transfers between devices: 88.5 us -> 121 us
  local copies, waits for them, and re-layouts: 14 us -> 2.96 us
  Pallas kernels: 44.1 us -> 39.3 us
    ppermute x56, waiting for transfers between devices: 88.5 us -> 121 us  [flip(): return lax.ppermute(values, axis, [(i, i ^ distance) for i in range(size)])]
    unnamed x94 -> x24, local copies, waits for them, and re-layouts: 11.2 us -> 2.6 us
    pallas_call x25 -> x26, Pallas kernels: 44.1 us -> 39.3 us  [kernel_call(): pl.pallas_call(kernel, out_shape=[jax.ShapeDtypeStruct(shape, dtype) for...]
  transfers between devices with their start and end apart: 56 -> 56, of which waited for: 26 -> 25; matrix products, arithmetic and copies ran while one was open for 4% -> 2% of each run, Pallas kernels for 17% -> 14%
where the time goes in v5:
time: 227 us
  waiting for transfers between devices  121 us (53%)
  starting transfers between devices  57.8 us (25%)
  Pallas kernels  39.3 us (17%)
  other arithmetic  4.69 us (2%)
  local copies, waits for them, and re-layouts  2.96 us (1%)
    ppermute x56, waiting for transfers between devices, flip(): return lax.ppermute(values, axis, [(i, i ^ distance) for i in range(size)])  121 us
    ppermute x56, starting transfers between devices, flip(): return lax.ppermute(values, axis, [(i, i ^ distance) for i in range(size)])  57.8 us
    pallas_call x26, Pallas kernels, kernel_call(): pl.pallas_call(kernel, out_shape=[jax.ShapeDtypeStruct(shape, dtype) for...  39.3 us
  transfers between devices with their start and end apart: 56, of which 25 were waited for; matrix products, arithmetic and copies ran while one was open for 2% of the time, Pallas kernels for 14%

profile of v5, /device:TPU:0, one launch (start us, length us, event | category | flops | bytes accessed | tf_op | source)
XLA Modules:
  0.0 226.9 jit_solution(11211717086742662608)
XLA Ops:
  1.3 3.2 %shard_map.246 = (bf16[528,256]{1,0:T(8,128)(2,1)}, bf16[528,256]{1,0:T(8,128)(2,1)}, bf16[528,256]{1,0:T(8,128)(2,1)}, bf16[528,256]{1,0:T(8,128)(2,1)}) custom-call(s32[3]{0:T(128)} %pad_add_fusion.2.where, bf16[512,256]{1,0:T(8,128)(2,1)} %x_in.1, bf16[256,512]{1,0:T(8,128)(2,1)} %query_in.1, bf16[256,256]{1,0:T(8,128)(2,1)} %key_in.1, ...), custom_call_target="tpu_custom_call" | custom-call | tf_op jit(solution)/shard_map/pallas_call | solution.py:60
  4.5 3.0 %collective-permute-start = (bf16[528,256]{1,0:T(8,128)(2,1)}, bf16[528,256]{1,0:T(8,128)(2,1)S(1)}, u32[]{:S(2)}, u32[]{:S(2)}) collective-permute-start(bf16[528,256]{1,0:T(8,128)(2,1)} %get-tuple-element.95), channel_id=1, source_target_pairs={{0,1},{1,0},{2,3},{3,2},{4,5},{5,4},{6,7},{7,6},{8,9},{9,8},{10,11... | collective-permute-start | bytes 811016 | tf_op jit(solution)/shard_map/ppermute | solution.py:32
  13.1 3.0 %collective-permute-start.10 = (bf16[768,256]{1,0:T(8,128)(2,1)}, bf16[768,256]{1,0:T(8,128)(2,1)S(1)}, u32[]{:S(2)}, u32[]{:S(2)}) collective-permute-start(bf16[768,256]{1,0:T(8,128)(2,1)} %get-tuple-element.102), channel_id=1, source_target_pairs={{0,3},{1,2},{2,1},{3,0},{4,7},{5,6},{6,5},{7,4},{8,11},{9,10},{10,... | collective-permute-start | bytes 1179656 | tf_op jit(solution)/shard_map/ppermute | solution.py:32
  18.2 12.3 %collective-permute-done.1.first2 = bf16[528,256]{1,0:T(8,128)(2,1)S(1)} collective-permute-done((bf16[528,256]{1,0:T(8,128)(2,1)}, bf16[528,256]{1,0:T(8,128)(2,1)S(1)}, u32[]{:S(2)}, u32[]{:S(2)}) %collective-permute-start.1) | collective-permute-done | bytes 270368 | tf_op jit(solution)/shard_map/ppermute | solution.py:32
  30.9 6.1 %collective-permute-done.8.first1 = bf16[768,256]{1,0:T(8,128)(2,1)S(1)} collective-permute-done((bf16[768,256]{1,0:T(8,128)(2,1)S(1)}, bf16[768,256]{1,0:T(8,128)(2,1)S(1)}, u32[]{:S(2)}, u32[]{:S(2)}) %collective-permute-start.8) | collective-permute-done | bytes 393248 | tf_op jit(solution)/shard_map/ppermute | solution.py:32
  39.2 4.4 %shard_map.248 = (f32[512,256]{1,0:T(8,128)S(1)}, bf16[512,256]{1,0:T(8,128)(2,1)S(1)}, bf16[512,128]{1,0:T(8,128)(2,1)S(1)}, f32[512,128]{1,0:T(8,128)S(1)}) custom-call(bf16[256,1024]{1,0:T(8,128)(2,1)S(1)} %shard_map.247.mine, bf16[256,1024]{1,0:T(8,128)(2,1)S(1)} %collective-permute-done.3.other, bf16[528,256]{1,0:T(8,128)(2,1)S(1)} %copy-done, ...), custom_call_target="tpu_custom_call" | custom-call | tf_op jit(solution)/shard_map/pallas_call | solution.py:60
  47.2 2.1 shard_map.253
  51.5 2.2 collective-permute-done.6.first3
  55.7 4.2 %collective-permute-done.12.near1 = bf16[256,576]{1,0:T(8,128)(2,1)S(1)} collective-permute-done((bf16[256,576]{1,0:T(8,128)(2,1)S(1)}, bf16[256,576]{1,0:T(8,128)(2,1)S(1)}, u32[]{:S(2)}, u32[]{:S(2)}) %collective-permute-start.12) | collective-permute-done | bytes 294944 | tf_op jit(solution)/shard_map/ppermute | solution.py:32
  62.5 4.8 %collective-permute-done.14.near3 = bf16[256,576]{1,0:T(8,128)(2,1)S(1)} collective-permute-done((bf16[256,576]{1,0:T(8,128)(2,1)S(1)}, bf16[256,576]{1,0:T(8,128)(2,1)S(1)}, u32[]{:S(2)}, u32[]{:S(2)}) %collective-permute-start.14) | collective-permute-done | bytes 294944 | tf_op jit(solution)/shard_map/ppermute | solution.py:32
  68.4 2.1 collective-permute-done.15.far1
  72.1 5.4 %collective-permute-done.16.far2 = bf16[256,576]{1,0:T(8,128)(2,1)S(1)} collective-permute-done((bf16[256,576]{1,0:T(8,128)(2,1)S(1)}, bf16[256,576]{1,0:T(8,128)(2,1)S(1)}, u32[]{:S(2)}, u32[]{:S(2)}) %collective-permute-start.16) | collective-permute-done | bytes 294944 | tf_op jit(solution)/shard_map/ppermute | solution.py:32
  81.0 2.0 shard_map.252
  83.0 2.6 %shard_map.254 = (f32[512,576]{1,0:T(8,128)S(1)}, f32[512,576]{1,0:T(8,128)S(1)}, bf16[512,576]{1,0:T(8,128)(2,1)S(1)}) custom-call(s32[3]{0:T(128)S(1)} %copy-done.7, bf16[512,1024]{1,0:T(8,128)(2,1)S(1)} %get-tuple-element.104.normed, bf16[256,576]{1,0:T(8,128)(2,1)S(1)} %get-tuple-element.105.near0, bf16[256,576]{1,0:T(8,128)(2,1)S(1)} %collective-permute-done.12.near1, ...), custom_call_target="tpu_custom_call" | custom-call | tf_op jit(solution)/shard_map/pallas_call | solution.py:60
  86.0 4.1 %collective-permute-done.19.down2 = bf16[576,256]{1,0:T(8,128)(2,1)S(1)} collective-permute-done((bf16[576,256]{1,0:T(8,128)(2,1)S(1)}, bf16[576,256]{1,0:T(8,128)(2,1)S(1)}, u32[]{:S(2)}, u32[]{:S(2)}) %collective-permute-start.19) | collective-permute-done | bytes 294944 | tf_op jit(solution)/shard_map/ppermute | solution.py:32
  90.1 3.8 %shard_map.259 = (bf16[512,576]{1,0:T(8,128)(2,1)S(1)}, bf16[512,576]{1,0:T(8,128)(2,1)S(1)}, bf16[256,1024]{1,0:T(8,128)(2,1)S(1)}, bf16[256,1024]{1,0:T(8,128)(2,1)S(1)}) custom-call(s32[3]{0:T(128)S(1)} %copy-done.7, bf16[256,1024]{1,0:T(8,128)(2,1)S(1)} %shard_map.258.cot_mine, bf16[256,1024]{1,0:T(8,128)(2,1)S(1)} %collective-permute-done.26.cot_other, ...), custom_call_target="tpu_custom_call" | custom-call | tf_op jit(solution)/shard_map/pallas_call | solution.py:60
  94.0 1.9 collective-permute-done.27.came
  100.3 2.9 %collective-permute-done.28.came1 = bf16[64,1024]{1,0:T(8,128)(2,1)S(1)} collective-permute-done((bf16[64,1024]{1,0:T(8,128)(2,1)S(1)}, bf16[64,1024]{1,0:T(8,128)(2,1)S(1)}, u32[]{:S(2)}, u32[]{:S(2)}) %collective-permute-start.28) | collective-permute-done | bytes 131104 | tf_op jit(solution)/shard_map/ppermute | solution.py:32
  103.1 2.5 %collective-permute-done.29.came2 = bf16[64,1024]{1,0:T(8,128)(2,1)S(1)} collective-permute-done((bf16[64,1024]{1,0:T(8,128)(2,1)S(1)}, bf16[64,1024]{1,0:T(8,128)(2,1)S(1)}, u32[]{:S(2)}, u32[]{:S(2)}) %collective-permute-start.29) | collective-permute-done | bytes 131104 | tf_op jit(solution)/shard_map/ppermute | solution.py:32
  110.0 2.4 %shard_map.265 = (bf16[2,4,64,576]{3,2,1,0:T(8,128)(2,1)S(1)}, bf16[2,4,64,576]{3,2,1,0:T(8,128)(2,1)S(1)}, bf16[2,4,64,576]{3,2,1,0:T(8,128)(2,1)S(1)}, bf16[2,4,64,576]{3,2,1,0:T(8,128)(2,1)S(1)}) custom-call(s32[3]{0:T(128)S(1)} %copy-done.7, bf16[512,1024]{1,0:T(8,128)(2,1)S(1)} %get-tuple-element.104.normed, ...), custom_call_target="tpu_custom_call" | custom-call | tf_op jit(solution)/shard_map/pallas_call | solution.py:60
  120.6 5.9 %shard_map.263 = (bf16[256,1024]{1,0:T(8,128)(2,1)S(1)}, bf16[256,1024]{1,0:T(8,128)(2,1)S(1)}, f32[8,512]{1,0:T(8,128)S(1)}, bf16[2,4,72,384]{3,2,1,0:T(8,128)(2,1)S(1)}, bf16[2,4,72,384]{3,2,1,0:T(8,128)(2,1)S(1)}) custom-call(s32[3]{0:T(128)S(1)} %copy-done.7, bf16[256,1024]{1,0:T(8,128)(2,1)S(1)} %shard_map.247.mine, ...), custom_call_target="tpu_custom_call" | custom-call | tf_op jit(solution)/shard_map/pallas_call | solution.py:60
  127.5 2.6 %collective-permute-done.41.came0 = bf16[2,4,64,576]{3,2,1,0:T(8,128)(2,1)S(1)} collective-permute-done((bf16[2,4,64,576]{3,2,1,0:T(8,128)(2,1)S(1)}, bf16[2,4,64,576]{3,2,1,0:T(8,128)(2,1)S(1)}, u32[]{:S(2)}, u32[]{:S(2)}) %collective-permute-start.41) | collective-permute-done | bytes 589856 | tf_op jit(solution)/shard_map/ppermute | solution.py:32
  130.2 2.6 %collective-permute-start.42 = (bf16[4,64,576]{2,1,0:T(8,128)(2,1)S(1)}, bf16[4,64,576]{2,1,0:T(8,128)(2,1)S(1)}, u32[]{:S(2)}, u32[]{:S(2)}) collective-permute-start(bf16[4,64,576]{2,1,0:T(8,128)(2,1)S(1)} %fusion), channel_id=1, source_target_pairs={{0,16},{8,24},{16,0},{24,8},{1,17},{9,25},{17,1},{25,9},{2,18},{10... | collective-permute-start | bytes 884744 | tf_op jit(solution)/shard_map/ppermute | solution.py:32
  132.8 18.4 %collective-permute-done.51.came1 = bf16[2,4,64,576]{3,2,1,0:T(8,128)(2,1)S(1)} collective-permute-done((bf16[2,4,64,576]{3,2,1,0:T(8,128)(2,1)S(1)}, bf16[2,4,64,576]{3,2,1,0:T(8,128)(2,1)S(1)}, u32[]{:S(2)}, u32[]{:S(2)}) %collective-permute-start.51) | collective-permute-done | bytes 589856 | tf_op jit(solution)/shard_map/ppermute | solution.py:32
  151.3 20.7 %collective-permute-done.43.came1 = bf16[2,4,72,384]{3,2,1,0:T(8,128)(2,1)S(1)} collective-permute-done((bf16[2,4,72,384]{3,2,1,0:T(8,128)(2,1)S(1)}, bf16[2,4,72,384]{3,2,1,0:T(8,128)(2,1)S(1)}, u32[]{:S(2)}, u32[]{:S(2)}) %collective-permute-start.43) | collective-permute-done | bytes 442400 | tf_op jit(solution)/shard_map/ppermute | solution.py:32
  172.1 1.9 collective-permute-start.44
  177.8 2.7 %collective-permute-done.37 = bf16[272,256]{1,0:T(8,128)(2,1)S(1)} collective-permute-done((bf16[272,256]{1,0:T(8,128)(2,1)S(1)}, bf16[272,256]{1,0:T(8,128)(2,1)S(1)}, u32[]{:S(2)}, u32[]{:S(2)}) %collective-permute-start.37) | collective-permute-done | bytes 139296 | tf_op jit(solution)/shard_map/ppermute | solution.py:32
  183.8 2.9 %collective-permute-start.24 = (bf16[256,256]{1,0:T(8,128)(2,1)S(1)}, bf16[256,256]{1,0:T(8,128)(2,1)S(1)}, u32[]{:S(2)}, u32[]{:S(2)}) collective-permute-start(bf16[256,256]{1,0:T(8,128)(2,1)S(1)} %get-tuple-element.120), channel_id=1, source_target_pairs={{0,3},{1,2},{2,1},{3,0},{4,7},{5,6},{6,5},{7,4},{8,11},{9,10},{10,... | collective-permute-start | bytes 393224 | tf_op jit(solution)/shard_map/ppermute | solution.py:32
  190.4 2.5 %collective-permute-start.47 = (bf16[136,576]{1,0:T(8,128)(2,1)S(1)}, bf16[136,576]{1,0:T(8,128)(2,1)S(1)}, u32[]{:S(2)}, u32[]{:S(2)}) collective-permute-start(bf16[136,576]{1,0:T(8,128)(2,1)S(1)} %get-tuple-element.154), channel_id=1, source_target_pairs={{0,3},{1,2},{2,1},{3,0},{4,7},{5,6},{6,5},{7,4},{8,11},{9,10},{10,... | collective-permute-start | bytes 470024 | tf_op jit(solution)/shard_map/ppermute | solution.py:32
  192.8 8.5 %collective-permute-done.52.far1 = bf16[4,64,576]{2,1,0:T(8,128)(2,1)S(1)} collective-permute-done((bf16[4,64,576]{2,1,0:T(8,128)(2,1)S(1)}, bf16[4,64,576]{2,1,0:T(8,128)(2,1)S(1)}, u32[]{:S(2)}, u32[]{:S(2)}) %collective-permute-start.52) | collective-permute-done | bytes 294944 | tf_op jit(solution)/shard_map/ppermute | solution.py:32
  201.5 10.1 %collective-permute-done.50.far0 = bf16[4,64,576]{2,1,0:T(8,128)(2,1)S(1)} collective-permute-done((bf16[4,64,576]{2,1,0:T(8,128)(2,1)S(1)}, bf16[4,64,576]{2,1,0:T(8,128)(2,1)S(1)}, u32[]{:S(2)}, u32[]{:S(2)}) %collective-permute-start.50) | collective-permute-done | bytes 294944 | tf_op jit(solution)/shard_map/ppermute | solution.py:32
  219.0 4.1 %collective-permute-done.54.came2 = bf16[128,576]{1,0:T(8,128)(2,1)S(1)} collective-permute-done((bf16[128,576]{1,0:T(8,128)(2,1)S(1)}, bf16[128,576]{1,0:T(8,128)(2,1)S(1)}, u32[]{:S(2)}, u32[]{:S(2)}) %collective-permute-start.54) | collective-permute-done | bytes 147488 | tf_op jit(solution)/shard_map/ppermute | solution.py:32
  (174 shorter events, 67.5 us)
Async XLA Ops:
  4.5 12.6 %collective-permute-start = (bf16[528,256]{1,0:T(8,128)(2,1)}, bf16[528,256]{1,0:T(8,128)(2,1)S(1)}, u32[]{:S(2)}, u32[]{:S(2)}) collective-permute-start(bf16[528,256]{1,0:T(8,128)(2,1)} %get-tuple-element.95), channel_id=1, source_target_pairs={{0,1},{1,0},{2,3},{3,2},{4,5},{5,4},{6,7},{7,6},{8,9},{9,8},{10,11... | collective-permute-start | bytes 811016 | tf_op jit(solution)/shard_map/ppermute | solution.py:32
  7.6 22.9 %collective-permute-start.1 = (bf16[528,256]{1,0:T(8,128)(2,1)}, bf16[528,256]{1,0:T(8,128)(2,1)S(1)}, u32[]{:S(2)}, u32[]{:S(2)}) collective-permute-start(bf16[528,256]{1,0:T(8,128)(2,1)} %get-tuple-element.96), channel_id=1, source_target_pairs={{0,2},{1,3},{2,0},{3,1},{4,6},{5,7},{6,4},{7,5},{8,10},{9,11},{10,... | collective-permute-start | bytes 811016 | tf_op jit(solution)/shard_map/ppermute | solution.py:32
  9.1 21.4 %collective-permute-start.2 = (bf16[528,256]{1,0:T(8,128)(2,1)}, bf16[528,256]{1,0:T(8,128)(2,1)S(1)}, u32[]{:S(2)}, u32[]{:S(2)}) collective-permute-start(bf16[528,256]{1,0:T(8,128)(2,1)} %get-tuple-element.97), channel_id=1, source_target_pairs={{0,3},{1,2},{2,1},{3,0},{4,7},{5,6},{6,5},{7,4},{8,11},{9,10},{10,... | collective-permute-start | bytes 811016 | tf_op jit(solution)/shard_map/ppermute | solution.py:32
  13.1 17.7 %collective-permute-start.10 = (bf16[768,256]{1,0:T(8,128)(2,1)}, bf16[768,256]{1,0:T(8,128)(2,1)S(1)}, u32[]{:S(2)}, u32[]{:S(2)}) collective-permute-start(bf16[768,256]{1,0:T(8,128)(2,1)} %get-tuple-element.102), channel_id=1, source_target_pairs={{0,3},{1,2},{2,1},{3,0},{4,7},{5,6},{6,5},{7,4},{8,11},{9,10},{10,... | collective-permute-start | bytes 1179656 | tf_op jit(solution)/shard_map/ppermute | solution.py:32
  16.1 20.9 %collective-permute-start.8 = (bf16[768,256]{1,0:T(8,128)(2,1)S(1)}, bf16[768,256]{1,0:T(8,128)(2,1)S(1)}, u32[]{:S(2)}, u32[]{:S(2)}) collective-permute-start(bf16[768,256]{1,0:T(8,128)(2,1)S(1)} %get-tuple-element.100), channel_id=1, source_target_pairs={{0,1},{1,0},{2,3},{3,2},{4,5},{5,4},{6,7},{7,6},{8,9},{9,8},{10,11... | collective-permute-start | bytes 1179656 | tf_op jit(solution)/shard_map/ppermute | solution.py:32
  17.1 21.3 %collective-permute-start.9 = (bf16[768,256]{1,0:T(8,128)(2,1)S(1)}, bf16[768,256]{1,0:T(8,128)(2,1)S(1)}, u32[]{:S(2)}, u32[]{:S(2)}) collective-permute-start(bf16[768,256]{1,0:T(8,128)(2,1)S(1)} %get-tuple-element.101), channel_id=1, source_target_pairs={{0,2},{1,3},{2,0},{3,1},{4,6},{5,7},{6,4},{7,5},{8,10},{9,11},{10,... | collective-permute-start | bytes 1179656 | tf_op jit(solution)/shard_map/ppermute | solution.py:32
  38.5 40.3 %collective-permute-start.11 = (bf16[512,1024]{1,0:T(8,128)(2,1)S(1)}, bf16[512,1024]{1,0:T(8,128)(2,1)S(1)}, u32[]{:S(2)}, u32[]{:S(2)}) collective-permute-start(bf16[512,1024]{1,0:T(8,128)(2,1)S(1)} %shard_map.251.joined.out_weight), channel_id=1, source_target_pairs={{0,4},{4,0},{1,5},{5,1},{2,6},{6,2},{3,7},{7,3},{8,12},{12,8},{9,1... | collective-permute-start | bytes 3145736 | tf_op jit(solution)/shard_map/ppermute | solution.py:32
  49.3 10.7 %collective-permute-start.12 = (bf16[256,576]{1,0:T(8,128)(2,1)S(1)}, bf16[256,576]{1,0:T(8,128)(2,1)S(1)}, u32[]{:S(2)}, u32[]{:S(2)}) collective-permute-start(bf16[256,576]{1,0:T(8,128)(2,1)S(1)} %get-tuple-element.106), channel_id=1, source_target_pairs={{0,1},{1,0},{2,3},{3,2},{4,5},{5,4},{6,7},{7,6},{8,9},{9,8},{10,11... | collective-permute-start | bytes 884744 | tf_op jit(solution)/shard_map/ppermute | solution.py:32
  50.6 10.9 %collective-permute-start.13 = (bf16[256,576]{1,0:T(8,128)(2,1)S(1)}, bf16[256,576]{1,0:T(8,128)(2,1)S(1)}, u32[]{:S(2)}, u32[]{:S(2)}) collective-permute-start(bf16[256,576]{1,0:T(8,128)(2,1)S(1)} %get-tuple-element.107), channel_id=1, source_target_pairs={{0,2},{1,3},{2,0},{3,1},{4,6},{5,7},{6,4},{7,5},{8,10},{9,11},{10,... | collective-permute-start | bytes 884744 | tf_op jit(solution)/shard_map/ppermute | solution.py:32
  53.9 25.7 %collective-permute-start.7 = (bf16[512,512]{1,0:T(8,128)(2,1)S(1)}, bf16[512,512]{1,0:T(8,128)(2,1)S(1)}, u32[]{:S(2)}, u32[]{:S(2)}) collective-permute-start(bf16[512,512]{1,0:T(8,128)(2,1)S(1)} %shard_map.249.context_near), channel_id=1, source_target_pairs={{0,4},{4,0},{1,5},{5,1},{2,6},{6,2},{3,7},{7,3},{8,12},{12,8},{9,1... | collective-permute-start | bytes 1572872 | tf_op jit(solution)/shard_map/ppermute | solution.py:32
  54.0 13.4 %collective-permute-start.14 = (bf16[256,576]{1,0:T(8,128)(2,1)S(1)}, bf16[256,576]{1,0:T(8,128)(2,1)S(1)}, u32[]{:S(2)}, u32[]{:S(2)}) collective-permute-start(bf16[256,576]{1,0:T(8,128)(2,1)S(1)} %get-tuple-element.108), channel_id=1, source_target_pairs={{0,3},{1,2},{2,1},{3,0},{4,7},{5,6},{6,5},{7,4},{8,11},{9,10},{10,... | collective-permute-start | bytes 884744 | tf_op jit(solution)/shard_map/ppermute | solution.py:32
  59.9 10.6 %collective-permute-start.15 = (bf16[256,576]{1,0:T(8,128)(2,1)S(1)}, bf16[256,576]{1,0:T(8,128)(2,1)S(1)}, u32[]{:S(2)}, u32[]{:S(2)}) collective-permute-start(bf16[256,576]{1,0:T(8,128)(2,1)S(1)} %collective-permute-done.12.near1), channel_id=1, source_target_pairs={{0,8},{8,0},{16,24},{24,16},{1,9},{9,1},{17,25},{25,17},{2,10},{10... | collective-permute-start | bytes 884744 | tf_op jit(solution)/shard_map/ppermute | solution.py:32
  61.5 16.0 %collective-permute-start.16 = (bf16[256,576]{1,0:T(8,128)(2,1)S(1)}, bf16[256,576]{1,0:T(8,128)(2,1)S(1)}, u32[]{:S(2)}, u32[]{:S(2)}) collective-permute-start(bf16[256,576]{1,0:T(8,128)(2,1)S(1)} %collective-permute-done.13.near2), channel_id=1, source_target_pairs={{0,8},{8,0},{16,24},{24,16},{1,9},{9,1},{17,25},{25,17},{2,10},{10... | collective-permute-start | bytes 884744 | tf_op jit(solution)/shard_map/ppermute | solution.py:32
  67.4 22.7 %collective-permute-start.26 = (bf16[256,1024]{1,0:T(8,128)(2,1)S(1)}, bf16[256,1024]{1,0:T(8,128)(2,1)S(1)}, u32[]{:S(2)}, u32[]{:S(2)}) collective-permute-start(bf16[256,1024]{1,0:T(8,128)(2,1)S(1)} %shard_map.258.cot_mine), channel_id=1, source_target_pairs={{0,4},{4,0},{1,5},{5,1},{2,6},{6,2},{3,7},{7,3},{8,12},{12,8},{9,1... | collective-permute-start | bytes 1572872 | tf_op jit(solution)/shard_map/ppermute | solution.py:32
  70.5 12.5 %collective-permute-start.17 = (bf16[256,576]{1,0:T(8,128)(2,1)S(1)}, bf16[256,576]{1,0:T(8,128)(2,1)S(1)}, u32[]{:S(2)}, u32[]{:S(2)}) collective-permute-start(bf16[256,576]{1,0:T(8,128)(2,1)S(1)} %collective-permute-done.14.near3), channel_id=1, source_target_pairs={{0,8},{8,0},{16,24},{24,16},{1,9},{9,1},{17,25},{25,17},{2,10},{10... | collective-permute-start | bytes 884744 | tf_op jit(solution)/shard_map/ppermute | solution.py:32
  78.8 11.3 %collective-permute-start.19 = (bf16[576,256]{1,0:T(8,128)(2,1)S(1)}, bf16[576,256]{1,0:T(8,128)(2,1)S(1)}, u32[]{:S(2)}, u32[]{:S(2)}) collective-permute-start(bf16[576,256]{1,0:T(8,128)(2,1)S(1)} %get-tuple-element.113), channel_id=1, source_target_pairs={{0,2},{1,3},{2,0},{3,1},{4,6},{5,7},{6,4},{7,5},{8,10},{9,11},{10,... | collective-permute-start | bytes 884744 | tf_op jit(solution)/shard_map/ppermute | solution.py:32
  79.6 10.5 %collective-permute-start.20 = (bf16[576,256]{1,0:T(8,128)(2,1)S(1)}, bf16[576,256]{1,0:T(8,128)(2,1)S(1)}, u32[]{:S(2)}, u32[]{:S(2)}) collective-permute-start(bf16[576,256]{1,0:T(8,128)(2,1)S(1)} %get-tuple-element.114), channel_id=1, source_target_pairs={{0,3},{1,2},{2,1},{3,0},{4,7},{5,6},{6,5},{7,4},{8,11},{9,10},{10,... | collective-permute-start | bytes 884744 | tf_op jit(solution)/shard_map/ppermute | solution.py:32
  112.4 17.7 %collective-permute-start.41 = (bf16[2,4,64,576]{3,2,1,0:T(8,128)(2,1)S(1)}, bf16[2,4,64,576]{3,2,1,0:T(8,128)(2,1)S(1)}, u32[]{:S(2)}, u32[]{:S(2)}) collective-permute-start(bf16[2,4,64,576]{3,2,1,0:T(8,128)(2,1)S(1)} %get-tuple-element.148), channel_id=1, source_target_pairs={{0,8},{8,0},{16,24},{24,16},{1,9},{9,1},{17,25},{25,17},{2,10},{10... | collective-permute-start | bytes 1769480 | tf_op jit(solution)/shard_map/ppermute | solution.py:32
  116.4 34.8 %collective-permute-start.51 = (bf16[2,4,64,576]{3,2,1,0:T(8,128)(2,1)S(1)}, bf16[2,4,64,576]{3,2,1,0:T(8,128)(2,1)S(1)}, u32[]{:S(2)}, u32[]{:S(2)}) collective-permute-start(bf16[2,4,64,576]{3,2,1,0:T(8,128)(2,1)S(1)} %get-tuple-element.167), channel_id=1, source_target_pairs={{0,8},{8,0},{16,24},{24,16},{1,9},{9,1},{17,25},{25,17},{2,10},{10... | collective-permute-start | bytes 1769480 | tf_op jit(solution)/shard_map/ppermute | solution.py:32
  119.3 56.7 %collective-permute-start.49 = (bf16[2,4,64,576]{3,2,1,0:T(8,128)(2,1)S(1)}, bf16[2,4,64,576]{3,2,1,0:T(8,128)(2,1)S(1)}, u32[]{:S(2)}, u32[]{:S(2)}) collective-permute-start(bf16[2,4,64,576]{3,2,1,0:T(8,128)(2,1)S(1)} %get-tuple-element.165), channel_id=1, source_target_pairs={{0,8},{8,0},{16,24},{24,16},{1,9},{9,1},{17,25},{25,17},{2,10},{10... | collective-permute-start | bytes 1769480 | tf_op jit(solution)/shard_map/ppermute | solution.py:32
  126.5 45.5 %collective-permute-start.43 = (bf16[2,4,72,384]{3,2,1,0:T(8,128)(2,1)S(1)}, bf16[2,4,72,384]{3,2,1,0:T(8,128)(2,1)S(1)}, u32[]{:S(2)}, u32[]{:S(2)}) collective-permute-start(bf16[2,4,72,384]{3,2,1,0:T(8,128)(2,1)S(1)} %get-tuple-element.150), channel_id=1, source_target_pairs={{0,8},{8,0},{16,24},{24,16},{1,9},{9,1},{17,25},{25,17},{2,10},{10... | collective-permute-start | bytes 1327112 | tf_op jit(solution)/shard_map/ppermute | solution.py:32
  127.5 46.5 %collective-permute-start.35 = (bf16[256,1024]{1,0:T(8,128)(2,1)S(1)}, bf16[256,1024]{1,0:T(8,128)(2,1)S(1)}, u32[]{:S(2)}, u32[]{:S(2)}) collective-permute-start(bf16[256,1024]{1,0:T(8,128)(2,1)S(1)} %get-tuple-element.139), channel_id=1, source_target_pairs={{0,4},{4,0},{1,5},{5,1},{2,6},{6,2},{3,7},{7,3},{8,12},{12,8},{9,1... | collective-permute-start | bytes 1572872 | tf_op jit(solution)/shard_map/ppermute | solution.py:32
  130.2 53.6 %collective-permute-start.42 = (bf16[4,64,576]{2,1,0:T(8,128)(2,1)S(1)}, bf16[4,64,576]{2,1,0:T(8,128)(2,1)S(1)}, u32[]{:S(2)}, u32[]{:S(2)}) collective-permute-start(bf16[4,64,576]{2,1,0:T(8,128)(2,1)S(1)} %fusion), channel_id=1, source_target_pairs={{0,16},{8,24},{16,0},{24,8},{1,17},{9,25},{17,1},{25,9},{2,18},{10... | collective-permute-start | bytes 884744 | tf_op jit(solution)/shard_map/ppermute | solution.py:32
  151.3 22.7 %collective-permute-start.36 = (f32[8,256]{1,0:T(8,128)S(1)}, f32[8,256]{1,0:T(8,128)S(1)}, u32[]{:S(2)}, u32[]{:S(2)}) collective-permute-start(f32[8,256]{1,0:T(8,128)S(1)} %slice.126), channel_id=1, source_target_pairs={{0,4},{4,0},{1,5},{5,1},{2,6},{6,2},{3,7},{7,3},{8,12},{12,8},{9,1... | collective-permute-start | bytes 24584 | tf_op jit(solution)/shard_map/ppermute | solution.py:32
  172.1 15.2 %collective-permute-start.44 = (bf16[4,72,384]{2,1,0:T(8,128)(2,1)S(1)}, bf16[4,72,384]{2,1,0:T(8,128)(2,1)S(1)}, u32[]{:S(2)}, u32[]{:S(2)}) collective-permute-start(bf16[4,72,384]{2,1,0:T(8,128)(2,1)S(1)} %fusion.7), channel_id=1, source_target_pairs={{0,16},{8,24},{16,0},{24,8},{1,17},{9,25},{17,1},{25,9},{2,18},{10... | collective-permute-start | bytes 663560 | tf_op jit(solution)/shard_map/ppermute | solution.py:32
  182.6 18.8 %collective-permute-start.52 = (bf16[4,64,576]{2,1,0:T(8,128)(2,1)S(1)}, bf16[4,64,576]{2,1,0:T(8,128)(2,1)S(1)}, u32[]{:S(2)}, u32[]{:S(2)}) collective-permute-start(bf16[4,64,576]{2,1,0:T(8,128)(2,1)S(1)} %fusion.2), channel_id=1, source_target_pairs={{0,16},{8,24},{16,0},{24,8},{1,17},{9,25},{17,1},{25,9},{2,18},{10... | collective-permute-start | bytes 884744 | tf_op jit(solution)/shard_map/ppermute | solution.py:32
  187.3 24.3 %collective-permute-start.50 = (bf16[4,64,576]{2,1,0:T(8,128)(2,1)S(1)}, bf16[4,64,576]{2,1,0:T(8,128)(2,1)S(1)}, u32[]{:S(2)}, u32[]{:S(2)}) collective-permute-start(bf16[4,64,576]{2,1,0:T(8,128)(2,1)S(1)} %fusion.1), channel_id=1, source_target_pairs={{0,16},{8,24},{16,0},{24,8},{1,17},{9,25},{17,1},{25,9},{2,18},{10... | collective-permute-start | bytes 884744 | tf_op jit(solution)/shard_map/ppermute | solution.py:32
  188.0 23.8 %collective-permute-start.45 = (bf16[136,576]{1,0:T(8,128)(2,1)S(1)}, bf16[136,576]{1,0:T(8,128)(2,1)S(1)}, u32[]{:S(2)}, u32[]{:S(2)}) collective-permute-start(bf16[136,576]{1,0:T(8,128)(2,1)S(1)} %get-tuple-element.152), channel_id=1, source_target_pairs={{0,1},{1,0},{2,3},{3,2},{4,5},{5,4},{6,7},{7,6},{8,9},{9,8},{10,11... | collective-permute-start | bytes 470024 | tf_op jit(solution)/shard_map/ppermute | solution.py:32
  189.0 24.3 %collective-permute-start.46 = (bf16[136,576]{1,0:T(8,128)(2,1)S(1)}, bf16[136,576]{1,0:T(8,128)(2,1)S(1)}, u32[]{:S(2)}, u32[]{:S(2)}) collective-permute-start(bf16[136,576]{1,0:T(8,128)(2,1)S(1)} %get-tuple-element.153), channel_id=1, source_target_pairs={{0,2},{1,3},{2,0},{3,1},{4,6},{5,7},{6,4},{7,5},{8,10},{9,11},{10,... | collective-permute-start | bytes 470024 | tf_op jit(solution)/shard_map/ppermute | solution.py:32
  190.4 23.5 %collective-permute-start.47 = (bf16[136,576]{1,0:T(8,128)(2,1)S(1)}, bf16[136,576]{1,0:T(8,128)(2,1)S(1)}, u32[]{:S(2)}, u32[]{:S(2)}) collective-permute-start(bf16[136,576]{1,0:T(8,128)(2,1)S(1)} %get-tuple-element.154), channel_id=1, source_target_pairs={{0,3},{1,2},{2,1},{3,0},{4,7},{5,6},{6,5},{7,4},{8,11},{9,10},{10,... | collective-permute-start | bytes 470024 | tf_op jit(solution)/shard_map/ppermute | solution.py:32
  201.4 24.6 %collective-permute-start.40 = (f32[256,256]{1,0:T(8,128)S(1)}, f32[256,256]{1,0:T(8,128)S(1)}, u32[]{:S(2)}, u32[]{:S(2)}) collective-permute-start(f32[256,256]{1,0:T(8,128)S(1)} %fusion.6), channel_id=1, source_target_pairs={{0,4},{4,0},{1,5},{5,1},{2,6},{6,2},{3,7},{7,3},{8,12},{12,8},{9,1... | collective-permute-start | bytes 786440 | tf_op jit(solution)/shard_map/ppermute | solution.py:32
  213.3 9.8 %collective-permute-start.54 = (bf16[128,576]{1,0:T(8,128)(2,1)S(1)}, bf16[128,576]{1,0:T(8,128)(2,1)S(1)}, u32[]{:S(2)}, u32[]{:S(2)}) collective-permute-start(bf16[128,576]{1,0:T(8,128)(2,1)S(1)} %get-tuple-element.170), channel_id=1, source_target_pairs={{0,2},{1,3},{2,0},{3,1},{4,6},{5,7},{6,4},{7,5},{8,10},{9,11},{10,... | collective-permute-start | bytes 442376 | tf_op jit(solution)/shard_map/ppermute | solution.py:32
  (36 other events, 295.8 us)

commit v6 on v5

--- a/solution.py
+++ b/solution.py
@@ -371,15 +371,9 @@
         out[rows:, :] = plane_sum(keep1, came1, far1, k).astype(BF16)
 
 
-def sum_last_kernel(
-    keep0, came0, far0, keep1, came1, far1, out0, out1, out2, out3
-):
-    rows, size = keep0.shape[2], keep1.shape[3]
+def sum_kernel(keep, came, far, out0, out1, out2, out3):
     for k, out in enumerate((out0, out1, out2, out3)):
-        out[:rows, :] = plane_sum(keep0, came0, far0, k).astype(BF16)
-        out[rows:, :size] = plane_sum(keep1, came1, far1, k).astype(BF16)
-        rest = out.shape[1] - size
-        out[rows:, size:] = jnp.zeros((out.shape[0] - rows, rest), BF16)
+        out[...] = plane_sum(keep, came, far, k).astype(BF16)
 
 
 def unpack_feed_kernel(where, came0, came1, came2, came3, down_out, gate_out):
@@ -390,24 +384,25 @@
         out[...] = jnp.concatenate([v[span].astype(F32) for v in pieces], axis=1)
 
 
+def unpack_up_kernel(where, came0, came1, came2, came3, up_out):
+    pieces = in_chip_order(where, [v[...] for v in (came0, came1, came2, came3)])
+    up_out[...] = jnp.concatenate([v.astype(F32) for v in pieces], axis=1)
+
+
 def unpack_last_kernel(
-    where, came0, came1, came2, came3,
-    up_out, query_out, key_out, value_out, output_out, gain_out,
+    where, came0, came1, came2, came3, query_out, key_out, value_out, output_out, gain_out
 ):
     rows = query_out.shape[0]
     pieces = in_chip_order(where, [v[...] for v in (came0, came1, came2, came3)])
     two = query_out.shape[1] // len(pieces)
     size = two // 2
     pieces = [v.astype(F32) for v in pieces]
-    up_out[...] = jnp.concatenate([v[:rows] for v in pieces], axis=1)
     for out, start, wide in (
         (query_out, 0, two), (key_out, two, size), (value_out, two + size, size),
         (output_out, 2 * two, two),
     ):
-        blocks = [v[rows : 2 * rows, start : start + wide] for v in pieces]
-        out[...] = jnp.concatenate(blocks, axis=1)
-    gains = [v[2 * rows :, : 3 * two] for v in pieces]
-    gain_out[...] = gains[0] + gains[1] + gains[2] + gains[3]
+        out[...] = jnp.concatenate([v[:rows, start : start + wide] for v in pieces], axis=1)
+    gain_out[...] = pieces[0][rows:] + pieces[1][rows:] + pieces[2][rows:] + pieces[3][rows:]
 
 
 def gain_kernel(where, ours, came, attention_out, feed_out, query_out, key_out):
@@ -812,6 +807,9 @@
             *gate_terms,
             room=16,
         )
+        up_out = kernel_call(
+            sum_kernel, [((rows, units), BF16)] * cols, *up_terms, room=12
+        )
     else:
         cot_all = jnp.concatenate([cot_mine, cot_other], axis=0)
         sums = [
@@ -825,6 +823,7 @@
             )
         ]
         feed_out = [jnp.concatenate([v[k] for v in sums[:2]], axis=0) for k in range(cols)]
+        up_out = [sums[2][k] for k in range(cols)]
     feed_in = exchange(feed_out)
     down_share, gate_share = kernel_call(
         unpack_feed_kernel,
@@ -832,6 +831,11 @@
         *feed_in,
         scalars=where,
         room=12,
+    )
+
+    up_in = exchange(up_out)
+    (up_share,) = kernel_call(
+        unpack_up_kernel, [((rows, cols * units), F32)], *up_in, scalars=where
     )
 
     result_mine, result_other = kernel_call(
@@ -888,24 +892,16 @@
 
     if planes == 4:
         mixed_terms = shifted(mixed_first, mixed_second)
-        last_out = kernel_call(
-            sum_last_kernel,
-            [((2 * rows + 8, units), BF16)] * cols,
-            *up_terms,
-            *mixed_terms,
-            room=16,
-        )
+        last_out = kernel_call(sum_kernel, [((rows + 8, mixed_size), BF16)] * cols, *mixed_terms)
     else:
         lines = jnp.broadcast_to(mixed_second[:, None], (cols, planes, 8, mixed_size))
         blocks = mixed_first.reshape(cols, planes, rows, mixed_size)
         mixed_sum = scattered(jnp.moveaxis(jnp.concatenate([blocks, lines], axis=2), 1, 0))
-        mixed_sum = jnp.pad(mixed_sum, ((0, 0), (0, 0), (0, units - mixed_size)))
-        last_out = [jnp.concatenate([sums[2][k], mixed_sum[k]], axis=0) for k in range(cols)]
+        last_out = [mixed_sum[k] for k in range(cols)]
     last_in = exchange(last_out)
-    up_share, query_share, key_share, value_share, output_share, gain_sums = kernel_call(
+    query_share, key_share, value_share, output_share, gain_sums = kernel_call(
         unpack_last_kernel,
         [
-            ((rows, cols * units), F32),
             ((rows, cols * q_size), F32),
             ((rows, cols * head), F32),
             ((rows, cols * head), F32),
@@ -914,7 +910,6 @@
         ],
         *last_in,
         scalars=where,
-        room=12,
     )
     gain_came = flip(gain_sums, "row", 1)
     if planes == 4:

time: 227 us -> 227 us (level)
    pallas_call x26 -> x28, Pallas kernels: 39.3 us -> 40.5 us  [kernel_call(): pl.pallas_call(kernel, out_shape=[jax.ShapeDtypeStruct(shape, dtype) for...]
    ppermute x56 -> x59, starting transfers between devices: 57.8 us -> 56.7 us  [flip(): return lax.ppermute(values, axis, [(i, i ^ distance) for i in range(size)])]
    ppermute x56 -> x59, waiting for transfers between devices: 121 us -> 120 us  [flip(): return lax.ppermute(values, axis, [(i, i ^ distance) for i in range(size)])]
  transfers between devices with their start and end apart: 56 -> 59, of which waited for: 25 -> 25; matrix products, arithmetic and copies ran while one was open for 2% -> 2% of each run, Pallas kernels for 14% -> 14%
where the time goes in v6:
time: 227 us
  waiting for transfers between devices  120 us (53%)
  starting transfers between devices  56.7 us (25%)
  Pallas kernels  40.5 us (18%)
  other arithmetic  4.7 us (2%)
  local copies, waits for them, and re-layouts  2.99 us (1%)
    ppermute x59, waiting for transfers between devices, flip(): return lax.ppermute(values, axis, [(i, i ^ distance) for i in range(size)])  120 us
    ppermute x59, starting transfers between devices, flip(): return lax.ppermute(values, axis, [(i, i ^ distance) for i in range(size)])  56.7 us
    pallas_call x28, Pallas kernels, kernel_call(): pl.pallas_call(kernel, out_shape=[jax.ShapeDtypeStruct(shape, dtype) for...  40.5 us
  transfers between devices with their start and end apart: 59, of which 25 were waited for; matrix products, arithmetic and copies ran while one was open for 2% of the time, Pallas kernels for 14%

profile of v6, /device:TPU:0, one launch (start us, length us, event | category | flops | bytes accessed | tf_op | source)
XLA Modules:
  0.0 226.6 jit_solution(806361189014027591)
XLA Ops:
  1.3 3.2 %shard_map.246 = (bf16[528,256]{1,0:T(8,128)(2,1)}, bf16[528,256]{1,0:T(8,128)(2,1)}, bf16[528,256]{1,0:T(8,128)(2,1)}, bf16[528,256]{1,0:T(8,128)(2,1)}) custom-call(s32[3]{0:T(128)} %pad_add_fusion.2.where, bf16[512,256]{1,0:T(8,128)(2,1)} %x_in.1, bf16[256,512]{1,0:T(8,128)(2,1)} %query_in.1, bf16[256,256]{1,0:T(8,128)(2,1)} %key_in.1, ...), custom_call_target="tpu_custom_call" | custom-call | tf_op jit(solution)/shard_map/pallas_call | solution.py:60
  4.5 3.0 %collective-permute-start = (bf16[528,256]{1,0:T(8,128)(2,1)}, bf16[528,256]{1,0:T(8,128)(2,1)S(1)}, u32[]{:S(2)}, u32[]{:S(2)}) collective-permute-start(bf16[528,256]{1,0:T(8,128)(2,1)} %get-tuple-element.98), channel_id=1, source_target_pairs={{0,1},{1,0},{2,3},{3,2},{4,5},{5,4},{6,7},{7,6},{8,9},{9,8},{10,11... | collective-permute-start | bytes 811016 | tf_op jit(solution)/shard_map/ppermute | solution.py:32
  13.1 3.0 %collective-permute-start.10 = (bf16[768,256]{1,0:T(8,128)(2,1)}, bf16[768,256]{1,0:T(8,128)(2,1)S(1)}, u32[]{:S(2)}, u32[]{:S(2)}) collective-permute-start(bf16[768,256]{1,0:T(8,128)(2,1)} %get-tuple-element.105), channel_id=1, source_target_pairs={{0,3},{1,2},{2,1},{3,0},{4,7},{5,6},{6,5},{7,4},{8,11},{9,10},{10,... | collective-permute-start | bytes 1179656 | tf_op jit(solution)/shard_map/ppermute | solution.py:32
  18.2 12.3 %collective-permute-done.1.first2 = bf16[528,256]{1,0:T(8,128)(2,1)S(1)} collective-permute-done((bf16[528,256]{1,0:T(8,128)(2,1)}, bf16[528,256]{1,0:T(8,128)(2,1)S(1)}, u32[]{:S(2)}, u32[]{:S(2)}) %collective-permute-start.1) | collective-permute-done | bytes 270368 | tf_op jit(solution)/shard_map/ppermute | solution.py:32
  30.9 6.1 %collective-permute-done.8.first1 = bf16[768,256]{1,0:T(8,128)(2,1)S(1)} collective-permute-done((bf16[768,256]{1,0:T(8,128)(2,1)S(1)}, bf16[768,256]{1,0:T(8,128)(2,1)S(1)}, u32[]{:S(2)}, u32[]{:S(2)}) %collective-permute-start.8) | collective-permute-done | bytes 393248 | tf_op jit(solution)/shard_map/ppermute | solution.py:32
  39.2 4.4 %shard_map.248 = (f32[512,256]{1,0:T(8,128)S(1)}, bf16[512,256]{1,0:T(8,128)(2,1)S(1)}, bf16[512,128]{1,0:T(8,128)(2,1)S(1)}, f32[512,128]{1,0:T(8,128)S(1)}) custom-call(bf16[256,1024]{1,0:T(8,128)(2,1)S(1)} %shard_map.247.mine, bf16[256,1024]{1,0:T(8,128)(2,1)S(1)} %collective-permute-done.3.other, bf16[528,256]{1,0:T(8,128)(2,1)S(1)} %copy-done, ...), custom_call_target="tpu_custom_call" | custom-call | tf_op jit(solution)/shard_map/pallas_call | solution.py:60
  47.1 2.1 shard_map.253
  51.5 2.2 collective-permute-done.6.first3
  54.0 1.7 collective-permute-start.14
  55.7 4.2 %collective-permute-done.12.near1 = bf16[256,576]{1,0:T(8,128)(2,1)S(1)} collective-permute-done((bf16[256,576]{1,0:T(8,128)(2,1)S(1)}, bf16[256,576]{1,0:T(8,128)(2,1)S(1)}, u32[]{:S(2)}, u32[]{:S(2)}) %collective-permute-start.12) | collective-permute-done | bytes 294944 | tf_op jit(solution)/shard_map/ppermute | solution.py:32
  62.6 4.8 %collective-permute-done.14.near3 = bf16[256,576]{1,0:T(8,128)(2,1)S(1)} collective-permute-done((bf16[256,576]{1,0:T(8,128)(2,1)S(1)}, bf16[256,576]{1,0:T(8,128)(2,1)S(1)}, u32[]{:S(2)}, u32[]{:S(2)}) %collective-permute-start.14) | collective-permute-done | bytes 294944 | tf_op jit(solution)/shard_map/ppermute | solution.py:32
  68.4 2.1 collective-permute-done.15.far1
  72.1 5.4 %collective-permute-done.16.far2 = bf16[256,576]{1,0:T(8,128)(2,1)S(1)} collective-permute-done((bf16[256,576]{1,0:T(8,128)(2,1)S(1)}, bf16[256,576]{1,0:T(8,128)(2,1)S(1)}, u32[]{:S(2)}, u32[]{:S(2)}) %collective-permute-start.16) | collective-permute-done | bytes 294944 | tf_op jit(solution)/shard_map/ppermute | solution.py:32
  81.0 2.0 shard_map.252
  83.0 2.6 %shard_map.254 = (f32[512,576]{1,0:T(8,128)S(1)}, f32[512,576]{1,0:T(8,128)S(1)}, bf16[512,576]{1,0:T(8,128)(2,1)S(1)}) custom-call(s32[3]{0:T(128)S(1)} %copy-done.13, bf16[512,1024]{1,0:T(8,128)(2,1)S(1)} %get-tuple-element.107.normed, bf16[256,576]{1,0:T(8,128)(2,1)S(1)} %get-tuple-element.108.near0, bf16[256,576]{1,0:T(8,128)(2,1)S(1)} %collective-permute-done.12.near1, ...), custom_call_target="tpu_custom_call" | custom-call | tf_op jit(solution)/shard_map/pallas_call | solution.py:60
  86.0 4.1 %collective-permute-done.19.down2 = bf16[576,256]{1,0:T(8,128)(2,1)S(1)} collective-permute-done((bf16[576,256]{1,0:T(8,128)(2,1)S(1)}, bf16[576,256]{1,0:T(8,128)(2,1)S(1)}, u32[]{:S(2)}, u32[]{:S(2)}) %collective-permute-start.19) | collective-permute-done | bytes 294944 | tf_op jit(solution)/shard_map/ppermute | solution.py:32
  90.1 3.8 %shard_map.259 = (bf16[512,576]{1,0:T(8,128)(2,1)S(1)}, bf16[512,576]{1,0:T(8,128)(2,1)S(1)}, bf16[256,1024]{1,0:T(8,128)(2,1)S(1)}, bf16[256,1024]{1,0:T(8,128)(2,1)S(1)}) custom-call(s32[3]{0:T(128)S(1)} %copy-done.13, bf16[256,1024]{1,0:T(8,128)(2,1)S(1)} %shard_map.258.cot_mine, bf16[256,1024]{1,0:T(8,128)(2,1)S(1)} %collective-permute-done.26.cot_other, ...), custom_call_target="tpu_custom_call" | custom-call | tf_op jit(solution)/shard_map/pallas_call | solution.py:60
  94.0 1.9 collective-permute-done.27.came
  100.3 2.9 %collective-permute-done.28.came1 = bf16[64,1024]{1,0:T(8,128)(2,1)S(1)} collective-permute-done((bf16[64,1024]{1,0:T(8,128)(2,1)S(1)}, bf16[64,1024]{1,0:T(8,128)(2,1)S(1)}, u32[]{:S(2)}, u32[]{:S(2)}) %collective-permute-start.28) | collective-permute-done | bytes 131104 | tf_op jit(solution)/shard_map/ppermute | solution.py:32
  103.1 2.5 %collective-permute-done.29.came2 = bf16[64,1024]{1,0:T(8,128)(2,1)S(1)} collective-permute-done((bf16[64,1024]{1,0:T(8,128)(2,1)S(1)}, bf16[64,1024]{1,0:T(8,128)(2,1)S(1)}, u32[]{:S(2)}, u32[]{:S(2)}) %collective-permute-start.29) | collective-permute-done | bytes 131104 | tf_op jit(solution)/shard_map/ppermute | solution.py:32
  107.7 2.4 %shard_map.269 = (bf16[2,4,64,576]{3,2,1,0:T(8,128)(2,1)S(1)}, bf16[2,4,64,576]{3,2,1,0:T(8,128)(2,1)S(1)}, bf16[2,4,64,576]{3,2,1,0:T(8,128)(2,1)S(1)}, bf16[2,4,64,576]{3,2,1,0:T(8,128)(2,1)S(1)}) custom-call(s32[3]{0:T(128)S(1)} %copy-done.13, bf16[512,1024]{1,0:T(8,128)(2,1)S(1)} %get-tuple-element.107.normed, ...), custom_call_target="tpu_custom_call" | custom-call | tf_op jit(solution)/shard_map/pallas_call | solution.py:60
  116.0 5.7 %collective-permute-done.32.came2 = bf16[64,1024]{1,0:T(8,128)(2,1)S(1)} collective-permute-done((bf16[64,1024]{1,0:T(8,128)(2,1)S(1)}, bf16[64,1024]{1,0:T(8,128)(2,1)S(1)}, u32[]{:S(2)}, u32[]{:S(2)}) %collective-permute-start.32) | collective-permute-done | bytes 131104 | tf_op jit(solution)/shard_map/ppermute | solution.py:32
  130.3 5.9 %shard_map.263 = (bf16[256,1024]{1,0:T(8,128)(2,1)S(1)}, bf16[256,1024]{1,0:T(8,128)(2,1)S(1)}, f32[8,512]{1,0:T(8,128)S(1)}, bf16[2,4,72,384]{3,2,1,0:T(8,128)(2,1)S(1)}, bf16[2,4,72,384]{3,2,1,0:T(8,128)(2,1)S(1)}) custom-call(s32[3]{0:T(128)S(1)} %copy-done.13, bf16[256,1024]{1,0:T(8,128)(2,1)S(1)} %shard_map.247.mine, ...), custom_call_target="tpu_custom_call" | custom-call | tf_op jit(solution)/shard_map/pallas_call | solution.py:60
  136.2 5.7 %collective-permute-done.49.came1 = bf16[2,4,64,576]{3,2,1,0:T(8,128)(2,1)S(1)} collective-permute-done((bf16[2,4,64,576]{3,2,1,0:T(8,128)(2,1)S(1)}, bf16[2,4,64,576]{3,2,1,0:T(8,128)(2,1)S(1)}, u32[]{:S(2)}, u32[]{:S(2)}) %collective-permute-start.49) | collective-permute-done | bytes 589856 | tf_op jit(solution)/shard_map/ppermute | solution.py:32
  142.0 11.9 %collective-permute-done.47.came0 = bf16[2,4,64,576]{3,2,1,0:T(8,128)(2,1)S(1)} collective-permute-done((bf16[2,4,64,576]{3,2,1,0:T(8,128)(2,1)S(1)}, bf16[2,4,64,576]{3,2,1,0:T(8,128)(2,1)S(1)}, u32[]{:S(2)}, u32[]{:S(2)}) %collective-permute-start.47) | collective-permute-done | bytes 589856 | tf_op jit(solution)/shard_map/ppermute | solution.py:32
  153.9 2.6 %collective-permute-start.55 = (bf16[4,64,576]{2,1,0:T(8,128)(2,1)S(1)}, bf16[4,64,576]{2,1,0:T(8,128)(2,1)S(1)}, u32[]{:S(2)}, u32[]{:S(2)}) collective-permute-start(bf16[4,64,576]{2,1,0:T(8,128)(2,1)S(1)} %fusion.2), channel_id=1, source_target_pairs={{0,16},{8,24},{16,0},{24,8},{1,17},{9,25},{17,1},{25,9},{2,18},{10... | collective-permute-start | bytes 884744 | tf_op jit(solution)/shard_map/ppermute | solution.py:32
  158.7 12.5 %collective-permute-done.55.far = bf16[4,64,576]{2,1,0:T(8,128)(2,1)S(1)} collective-permute-done((bf16[4,64,576]{2,1,0:T(8,128)(2,1)S(1)}, bf16[4,64,576]{2,1,0:T(8,128)(2,1)S(1)}, u32[]{:S(2)}, u32[]{:S(2)}) %collective-permute-start.55) | collective-permute-done | bytes 294944 | tf_op jit(solution)/shard_map/ppermute | solution.py:32
  173.4 2.1 collective-permute-done.41.came
  183.2 23.8 %collective-permute-done.42.far = bf16[4,72,384]{2,1,0:T(8,128)(2,1)S(1)} collective-permute-done((bf16[4,72,384]{2,1,0:T(8,128)(2,1)S(1)}, bf16[4,72,384]{2,1,0:T(8,128)(2,1)S(1)}, u32[]{:S(2)}, u32[]{:S(2)}) %collective-permute-start.42) | collective-permute-done | bytes 221216 | tf_op jit(solution)/shard_map/ppermute | solution.py:32
  208.8 1.9 collective-permute-start.45
  214.6 1.8 collective-permute-start.53
  220.0 2.9 %collective-permute-done.52.came2 = bf16[128,576]{1,0:T(8,128)(2,1)S(1)} collective-permute-done((bf16[128,576]{1,0:T(8,128)(2,1)S(1)}, bf16[128,576]{1,0:T(8,128)(2,1)S(1)}, u32[]{:S(2)}, u32[]{:S(2)}) %collective-permute-start.52) | collective-permute-done | bytes 147488 | tf_op jit(solution)/shard_map/ppermute | solution.py:32
  (197 shorter events, 71.7 us)
Async XLA Ops:
  4.5 12.6 %collective-permute-start = (bf16[528,256]{1,0:T(8,128)(2,1)}, bf16[528,256]{1,0:T(8,128)(2,1)S(1)}, u32[]{:S(2)}, u32[]{:S(2)}) collective-permute-start(bf16[528,256]{1,0:T(8,128)(2,1)} %get-tuple-element.98), channel_id=1, source_target_pairs={{0,1},{1,0},{2,3},{3,2},{4,5},{5,4},{6,7},{7,6},{8,9},{9,8},{10,11... | collective-permute-start | bytes 811016 | tf_op jit(solution)/shard_map/ppermute | solution.py:32
  7.6 22.9 %collective-permute-start.1 = (bf16[528,256]{1,0:T(8,128)(2,1)}, bf16[528,256]{1,0:T(8,128)(2,1)S(1)}, u32[]{:S(2)}, u32[]{:S(2)}) collective-permute-start(bf16[528,256]{1,0:T(8,128)(2,1)} %get-tuple-element.99), channel_id=1, source_target_pairs={{0,2},{1,3},{2,0},{3,1},{4,6},{5,7},{6,4},{7,5},{8,10},{9,11},{10,... | collective-permute-start | bytes 811016 | tf_op jit(solution)/shard_map/ppermute | solution.py:32
  9.1 21.4 %collective-permute-start.2 = (bf16[528,256]{1,0:T(8,128)(2,1)}, bf16[528,256]{1,0:T(8,128)(2,1)S(1)}, u32[]{:S(2)}, u32[]{:S(2)}) collective-permute-start(bf16[528,256]{1,0:T(8,128)(2,1)} %get-tuple-element.100), channel_id=1, source_target_pairs={{0,3},{1,2},{2,1},{3,0},{4,7},{5,6},{6,5},{7,4},{8,11},{9,10},{10,... | collective-permute-start | bytes 811016 | tf_op jit(solution)/shard_map/ppermute | solution.py:32
  13.1 17.7 %collective-permute-start.10 = (bf16[768,256]{1,0:T(8,128)(2,1)}, bf16[768,256]{1,0:T(8,128)(2,1)S(1)}, u32[]{:S(2)}, u32[]{:S(2)}) collective-permute-start(bf16[768,256]{1,0:T(8,128)(2,1)} %get-tuple-element.105), channel_id=1, source_target_pairs={{0,3},{1,2},{2,1},{3,0},{4,7},{5,6},{6,5},{7,4},{8,11},{9,10},{10,... | collective-permute-start | bytes 1179656 | tf_op jit(solution)/shard_map/ppermute | solution.py:32
  16.1 20.9 %collective-permute-start.8 = (bf16[768,256]{1,0:T(8,128)(2,1)S(1)}, bf16[768,256]{1,0:T(8,128)(2,1)S(1)}, u32[]{:S(2)}, u32[]{:S(2)}) collective-permute-start(bf16[768,256]{1,0:T(8,128)(2,1)S(1)} %get-tuple-element.103), channel_id=1, source_target_pairs={{0,1},{1,0},{2,3},{3,2},{4,5},{5,4},{6,7},{7,6},{8,9},{9,8},{10,11... | collective-permute-start | bytes 1179656 | tf_op jit(solution)/shard_map/ppermute | solution.py:32
  17.1 21.3 %collective-permute-start.9 = (bf16[768,256]{1,0:T(8,128)(2,1)S(1)}, bf16[768,256]{1,0:T(8,128)(2,1)S(1)}, u32[]{:S(2)}, u32[]{:S(2)}) collective-permute-start(bf16[768,256]{1,0:T(8,128)(2,1)S(1)} %get-tuple-element.104), channel_id=1, source_target_pairs={{0,2},{1,3},{2,0},{3,1},{4,6},{5,7},{6,4},{7,5},{8,10},{9,11},{10,... | collective-permute-start | bytes 1179656 | tf_op jit(solution)/shard_map/ppermute | solution.py:32
  38.5 40.3 %collective-permute-start.11 = (bf16[512,1024]{1,0:T(8,128)(2,1)S(1)}, bf16[512,1024]{1,0:T(8,128)(2,1)S(1)}, u32[]{:S(2)}, u32[]{:S(2)}) collective-permute-start(bf16[512,1024]{1,0:T(8,128)(2,1)S(1)} %shard_map.251.joined.out_weight), channel_id=1, source_target_pairs={{0,4},{4,0},{1,5},{5,1},{2,6},{6,2},{3,7},{7,3},{8,12},{12,8},{9,1... | collective-permute-start | bytes 3145736 | tf_op jit(solution)/shard_map/ppermute | solution.py:32
  50.6 10.9 %collective-permute-start.13 = (bf16[256,576]{1,0:T(8,128)(2,1)S(1)}, bf16[256,576]{1,0:T(8,128)(2,1)S(1)}, u32[]{:S(2)}, u32[]{:S(2)}) collective-permute-start(bf16[256,576]{1,0:T(8,128)(2,1)S(1)} %get-tuple-element.110), channel_id=1, source_target_pairs={{0,2},{1,3},{2,0},{3,1},{4,6},{5,7},{6,4},{7,5},{8,10},{9,11},{10,... | collective-permute-start | bytes 884744 | tf_op jit(solution)/shard_map/ppermute | solution.py:32
  53.9 25.7 %collective-permute-start.7 = (bf16[512,512]{1,0:T(8,128)(2,1)S(1)}, bf16[512,512]{1,0:T(8,128)(2,1)S(1)}, u32[]{:S(2)}, u32[]{:S(2)}) collective-permute-start(bf16[512,512]{1,0:T(8,128)(2,1)S(1)} %shard_map.249.context_near), channel_id=1, source_target_pairs={{0,4},{4,0},{1,5},{5,1},{2,6},{6,2},{3,7},{7,3},{8,12},{12,8},{9,1... | collective-permute-start | bytes 1572872 | tf_op jit(solution)/shard_map/ppermute | solution.py:32
  54.0 13.4 %collective-permute-start.14 = (bf16[256,576]{1,0:T(8,128)(2,1)S(1)}, bf16[256,576]{1,0:T(8,128)(2,1)S(1)}, u32[]{:S(2)}, u32[]{:S(2)}) collective-permute-start(bf16[256,576]{1,0:T(8,128)(2,1)S(1)} %get-tuple-element.111), channel_id=1, source_target_pairs={{0,3},{1,2},{2,1},{3,0},{4,7},{5,6},{6,5},{7,4},{8,11},{9,10},{10,... | collective-permute-start | bytes 884744 | tf_op jit(solution)/shard_map/ppermute | solution.py:32
  61.5 16.0 %collective-permute-start.16 = (bf16[256,576]{1,0:T(8,128)(2,1)S(1)}, bf16[256,576]{1,0:T(8,128)(2,1)S(1)}, u32[]{:S(2)}, u32[]{:S(2)}) collective-permute-start(bf16[256,576]{1,0:T(8,128)(2,1)S(1)} %collective-permute-done.13.near2), channel_id=1, source_target_pairs={{0,8},{8,0},{16,24},{24,16},{1,9},{9,1},{17,25},{25,17},{2,10},{10... | collective-permute-start | bytes 884744 | tf_op jit(solution)/shard_map/ppermute | solution.py:32
  67.4 22.8 %collective-permute-start.26 = (bf16[256,1024]{1,0:T(8,128)(2,1)S(1)}, bf16[256,1024]{1,0:T(8,128)(2,1)S(1)}, u32[]{:S(2)}, u32[]{:S(2)}) collective-permute-start(bf16[256,1024]{1,0:T(8,128)(2,1)S(1)} %shard_map.258.cot_mine), channel_id=1, source_target_pairs={{0,4},{4,0},{1,5},{5,1},{2,6},{6,2},{3,7},{7,3},{8,12},{12,8},{9,1... | collective-permute-start | bytes 1572872 | tf_op jit(solution)/shard_map/ppermute | solution.py:32
  70.5 12.5 %collective-permute-start.17 = (bf16[256,576]{1,0:T(8,128)(2,1)S(1)}, bf16[256,576]{1,0:T(8,128)(2,1)S(1)}, u32[]{:S(2)}, u32[]{:S(2)}) collective-permute-start(bf16[256,576]{1,0:T(8,128)(2,1)S(1)} %collective-permute-done.14.near3), channel_id=1, source_target_pairs={{0,8},{8,0},{16,24},{24,16},{1,9},{9,1},{17,25},{25,17},{2,10},{10... | collective-permute-start | bytes 884744 | tf_op jit(solution)/shard_map/ppermute | solution.py:32
  78.8 11.3 %collective-permute-start.19 = (bf16[576,256]{1,0:T(8,128)(2,1)S(1)}, bf16[576,256]{1,0:T(8,128)(2,1)S(1)}, u32[]{:S(2)}, u32[]{:S(2)}) collective-permute-start(bf16[576,256]{1,0:T(8,128)(2,1)S(1)} %get-tuple-element.116), channel_id=1, source_target_pairs={{0,2},{1,3},{2,0},{3,1},{4,6},{5,7},{6,4},{7,5},{8,10},{9,11},{10,... | collective-permute-start | bytes 884744 | tf_op jit(solution)/shard_map/ppermute | solution.py:32
  110.2 17.7 %collective-permute-start.54 = (bf16[2,4,64,576]{3,2,1,0:T(8,128)(2,1)S(1)}, bf16[2,4,64,576]{3,2,1,0:T(8,128)(2,1)S(1)}, u32[]{:S(2)}, u32[]{:S(2)}) collective-permute-start(bf16[2,4,64,576]{3,2,1,0:T(8,128)(2,1)S(1)} %get-tuple-element.175), channel_id=1, source_target_pairs={{0,8},{8,0},{16,24},{24,16},{1,9},{9,1},{17,25},{25,17},{2,10},{10... | collective-permute-start | bytes 1769480 | tf_op jit(solution)/shard_map/ppermute | solution.py:32
  112.8 13.0 %collective-permute-start.21 = (bf16[256,1024]{1,0:T(8,128)(2,1)S(1)}, bf16[256,1024]{1,0:T(8,128)(2,1)S(1)}, u32[]{:S(2)}, u32[]{:S(2)}) collective-permute-start(bf16[256,1024]{1,0:T(8,128)(2,1)S(1)} %get-tuple-element.119), channel_id=1, source_target_pairs={{0,4},{4,0},{1,5},{5,1},{2,6},{6,2},{3,7},{7,3},{8,12},{12,8},{9,1... | collective-permute-start | bytes 1572872 | tf_op jit(solution)/shard_map/ppermute | solution.py:32
  112.9 29.0 %collective-permute-start.49 = (bf16[2,4,64,576]{3,2,1,0:T(8,128)(2,1)S(1)}, bf16[2,4,64,576]{3,2,1,0:T(8,128)(2,1)S(1)}, u32[]{:S(2)}, u32[]{:S(2)}) collective-permute-start(bf16[2,4,64,576]{3,2,1,0:T(8,128)(2,1)S(1)} %get-tuple-element.168), channel_id=1, source_target_pairs={{0,8},{8,0},{16,24},{24,16},{1,9},{9,1},{17,25},{25,17},{2,10},{10... | collective-permute-start | bytes 1769480 | tf_op jit(solution)/shard_map/ppermute | solution.py:32
  124.1 29.8 %collective-permute-start.47 = (bf16[2,4,64,576]{3,2,1,0:T(8,128)(2,1)S(1)}, bf16[2,4,64,576]{3,2,1,0:T(8,128)(2,1)S(1)}, u32[]{:S(2)}, u32[]{:S(2)}) collective-permute-start(bf16[2,4,64,576]{3,2,1,0:T(8,128)(2,1)S(1)} %get-tuple-element.164), channel_id=1, source_target_pairs={{0,8},{8,0},{16,24},{24,16},{1,9},{9,1},{17,25},{25,17},{2,10},{10... | collective-permute-start | bytes 1769480 | tf_op jit(solution)/shard_map/ppermute | solution.py:32
  125.9 30.5 %collective-permute-start.22 = (bf16[256,256]{1,0:T(8,128)(2,1)S(1)}, bf16[256,256]{1,0:T(8,128)(2,1)S(1)}, u32[]{:S(2)}, u32[]{:S(2)}) collective-permute-start(bf16[256,256]{1,0:T(8,128)(2,1)S(1)} %get-tuple-element.121), channel_id=1, source_target_pairs={{0,1},{1,0},{2,3},{3,2},{4,5},{5,4},{6,7},{7,6},{8,9},{9,8},{10,11... | collective-permute-start | bytes 393224 | tf_op jit(solution)/shard_map/ppermute | solution.py:32
  127.9 30.3 %collective-permute-start.23 = (bf16[256,256]{1,0:T(8,128)(2,1)S(1)}, bf16[256,256]{1,0:T(8,128)(2,1)S(1)}, u32[]{:S(2)}, u32[]{:S(2)}) collective-permute-start(bf16[256,256]{1,0:T(8,128)(2,1)S(1)} %get-tuple-element.122), channel_id=1, source_target_pairs={{0,2},{1,3},{2,0},{3,1},{4,6},{5,7},{6,4},{7,5},{8,10},{9,11},{10,... | collective-permute-start | bytes 393224 | tf_op jit(solution)/shard_map/ppermute | solution.py:32
  128.8 29.8 %collective-permute-start.24 = (bf16[256,256]{1,0:T(8,128)(2,1)S(1)}, bf16[256,256]{1,0:T(8,128)(2,1)S(1)}, u32[]{:S(2)}, u32[]{:S(2)}) collective-permute-start(bf16[256,256]{1,0:T(8,128)(2,1)S(1)} %get-tuple-element.123), channel_id=1, source_target_pairs={{0,3},{1,2},{2,1},{3,0},{4,7},{5,6},{6,5},{7,4},{8,11},{9,10},{10,... | collective-permute-start | bytes 393224 | tf_op jit(solution)/shard_map/ppermute | solution.py:32
  141.9 29.4 %collective-permute-start.35 = (bf16[256,1024]{1,0:T(8,128)(2,1)S(1)}, bf16[256,1024]{1,0:T(8,128)(2,1)S(1)}, u32[]{:S(2)}, u32[]{:S(2)}) collective-permute-start(bf16[256,1024]{1,0:T(8,128)(2,1)S(1)} %get-tuple-element.142), channel_id=1, source_target_pairs={{0,4},{4,0},{1,5},{5,1},{2,6},{6,2},{3,7},{7,3},{8,12},{12,8},{9,1... | collective-permute-start | bytes 1572872 | tf_op jit(solution)/shard_map/ppermute | solution.py:32
  153.9 17.3 %collective-permute-start.55 = (bf16[4,64,576]{2,1,0:T(8,128)(2,1)S(1)}, bf16[4,64,576]{2,1,0:T(8,128)(2,1)S(1)}, u32[]{:S(2)}, u32[]{:S(2)}) collective-permute-start(bf16[4,64,576]{2,1,0:T(8,128)(2,1)S(1)} %fusion.2), channel_id=1, source_target_pairs={{0,16},{8,24},{16,0},{24,8},{1,17},{9,25},{17,1},{25,9},{2,18},{10... | collective-permute-start | bytes 884744 | tf_op jit(solution)/shard_map/ppermute | solution.py:32
  156.5 19.0 %collective-permute-start.41 = (bf16[2,4,72,384]{3,2,1,0:T(8,128)(2,1)S(1)}, bf16[2,4,72,384]{3,2,1,0:T(8,128)(2,1)S(1)}, u32[]{:S(2)}, u32[]{:S(2)}) collective-permute-start(bf16[2,4,72,384]{3,2,1,0:T(8,128)(2,1)S(1)} %get-tuple-element.149), channel_id=1, source_target_pairs={{0,8},{8,0},{16,24},{24,16},{1,9},{9,1},{17,25},{25,17},{2,10},{10... | collective-permute-start | bytes 1327112 | tf_op jit(solution)/shard_map/ppermute | solution.py:32
  158.2 49.0 %collective-permute-start.50 = (bf16[4,64,576]{2,1,0:T(8,128)(2,1)S(1)}, bf16[4,64,576]{2,1,0:T(8,128)(2,1)S(1)}, u32[]{:S(2)}, u32[]{:S(2)}) collective-permute-start(bf16[4,64,576]{2,1,0:T(8,128)(2,1)S(1)} %fusion.1), channel_id=1, source_target_pairs={{0,16},{8,24},{16,0},{24,8},{1,17},{9,25},{17,1},{25,9},{2,18},{10... | collective-permute-start | bytes 884744 | tf_op jit(solution)/shard_map/ppermute | solution.py:32
  158.6 12.7 %collective-permute-start.36 = (f32[8,256]{1,0:T(8,128)S(1)}, f32[8,256]{1,0:T(8,128)S(1)}, u32[]{:S(2)}, u32[]{:S(2)}) collective-permute-start(f32[8,256]{1,0:T(8,128)S(1)} %slice.126), channel_id=1, source_target_pairs={{0,4},{4,0},{1,5},{5,1},{2,6},{6,2},{3,7},{7,3},{8,12},{12,8},{9,1... | collective-permute-start | bytes 24584 | tf_op jit(solution)/shard_map/ppermute | solution.py:32
  171.2 11.1 %collective-permute-start.25 = (bf16[256,256]{1,0:T(8,128)(2,1)S(1)}, bf16[256,256]{1,0:T(8,128)(2,1)S(1)}, u32[]{:S(2)}, u32[]{:S(2)}) collective-permute-start(bf16[256,256]{1,0:T(8,128)(2,1)S(1)} %add_convert_fusion.4), channel_id=1, source_target_pairs={{0,4},{4,0},{1,5},{5,1},{2,6},{6,2},{3,7},{7,3},{8,12},{12,8},{9,1... | collective-permute-start | bytes 393224 | tf_op jit(solution)/shard_map/ppermute | solution.py:32
  178.1 29.9 %collective-permute-start.48 = (bf16[4,64,576]{2,1,0:T(8,128)(2,1)S(1)}, bf16[4,64,576]{2,1,0:T(8,128)(2,1)S(1)}, u32[]{:S(2)}, u32[]{:S(2)}) collective-permute-start(bf16[4,64,576]{2,1,0:T(8,128)(2,1)S(1)} %fusion), channel_id=1, source_target_pairs={{0,16},{8,24},{16,0},{24,8},{1,17},{9,25},{17,1},{25,9},{2,18},{10... | collective-permute-start | bytes 884744 | tf_op jit(solution)/shard_map/ppermute | solution.py:32
  179.7 29.1 %collective-permute-start.56 = (bf16[64,576]{1,0:T(8,128)(2,1)S(1)}, bf16[64,576]{1,0:T(8,128)(2,1)S(1)}, u32[]{:S(2)}, u32[]{:S(2)}) collective-permute-start(bf16[64,576]{1,0:T(8,128)(2,1)S(1)} %get-tuple-element.177), channel_id=1, source_target_pairs={{0,1},{1,0},{2,3},{3,2},{4,5},{5,4},{6,7},{7,6},{8,9},{9,8},{10,11... | collective-permute-start | bytes 221192 | tf_op jit(solution)/shard_map/ppermute | solution.py:32
  182.2 28.6 %collective-permute-start.57 = (bf16[64,576]{1,0:T(8,128)(2,1)S(1)}, bf16[64,576]{1,0:T(8,128)(2,1)S(1)}, u32[]{:S(2)}, u32[]{:S(2)}) collective-permute-start(bf16[64,576]{1,0:T(8,128)(2,1)S(1)} %get-tuple-element.178), channel_id=1, source_target_pairs={{0,2},{1,3},{2,0},{3,1},{4,6},{5,7},{6,4},{7,5},{8,10},{9,11},{10,... | collective-permute-start | bytes 221192 | tf_op jit(solution)/shard_map/ppermute | solution.py:32
  182.2 24.8 %collective-permute-start.42 = (bf16[4,72,384]{2,1,0:T(8,128)(2,1)S(1)}, bf16[4,72,384]{2,1,0:T(8,128)(2,1)S(1)}, u32[]{:S(2)}, u32[]{:S(2)}) collective-permute-start(bf16[4,72,384]{2,1,0:T(8,128)(2,1)S(1)} %fusion.7), channel_id=1, source_target_pairs={{0,16},{8,24},{16,0},{24,8},{1,17},{9,25},{17,1},{25,9},{2,18},{10... | collective-permute-start | bytes 663560 | tf_op jit(solution)/shard_map/ppermute | solution.py:32
  207.1 18.7 %collective-permute-start.40 = (f32[256,256]{1,0:T(8,128)S(1)}, f32[256,256]{1,0:T(8,128)S(1)}, u32[]{:S(2)}, u32[]{:S(2)}) collective-permute-start(f32[256,256]{1,0:T(8,128)S(1)} %fusion.6), channel_id=1, source_target_pairs={{0,4},{4,0},{1,5},{5,1},{2,6},{6,2},{3,7},{7,3},{8,12},{12,8},{9,1... | collective-permute-start | bytes 786440 | tf_op jit(solution)/shard_map/ppermute | solution.py:32
  (48 other events, 631.1 us)

commit v7 on v6

--- a/solution.py
+++ b/solution.py
@@ -47,16 +47,19 @@
     return result
 
 
-def kernel_call(kernel, outs, *args, scalars=None, scratch=(), fetch=0, room=8):
+def kernel_call(kernel, outs, *args, placed=False, scratch=(), fetch=0, room=8):
     specs = [pl.BlockSpec(memory_space=pltpu.HBM)] * fetch
     specs = specs + [pl.BlockSpec(memory_space=pltpu.VMEM)] * (len(args) - fetch)
     scratch_shapes = [pltpu.VMEM(shape, dtype) for shape, dtype in scratch]
     if fetch:
         scratch_shapes = [pltpu.VMEM(v.shape, v.dtype) for v in args[:fetch]] + scratch_shapes
         scratch_shapes.append(pltpu.SemaphoreType.DMA((fetch,)))
-    if scalars is not None:
-        args = (scalars,) + args
-        specs = [pl.BlockSpec(memory_space=pltpu.SMEM)] + specs
+    if placed:
+        plain = kernel
+
+        def kernel(*refs):
+            plain(tuple(lax.axis_index(axis) for axis in ("row", "col", "dp")), *refs)
+
     return pl.pallas_call(
         kernel,
         out_shape=[jax.ShapeDtypeStruct(shape, dtype) for shape, dtype in outs],
@@ -614,7 +617,6 @@
     width = part * cols
     half = tokens // 2
     row = lax.axis_index("row")
-    col = lax.axis_index("col")
     plane = lax.axis_index("dp")
 
     def mine_first(values):
@@ -625,7 +627,6 @@
 
     q_size = query_weight.shape[1] // cols
     units = gate_weight.shape[1] // cols
-    where = jnp.stack([row, col, plane]).astype(jnp.int32)
     shapes = [((half + 16 + part, part), BF16)] * cols
     first_in = exchange(
         kernel_call(
@@ -637,7 +638,7 @@
             value_weight,
             attention_gain.reshape(1, part),
             feedforward_gain.reshape(1, part),
-            scalars=where,
+            placed=True,
             fetch=4, room=60),
     )
     (input_mine,) = kernel_call(join_first_kernel, [((half, width), BF16)], *first_in, room=10)
@@ -649,7 +650,7 @@
         [((part, units), BF16)] * (cols + 1),
         gate_weight,
         up_weight,
-        scalars=where,
+        placed=True,
         fetch=2, room=12)
     near_parts = exchange(gate_in[:cols])
     far_parts = [gate_in[cols]] + [flip(v, "dp", 1) for v in near_parts[1:]]
@@ -659,7 +660,7 @@
         [((half + inner_size, part), BF16)] * cols,
         output_weight,
         cotangent,
-        scalars=where,
+        placed=True,
         fetch=2,
     )
     second_parts = exchange(two_out)
@@ -667,7 +668,7 @@
         pack_three_kernel,
         [((units, part), BF16)] * cols,
         down_weight,
-        scalars=where,
+        placed=True,
         fetch=1,
     )
     down_parts = exchange(three_out)
@@ -722,7 +723,7 @@
         second_in,
         second_far,
         *first_in,
-        scalars=where,
+        placed=True,
         scratch=[((half, width), F32)], room=24)
     gate_pre, up_pre, hidden = kernel_call(
         hidden_kernel,
@@ -730,7 +731,7 @@
         normed_two,
         *near_parts,
         *far_parts,
-        scalars=where, room=24)
+        placed=True, room=24)
     rows = part // planes
     if planes == 4:
         down_dealt = kernel_call(
@@ -739,7 +740,7 @@
             cot_mine,
             cot_other,
             hidden,
-            scalars=where,
+            placed=True,
             scratch=[((part, units), BF16)], room=14)
     gate_grad, up_grad, two_mine, two_other = kernel_call(
         backward_kernel,
@@ -751,7 +752,7 @@
         *down_parts,
         *near_parts,
         *far_parts,
-        scalars=where, room=30)
+        placed=True, room=30)
 
     two_came = flip(two_other, "row", 1)
     two_pieces = kernel_call(
@@ -759,7 +760,7 @@
         [((share, width), BF16)] * cols,
         two_mine,
         two_came,
-        scalars=where,
+        placed=True,
         scratch=[((half, width), BF16)],
     )
     two_in = exchange(two_pieces)
@@ -770,11 +771,11 @@
         first_share,
         cot_mine,
         *first_in,
-        scalars=where,
+        placed=True,
     )
     first_back = exchange(first_pieces)
     (first_half,) = kernel_call(
-        join_tokens_kernel, [((half, width), BF16)], *first_back, scalars=where
+        join_tokens_kernel, [((half, width), BF16)], *first_back, placed=True
     )
     first_other = flip(first_half, "row", 1)
 
@@ -793,7 +794,7 @@
             normed_two,
             gate_grad,
             up_grad,
-            scalars=where,
+            placed=True,
             scratch=[((part, units), BF16)], room=20)
         dealt = list(down_dealt) + list(dealt)
         down_terms, gate_terms, up_terms = [
@@ -829,14 +830,12 @@
         unpack_feed_kernel,
         [((rows, cols * units), F32)] * 2,
         *feed_in,
-        scalars=where,
+        placed=True,
         room=12,
     )
 
     up_in = exchange(up_out)
-    (up_share,) = kernel_call(
-        unpack_up_kernel, [((rows, cols * units), F32)], *up_in, scalars=where
-    )
+    (up_share,) = kernel_call(unpack_up_kernel, [((rows, cols * units), F32)], *up_in, placed=True)
 
     result_mine, result_other = kernel_call(
         result_kernel, [((half, width), BF16)] * 2, hidden, *down_parts, room=12)
@@ -866,7 +865,7 @@
         first_other,
         second_in,
         feedforward_part,
-        scalars=where,
+        placed=True,
         scratch=[((part, mixed_size), BF16)], room=34)
     one_came = flip(one_other, "row", 1)
     inner_came = flip(inner_part[:, half:], "row", 1)
@@ -909,7 +908,7 @@
             ((8, mixed_size), F32),
         ],
         *last_in,
-        scalars=where,
+        placed=True,
     )
     gain_came = flip(gain_sums, "row", 1)
     if planes == 4:
@@ -920,7 +919,7 @@
                 [((1, rows), F32), ((1, rows), F32), ((1, head), F32), ((1, head), F32)],
                 gain_sums,
                 gain_came,
-                scalars=where,
+                placed=True,
             )
         ]
     else:

time: 227 us -> 223 us (0.982)
  Pallas kernels: 40.5 us -> 32.1 us
  waiting for transfers between devices: 120 us -> 126 us
    pallas_call x28, Pallas kernels: 40.5 us -> 32.1 us  [kernel_call(): pl.pallas_call(kernel, out_shape=[jax.ShapeDtypeStruct(shape, dtype) for...]
    ppermute x59, waiting for transfers between devices: 120 us -> 126 us  [flip(): return lax.ppermute(values, axis, [(i, i ^ distance) for i in range(size)])]
  transfers between devices with their start and end apart: 59 -> 59, of which waited for: 25 -> 30; matrix products, arithmetic and copies ran while one was open for 2% -> 2% of each run, Pallas kernels for 14% -> 11%
where the time goes in v7:
time: 223 us
  waiting for transfers between devices  126 us (57%)
  starting transfers between devices  57 us (26%)
  Pallas kernels  32.1 us (14%)
  other arithmetic  4.12 us (2%)
  local copies, waits for them, and re-layouts  2.33 us (1%)
    ppermute x59, waiting for transfers between devices, flip(): return lax.ppermute(values, axis, [(i, i ^ distance) for i in range(size)])  126 us
    ppermute x59, starting transfers between devices, flip(): return lax.ppermute(values, axis, [(i, i ^ distance) for i in range(size)])  57 us
    pallas_call x28, Pallas kernels, kernel_call(): pl.pallas_call(kernel, out_shape=[jax.ShapeDtypeStruct(shape, dtype) for...  32.1 us
  transfers between devices with their start and end apart: 59, of which 30 were waited for; matrix products, arithmetic and copies ran while one was open for 2% of the time, Pallas kernels for 11%

profile of v7, /device:TPU:0, one launch (start us, length us, event | category | flops | bytes accessed | tf_op | source)
XLA Modules:
  0.0 223.0 jit_solution(2801457471126324736)
XLA Ops:
  0.7 3.3 %shard_map.246 = (bf16[528,256]{1,0:T(8,128)(2,1)}, bf16[528,256]{1,0:T(8,128)(2,1)}, bf16[528,256]{1,0:T(8,128)(2,1)}, bf16[528,256]{1,0:T(8,128)(2,1)}) custom-call(bf16[512,256]{1,0:T(8,128)(2,1)} %refs_0_.4, bf16[256,512]{1,0:T(8,128)(2,1)} %refs_1_.3, bf16[256,256]{1,0:T(8,128)(2,1)} %refs_2_.1, bf16[256,256]{1,0:T(8,128)(2,1)} %refs_3_.1, ...), custom_call_target="tpu_custom_call" | custom-call | tf_op jit(solution)/shard_map/pallas_call | solution.py:63
  4.0 3.0 %collective-permute-start = (bf16[528,256]{1,0:T(8,128)(2,1)}, bf16[528,256]{1,0:T(8,128)(2,1)S(1)}, u32[]{:S(2)}, u32[]{:S(2)}) collective-permute-start(bf16[528,256]{1,0:T(8,128)(2,1)} %get-tuple-element.98), channel_id=1, source_target_pairs={{0,1},{1,0},{2,3},{3,2},{4,5},{5,4},{6,7},{7,6},{8,9},{9,8},{10,11... | collective-permute-start | bytes 811016 | tf_op jit(solution)/shard_map/ppermute | solution.py:32
  11.3 3.0 %collective-permute-start.10 = (bf16[768,256]{1,0:T(8,128)(2,1)}, bf16[768,256]{1,0:T(8,128)(2,1)S(1)}, u32[]{:S(2)}, u32[]{:S(2)}) collective-permute-start(bf16[768,256]{1,0:T(8,128)(2,1)} %get-tuple-element.105), channel_id=1, source_target_pairs={{0,3},{1,2},{2,1},{3,0},{4,7},{5,6},{6,5},{7,4},{8,11},{9,10},{10,... | collective-permute-start | bytes 1179656 | tf_op jit(solution)/shard_map/ppermute | solution.py:32
  17.6 12.3 %collective-permute-done.1.first2.refs_8_.refs_4_ = bf16[528,256]{1,0:T(8,128)(2,1)S(1)} collective-permute-done((bf16[528,256]{1,0:T(8,128)(2,1)}, bf16[528,256]{1,0:T(8,128)(2,1)S(1)}, u32[]{:S(2)}, u32[]{:S(2)}) %collective-permute-start.1) | collective-permute-done | bytes 270368 | tf_op jit(solution)/shard_map/ppermute | solution.py:32
  30.3 6.1 %collective-permute-done.8.first1 = bf16[768,256]{1,0:T(8,128)(2,1)S(1)} collective-permute-done((bf16[768,256]{1,0:T(8,128)(2,1)S(1)}, bf16[768,256]{1,0:T(8,128)(2,1)S(1)}, u32[]{:S(2)}, u32[]{:S(2)}) %collective-permute-start.8) | collective-permute-done | bytes 393248 | tf_op jit(solution)/shard_map/ppermute | solution.py:32
  38.6 4.4 %shard_map.248 = (f32[512,256]{1,0:T(8,128)S(1)}, bf16[512,256]{1,0:T(8,128)(2,1)S(1)}, bf16[512,128]{1,0:T(8,128)(2,1)S(1)}, f32[512,128]{1,0:T(8,128)S(1)}) custom-call(bf16[256,1024]{1,0:T(8,128)(2,1)S(1)} %shard_map.247.mine.refs_0_, bf16[256,1024]{1,0:T(8,128)(2,1)S(1)} %collective-permute-done.3.other.refs_1_, bf16[528,256]{1,0:T(8,128)(2,1)S(1)} %copy-done, ...), custom_call_target="tpu_custom_call" | custom-call | tf_op jit(solution)/shard_map/pallas_call | solution.py:63
  51.0 2.2 %collective-permute-done.6.first3 = bf16[512,128]{1,0:T(8,128)(2,1)S(1)} collective-permute-done((bf16[512,128]{1,0:T(8,128)(2,1)S(1)}, bf16[512,128]{1,0:T(8,128)(2,1)S(1)}, u32[]{:S(2)}, u32[]{:S(2)}) %collective-permute-start.6) | collective-permute-done | bytes 131104 | tf_op jit(solution)/shard_map/ppermute | solution.py:32
  53.4 1.8 collective-permute-start.14
  55.2 4.1 %collective-permute-done.12.refs_2_.refs_9_ = bf16[256,576]{1,0:T(8,128)(2,1)S(1)} collective-permute-done((bf16[256,576]{1,0:T(8,128)(2,1)S(1)}, bf16[256,576]{1,0:T(8,128)(2,1)S(1)}, u32[]{:S(2)}, u32[]{:S(2)}) %collective-permute-start.12) | collective-permute-done | bytes 294944 | tf_op jit(solution)/shard_map/ppermute | solution.py:32
  61.9 4.9 %collective-permute-done.14.refs_4_.refs_11_ = bf16[256,576]{1,0:T(8,128)(2,1)S(1)} collective-permute-done((bf16[256,576]{1,0:T(8,128)(2,1)S(1)}, bf16[256,576]{1,0:T(8,128)(2,1)S(1)}, u32[]{:S(2)}, u32[]{:S(2)}) %collective-permute-start.14) | collective-permute-done | bytes 294944 | tf_op jit(solution)/shard_map/ppermute | solution.py:32
  67.3 2.6 %collective-permute-done.15.refs_6_.refs_13_ = bf16[256,576]{1,0:T(8,128)(2,1)S(1)} collective-permute-done((bf16[256,576]{1,0:T(8,128)(2,1)S(1)}, bf16[256,576]{1,0:T(8,128)(2,1)S(1)}, u32[]{:S(2)}, u32[]{:S(2)}) %collective-permute-start.15) | collective-permute-done | bytes 294944 | tf_op jit(solution)/shard_map/ppermute | solution.py:32
  71.5 5.4 %collective-permute-done.16.refs_7_.refs_14_ = bf16[256,576]{1,0:T(8,128)(2,1)S(1)} collective-permute-done((bf16[256,576]{1,0:T(8,128)(2,1)S(1)}, bf16[256,576]{1,0:T(8,128)(2,1)S(1)}, u32[]{:S(2)}, u32[]{:S(2)}) %collective-permute-start.16) | collective-permute-done | bytes 294944 | tf_op jit(solution)/shard_map/ppermute | solution.py:32
  82.1 2.0 shard_map.254
  85.5 4.2 %collective-permute-done.19.down2.refs_6_ = bf16[576,256]{1,0:T(8,128)(2,1)S(1)} collective-permute-done((bf16[576,256]{1,0:T(8,128)(2,1)S(1)}, bf16[576,256]{1,0:T(8,128)(2,1)S(1)}, u32[]{:S(2)}, u32[]{:S(2)}) %collective-permute-start.19) | collective-permute-done | bytes 294944 | tf_op jit(solution)/shard_map/ppermute | solution.py:32
  89.7 3.2 %shard_map.259 = (bf16[512,576]{1,0:T(8,128)(2,1)S(1)}, bf16[512,576]{1,0:T(8,128)(2,1)S(1)}, bf16[256,1024]{1,0:T(8,128)(2,1)S(1)}, bf16[256,1024]{1,0:T(8,128)(2,1)S(1)}) custom-call(bf16[256,1024]{1,0:T(8,128)(2,1)S(1)} %shard_map.258.refs_0_.refs_5_, bf16[256,1024]{1,0:T(8,128)(2,1)S(1)} %collective-permute-done.26.refs_1_, ...), custom_call_target="tpu_custom_call" | custom-call | tf_op jit(solution)/shard_map/pallas_call | solution.py:63
  93.0 1.9 collective-permute-done.27.refs_1_
  98.8 2.9 %collective-permute-done.28.refs_1_ = bf16[64,1024]{1,0:T(8,128)(2,1)S(1)} collective-permute-done((bf16[64,1024]{1,0:T(8,128)(2,1)S(1)}, bf16[64,1024]{1,0:T(8,128)(2,1)S(1)}, u32[]{:S(2)}, u32[]{:S(2)}) %collective-permute-start.28) | collective-permute-done | bytes 131104 | tf_op jit(solution)/shard_map/ppermute | solution.py:32
  105.7 1.9 shard_map.269
  113.3 5.9 %collective-permute-done.32.refs_2_ = bf16[64,1024]{1,0:T(8,128)(2,1)S(1)} collective-permute-done((bf16[64,1024]{1,0:T(8,128)(2,1)S(1)}, bf16[64,1024]{1,0:T(8,128)(2,1)S(1)}, u32[]{:S(2)}, u32[]{:S(2)}) %collective-permute-start.32) | collective-permute-done | bytes 131104 | tf_op jit(solution)/shard_map/ppermute | solution.py:32
  123.2 2.1 collective-permute-done.54.came
  127.6 5.5 %shard_map.263 = (bf16[256,1024]{1,0:T(8,128)(2,1)S(1)}, bf16[256,1024]{1,0:T(8,128)(2,1)S(1)}, f32[8,512]{1,0:T(8,128)S(1)}, bf16[2,4,72,384]{3,2,1,0:T(8,128)(2,1)S(1)}, bf16[2,4,72,384]{3,2,1,0:T(8,128)(2,1)S(1)}) custom-call(bf16[256,1024]{1,0:T(8,128)(2,1)S(1)} %shard_map.247.mine.refs_0_, bf16[256,1024]{1,0:T(8,128)(2,1)S(1)} %collective-permute-done.3.other.refs_1_, ...), custom_call_target="tpu_custom_call" | custom-call | tf_op jit(solution)/shard_map/pallas_call | solution.py:63
  133.1 6.3 %collective-permute-done.49.came1 = bf16[2,4,64,576]{3,2,1,0:T(8,128)(2,1)S(1)} collective-permute-done((bf16[2,4,64,576]{3,2,1,0:T(8,128)(2,1)S(1)}, bf16[2,4,64,576]{3,2,1,0:T(8,128)(2,1)S(1)}, u32[]{:S(2)}, u32[]{:S(2)}) %collective-permute-start.49) | collective-permute-done | bytes 589856 | tf_op jit(solution)/shard_map/ppermute | solution.py:32
  139.4 11.9 %collective-permute-done.47.came0 = bf16[2,4,64,576]{3,2,1,0:T(8,128)(2,1)S(1)} collective-permute-done((bf16[2,4,64,576]{3,2,1,0:T(8,128)(2,1)S(1)}, bf16[2,4,64,576]{3,2,1,0:T(8,128)(2,1)S(1)}, u32[]{:S(2)}, u32[]{:S(2)}) %collective-permute-start.47) | collective-permute-done | bytes 589856 | tf_op jit(solution)/shard_map/ppermute | solution.py:32
  151.3 2.6 %collective-permute-start.55 = (bf16[4,64,576]{2,1,0:T(8,128)(2,1)S(1)}, bf16[4,64,576]{2,1,0:T(8,128)(2,1)S(1)}, u32[]{:S(2)}, u32[]{:S(2)}) collective-permute-start(bf16[4,64,576]{2,1,0:T(8,128)(2,1)S(1)} %fusion.2), channel_id=1, source_target_pairs={{0,16},{8,24},{16,0},{24,8},{1,17},{9,25},{17,1},{25,9},{2,18},{10... | collective-permute-start | bytes 884744 | tf_op jit(solution)/shard_map/ppermute | solution.py:32
  156.0 12.5 %collective-permute-done.55.far = bf16[4,64,576]{2,1,0:T(8,128)(2,1)S(1)} collective-permute-done((bf16[4,64,576]{2,1,0:T(8,128)(2,1)S(1)}, bf16[4,64,576]{2,1,0:T(8,128)(2,1)S(1)}, u32[]{:S(2)}, u32[]{:S(2)}) %collective-permute-start.55) | collective-permute-done | bytes 294944 | tf_op jit(solution)/shard_map/ppermute | solution.py:32
  170.8 2.2 collective-permute-done.41.came
  175.4 1.6 collective-permute-done.38
  178.2 1.7 collective-permute-done.39
  180.6 23.9 %collective-permute-done.42.far = bf16[4,72,384]{2,1,0:T(8,128)(2,1)S(1)} collective-permute-done((bf16[4,72,384]{2,1,0:T(8,128)(2,1)S(1)}, bf16[4,72,384]{2,1,0:T(8,128)(2,1)S(1)}, u32[]{:S(2)}, u32[]{:S(2)}) %collective-permute-start.42) | collective-permute-done | bytes 221216 | tf_op jit(solution)/shard_map/ppermute | solution.py:32
  206.3 1.8 collective-permute-start.45
  212.0 1.8 collective-permute-start.53
  217.5 2.9 %collective-permute-done.53.refs_3_ = bf16[128,576]{1,0:T(8,128)(2,1)S(1)} collective-permute-done((bf16[128,576]{1,0:T(8,128)(2,1)S(1)}, bf16[128,576]{1,0:T(8,128)(2,1)S(1)}, u32[]{:S(2)}, u32[]{:S(2)}) %collective-permute-start.53) | collective-permute-done | bytes 147488 | tf_op jit(solution)/shard_map/ppermute | solution.py:32
  (192 shorter events, 69.9 us)
Async XLA Ops:
  4.0 11.4 %collective-permute-start = (bf16[528,256]{1,0:T(8,128)(2,1)}, bf16[528,256]{1,0:T(8,128)(2,1)S(1)}, u32[]{:S(2)}, u32[]{:S(2)}) collective-permute-start(bf16[528,256]{1,0:T(8,128)(2,1)} %get-tuple-element.98), channel_id=1, source_target_pairs={{0,1},{1,0},{2,3},{3,2},{4,5},{5,4},{6,7},{7,6},{8,9},{9,8},{10,11... | collective-permute-start | bytes 811016 | tf_op jit(solution)/shard_map/ppermute | solution.py:32
  7.0 22.9 %collective-permute-start.1 = (bf16[528,256]{1,0:T(8,128)(2,1)}, bf16[528,256]{1,0:T(8,128)(2,1)S(1)}, u32[]{:S(2)}, u32[]{:S(2)}) collective-permute-start(bf16[528,256]{1,0:T(8,128)(2,1)} %get-tuple-element.99), channel_id=1, source_target_pairs={{0,2},{1,3},{2,0},{3,1},{4,6},{5,7},{6,4},{7,5},{8,10},{9,11},{10,... | collective-permute-start | bytes 811016 | tf_op jit(solution)/shard_map/ppermute | solution.py:32
  8.5 21.4 %collective-permute-start.2 = (bf16[528,256]{1,0:T(8,128)(2,1)}, bf16[528,256]{1,0:T(8,128)(2,1)S(1)}, u32[]{:S(2)}, u32[]{:S(2)}) collective-permute-start(bf16[528,256]{1,0:T(8,128)(2,1)} %get-tuple-element.100), channel_id=1, source_target_pairs={{0,3},{1,2},{2,1},{3,0},{4,7},{5,6},{6,5},{7,4},{8,11},{9,10},{10,... | collective-permute-start | bytes 811016 | tf_op jit(solution)/shard_map/ppermute | solution.py:32
  11.3 18.9 %collective-permute-start.10 = (bf16[768,256]{1,0:T(8,128)(2,1)}, bf16[768,256]{1,0:T(8,128)(2,1)S(1)}, u32[]{:S(2)}, u32[]{:S(2)}) collective-permute-start(bf16[768,256]{1,0:T(8,128)(2,1)} %get-tuple-element.105), channel_id=1, source_target_pairs={{0,3},{1,2},{2,1},{3,0},{4,7},{5,6},{6,5},{7,4},{8,11},{9,10},{10,... | collective-permute-start | bytes 1179656 | tf_op jit(solution)/shard_map/ppermute | solution.py:32
  14.3 22.1 %collective-permute-start.8 = (bf16[768,256]{1,0:T(8,128)(2,1)S(1)}, bf16[768,256]{1,0:T(8,128)(2,1)S(1)}, u32[]{:S(2)}, u32[]{:S(2)}) collective-permute-start(bf16[768,256]{1,0:T(8,128)(2,1)S(1)} %get-tuple-element.103), channel_id=1, source_target_pairs={{0,1},{1,0},{2,3},{3,2},{4,5},{5,4},{6,7},{7,6},{8,9},{9,8},{10,11... | collective-permute-start | bytes 1179656 | tf_op jit(solution)/shard_map/ppermute | solution.py:32
  15.3 22.5 %collective-permute-start.9 = (bf16[768,256]{1,0:T(8,128)(2,1)S(1)}, bf16[768,256]{1,0:T(8,128)(2,1)S(1)}, u32[]{:S(2)}, u32[]{:S(2)}) collective-permute-start(bf16[768,256]{1,0:T(8,128)(2,1)S(1)} %get-tuple-element.104), channel_id=1, source_target_pairs={{0,2},{1,3},{2,0},{3,1},{4,6},{5,7},{6,4},{7,5},{8,10},{9,11},{10,... | collective-permute-start | bytes 1179656 | tf_op jit(solution)/shard_map/ppermute | solution.py:32
  37.9 40.2 %collective-permute-start.11 = (bf16[512,1024]{1,0:T(8,128)(2,1)S(1)}, bf16[512,1024]{1,0:T(8,128)(2,1)S(1)}, u32[]{:S(2)}, u32[]{:S(2)}) collective-permute-start(bf16[512,1024]{1,0:T(8,128)(2,1)S(1)} %shard_map.251.refs_4_.refs_17_), channel_id=1, source_target_pairs={{0,4},{4,0},{1,5},{5,1},{2,6},{6,2},{3,7},{7,3},{8,12},{12,8},{9,1... | collective-permute-start | bytes 3145736 | tf_op jit(solution)/shard_map/ppermute | solution.py:32
  49.5 11.4 %collective-permute-start.13 = (bf16[256,576]{1,0:T(8,128)(2,1)S(1)}, bf16[256,576]{1,0:T(8,128)(2,1)S(1)}, u32[]{:S(2)}, u32[]{:S(2)}) collective-permute-start(bf16[256,576]{1,0:T(8,128)(2,1)S(1)} %get-tuple-element.110), channel_id=1, source_target_pairs={{0,2},{1,3},{2,0},{3,1},{4,6},{5,7},{6,4},{7,5},{8,10},{9,11},{10,... | collective-permute-start | bytes 884744 | tf_op jit(solution)/shard_map/ppermute | solution.py:32
  53.3 26.2 %collective-permute-start.7 = (bf16[512,512]{1,0:T(8,128)(2,1)S(1)}, bf16[512,512]{1,0:T(8,128)(2,1)S(1)}, u32[]{:S(2)}, u32[]{:S(2)}) collective-permute-start(bf16[512,512]{1,0:T(8,128)(2,1)S(1)} %shard_map.249.refs_2_), channel_id=1, source_target_pairs={{0,4},{4,0},{1,5},{5,1},{2,6},{6,2},{3,7},{7,3},{8,12},{12,8},{9,1... | collective-permute-start | bytes 1572872 | tf_op jit(solution)/shard_map/ppermute | solution.py:32
  53.4 13.4 %collective-permute-start.14 = (bf16[256,576]{1,0:T(8,128)(2,1)S(1)}, bf16[256,576]{1,0:T(8,128)(2,1)S(1)}, u32[]{:S(2)}, u32[]{:S(2)}) collective-permute-start(bf16[256,576]{1,0:T(8,128)(2,1)S(1)} %get-tuple-element.111), channel_id=1, source_target_pairs={{0,3},{1,2},{2,1},{3,0},{4,7},{5,6},{6,5},{7,4},{8,11},{9,10},{10,... | collective-permute-start | bytes 884744 | tf_op jit(solution)/shard_map/ppermute | solution.py:32
  60.9 16.0 %collective-permute-start.16 = (bf16[256,576]{1,0:T(8,128)(2,1)S(1)}, bf16[256,576]{1,0:T(8,128)(2,1)S(1)}, u32[]{:S(2)}, u32[]{:S(2)}) collective-permute-start(bf16[256,576]{1,0:T(8,128)(2,1)S(1)} %collective-permute-done.13.refs_3_.refs_10_), channel_id=1, source_target_pairs={{0,8},{8,0},{16,24},{24,16},{1,9},{9,1},{17,25},{25,17},{2,10},{10... | collective-permute-start | bytes 884744 | tf_op jit(solution)/shard_map/ppermute | solution.py:32
  66.8 23.0 %collective-permute-start.26 = (bf16[256,1024]{1,0:T(8,128)(2,1)S(1)}, bf16[256,1024]{1,0:T(8,128)(2,1)S(1)}, u32[]{:S(2)}, u32[]{:S(2)}) collective-permute-start(bf16[256,1024]{1,0:T(8,128)(2,1)S(1)} %shard_map.258.refs_0_.refs_5_), channel_id=1, source_target_pairs={{0,4},{4,0},{1,5},{5,1},{2,6},{6,2},{3,7},{7,3},{8,12},{12,8},{9,1... | collective-permute-start | bytes 1572872 | tf_op jit(solution)/shard_map/ppermute | solution.py:32
  69.9 12.2 %collective-permute-start.17 = (bf16[256,576]{1,0:T(8,128)(2,1)S(1)}, bf16[256,576]{1,0:T(8,128)(2,1)S(1)}, u32[]{:S(2)}, u32[]{:S(2)}) collective-permute-start(bf16[256,576]{1,0:T(8,128)(2,1)S(1)} %collective-permute-done.14.refs_4_.refs_11_), channel_id=1, source_target_pairs={{0,8},{8,0},{16,24},{24,16},{1,9},{9,1},{17,25},{25,17},{2,10},{10... | collective-permute-start | bytes 884744 | tf_op jit(solution)/shard_map/ppermute | solution.py:32
  78.2 11.6 %collective-permute-start.19 = (bf16[576,256]{1,0:T(8,128)(2,1)S(1)}, bf16[576,256]{1,0:T(8,128)(2,1)S(1)}, u32[]{:S(2)}, u32[]{:S(2)}) collective-permute-start(bf16[576,256]{1,0:T(8,128)(2,1)S(1)} %get-tuple-element.116), channel_id=1, source_target_pairs={{0,2},{1,3},{2,0},{3,1},{4,6},{5,7},{6,4},{7,5},{8,10},{9,11},{10,... | collective-permute-start | bytes 884744 | tf_op jit(solution)/shard_map/ppermute | solution.py:32
  107.6 17.7 %collective-permute-start.54 = (bf16[2,4,64,576]{3,2,1,0:T(8,128)(2,1)S(1)}, bf16[2,4,64,576]{3,2,1,0:T(8,128)(2,1)S(1)}, u32[]{:S(2)}, u32[]{:S(2)}) collective-permute-start(bf16[2,4,64,576]{3,2,1,0:T(8,128)(2,1)S(1)} %get-tuple-element.175), channel_id=1, source_target_pairs={{0,8},{8,0},{16,24},{24,16},{1,9},{9,1},{17,25},{25,17},{2,10},{10... | collective-permute-start | bytes 1769480 | tf_op jit(solution)/shard_map/ppermute | solution.py:32
  110.2 12.0 %collective-permute-start.21 = (bf16[256,1024]{1,0:T(8,128)(2,1)S(1)}, bf16[256,1024]{1,0:T(8,128)(2,1)S(1)}, u32[]{:S(2)}, u32[]{:S(2)}) collective-permute-start(bf16[256,1024]{1,0:T(8,128)(2,1)S(1)} %get-tuple-element.119), channel_id=1, source_target_pairs={{0,4},{4,0},{1,5},{5,1},{2,6},{6,2},{3,7},{7,3},{8,12},{12,8},{9,1... | collective-permute-start | bytes 1572872 | tf_op jit(solution)/shard_map/ppermute | solution.py:32
  110.3 29.0 %collective-permute-start.49 = (bf16[2,4,64,576]{3,2,1,0:T(8,128)(2,1)S(1)}, bf16[2,4,64,576]{3,2,1,0:T(8,128)(2,1)S(1)}, u32[]{:S(2)}, u32[]{:S(2)}) collective-permute-start(bf16[2,4,64,576]{3,2,1,0:T(8,128)(2,1)S(1)} %get-tuple-element.168), channel_id=1, source_target_pairs={{0,8},{8,0},{16,24},{24,16},{1,9},{9,1},{17,25},{25,17},{2,10},{10... | collective-permute-start | bytes 1769480 | tf_op jit(solution)/shard_map/ppermute | solution.py:32
  120.6 30.7 %collective-permute-start.47 = (bf16[2,4,64,576]{3,2,1,0:T(8,128)(2,1)S(1)}, bf16[2,4,64,576]{3,2,1,0:T(8,128)(2,1)S(1)}, u32[]{:S(2)}, u32[]{:S(2)}) collective-permute-start(bf16[2,4,64,576]{3,2,1,0:T(8,128)(2,1)S(1)} %get-tuple-element.164), channel_id=1, source_target_pairs={{0,8},{8,0},{16,24},{24,16},{1,9},{9,1},{17,25},{25,17},{2,10},{10... | collective-permute-start | bytes 1769480 | tf_op jit(solution)/shard_map/ppermute | solution.py:32
  122.4 31.5 %collective-permute-start.22 = (bf16[256,256]{1,0:T(8,128)(2,1)S(1)}, bf16[256,256]{1,0:T(8,128)(2,1)S(1)}, u32[]{:S(2)}, u32[]{:S(2)}) collective-permute-start(bf16[256,256]{1,0:T(8,128)(2,1)S(1)} %get-tuple-element.121), channel_id=1, source_target_pairs={{0,1},{1,0},{2,3},{3,2},{4,5},{5,4},{6,7},{7,6},{8,9},{9,8},{10,11... | collective-permute-start | bytes 393224 | tf_op jit(solution)/shard_map/ppermute | solution.py:32
  125.3 30.3 %collective-permute-start.23 = (bf16[256,256]{1,0:T(8,128)(2,1)S(1)}, bf16[256,256]{1,0:T(8,128)(2,1)S(1)}, u32[]{:S(2)}, u32[]{:S(2)}) collective-permute-start(bf16[256,256]{1,0:T(8,128)(2,1)S(1)} %get-tuple-element.122), channel_id=1, source_target_pairs={{0,2},{1,3},{2,0},{3,1},{4,6},{5,7},{6,4},{7,5},{8,10},{9,11},{10,... | collective-permute-start | bytes 393224 | tf_op jit(solution)/shard_map/ppermute | solution.py:32
  126.4 29.6 %collective-permute-start.24 = (bf16[256,256]{1,0:T(8,128)(2,1)S(1)}, bf16[256,256]{1,0:T(8,128)(2,1)S(1)}, u32[]{:S(2)}, u32[]{:S(2)}) collective-permute-start(bf16[256,256]{1,0:T(8,128)(2,1)S(1)} %get-tuple-element.123), channel_id=1, source_target_pairs={{0,3},{1,2},{2,1},{3,0},{4,7},{5,6},{6,5},{7,4},{8,11},{9,10},{10,... | collective-permute-start | bytes 393224 | tf_op jit(solution)/shard_map/ppermute | solution.py:32
  139.3 29.3 %collective-permute-start.35 = (bf16[256,1024]{1,0:T(8,128)(2,1)S(1)}, bf16[256,1024]{1,0:T(8,128)(2,1)S(1)}, u32[]{:S(2)}, u32[]{:S(2)}) collective-permute-start(bf16[256,1024]{1,0:T(8,128)(2,1)S(1)} %get-tuple-element.142), channel_id=1, source_target_pairs={{0,4},{4,0},{1,5},{5,1},{2,6},{6,2},{3,7},{7,3},{8,12},{12,8},{9,1... | collective-permute-start | bytes 1572872 | tf_op jit(solution)/shard_map/ppermute | solution.py:32
  151.3 17.2 %collective-permute-start.55 = (bf16[4,64,576]{2,1,0:T(8,128)(2,1)S(1)}, bf16[4,64,576]{2,1,0:T(8,128)(2,1)S(1)}, u32[]{:S(2)}, u32[]{:S(2)}) collective-permute-start(bf16[4,64,576]{2,1,0:T(8,128)(2,1)S(1)} %fusion.2), channel_id=1, source_target_pairs={{0,16},{8,24},{16,0},{24,8},{1,17},{9,25},{17,1},{25,9},{2,18},{10... | collective-permute-start | bytes 884744 | tf_op jit(solution)/shard_map/ppermute | solution.py:32
  153.9 19.1 %collective-permute-start.41 = (bf16[2,4,72,384]{3,2,1,0:T(8,128)(2,1)S(1)}, bf16[2,4,72,384]{3,2,1,0:T(8,128)(2,1)S(1)}, u32[]{:S(2)}, u32[]{:S(2)}) collective-permute-start(bf16[2,4,72,384]{3,2,1,0:T(8,128)(2,1)S(1)} %get-tuple-element.149), channel_id=1, source_target_pairs={{0,8},{8,0},{16,24},{24,16},{1,9},{9,1},{17,25},{25,17},{2,10},{10... | collective-permute-start | bytes 1327112 | tf_op jit(solution)/shard_map/ppermute | solution.py:32
  155.6 49.0 %collective-permute-start.50 = (bf16[4,64,576]{2,1,0:T(8,128)(2,1)S(1)}, bf16[4,64,576]{2,1,0:T(8,128)(2,1)S(1)}, u32[]{:S(2)}, u32[]{:S(2)}) collective-permute-start(bf16[4,64,576]{2,1,0:T(8,128)(2,1)S(1)} %fusion.1), channel_id=1, source_target_pairs={{0,16},{8,24},{16,0},{24,8},{1,17},{9,25},{17,1},{25,9},{2,18},{10... | collective-permute-start | bytes 884744 | tf_op jit(solution)/shard_map/ppermute | solution.py:32
  155.9 12.7 %collective-permute-start.36 = (f32[8,256]{1,0:T(8,128)S(1)}, f32[8,256]{1,0:T(8,128)S(1)}, u32[]{:S(2)}, u32[]{:S(2)}) collective-permute-start(f32[8,256]{1,0:T(8,128)S(1)} %slice.126), channel_id=1, source_target_pairs={{0,4},{4,0},{1,5},{5,1},{2,6},{6,2},{3,7},{7,3},{8,12},{12,8},{9,1... | collective-permute-start | bytes 24584 | tf_op jit(solution)/shard_map/ppermute | solution.py:32
  168.5 11.4 %collective-permute-start.25 = (bf16[256,256]{1,0:T(8,128)(2,1)S(1)}, bf16[256,256]{1,0:T(8,128)(2,1)S(1)}, u32[]{:S(2)}, u32[]{:S(2)}) collective-permute-start(bf16[256,256]{1,0:T(8,128)(2,1)S(1)} %add_convert_fusion.4), channel_id=1, source_target_pairs={{0,4},{4,0},{1,5},{5,1},{2,6},{6,2},{3,7},{7,3},{8,12},{12,8},{9,1... | collective-permute-start | bytes 393224 | tf_op jit(solution)/shard_map/ppermute | solution.py:32
  175.4 30.4 %collective-permute-start.48 = (bf16[4,64,576]{2,1,0:T(8,128)(2,1)S(1)}, bf16[4,64,576]{2,1,0:T(8,128)(2,1)S(1)}, u32[]{:S(2)}, u32[]{:S(2)}) collective-permute-start(bf16[4,64,576]{2,1,0:T(8,128)(2,1)S(1)} %fusion), channel_id=1, source_target_pairs={{0,16},{8,24},{16,0},{24,8},{1,17},{9,25},{17,1},{25,9},{2,18},{10... | collective-permute-start | bytes 884744 | tf_op jit(solution)/shard_map/ppermute | solution.py:32
  177.1 29.3 %collective-permute-start.56 = (bf16[64,576]{1,0:T(8,128)(2,1)S(1)}, bf16[64,576]{1,0:T(8,128)(2,1)S(1)}, u32[]{:S(2)}, u32[]{:S(2)}) collective-permute-start(bf16[64,576]{1,0:T(8,128)(2,1)S(1)} %get-tuple-element.177), channel_id=1, source_target_pairs={{0,1},{1,0},{2,3},{3,2},{4,5},{5,4},{6,7},{7,6},{8,9},{9,8},{10,11... | collective-permute-start | bytes 221192 | tf_op jit(solution)/shard_map/ppermute | solution.py:32
  179.9 28.2 %collective-permute-start.57 = (bf16[64,576]{1,0:T(8,128)(2,1)S(1)}, bf16[64,576]{1,0:T(8,128)(2,1)S(1)}, u32[]{:S(2)}, u32[]{:S(2)}) collective-permute-start(bf16[64,576]{1,0:T(8,128)(2,1)S(1)} %get-tuple-element.178), channel_id=1, source_target_pairs={{0,2},{1,3},{2,0},{3,1},{4,6},{5,7},{6,4},{7,5},{8,10},{9,11},{10,... | collective-permute-start | bytes 221192 | tf_op jit(solution)/shard_map/ppermute | solution.py:32
  179.9 24.5 %collective-permute-start.42 = (bf16[4,72,384]{2,1,0:T(8,128)(2,1)S(1)}, bf16[4,72,384]{2,1,0:T(8,128)(2,1)S(1)}, u32[]{:S(2)}, u32[]{:S(2)}) collective-permute-start(bf16[4,72,384]{2,1,0:T(8,128)(2,1)S(1)} %fusion.7), channel_id=1, source_target_pairs={{0,16},{8,24},{16,0},{24,8},{1,17},{9,25},{17,1},{25,9},{2,18},{10... | collective-permute-start | bytes 663560 | tf_op jit(solution)/shard_map/ppermute | solution.py:32
  204.5 17.7 %collective-permute-start.40 = (f32[256,256]{1,0:T(8,128)S(1)}, f32[256,256]{1,0:T(8,128)S(1)}, u32[]{:S(2)}, u32[]{:S(2)}) collective-permute-start(f32[256,256]{1,0:T(8,128)S(1)} %fusion.6), channel_id=1, source_target_pairs={{0,4},{4,0},{1,5},{5,1},{2,6},{6,2},{3,7},{7,3},{8,12},{12,8},{9,1... | collective-permute-start | bytes 786440 | tf_op jit(solution)/shard_map/ppermute | solution.py:32
  (46 other events, 605.1 us)

commit v8 on v7

--- a/solution.py
+++ b/solution.py
@@ -114,17 +114,14 @@
         out[half + 16 :, q_size:] = jnp.concatenate(both, axis=1)
 
 
-def pack_two_kernel(
-    where, weight_in, cot_in, out0, out1, out2, out3, weight, cot, semaphores
-):
-    fetched((weight_in, cot_in), (weight, cot), semaphores)
+def pack_two_kernel(where, weight_in, out0, out1, out2, out3, weight, semaphores):
+    fetched((weight_in,), (weight,), semaphores)
     outs = (out0, out1, out2, out3)
-    size, half = weight.shape[0] // len(outs), cot.shape[0] // 2
+    size = weight.shape[0] // len(outs)
     for k, out in enumerate(outs):
-        out[:half, :] = cot[pl.ds(pl.multiple_of(where[0] * half, half), half), :]
         for j in range(len(outs)):
             source = pl.multiple_of((where[1] ^ (k ^ j)) * size, size)
-            out[half + j * size : half + (j + 1) * size, :] = weight[pl.ds(source, size), :]
+            out[j * size : (j + 1) * size, :] = weight[pl.ds(source, size), :]
 
 
 def pack_three_kernel(where, down_in, out0, out1, out2, out3, down, semaphores):
@@ -657,13 +654,13 @@
     inner_size = output_weight.shape[0]
     two_out = kernel_call(
         pack_two_kernel,
-        [((half + inner_size, part), BF16)] * cols,
+        [((inner_size, part), BF16)] * cols,
         output_weight,
-        cotangent,
         placed=True,
-        fetch=2,
+        fetch=1,
     )
     second_parts = exchange(two_out)
+    cot_parts = spread(lax.dynamic_slice_in_dim(cotangent, row * half, half, 0))
     three_out = kernel_call(
         pack_three_kernel,
         [((units, part), BF16)] * cols,
@@ -709,7 +706,7 @@
     context_far = flip(context_near, "row", 1)
     (second_in,) = kernel_call(join_kernel, [((inner_size, width), BF16)], *second_parts, room=10)
     second_far = flip(second_in, "row", 1)
-    (cot_mine,) = kernel_call(join_first_kernel, [((half, width), BF16)], *second_parts, room=10)
+    (cot_mine,) = kernel_call(join_first_kernel, [((half, width), BF16)], *cot_parts, room=10)
     cot_other = flip(cot_mine, "row", 1)
 
     share = half // cols

time: 223 us -> 232 us (1.040)
  waiting for transfers between devices: 126 us -> 114 us
  local copies, waits for them, and re-layouts: 2.33 us -> 10.9 us
  starting transfers between devices: 57 us -> 62.5 us
  other arithmetic: 4.12 us -> 8.21 us
    ppermute x59 -> x62, waiting for transfers between devices: 126 us -> 114 us  [flip(): return lax.ppermute(values, axis, [(i, i ^ distance) for i in range(size)])]
    unnamed x32 -> x46, local copies, waits for them, and re-layouts: 1.97 us -> 7.66 us
    ppermute x59 -> x62, starting transfers between devices: 57 us -> 62.5 us  [flip(): return lax.ppermute(values, axis, [(i, i ^ distance) for i in range(size)])]
  transfers between devices with their start and end apart: 59 -> 62, of which waited for: 30 -> 26; matrix products, arithmetic and copies ran while one was open for 2% -> 5% of each run, Pallas kernels for 11% -> 12%
where the time goes in v8:
time: 232 us; the launch traced here: 231 us
  waiting for transfers between devices  114 us (49%)
  starting transfers between devices  62.5 us (27%)
  Pallas kernels  34.3 us (15%)
  local copies, waits for them, and re-layouts  10.9 us (5%)
  other arithmetic  8.21 us (4%)
    ppermute x62, waiting for transfers between devices, flip(): return lax.ppermute(values, axis, [(i, i ^ distance) for i in range(size)])  114 us
    ppermute x62, starting transfers between devices, flip(): return lax.ppermute(values, axis, [(i, i ^ distance) for i in range(size)])  62.5 us
    pallas_call x28, Pallas kernels, kernel_call(): pl.pallas_call(kernel, out_shape=[jax.ShapeDtypeStruct(shape, dtype) for...  34.3 us
    unnamed x46, local copies, waits for them, and re-layouts  7.66 us
  transfers between devices with their start and end apart: 62, of which 26 were waited for; matrix products, arithmetic and copies ran while one was open for 5% of the time, Pallas kernels for 12%

profile of v8, /device:TPU:0, one launch (start us, length us, event | category | flops | bytes accessed | tf_op | source)
XLA Modules:
  0.0 231.0 jit_solution(2574899302720657095)
XLA Ops:
  0.7 3.3 %shard_map.246 = (bf16[528,256]{1,0:T(8,128)(2,1)}, bf16[528,256]{1,0:T(8,128)(2,1)}, bf16[528,256]{1,0:T(8,128)(2,1)}, bf16[528,256]{1,0:T(8,128)(2,1)}) custom-call(bf16[512,256]{1,0:T(8,128)(2,1)} %refs_0_.4, bf16[256,512]{1,0:T(8,128)(2,1)} %refs_1_.2, bf16[256,256]{1,0:T(8,128)(2,1)} %refs_2_.1, bf16[256,256]{1,0:T(8,128)(2,1)} %refs_3_.1, ...), custom_call_target="tpu_custom_call" | custom-call | tf_op jit(solution)/shard_map/pallas_call | solution.py:63
  4.0 3.0 %collective-permute-start = (bf16[528,256]{1,0:T(8,128)(2,1)}, bf16[528,256]{1,0:T(8,128)(2,1)S(1)}, u32[]{:S(2)}, u32[]{:S(2)}) collective-permute-start(bf16[528,256]{1,0:T(8,128)(2,1)} %get-tuple-element.98), channel_id=1, source_target_pairs={{0,1},{1,0},{2,3},{3,2},{4,5},{5,4},{6,7},{7,6},{8,9},{9,8},{10,11... | collective-permute-start | bytes 811016 | tf_op jit(solution)/shard_map/ppermute | solution.py:32
  11.1 2.9 %collective-permute-start.10 = (bf16[512,256]{1,0:T(8,128)(2,1)}, bf16[512,256]{1,0:T(8,128)(2,1)S(1)}, u32[]{:S(2)}, u32[]{:S(2)}) collective-permute-start(bf16[512,256]{1,0:T(8,128)(2,1)} %get-tuple-element.105), channel_id=1, source_target_pairs={{0,3},{1,2},{2,1},{3,0},{4,7},{5,6},{6,5},{7,4},{8,11},{9,10},{10,... | collective-permute-start | bytes 786440 | tf_op jit(solution)/shard_map/ppermute | solution.py:32
  19.6 7.5 %collective-permute-done.1.first2.refs_8_.refs_4_ = bf16[528,256]{1,0:T(8,128)(2,1)S(1)} collective-permute-done((bf16[528,256]{1,0:T(8,128)(2,1)}, bf16[528,256]{1,0:T(8,128)(2,1)S(1)}, u32[]{:S(2)}, u32[]{:S(2)}) %collective-permute-start.1) | collective-permute-done | bytes 270368 | tf_op jit(solution)/shard_map/ppermute | solution.py:32
  28.2 3.4 %collective-permute-done.8.first1 = bf16[512,256]{1,0:T(8,128)(2,1)S(1)} collective-permute-done((bf16[512,256]{1,0:T(8,128)(2,1)}, bf16[512,256]{1,0:T(8,128)(2,1)S(1)}, u32[]{:S(2)}, u32[]{:S(2)}) %collective-permute-start.8) | collective-permute-done | bytes 262176 | tf_op jit(solution)/shard_map/ppermute | solution.py:32
  41.1 4.4 %shard_map.248 = (f32[512,256]{1,0:T(8,128)S(1)}, bf16[512,256]{1,0:T(8,128)(2,1)S(1)}, bf16[512,128]{1,0:T(8,128)(2,1)S(1)}, f32[512,128]{1,0:T(8,128)S(1)}) custom-call(bf16[256,1024]{1,0:T(8,128)(2,1)S(1)} %shard_map.247.mine.refs_0_, bf16[256,1024]{1,0:T(8,128)(2,1)S(1)} %collective-permute-done.3.other.refs_1_, bf16[528,256]{1,0:T(8,128)(2,1)S(1)} %copy-done.1, ...), custom_call_target="tpu_custom_call" | custom-call | tf_op jit(solution)/shard_map/pallas_call | solution.py:63
  45.5 2.1 collective-permute-start.4
  51.9 3.0 %collective-permute-start.28 = (bf16[256,256]{1,0:T(8,128)(2,1)}, bf16[256,256]{1,0:T(8,128)(2,1)S(1)}, u32[]{:S(2)}, u32[]{:S(2)}) collective-permute-start(bf16[256,256]{1,0:T(8,128)(2,1)} %constant_dynamic-slice_fusion.first0), channel_id=1, source_target_pairs={{0,3},{1,2},{2,1},{3,0},{4,7},{5,6},{6,5},{7,4},{8,11},{9,10},{10,... | collective-permute-start | bytes 393224 | tf_op jit(solution)/shard_map/ppermute | solution.py:32
  56.5 3.1 %collective-permute-done.5.first2 = bf16[512,128]{1,0:T(8,128)(2,1)S(1)} collective-permute-done((bf16[512,128]{1,0:T(8,128)(2,1)S(1)}, bf16[512,128]{1,0:T(8,128)(2,1)S(1)}, u32[]{:S(2)}, u32[]{:S(2)}) %collective-permute-start.5) | collective-permute-done | bytes 131104 | tf_op jit(solution)/shard_map/ppermute | solution.py:32
  63.6 3.2 %collective-permute-done.12.refs_2_.refs_9_ = bf16[256,576]{1,0:T(8,128)(2,1)S(1)} collective-permute-done((bf16[256,576]{1,0:T(8,128)(2,1)S(1)}, bf16[256,576]{1,0:T(8,128)(2,1)S(1)}, u32[]{:S(2)}, u32[]{:S(2)}) %collective-permute-start.12) | collective-permute-done | bytes 294944 | tf_op jit(solution)/shard_map/ppermute | solution.py:32
  68.4 7.2 %collective-permute-done.13.refs_3_.refs_10_ = bf16[256,576]{1,0:T(8,128)(2,1)S(1)} collective-permute-done((bf16[256,576]{1,0:T(8,128)(2,1)S(1)}, bf16[256,576]{1,0:T(8,128)(2,1)S(1)}, u32[]{:S(2)}, u32[]{:S(2)}) %collective-permute-start.13) | collective-permute-done | bytes 294944 | tf_op jit(solution)/shard_map/ppermute | solution.py:32
  79.4 4.3 %collective-permute-done.16.refs_7_.refs_14_ = bf16[256,576]{1,0:T(8,128)(2,1)S(1)} collective-permute-done((bf16[256,576]{1,0:T(8,128)(2,1)S(1)}, bf16[256,576]{1,0:T(8,128)(2,1)S(1)}, u32[]{:S(2)}, u32[]{:S(2)}) %collective-permute-start.16) | collective-permute-done | bytes 294944 | tf_op jit(solution)/shard_map/ppermute | solution.py:32
  84.4 2.8 %collective-permute-start.19 = (bf16[576,256]{1,0:T(8,128)(2,1)S(1)}, bf16[576,256]{1,0:T(8,128)(2,1)S(1)}, u32[]{:S(2)}, u32[]{:S(2)}) collective-permute-start(bf16[576,256]{1,0:T(8,128)(2,1)S(1)} %get-tuple-element.116), channel_id=1, source_target_pairs={{0,2},{1,3},{2,0},{3,1},{4,6},{5,7},{6,4},{7,5},{8,10},{9,11},{10,... | collective-permute-start | bytes 884744 | tf_op jit(solution)/shard_map/ppermute | solution.py:32
  88.7 2.7 %shard_map.252 = (bf16[512,1024]{1,0:T(8,128)(2,1)S(1)}, f32[256,256]{1,0:T(8,128)S(1)}, f32[64,1024]{1,0:T(8,128)S(1)}) custom-call(bf16[256,1024]{1,0:T(8,128)(2,1)S(1)} %shard_map.247.mine.refs_0_, bf16[256,1024]{1,0:T(8,128)(2,1)S(1)} %collective-permute-done.3.other.refs_1_, bf16[512,512]{1,0:T(8,128)(2,1)S(1)} %shard_map.249.refs_2_, ...), custom_call_target="tpu_custom_call" | custom-call | tf_op jit(solution)/shard_map/pallas_call | solution.py:63
  91.5 2.0 shard_map.254
  93.5 2.4 %collective-permute-done.19.down2.refs_6_ = bf16[576,256]{1,0:T(8,128)(2,1)S(1)} collective-permute-done((bf16[576,256]{1,0:T(8,128)(2,1)S(1)}, bf16[576,256]{1,0:T(8,128)(2,1)S(1)}, u32[]{:S(2)}, u32[]{:S(2)}) %collective-permute-start.19) | collective-permute-done | bytes 294944 | tf_op jit(solution)/shard_map/ppermute | solution.py:32
  97.8 3.2 %shard_map.259 = (bf16[512,576]{1,0:T(8,128)(2,1)S(1)}, bf16[512,576]{1,0:T(8,128)(2,1)S(1)}, bf16[256,1024]{1,0:T(8,128)(2,1)S(1)}, bf16[256,1024]{1,0:T(8,128)(2,1)S(1)}) custom-call(bf16[256,1024]{1,0:T(8,128)(2,1)S(1)} %shard_map.258.refs_0_.refs_5_, bf16[256,1024]{1,0:T(8,128)(2,1)S(1)} %collective-permute-done.29.refs_1_, ...), custom_call_target="tpu_custom_call" | custom-call | tf_op jit(solution)/shard_map/pallas_call | solution.py:63
  106.8 2.9 %collective-permute-done.31.refs_1_ = bf16[64,1024]{1,0:T(8,128)(2,1)S(1)} collective-permute-done((bf16[64,1024]{1,0:T(8,128)(2,1)S(1)}, bf16[64,1024]{1,0:T(8,128)(2,1)S(1)}, u32[]{:S(2)}, u32[]{:S(2)}) %collective-permute-start.31) | collective-permute-done | bytes 131104 | tf_op jit(solution)/shard_map/ppermute | solution.py:32
  109.7 2.3 %collective-permute-done.32.refs_2_ = bf16[64,1024]{1,0:T(8,128)(2,1)S(1)} collective-permute-done((bf16[64,1024]{1,0:T(8,128)(2,1)S(1)}, bf16[64,1024]{1,0:T(8,128)(2,1)S(1)}, u32[]{:S(2)}, u32[]{:S(2)}) %collective-permute-start.32) | collective-permute-done | bytes 131104 | tf_op jit(solution)/shard_map/ppermute | solution.py:32
  121.3 5.9 %collective-permute-done.35.refs_2_ = bf16[64,1024]{1,0:T(8,128)(2,1)S(1)} collective-permute-done((bf16[64,1024]{1,0:T(8,128)(2,1)S(1)}, bf16[64,1024]{1,0:T(8,128)(2,1)S(1)}, u32[]{:S(2)}, u32[]{:S(2)}) %collective-permute-start.35) | collective-permute-done | bytes 131104 | tf_op jit(solution)/shard_map/ppermute | solution.py:32
  131.2 2.2 collective-permute-done.57.came
  135.6 5.4 %shard_map.263 = (bf16[256,1024]{1,0:T(8,128)(2,1)S(1)}, bf16[256,1024]{1,0:T(8,128)(2,1)S(1)}, f32[8,512]{1,0:T(8,128)S(1)}, bf16[2,4,72,384]{3,2,1,0:T(8,128)(2,1)S(1)}, bf16[2,4,72,384]{3,2,1,0:T(8,128)(2,1)S(1)}) custom-call(bf16[256,1024]{1,0:T(8,128)(2,1)S(1)} %shard_map.247.mine.refs_0_, bf16[256,1024]{1,0:T(8,128)(2,1)S(1)} %collective-permute-done.3.other.refs_1_, ...), custom_call_target="tpu_custom_call" | custom-call | tf_op jit(solution)/shard_map/pallas_call | solution.py:63
  141.0 6.3 %collective-permute-done.52.came1 = bf16[2,4,64,576]{3,2,1,0:T(8,128)(2,1)S(1)} collective-permute-done((bf16[2,4,64,576]{3,2,1,0:T(8,128)(2,1)S(1)}, bf16[2,4,64,576]{3,2,1,0:T(8,128)(2,1)S(1)}, u32[]{:S(2)}, u32[]{:S(2)}) %collective-permute-start.52) | collective-permute-done | bytes 589856 | tf_op jit(solution)/shard_map/ppermute | solution.py:32
  147.5 12.0 %collective-permute-done.50.came0 = bf16[2,4,64,576]{3,2,1,0:T(8,128)(2,1)S(1)} collective-permute-done((bf16[2,4,64,576]{3,2,1,0:T(8,128)(2,1)S(1)}, bf16[2,4,64,576]{3,2,1,0:T(8,128)(2,1)S(1)}, u32[]{:S(2)}, u32[]{:S(2)}) %collective-permute-start.50) | collective-permute-done | bytes 589856 | tf_op jit(solution)/shard_map/ppermute | solution.py:32
  159.5 2.6 %collective-permute-start.58 = (bf16[4,64,576]{2,1,0:T(8,128)(2,1)S(1)}, bf16[4,64,576]{2,1,0:T(8,128)(2,1)S(1)}, u32[]{:S(2)}, u32[]{:S(2)}) collective-permute-start(bf16[4,64,576]{2,1,0:T(8,128)(2,1)S(1)} %fusion.2), channel_id=1, source_target_pairs={{0,16},{8,24},{16,0},{24,8},{1,17},{9,25},{17,1},{25,9},{2,18},{10... | collective-permute-start | bytes 884744 | tf_op jit(solution)/shard_map/ppermute | solution.py:32
  164.3 12.5 %collective-permute-done.58.far = bf16[4,64,576]{2,1,0:T(8,128)(2,1)S(1)} collective-permute-done((bf16[4,64,576]{2,1,0:T(8,128)(2,1)S(1)}, bf16[4,64,576]{2,1,0:T(8,128)(2,1)S(1)}, u32[]{:S(2)}, u32[]{:S(2)}) %collective-permute-start.58) | collective-permute-done | bytes 294944 | tf_op jit(solution)/shard_map/ppermute | solution.py:32
  178.9 2.5 %collective-permute-done.44.came = bf16[2,4,72,384]{3,2,1,0:T(8,128)(2,1)S(1)} collective-permute-done((bf16[2,4,72,384]{3,2,1,0:T(8,128)(2,1)S(1)}, bf16[2,4,72,384]{3,2,1,0:T(8,128)(2,1)S(1)}, u32[]{:S(2)}, u32[]{:S(2)}) %collective-permute-start.44) | collective-permute-done | bytes 442400 | tf_op jit(solution)/shard_map/ppermute | solution.py:32
  181.6 2.1 collective-permute-done.40
  184.8 2.9 %collective-permute-start.59 = (bf16[64,576]{1,0:T(8,128)(2,1)S(1)}, bf16[64,576]{1,0:T(8,128)(2,1)S(1)}, u32[]{:S(2)}, u32[]{:S(2)}) collective-permute-start(bf16[64,576]{1,0:T(8,128)(2,1)S(1)} %get-tuple-element.177), channel_id=1, source_target_pairs={{0,1},{1,0},{2,3},{3,2},{4,5},{5,4},{6,7},{7,6},{8,9},{9,8},{10,11... | collective-permute-start | bytes 221192 | tf_op jit(solution)/shard_map/ppermute | solution.py:32
  188.6 24.2 %collective-permute-done.45.far = bf16[4,72,384]{2,1,0:T(8,128)(2,1)S(1)} collective-permute-done((bf16[4,72,384]{2,1,0:T(8,128)(2,1)S(1)}, bf16[4,72,384]{2,1,0:T(8,128)(2,1)S(1)}, u32[]{:S(2)}, u32[]{:S(2)}) %collective-permute-start.45) | collective-permute-done | bytes 221216 | tf_op jit(solution)/shard_map/ppermute | solution.py:32
  214.2 2.2 collective-permute-start.48
  220.2 3.5 %collective-permute-start.56 = (bf16[128,576]{1,0:T(8,128)(2,1)S(1)}, bf16[128,576]{1,0:T(8,128)(2,1)S(1)}, u32[]{:S(2)}, u32[]{:S(2)}) collective-permute-start(bf16[128,576]{1,0:T(8,128)(2,1)S(1)} %get-tuple-element.172), channel_id=1, source_target_pairs={{0,3},{1,2},{2,1},{3,0},{4,7},{5,6},{6,5},{7,4},{8,11},{9,10},{10,... | collective-permute-start | bytes 442376 | tf_op jit(solution)/shard_map/ppermute | solution.py:32
  (213 shorter events, 79.6 us)
Async XLA Ops:
  4.0 15.4 %collective-permute-start = (bf16[528,256]{1,0:T(8,128)(2,1)}, bf16[528,256]{1,0:T(8,128)(2,1)S(1)}, u32[]{:S(2)}, u32[]{:S(2)}) collective-permute-start(bf16[528,256]{1,0:T(8,128)(2,1)} %get-tuple-element.98), channel_id=1, source_target_pairs={{0,1},{1,0},{2,3},{3,2},{4,5},{5,4},{6,7},{7,6},{8,9},{9,8},{10,11... | collective-permute-start | bytes 811016 | tf_op jit(solution)/shard_map/ppermute | solution.py:32
  7.0 20.1 %collective-permute-start.1 = (bf16[528,256]{1,0:T(8,128)(2,1)}, bf16[528,256]{1,0:T(8,128)(2,1)S(1)}, u32[]{:S(2)}, u32[]{:S(2)}) collective-permute-start(bf16[528,256]{1,0:T(8,128)(2,1)} %get-tuple-element.99), channel_id=1, source_target_pairs={{0,2},{1,3},{2,0},{3,1},{4,6},{5,7},{6,4},{7,5},{8,10},{9,11},{10,... | collective-permute-start | bytes 811016 | tf_op jit(solution)/shard_map/ppermute | solution.py:32
  8.5 18.6 %collective-permute-start.2 = (bf16[528,256]{1,0:T(8,128)(2,1)}, bf16[528,256]{1,0:T(8,128)(2,1)S(1)}, u32[]{:S(2)}, u32[]{:S(2)}) collective-permute-start(bf16[528,256]{1,0:T(8,128)(2,1)} %get-tuple-element.100), channel_id=1, source_target_pairs={{0,3},{1,2},{2,1},{3,0},{4,7},{5,6},{6,5},{7,4},{8,11},{9,10},{10,... | collective-permute-start | bytes 811016 | tf_op jit(solution)/shard_map/ppermute | solution.py:32
  11.1 16.4 %collective-permute-start.10 = (bf16[512,256]{1,0:T(8,128)(2,1)}, bf16[512,256]{1,0:T(8,128)(2,1)S(1)}, u32[]{:S(2)}, u32[]{:S(2)}) collective-permute-start(bf16[512,256]{1,0:T(8,128)(2,1)} %get-tuple-element.105), channel_id=1, source_target_pairs={{0,3},{1,2},{2,1},{3,0},{4,7},{5,6},{6,5},{7,4},{8,11},{9,10},{10,... | collective-permute-start | bytes 786440 | tf_op jit(solution)/shard_map/ppermute | solution.py:32
  14.0 17.6 %collective-permute-start.8 = (bf16[512,256]{1,0:T(8,128)(2,1)}, bf16[512,256]{1,0:T(8,128)(2,1)S(1)}, u32[]{:S(2)}, u32[]{:S(2)}) collective-permute-start(bf16[512,256]{1,0:T(8,128)(2,1)} %get-tuple-element.103), channel_id=1, source_target_pairs={{0,1},{1,0},{2,3},{3,2},{4,5},{5,4},{6,7},{7,6},{8,9},{9,8},{10,11... | collective-permute-start | bytes 786440 | tf_op jit(solution)/shard_map/ppermute | solution.py:32
  19.4 13.0 %collective-permute-start.9 = (bf16[512,256]{1,0:T(8,128)(2,1)S(1)}, bf16[512,256]{1,0:T(8,128)(2,1)S(1)}, u32[]{:S(2)}, u32[]{:S(2)}) collective-permute-start(bf16[512,256]{1,0:T(8,128)(2,1)S(1)} %get-tuple-element.104), channel_id=1, source_target_pairs={{0,2},{1,3},{2,0},{3,1},{4,6},{5,7},{6,4},{7,5},{8,10},{9,11},{10,... | collective-permute-start | bytes 786440 | tf_op jit(solution)/shard_map/ppermute | solution.py:32
  27.1 22.0 %collective-permute-start.26 = (bf16[256,256]{1,0:T(8,128)(2,1)}, bf16[256,256]{1,0:T(8,128)(2,1)}, u32[]{:S(2)}, u32[]{:S(2)}) collective-permute-start(bf16[256,256]{1,0:T(8,128)(2,1)} %constant_dynamic-slice_fusion.first0), channel_id=1, source_target_pairs={{0,1},{1,0},{2,3},{3,2},{4,5},{5,4},{6,7},{7,6},{8,9},{9,8},{10,11... | collective-permute-start | bytes 393224 | tf_op jit(solution)/shard_map/ppermute | solution.py:32
  27.2 13.9 %collective-permute-start.3 = (bf16[256,1024]{1,0:T(8,128)(2,1)S(1)}, bf16[256,1024]{1,0:T(8,128)(2,1)S(1)}, u32[]{:S(2)}, u32[]{:S(2)}) collective-permute-start(bf16[256,1024]{1,0:T(8,128)(2,1)S(1)} %shard_map.247.mine.refs_0_), channel_id=1, source_target_pairs={{0,4},{4,0},{1,5},{5,1},{2,6},{6,2},{3,7},{7,3},{8,12},{12,8},{9,1... | collective-permute-start | bytes 1572872 | tf_op jit(solution)/shard_map/ppermute | solution.py:32
  37.0 47.4 %collective-permute-start.11 = (bf16[512,1024]{1,0:T(8,128)(2,1)S(1)}, bf16[512,1024]{1,0:T(8,128)(2,1)}, u32[]{:S(2)}, u32[]{:S(2)}) collective-permute-start(bf16[512,1024]{1,0:T(8,128)(2,1)S(1)} %shard_map.251.refs_4_.refs_17_), channel_id=1, source_target_pairs={{0,4},{4,0},{1,5},{5,1},{2,6},{6,2},{3,7},{7,3},{8,12},{12,8},{9,1... | collective-permute-start | bytes 3145736 | tf_op jit(solution)/shard_map/ppermute | solution.py:32
  49.1 13.3 %collective-permute-start.27 = (bf16[256,256]{1,0:T(8,128)(2,1)}, bf16[256,256]{1,0:T(8,128)(2,1)S(1)}, u32[]{:S(2)}, u32[]{:S(2)}) collective-permute-start(bf16[256,256]{1,0:T(8,128)(2,1)} %constant_dynamic-slice_fusion.first0), channel_id=1, source_target_pairs={{0,2},{1,3},{2,0},{3,1},{4,6},{5,7},{6,4},{7,5},{8,10},{9,11},{10,... | collective-permute-start | bytes 393224 | tf_op jit(solution)/shard_map/ppermute | solution.py:32
  59.6 16.1 %collective-permute-start.13 = (bf16[256,576]{1,0:T(8,128)(2,1)S(1)}, bf16[256,576]{1,0:T(8,128)(2,1)S(1)}, u32[]{:S(2)}, u32[]{:S(2)}) collective-permute-start(bf16[256,576]{1,0:T(8,128)(2,1)S(1)} %get-tuple-element.110), channel_id=1, source_target_pairs={{0,2},{1,3},{2,0},{3,1},{4,6},{5,7},{6,4},{7,5},{8,10},{9,11},{10,... | collective-permute-start | bytes 884744 | tf_op jit(solution)/shard_map/ppermute | solution.py:32
  62.4 24.8 %collective-permute-start.7 = (bf16[512,512]{1,0:T(8,128)(2,1)S(1)}, bf16[512,512]{1,0:T(8,128)(2,1)S(1)}, u32[]{:S(2)}, u32[]{:S(2)}) collective-permute-start(bf16[512,512]{1,0:T(8,128)(2,1)S(1)} %shard_map.249.refs_2_), channel_id=1, source_target_pairs={{0,4},{4,0},{1,5},{5,1},{2,6},{6,2},{3,7},{7,3},{8,12},{12,8},{9,1... | collective-permute-start | bytes 1572872 | tf_op jit(solution)/shard_map/ppermute | solution.py:32
  62.4 15.9 %collective-permute-start.14 = (bf16[256,576]{1,0:T(8,128)(2,1)S(1)}, bf16[256,576]{1,0:T(8,128)(2,1)S(1)}, u32[]{:S(2)}, u32[]{:S(2)}) collective-permute-start(bf16[256,576]{1,0:T(8,128)(2,1)S(1)} %get-tuple-element.111), channel_id=1, source_target_pairs={{0,3},{1,2},{2,1},{3,0},{4,7},{5,6},{6,5},{7,4},{8,11},{9,10},{10,... | collective-permute-start | bytes 884744 | tf_op jit(solution)/shard_map/ppermute | solution.py:32
  66.8 12.0 %collective-permute-start.15 = (bf16[256,576]{1,0:T(8,128)(2,1)S(1)}, bf16[256,576]{1,0:T(8,128)(2,1)S(1)}, u32[]{:S(2)}, u32[]{:S(2)}) collective-permute-start(bf16[256,576]{1,0:T(8,128)(2,1)S(1)} %collective-permute-done.12.refs_2_.refs_9_), channel_id=1, source_target_pairs={{0,8},{8,0},{16,24},{24,16},{1,9},{9,1},{17,25},{25,17},{2,10},{10... | collective-permute-start | bytes 884744 | tf_op jit(solution)/shard_map/ppermute | solution.py:32
  78.3 19.5 %collective-permute-start.29 = (bf16[256,1024]{1,0:T(8,128)(2,1)S(1)}, bf16[256,1024]{1,0:T(8,128)(2,1)S(1)}, u32[]{:S(2)}, u32[]{:S(2)}) collective-permute-start(bf16[256,1024]{1,0:T(8,128)(2,1)S(1)} %shard_map.258.refs_0_.refs_5_), channel_id=1, source_target_pairs={{0,4},{4,0},{1,5},{5,1},{2,6},{6,2},{3,7},{7,3},{8,12},{12,8},{9,1... | collective-permute-start | bytes 1572872 | tf_op jit(solution)/shard_map/ppermute | solution.py:32
  78.9 12.5 %collective-permute-start.17 = (bf16[256,576]{1,0:T(8,128)(2,1)S(1)}, bf16[256,576]{1,0:T(8,128)(2,1)S(1)}, u32[]{:S(2)}, u32[]{:S(2)}) collective-permute-start(bf16[256,576]{1,0:T(8,128)(2,1)S(1)} %collective-permute-done.14.refs_4_.refs_11_), channel_id=1, source_target_pairs={{0,8},{8,0},{16,24},{24,16},{1,9},{9,1},{17,25},{25,17},{2,10},{10... | collective-permute-start | bytes 884744 | tf_op jit(solution)/shard_map/ppermute | solution.py:32
  115.7 17.7 %collective-permute-start.57 = (bf16[2,4,64,576]{3,2,1,0:T(8,128)(2,1)S(1)}, bf16[2,4,64,576]{3,2,1,0:T(8,128)(2,1)S(1)}, u32[]{:S(2)}, u32[]{:S(2)}) collective-permute-start(bf16[2,4,64,576]{3,2,1,0:T(8,128)(2,1)S(1)} %get-tuple-element.175), channel_id=1, source_target_pairs={{0,8},{8,0},{16,24},{24,16},{1,9},{9,1},{17,25},{25,17},{2,10},{10... | collective-permute-start | bytes 1769480 | tf_op jit(solution)/shard_map/ppermute | solution.py:32
  118.4 29.0 %collective-permute-start.52 = (bf16[2,4,64,576]{3,2,1,0:T(8,128)(2,1)S(1)}, bf16[2,4,64,576]{3,2,1,0:T(8,128)(2,1)S(1)}, u32[]{:S(2)}, u32[]{:S(2)}) collective-permute-start(bf16[2,4,64,576]{3,2,1,0:T(8,128)(2,1)S(1)} %get-tuple-element.168), channel_id=1, source_target_pairs={{0,8},{8,0},{16,24},{24,16},{1,9},{9,1},{17,25},{25,17},{2,10},{10... | collective-permute-start | bytes 1769480 | tf_op jit(solution)/shard_map/ppermute | solution.py:32
  128.7 30.8 %collective-permute-start.50 = (bf16[2,4,64,576]{3,2,1,0:T(8,128)(2,1)S(1)}, bf16[2,4,64,576]{3,2,1,0:T(8,128)(2,1)S(1)}, u32[]{:S(2)}, u32[]{:S(2)}) collective-permute-start(bf16[2,4,64,576]{3,2,1,0:T(8,128)(2,1)S(1)} %get-tuple-element.164), channel_id=1, source_target_pairs={{0,8},{8,0},{16,24},{24,16},{1,9},{9,1},{17,25},{25,17},{2,10},{10... | collective-permute-start | bytes 1769480 | tf_op jit(solution)/shard_map/ppermute | solution.py:32
  130.5 31.6 %collective-permute-start.22 = (bf16[256,256]{1,0:T(8,128)(2,1)S(1)}, bf16[256,256]{1,0:T(8,128)(2,1)S(1)}, u32[]{:S(2)}, u32[]{:S(2)}) collective-permute-start(bf16[256,256]{1,0:T(8,128)(2,1)S(1)} %get-tuple-element.121), channel_id=1, source_target_pairs={{0,1},{1,0},{2,3},{3,2},{4,5},{5,4},{6,7},{7,6},{8,9},{9,8},{10,11... | collective-permute-start | bytes 393224 | tf_op jit(solution)/shard_map/ppermute | solution.py:32
  133.3 30.4 %collective-permute-start.23 = (bf16[256,256]{1,0:T(8,128)(2,1)S(1)}, bf16[256,256]{1,0:T(8,128)(2,1)S(1)}, u32[]{:S(2)}, u32[]{:S(2)}) collective-permute-start(bf16[256,256]{1,0:T(8,128)(2,1)S(1)} %get-tuple-element.122), channel_id=1, source_target_pairs={{0,2},{1,3},{2,0},{3,1},{4,6},{5,7},{6,4},{7,5},{8,10},{9,11},{10,... | collective-permute-start | bytes 393224 | tf_op jit(solution)/shard_map/ppermute | solution.py:32
  134.1 30.1 %collective-permute-start.24 = (bf16[256,256]{1,0:T(8,128)(2,1)S(1)}, bf16[256,256]{1,0:T(8,128)(2,1)S(1)}, u32[]{:S(2)}, u32[]{:S(2)}) collective-permute-start(bf16[256,256]{1,0:T(8,128)(2,1)S(1)} %get-tuple-element.123), channel_id=1, source_target_pairs={{0,3},{1,2},{2,1},{3,0},{4,7},{5,6},{6,5},{7,4},{8,11},{9,10},{10,... | collective-permute-start | bytes 393224 | tf_op jit(solution)/shard_map/ppermute | solution.py:32
  147.4 29.5 %collective-permute-start.38 = (bf16[256,1024]{1,0:T(8,128)(2,1)S(1)}, bf16[256,1024]{1,0:T(8,128)(2,1)S(1)}, u32[]{:S(2)}, u32[]{:S(2)}) collective-permute-start(bf16[256,1024]{1,0:T(8,128)(2,1)S(1)} %get-tuple-element.142), channel_id=1, source_target_pairs={{0,4},{4,0},{1,5},{5,1},{2,6},{6,2},{3,7},{7,3},{8,12},{12,8},{9,1... | collective-permute-start | bytes 1572872 | tf_op jit(solution)/shard_map/ppermute | solution.py:32
  159.5 17.3 %collective-permute-start.58 = (bf16[4,64,576]{2,1,0:T(8,128)(2,1)S(1)}, bf16[4,64,576]{2,1,0:T(8,128)(2,1)S(1)}, u32[]{:S(2)}, u32[]{:S(2)}) collective-permute-start(bf16[4,64,576]{2,1,0:T(8,128)(2,1)S(1)} %fusion.2), channel_id=1, source_target_pairs={{0,16},{8,24},{16,0},{24,8},{1,17},{9,25},{17,1},{25,9},{2,18},{10... | collective-permute-start | bytes 884744 | tf_op jit(solution)/shard_map/ppermute | solution.py:32
  162.1 19.2 %collective-permute-start.44 = (bf16[2,4,72,384]{3,2,1,0:T(8,128)(2,1)S(1)}, bf16[2,4,72,384]{3,2,1,0:T(8,128)(2,1)S(1)}, u32[]{:S(2)}, u32[]{:S(2)}) collective-permute-start(bf16[2,4,72,384]{3,2,1,0:T(8,128)(2,1)S(1)} %get-tuple-element.149), channel_id=1, source_target_pairs={{0,8},{8,0},{16,24},{24,16},{1,9},{9,1},{17,25},{25,17},{2,10},{10... | collective-permute-start | bytes 1327112 | tf_op jit(solution)/shard_map/ppermute | solution.py:32
  163.8 49.1 %collective-permute-start.53 = (bf16[4,64,576]{2,1,0:T(8,128)(2,1)S(1)}, bf16[4,64,576]{2,1,0:T(8,128)(2,1)S(1)}, u32[]{:S(2)}, u32[]{:S(2)}) collective-permute-start(bf16[4,64,576]{2,1,0:T(8,128)(2,1)S(1)} %fusion.1), channel_id=1, source_target_pairs={{0,16},{8,24},{16,0},{24,8},{1,17},{9,25},{17,1},{25,9},{2,18},{10... | collective-permute-start | bytes 884744 | tf_op jit(solution)/shard_map/ppermute | solution.py:32
  164.2 12.7 %collective-permute-start.39 = (f32[8,256]{1,0:T(8,128)S(1)}, f32[8,256]{1,0:T(8,128)S(1)}, u32[]{:S(2)}, u32[]{:S(2)}) collective-permute-start(f32[8,256]{1,0:T(8,128)S(1)} %slice.126), channel_id=1, source_target_pairs={{0,4},{4,0},{1,5},{5,1},{2,6},{6,2},{3,7},{7,3},{8,12},{12,8},{9,1... | collective-permute-start | bytes 24584 | tf_op jit(solution)/shard_map/ppermute | solution.py:32
  183.6 29.3 %collective-permute-start.51 = (bf16[4,64,576]{2,1,0:T(8,128)(2,1)S(1)}, bf16[4,64,576]{2,1,0:T(8,128)(2,1)S(1)}, u32[]{:S(2)}, u32[]{:S(2)}) collective-permute-start(bf16[4,64,576]{2,1,0:T(8,128)(2,1)S(1)} %fusion), channel_id=1, source_target_pairs={{0,16},{8,24},{16,0},{24,8},{1,17},{9,25},{17,1},{25,9},{2,18},{10... | collective-permute-start | bytes 884744 | tf_op jit(solution)/shard_map/ppermute | solution.py:32
  184.8 29.4 %collective-permute-start.59 = (bf16[64,576]{1,0:T(8,128)(2,1)S(1)}, bf16[64,576]{1,0:T(8,128)(2,1)S(1)}, u32[]{:S(2)}, u32[]{:S(2)}) collective-permute-start(bf16[64,576]{1,0:T(8,128)(2,1)S(1)} %get-tuple-element.177), channel_id=1, source_target_pairs={{0,1},{1,0},{2,3},{3,2},{4,5},{5,4},{6,7},{7,6},{8,9},{9,8},{10,11... | collective-permute-start | bytes 221192 | tf_op jit(solution)/shard_map/ppermute | solution.py:32
  188.3 28.2 %collective-permute-start.60 = (bf16[64,576]{1,0:T(8,128)(2,1)S(1)}, bf16[64,576]{1,0:T(8,128)(2,1)S(1)}, u32[]{:S(2)}, u32[]{:S(2)}) collective-permute-start(bf16[64,576]{1,0:T(8,128)(2,1)S(1)} %get-tuple-element.178), channel_id=1, source_target_pairs={{0,2},{1,3},{2,0},{3,1},{4,6},{5,7},{6,4},{7,5},{8,10},{9,11},{10,... | collective-permute-start | bytes 221192 | tf_op jit(solution)/shard_map/ppermute | solution.py:32
  188.3 24.4 %collective-permute-start.45 = (bf16[4,72,384]{2,1,0:T(8,128)(2,1)S(1)}, bf16[4,72,384]{2,1,0:T(8,128)(2,1)S(1)}, u32[]{:S(2)}, u32[]{:S(2)}) collective-permute-start(bf16[4,72,384]{2,1,0:T(8,128)(2,1)S(1)} %fusion.7), channel_id=1, source_target_pairs={{0,16},{8,24},{16,0},{24,8},{1,17},{9,25},{17,1},{25,9},{2,18},{10... | collective-permute-start | bytes 663560 | tf_op jit(solution)/shard_map/ppermute | solution.py:32
  212.8 17.4 %collective-permute-start.43 = (f32[256,256]{1,0:T(8,128)S(1)}, f32[256,256]{1,0:T(8,128)S(1)}, u32[]{:S(2)}, u32[]{:S(2)}) collective-permute-start(f32[256,256]{1,0:T(8,128)S(1)} %fusion.6), channel_id=1, source_target_pairs={{0,4},{4,0},{1,5},{5,1},{2,6},{6,2},{3,7},{7,3},{8,12},{12,8},{9,1... | collective-permute-start | bytes 786440 | tf_op jit(solution)/shard_map/ppermute | solution.py:32
  (56 other events, 698.1 us)
